TPU v7x, 32 devices: a whole 2x2x4 slice. The times are simulated.
32 devices in a mesh: seq: 8 (over z, core), ctx: 4 (over y, x).
Axes of the slice: x: 2, y: 2, z: 4, core: 2. Of those that a mesh axis runs over, the one named last changes fastest.
Arguments:
- tokens: bfloat16 [8, 2048, 896], P('seq', 'ctx'), may hold values from -6 to 6
- attention_gain: bfloat16 [896], P('ctx'), may hold values from 0.5 to 1.5
- project_weight: bfloat16 [896, 1152], P('seq', 'ctx'), may hold values from -0.1875 to 0.1875
- project_bias: bfloat16 [1152], P('ctx'), may hold values from -1.1953125 to 1.1953125
- output_weight: bfloat16 [896, 896], P('seq', 'ctx'), may hold values from -0.75 to 0.75
- feedforward_gain: bfloat16 [896], P('ctx'), may hold values from 0.5 to 1.5
- gate_weight: bfloat16 [896, 4864], P('seq', 'ctx'), may hold values from -0.1875 to 0.1875
- up_weight: bfloat16 [896, 4864], P('seq', 'ctx'), may hold values from -0.1875 to 0.1875
- down_weight: bfloat16 [4864, 896], P('seq', 'ctx'), may hold values from -0.078125 to 0.078125
- cotangent: bfloat16 [8, 2048, 896], P('seq', 'ctx'), may hold values from -6 to 6
Outputs:
- layer_output: bfloat16 [8, 2048, 896], P('seq', 'ctx')
- tokens_gradient: float32 [8, 2048, 896], P('seq', 'ctx')
- attention_gain_gradient: float32 [896], P('ctx')
- project_weight_gradient: float32 [896, 1152], P('seq', 'ctx')
- project_bias_gradient: float32 [1152], P('ctx')
- output_weight_gradient: float32 [896, 896], P('seq', 'ctx')
- feedforward_gain_gradient: float32 [896], P('ctx')
- gate_weight_gradient: float32 [896, 4864], P('seq', 'ctx')
- up_weight_gradient: float32 [896, 4864], P('seq', 'ctx')
- down_weight_gradient: float32 [4864, 896], P('seq', 'ctx')
All inputs are finite; a program needn't handle non-finite values.
Results may differ from a plain program's by a relative error of at most 0.02.
Values may be sent and summed in bfloat16 or wider, within the bound.
No kernel may reach another device: no remote copies, remote signals or barrier semaphores. Data moves between devices by JAX's collectives and lax.ppermute only.
A program may use at most 192 MiB of HBM per device.

v0:
```python
import jax
import jax.numpy as jnp
from jax import lax
from jax.sharding import PartitionSpec as P

HEADS = 14
KV_HEADS = 2
HEAD_DIM = 64


norm_eps = 1e-06
rope_base = 1000000.0
masked_value = -1e30


def inverse_rms(tensor):
    return lax.rsqrt(jnp.mean(tensor * tensor, axis=-1, keepdims=True) + norm_eps)


def rotate(tensor, positions, forward):
    half_width = tensor.shape[-1] // 2
    steps_up = jnp.arange(half_width).astype(jnp.float32)
    frequency = jnp.power(jnp.asarray(rope_base, jnp.float32), -2.0 * steps_up / tensor.shape[-1])
    angles = positions.astype(jnp.float32)[:, None] * frequency[None, :]
    cosine = jnp.cos(angles)[:, None, :]
    sine_part = jnp.sin(angles)[:, None, :]
    first_half = tensor[..., :half_width]
    second = tensor[..., half_width:]
    if forward:
        return jnp.concatenate(
            [first_half * cosine - second * sine_part, second * cosine + first_half * sine_part],
            axis=-1,
        )
    return jnp.concatenate(
        [first_half * cosine + second * sine_part, second * cosine - first_half * sine_part],
        axis=-1,
    )


def collect(shards):
    widened = (
        lax.all_gather(shards[0], "ctx", axis=1, tiled=True),
        lax.all_gather(shards[1], "ctx", axis=1, tiled=True),
        lax.all_gather(shards[2], "ctx", axis=1, tiled=True),
        lax.all_gather(shards[3], "ctx", axis=1, tiled=True),
        lax.all_gather(shards[4], "ctx", axis=1, tiled=True),
        lax.all_gather(shards[5], "ctx", axis=1, tiled=True),
        lax.all_gather(shards[6], "ctx", axis=1, tiled=True),
        lax.all_gather(shards[7], "ctx", axis=1, tiled=True),
    )
    complete = (
        lax.all_gather(widened[0], "seq", axis=0, tiled=True),
        lax.all_gather(widened[1], "seq", axis=0, tiled=True),
        lax.all_gather(widened[2], "seq", axis=0, tiled=True),
        lax.all_gather(widened[3], "seq", axis=0, tiled=True),
        lax.all_gather(widened[4], "seq", axis=0, tiled=True),
    )
    return (
        complete[0],
        complete[1],
        complete[2],
        complete[3],
        complete[4],
        widened[5][0],
        widened[6][0],
        widened[7][0],
    )


def key_block(source, key_index, block_size):
    return lax.dynamic_slice_in_dim(source, key_index * block_size, block_size, 1)


def block_scores(query_rows, positions, keys_all, key_index, block_size):
    key_rows = key_block(keys_all, key_index, block_size)
    raw_scores = jnp.einsum(
        "sqhrd,skhd->shrqk", query_rows, key_rows, preferred_element_type=jnp.float32
    ) * HEAD_DIM ** (-0.5)
    key_pos = key_index * block_size + jnp.arange(block_size, dtype=jnp.int32)
    allowed = key_pos[None, :] <= positions[:, None]
    return (raw_scores, allowed, key_rows)


def attend_forward(query_rows, positions, keys_all, values_all):
    block_size = min(256, keys_all.shape[1])
    block_count = positions[-1] // block_size + 1
    start_max = jnp.full(
        (query_rows.shape[0], query_rows.shape[2], query_rows.shape[3], query_rows.shape[1]),
        masked_value,
        jnp.float32,
    )

    def first_pass(key_index, carry_state):
        running_max, denominator = carry_state
        raw_scores, allowed, key_rows = block_scores(
            query_rows, positions, keys_all, key_index, block_size
        )
        raw_scores = jnp.where(allowed, raw_scores, masked_value)
        new_max = jnp.maximum(running_max, jnp.max(raw_scores, axis=-1))
        denominator = denominator * jnp.exp(running_max - new_max) + jnp.sum(
            jnp.exp(raw_scores - new_max[..., None]), axis=-1
        )
        return (new_max, denominator)

    running_max, denominator = lax.fori_loop(
        0, block_count, first_pass, (start_max, jnp.zeros_like(start_max))
    )
    log_total = running_max + jnp.log(denominator)

    def second_pass(key_index, accumulated):
        raw_scores, allowed, key_rows = block_scores(
            query_rows, positions, keys_all, key_index, block_size
        )
        value_rows = key_block(values_all, key_index, block_size)
        soft_weights = jnp.where(allowed, jnp.exp(raw_scores - log_total[..., None]), 0.0)
        return accumulated + jnp.einsum(
            "shrqk,skhd->sqhrd",
            soft_weights.astype(jnp.bfloat16),
            value_rows,
            preferred_element_type=jnp.float32,
        )

    accumulated = lax.fori_loop(
        0, block_count, second_pass, jnp.zeros(query_rows.shape, jnp.float32)
    )
    return (accumulated, log_total)


def attend_backward(
    query_rows,
    positions,
    keys_all,
    values_all,
    log_total,
    row_delta,
    grad_rows,
    key_grads,
    value_grads,
):
    block_size = min(256, keys_all.shape[1])
    block_count = positions[-1] // block_size + 1
    head_scale = HEAD_DIM ** (-0.5)

    def step(key_index, carry_state):
        grad_query, key_acc, value_acc = carry_state
        raw_scores, allowed, key_rows = block_scores(
            query_rows, positions, keys_all, key_index, block_size
        )
        value_rows = key_block(values_all, key_index, block_size)
        soft_weights = jnp.where(allowed, jnp.exp(raw_scores - log_total[..., None]), 0.0)
        grad_soft = jnp.einsum(
            "sqhrd,skhd->shrqk", grad_rows, value_rows, preferred_element_type=jnp.float32
        )
        grad_scores = (soft_weights * (grad_soft - row_delta[..., None])).astype(jnp.bfloat16)
        grad_query = (
            grad_query
            + jnp.einsum(
                "shrqk,skhd->sqhrd", grad_scores, key_rows, preferred_element_type=jnp.float32
            )
            * head_scale
        )
        key_part = (
            jnp.einsum(
                "shrqk,sqhrd->skhd", grad_scores, query_rows, preferred_element_type=jnp.float32
            )
            * head_scale
        )
        value_part = jnp.einsum(
            "shrqk,sqhrd->skhd",
            soft_weights.astype(jnp.bfloat16),
            grad_rows,
            preferred_element_type=jnp.float32,
        )
        key_acc = lax.dynamic_update_slice_in_dim(
            key_acc, key_block(key_acc, key_index, block_size) + key_part, key_index * block_size, 1
        )
        value_acc = lax.dynamic_update_slice_in_dim(
            value_acc,
            key_block(value_acc, key_index, block_size) + value_part,
            key_index * block_size,
            1,
        )
        return (grad_query, key_acc, value_acc)

    return lax.fori_loop(
        0, block_count, step, (jnp.zeros(query_rows.shape, jnp.float32), key_grads, value_grads)
    )


def on_device(
    tokens,
    attention_gain,
    project_weight,
    project_bias,
    output_weight,
    feedforward_gain,
    gate_weight,
    up_weight,
    down_weight,
    cotangent,
):
    sequence_count, block_rows, model_width = tokens.shape
    ctx_place = lax.axis_index("ctx")
    half_rows = block_rows // 2
    query_width = HEADS * HEAD_DIM
    key_width = KV_HEADS * HEAD_DIM
    group_heads = HEADS // KV_HEADS

    def to_groups(tensor):
        return tensor.reshape(sequence_count, tensor.shape[1], KV_HEADS, group_heads, HEAD_DIM)

    positions = ctx_place * block_rows + jnp.arange(block_rows, dtype=jnp.int32)
    front_pos = positions[:half_rows]
    back_pos = positions[half_rows:]
    shards = (
        project_weight,
        output_weight,
        gate_weight,
        up_weight,
        down_weight,
        attention_gain[None, :],
        project_bias[None, :],
        feedforward_gain[None, :],
    )
    (
        project_full,
        output_full,
        gate_full,
        up_full,
        down_full,
        attention_full,
        bias_full,
        feedforward_full,
    ) = collect(shards)
    inputs = tokens.astype(jnp.float32)
    inverse_attention = inverse_rms(inputs)
    normed = (inputs * inverse_attention * attention_full.astype(jnp.float32)).astype(jnp.bfloat16)
    projected = jnp.einsum(
        "sbd,de->sbe", normed, project_full, preferred_element_type=jnp.float32
    ) + bias_full.astype(jnp.float32)
    queries = rotate(
        projected[..., :query_width].reshape(sequence_count, block_rows, HEADS, HEAD_DIM),
        positions,
        True,
    ).astype(jnp.bfloat16)
    key_heads = (
        rotate(
            projected[..., query_width : query_width + key_width].reshape(
                sequence_count, block_rows, KV_HEADS, HEAD_DIM
            ),
            positions,
            True,
        )
        .astype(jnp.bfloat16)
        .reshape(sequence_count, block_rows, key_width)
    )
    value_heads = projected[..., query_width + key_width :].astype(jnp.bfloat16)
    keys_all, values_all = (
        lax.all_gather(key_heads, "ctx", axis=1, tiled=True),
        lax.all_gather(value_heads, "ctx", axis=1, tiled=True),
    )
    seq_length = keys_all.shape[1]
    keys_all = keys_all.reshape(sequence_count, seq_length, KV_HEADS, HEAD_DIM)
    values_all = values_all.reshape(sequence_count, seq_length, KV_HEADS, HEAD_DIM)
    front_queries = to_groups(
        queries[:, :half_rows].reshape(sequence_count, half_rows, query_width)
    )
    back_queries = to_groups(queries[:, half_rows:].reshape(sequence_count, half_rows, query_width))
    front_out, front_total = attend_forward(front_queries, front_pos, keys_all, values_all)
    back_out, back_total = attend_forward(back_queries, back_pos, keys_all, values_all)
    front_low = front_out.reshape(sequence_count, half_rows, query_width).astype(jnp.bfloat16)
    back_low = back_out.reshape(sequence_count, half_rows, query_width).astype(jnp.bfloat16)
    mixed_heads = jnp.concatenate([front_low, back_low], axis=1)
    hidden = inputs + jnp.einsum(
        "sbe,ed->sbd", mixed_heads, output_full, preferred_element_type=jnp.float32
    )
    inverse_ffn = inverse_rms(hidden)
    normed_ffn = (hidden * inverse_ffn * feedforward_full.astype(jnp.float32)).astype(jnp.bfloat16)
    gate_value = jnp.einsum(
        "sbd,df->sbf", normed_ffn, gate_full, preferred_element_type=jnp.float32
    )
    up_value = jnp.einsum("sbd,df->sbf", normed_ffn, up_full, preferred_element_type=jnp.float32)
    sigmoid_gate = jax.nn.sigmoid(gate_value)
    active = (gate_value * sigmoid_gate * up_value).astype(jnp.bfloat16)
    layer_output = (
        hidden + jnp.einsum("sbf,fd->sbd", active, down_full, preferred_element_type=jnp.float32)
    ).astype(jnp.bfloat16)
    renewed = lax.optimization_barrier((shards, layer_output))[0]
    renewed_set = collect(renewed)
    project_back, output_back, gate_back, up_back, down_back, attention_back = (
        renewed_set[0],
        renewed_set[1],
        renewed_set[2],
        renewed_set[3],
        renewed_set[4],
        renewed_set[5],
    )
    feedforward_back = renewed_set[7]
    grad_top = cotangent.astype(jnp.float32)
    grad_down_weight = jnp.einsum(
        "sbf,sbd->fd", active, cotangent, preferred_element_type=jnp.float32
    )
    grad_active = jnp.einsum(
        "sbd,fd->sbf", cotangent, down_back, preferred_element_type=jnp.float32
    )
    grad_gate = (
        grad_active * up_value * sigmoid_gate * (1.0 + gate_value * (1.0 - sigmoid_gate))
    ).astype(jnp.bfloat16)
    grad_up = (grad_active * gate_value * sigmoid_gate).astype(jnp.bfloat16)
    grad_gate_weight = jnp.einsum(
        "sbd,sbf->df", normed_ffn, grad_gate, preferred_element_type=jnp.float32
    )
    grad_up_weight = jnp.einsum(
        "sbd,sbf->df", normed_ffn, grad_up, preferred_element_type=jnp.float32
    )
    grad_normed_ffn = jnp.einsum(
        "sbf,df->sbd", grad_gate, gate_back, preferred_element_type=jnp.float32
    ) + jnp.einsum("sbf,df->sbd", grad_up, up_back, preferred_element_type=jnp.float32)
    grad_ffn_gain = jnp.sum(grad_normed_ffn * hidden * inverse_ffn, axis=(0, 1))
    weighted_ffn = grad_normed_ffn * feedforward_back.astype(jnp.float32)
    grad_hidden = (
        grad_top
        + inverse_ffn * weighted_ffn
        - hidden
        * inverse_ffn
        * inverse_ffn
        * inverse_ffn
        * jnp.mean(weighted_ffn * hidden, axis=-1, keepdims=True)
    )
    hidden_low = grad_hidden.astype(jnp.bfloat16)
    grad_output_weight = jnp.einsum(
        "sbe,sbd->ed", mixed_heads, hidden_low, preferred_element_type=jnp.float32
    )
    grad_mixed = jnp.einsum(
        "sbd,ed->sbe", hidden_low, output_back, preferred_element_type=jnp.float32
    ).astype(jnp.bfloat16)
    grad_front = grad_mixed[:, :half_rows]
    grad_back = grad_mixed[:, half_rows:]

    def delta_of(grad_half, out_half):
        summed = jnp.sum(to_groups(grad_half).astype(jnp.float32) * out_half, axis=-1)
        return jnp.transpose(summed, (0, 2, 3, 1))

    key_grads = jnp.zeros((sequence_count, seq_length, KV_HEADS, HEAD_DIM), jnp.float32)
    value_grads = jnp.zeros((sequence_count, seq_length, KV_HEADS, HEAD_DIM), jnp.float32)
    front_dq, key_grads, value_grads = attend_backward(
        front_queries,
        front_pos,
        keys_all,
        values_all,
        front_total,
        delta_of(grad_front, front_out),
        to_groups(grad_front),
        key_grads,
        value_grads,
    )
    back_dq, key_grads, value_grads = attend_backward(
        back_queries,
        back_pos,
        keys_all,
        values_all,
        back_total,
        delta_of(grad_back, back_out),
        to_groups(grad_back),
        key_grads,
        value_grads,
    )

    def unrotate(grad_groups, half_pos):
        turned = rotate(
            grad_groups.reshape(sequence_count, grad_groups.shape[1], HEADS, HEAD_DIM),
            half_pos,
            False,
        )
        return turned.astype(jnp.bfloat16).reshape(
            sequence_count, grad_groups.shape[1], query_width
        )

    grad_queries = jnp.concatenate(
        [unrotate(front_dq, front_pos), unrotate(back_dq, back_pos)], axis=1
    )
    key_flat = key_grads.reshape(sequence_count, seq_length, key_width)
    value_flat = value_grads.reshape(sequence_count, seq_length, key_width)
    key_sum, value_sum = (
        lax.psum_scatter(
            key_flat.astype(jnp.bfloat16), "ctx", scatter_dimension=1, tiled=True
        ).astype(jnp.float32),
        lax.psum_scatter(
            value_flat.astype(jnp.bfloat16), "ctx", scatter_dimension=1, tiled=True
        ).astype(jnp.float32),
    )
    grad_keys = (
        rotate(key_sum.reshape(sequence_count, block_rows, KV_HEADS, HEAD_DIM), positions, False)
        .astype(jnp.bfloat16)
        .reshape(sequence_count, block_rows, key_width)
    )
    grad_values = value_sum.astype(jnp.bfloat16)
    grad_projected = jnp.concatenate([grad_queries, grad_keys, grad_values], axis=-1)
    grad_project_weight = jnp.einsum(
        "sbd,sbe->de", normed, grad_projected, preferred_element_type=jnp.float32
    )
    grad_project_bias = jnp.sum(grad_projected.astype(jnp.float32), axis=(0, 1))
    grad_normed = jnp.einsum(
        "sbe,de->sbd", grad_projected, project_back, preferred_element_type=jnp.float32
    )
    grad_attention_gain = jnp.sum(grad_normed * inputs * inverse_attention, axis=(0, 1))
    weighted_attention = grad_normed * attention_back.astype(jnp.float32)
    tokens_gradient = (
        grad_hidden
        + inverse_attention * weighted_attention
        - inputs
        * inverse_attention
        * inverse_attention
        * inverse_attention
        * jnp.mean(weighted_attention * inputs, axis=-1, keepdims=True)
    )
    reduced = (
        lax.psum_scatter(
            grad_project_weight.astype(jnp.bfloat16), "ctx", scatter_dimension=1, tiled=True
        ).astype(jnp.float32),
        lax.psum_scatter(
            grad_output_weight.astype(jnp.bfloat16), "ctx", scatter_dimension=1, tiled=True
        ).astype(jnp.float32),
        lax.psum_scatter(
            grad_gate_weight.astype(jnp.bfloat16), "ctx", scatter_dimension=1, tiled=True
        ).astype(jnp.float32),
        lax.psum_scatter(
            grad_up_weight.astype(jnp.bfloat16), "ctx", scatter_dimension=1, tiled=True
        ).astype(jnp.float32),
        lax.psum_scatter(
            grad_down_weight.astype(jnp.bfloat16), "ctx", scatter_dimension=1, tiled=True
        ).astype(jnp.float32),
        lax.psum_scatter(
            grad_attention_gain[None, :].astype(jnp.bfloat16),
            "ctx",
            scatter_dimension=1,
            tiled=True,
        ).astype(jnp.float32),
        lax.psum_scatter(
            grad_project_bias[None, :].astype(jnp.bfloat16), "ctx", scatter_dimension=1, tiled=True
        ).astype(jnp.float32),
        lax.psum_scatter(
            grad_ffn_gain[None, :].astype(jnp.bfloat16), "ctx", scatter_dimension=1, tiled=True
        ).astype(jnp.float32),
    )
    row_sums = (
        lax.psum_scatter(
            reduced[0].astype(jnp.bfloat16), "seq", scatter_dimension=0, tiled=True
        ).astype(jnp.float32),
        lax.psum_scatter(
            reduced[1].astype(jnp.bfloat16), "seq", scatter_dimension=0, tiled=True
        ).astype(jnp.float32),
        lax.psum_scatter(
            reduced[2].astype(jnp.bfloat16), "seq", scatter_dimension=0, tiled=True
        ).astype(jnp.float32),
        lax.psum_scatter(
            reduced[3].astype(jnp.bfloat16), "seq", scatter_dimension=0, tiled=True
        ).astype(jnp.float32),
        lax.psum_scatter(
            reduced[4].astype(jnp.bfloat16), "seq", scatter_dimension=0, tiled=True
        ).astype(jnp.float32),
    )
    vector_totals = lax.psum((reduced[5][0], reduced[6][0], reduced[7][0]), "seq")
    return (
        layer_output,
        tokens_gradient,
        vector_totals[0],
        row_sums[0],
        vector_totals[1],
        row_sums[1],
        vector_totals[2],
        row_sums[2],
        row_sums[3],
        row_sums[4],
    )


def solution(mesh):
    placed = (
        P("seq", "ctx", None),
        P("ctx"),
        P("seq", "ctx"),
        P("ctx"),
        P("seq", "ctx"),
        P("ctx"),
        P("seq", "ctx"),
        P("seq", "ctx"),
        P("seq", "ctx"),
        P("seq", "ctx", None),
    )
    return jax.shard_map(
        on_device,
        mesh=mesh,
        in_specs=placed,
        out_specs=(
            P("seq", "ctx", None),
            P("seq", "ctx", None),
            P("ctx"),
            P("seq", "ctx"),
            P("ctx"),
            P("seq", "ctx"),
            P("ctx"),
            P("seq", "ctx"),
            P("seq", "ctx"),
            P("seq", "ctx"),
        ),
        check_vma=False,
    )
```

profile of v0, /device:TPU:2, one launch (start us, length us, event | category | flops | bytes accessed | tf_op | source)
XLA Modules:
  0.0 1612.8 jit_solution(646859584879699531)
XLA Ops:
  9.4 9.1 all_gather.82
  20.4 8.5 all_gather.87
  29.9 9.0 all-gather.48.cloned.1.call-done
  42.6 25.6 %all-gather.50.cloned.1.call-done = bf16[4,1216,112]{1,2,0:T(8,128)(2,1)} async-done(((bf16[1,1216,112]{1,2,0:T(8,128)(2,1)}), bf16[4,1216,112]{1,2,0:T(8,128)(2,1)}) %all-gather.50.cloned.1.call-update) | async-done | bytes 1089552 | tf_op jit(solution)/shard_map/all_gather | solution.py:45
  80.9 8.2 all-reduce.7
  100.0 28.5 %all-gather.24.cloned.1.call-done = bf16[896,1152]{1,0:T(8,128)(2,1)} async-done(((bf16[112,1152]{1,0:T(8,128)(2,1)}), bf16[896,1152]{1,0:T(8,128)(2,1)}) %all-gather.24.cloned.1.call-update) | async-done | bytes 2064400 | tf_op jit(solution)/shard_map/all_gather | solution.py:52
  132.0 10.0 all_gather.86
  150.7 16.4 %all_gather.85 = bf16[1,2048,128]{2,1,0:T(8,128)(2,1)S(1)} all-gather(bf16[1,512,128]{2,1,0:T(8,128)(2,1)S(1)} %slice.135), channel_id=1, replica_groups=mesh['seq'=8,'ctx'=4] {'ctx'}, dimensions={1}, use_global_device_ids=true | all-gather | bytes 655360 | tf_op jit(solution)/shard_map/all_gather | solution.py:260
  179.4 8.6 while.75
  193.8 47.4 %all-gather.28.cloned.1.call-done = bf16[896,4864]{1,0:T(8,128)(2,1)} async-done(((bf16[112,4864]{1,0:T(8,128)(2,1)}), bf16[896,4864]{1,0:T(8,128)(2,1)}) %all-gather.28.cloned.1.call-update) | async-done | bytes 8716304 | tf_op jit(solution)/shard_map/all_gather | solution.py:54
  241.2 11.3 fusion.225
  252.5 73.6 %all-gather.30.cloned.1.call-done = bf16[896,4864]{1,0:T(8,128)(2,1)} async-done(((bf16[112,4864]{1,0:T(8,128)(2,1)}), bf16[896,4864]{1,0:T(8,128)(2,1)}) %all-gather.30.cloned.1.call-update) | async-done | bytes 8716304 | tf_op jit(solution)/shard_map/all_gather | solution.py:55
  326.1 13.6 multiply_convert_fusion
  339.8 71.3 %all-gather.34.cloned.1.call-done = bf16[4864,896]{1,0:T(8,128)(2,1)} async-done(((bf16[608,896]{1,0:T(8,128)(2,1)}), bf16[4864,896]{1,0:T(8,128)(2,1)}) %all-gather.34.cloned.1.call-update) | async-done | bytes 8716304 | tf_op jit(solution)/shard_map/all_gather | solution.py:56
  411.1 10.8 fusion.202
  423.3 24.7 %all-gather.36.cloned.1.call-done = bf16[608,896]{0,1:T(8,128)(2,1)} async-done(((bf16[608,224]{0,1:T(8,128)(2,1)}), bf16[608,896]{0,1:T(8,128)(2,1)}) %all-gather.36.cloned.1.call-update) | async-done | bytes 1089552 | tf_op jit(solution)/shard_map/all_gather | solution.py:46
  450.8 26.3 %all-gather.52.cloned.1.call-done = bf16[4,1216,112]{1,2,0:T(8,128)(2,1)} async-done(((bf16[1,1216,112]{1,2,0:T(8,128)(2,1)}), bf16[4,1216,112]{1,2,0:T(8,128)(2,1)}) %all-gather.52.cloned.1.call-update) | async-done | bytes 1089552 | tf_op jit(solution)/shard_map/all_gather | solution.py:44
  480.8 25.6 %all-gather.54.cloned.1.call-done = bf16[4,1216,112]{1,2,0:T(8,128)(2,1)} async-done(((bf16[1,1216,112]{1,2,0:T(8,128)(2,1)}), bf16[4,1216,112]{1,2,0:T(8,128)(2,1)}) %all-gather.54.cloned.1.call-update) | async-done | bytes 1089552 | tf_op jit(solution)/shard_map/all_gather | solution.py:45
  511.3 8.6 all-reduce.6
  520.8 9.1 all_gather.103
  530.8 62.0 %all-gather.38.cloned.1.call-done = bf16[4864,896]{1,0:T(8,128)(2,1)} async-done(((bf16[608,896]{1,0:T(8,128)(2,1)}), bf16[4864,896]{1,0:T(8,128)(2,1)}) %all-gather.38.cloned.1.call-update) | async-done | bytes 8716304 | tf_op jit(solution)/shard_map/all_gather | solution.py:56
  592.8 16.2 %fusion.186 = (bf16[512,4864]{1,0:T(8,128)(2,1)}, bf16[512,4864]{1,0:T(8,128)(2,1)}) fusion(f32[512,4864]{1,0:T(8,128)} %fusion.225, f32[512,4864]{1,0:T(8,128)} %get-tuple-element.567, bf16[4864,896]{1,0:T(8,128)(2,1)} %all-gather.38.cloned.1.call-done, bf16[1,512,896]{2,1,0:T(8,128)(2,1)} %param.31), kind=kOutput, calls=%fused_computation.152 | convolution fusion | flops 4495114240 | bytes 39518208 | tf_op jit(solution)/shard_map/sbd,fd->sbf/dot_general | solution.py:303
  609.0 68.8 %all-gather.40.cloned.1.call-done = bf16[896,4864]{1,0:T(8,128)(2,1)} async-done(((bf16[112,4864]{1,0:T(8,128)(2,1)}), bf16[896,4864]{1,0:T(8,128)(2,1)}) %all-gather.40.cloned.1.call-update) | async-done | bytes 8716304 | tf_op jit(solution)/shard_map/all_gather | solution.py:54
  677.8 10.7 fusion.226
  688.5 74.1 %all-gather.42.cloned.1.call-done = bf16[896,4864]{1,0:T(8,128)(2,1)} async-done(((bf16[112,4864]{1,0:T(8,128)(2,1)}), bf16[896,4864]{1,0:T(8,128)(2,1)}) %all-gather.42.cloned.1.call-update) | async-done | bytes 8716304 | tf_op jit(solution)/shard_map/all_gather | solution.py:55
  762.6 11.0 fusion.199
  775.5 12.9 all-gather.44.cloned.1.call-done
  794.7 20.1 %while.76 = (s32[]{:T(128)}, f32[1,256,2,7,64]{1,4,3,2,0:T(8,128)S(1)}, f32[1,2048,2,64]{1,3,2,0:T(8,128)S(1)}, f32[1,2048,2,64]{1,3,2,0:T(8,128)}, s32[]{:T(128...) while((s32[]{:T(128)}, ...), condition=%wide.region_17.18_spmd, body=%wide.region_16.17_spmd.sunk | while | flops 597000448 | bytes 22983928 | solution.py:185
  817.7 32.2 %while.77 = (s32[]{:T(128)}, f32[1,256,2,7,64]{1,4,3,2,0:T(8,128)S(1)}, f32[1,2048,2,64]{1,3,2,0:T(8,128)}, f32[1,2048,2,64]{1,3,2,0:T(8,128)}, s32[]{:T(128)}, ...) while((s32[]{:T(128)}, ...), condition=%wide.region_20.21_spmd, body=%wide.region_19.20_spmd.sunk | while | flops 597000448 | bytes 21148892 | solution.py:185
  854.3 68.9 %all_gather.105 = bf16[112,1152]{0,1:T(8,128)(2,1)S(1)} all-gather(bf16[112,288]{0,1:T(8,128)(2,1)S(1)} %copy-done.20), channel_id=1, replica_groups=mesh['seq'=8,'ctx'=4] {'ctx'}, dimensions={1}, use_global_device_ids=true | all-gather | bytes 322560 | tf_op jit(solution)/shard_map/all_gather | solution.py:42
  928.6 10.6 convolution_convert_fusion
  941.7 22.1 %reduce-scatter.34.cloned.1.call-done = bf16[1,512,128]{1,2,0:T(8,128)(2,1)} async-done(((bf16[1,2048,128]{1,2,0:T(8,128)(2,1)}), bf16[1,512,128]{1,2,0:T(8,128)(2,1)}) %reduce-scatter.34.cloned.1.call-update) | async-done | bytes 131088 | tf_op jit(solution)/shard_map/reduce_scatter | solution.py:388
  967.6 10.0 convolution_convert_fusion.2
  977.9 10.0 convolution_convert_fusion.1
  1000.8 26.9 %reduce-scatter.38.cloned.1.call-done = bf16[896,224]{0,1:T(8,128)(2,1)} async-done(((bf16[896,896]{0,1:T(8,128)(2,1)}), bf16[896,224]{0,1:T(8,128)(2,1)}) %reduce-scatter.38.cloned.1.call-update) | async-done | bytes 401424 | tf_op jit(solution)/shard_map/reduce_scatter | solution.py:421
  1029.7 90.0 %reduce-scatter.44.cloned.1.call-done = bf16[4864,224]{0,1:T(8,128)(2,1)} async-done(((bf16[4864,896]{0,1:T(8,128)(2,1)}), bf16[4864,224]{0,1:T(8,128)(2,1)}) %reduce-scatter.44.cloned.1.call-update) | async-done | bytes 2179088 | tf_op jit(solution)/shard_map/reduce_scatter | solution.py:430
  1124.1 33.7 %reduce-scatter.36.cloned.1.call-done = bf16[896,288]{0,1:T(8,128)(2,1)} async-done(((bf16[896,1152]{0,1:T(8,128)(2,1)}), bf16[896,288]{0,1:T(8,128)(2,1)}) %reduce-scatter.36.cloned.1.call-update) | async-done | bytes 516112 | tf_op jit(solution)/shard_map/reduce_scatter | solution.py:418
  1160.1 90.2 %reduce-scatter.40.cloned.1.call-done = bf16[896,1216]{0,1:T(8,128)(2,1)} async-done(((bf16[896,4864]{0,1:T(8,128)(2,1)}), bf16[896,1216]{0,1:T(8,128)(2,1)}) %reduce-scatter.40.cloned.1.call-update) | async-done | bytes 2179088 | tf_op jit(solution)/shard_map/reduce_scatter | solution.py:424
  1254.5 88.4 %reduce-scatter.42.cloned.1.call-done = bf16[896,1216]{0,1:T(8,128)(2,1)} async-done(((bf16[896,4864]{0,1:T(8,128)(2,1)}), bf16[896,1216]{0,1:T(8,128)(2,1)}) %reduce-scatter.42.cloned.1.call-update) | async-done | bytes 2179088 | tf_op jit(solution)/shard_map/reduce_scatter | solution.py:427
  1347.1 22.7 %reduce-scatter.54.cloned.1.call-done = bf16[224,1]{1,0:T(8,128)(2,1)} async-done(((bf16[896,1]{1,0:T(8,128)(2,1)}), bf16[224,1]{1,0:T(8,128)(2,1)}) %reduce-scatter.54.cloned.1.call-update) | async-done | bytes 464
  1374.1 23.1 %reduce-scatter.46.cloned.1.call-done = bf16[224,1]{1,0:T(8,128)(2,1)} async-done(((bf16[896,1]{1,0:T(8,128)(2,1)}), bf16[224,1]{1,0:T(8,128)(2,1)}) %reduce-scatter.46.cloned.1.call-update) | async-done | bytes 464
  1398.1 26.8 %reduce-scatter.50.cloned.1.call-done = bf16[288,1]{1,0:T(8,128)(2,1)} async-done(((bf16[1152,1]{1,0:T(8,128)(2,1)}), bf16[288,1]{1,0:T(8,128)(2,1)}) %reduce-scatter.50.cloned.1.call-update) | async-done | bytes 592
  1425.9 16.8 %all-reduce.5 = (f32[224]{0:T(256)}, f32[288]{0:T(512)}, f32[224]{0:T(256)}) all-reduce(f32[224]{0:T(256)S(1)} %bitcast.753, f32[288]{0:T(512)S(1)} %convert_reduce_fusion, f32[224]{0:T(256)S(1)} %bitcast.752), channel_id=1, replica_groups=mesh['seq'=8,'ctx'=4] {'seq'}, use_global_device_ids=true, to_apply=%region_26.27 | all-reduce | flops 736 | bytes 5888 | tf_op jit(solution)/shard_map/psum | solution.py:463
  1442.7 15.9 reduce-scatter.52.cloned.1.call-done
  1460.3 35.6 %reduce-scatter.60.cloned.1.call-done = bf16[608,224]{1,0:T(8,128)(2,1)} async-done(((bf16[4864,224]{1,0:T(8,128)(2,1)}), bf16[608,224]{1,0:T(8,128)(2,1)}) %reduce-scatter.60.cloned.1.call-update) | async-done | bytes 272400
  1497.9 30.9 %reduce-scatter.48.cloned.1.call-done = bf16[112,288]{1,0:T(8,128)(2,1)} async-done(((bf16[896,288]{1,0:T(8,128)(2,1)}), bf16[112,288]{1,0:T(8,128)(2,1)}) %reduce-scatter.48.cloned.1.call-update) | async-done | bytes 64528
  1530.5 35.1 %reduce-scatter.56.cloned.1.call-done = bf16[112,1216]{1,0:T(8,128)(2,1)} async-done(((bf16[896,1216]{1,0:T(8,128)(2,1)}), bf16[112,1216]{1,0:T(8,128)(2,1)}) %reduce-scatter.56.cloned.1.call-update) | async-done | bytes 272400
  1567.9 35.5 %reduce-scatter.58.cloned.1.call-done = bf16[112,1216]{1,0:T(8,128)(2,1)} async-done(((bf16[896,1216]{1,0:T(8,128)(2,1)}), bf16[112,1216]{1,0:T(8,128)(2,1)}) %reduce-scatter.58.cloned.1.call-update) | async-done | bytes 272400
  (381 shorter events, 218.4 us)
Async XLA Ops:
  7.2 31.7 %all-gather.48.cloned.1.call-start = ((), (), s32[]{:S(2)}) async-start(), calls=%async_computation.34 | async-start | bytes 1433600 | tf_op jit(solution)/shard_map/all_gather | solution.py:44
  7.9 60.3 %all-gather.50.cloned.1.call-start = ((), (), s32[]{:S(2)}) async-start(), calls=%async_computation.35 | async-start | bytes 1433600 | tf_op jit(solution)/shard_map/all_gather | solution.py:45
  8.7 88.9 %all-gather.32.cloned.1.call-start = ((), (), s32[]{:S(2)}) async-start(), calls=%async_computation.19 | async-start | bytes 1433600 | tf_op jit(solution)/shard_map/all_gather | solution.py:46
  9.4 119.1 %all-gather.24.cloned.1.call-start = ((), (), s32[]{:S(2)}) async-start(), calls=%async_computation.15 | async-start | bytes 2322432 | tf_op jit(solution)/shard_map/all_gather | solution.py:52
  19.5 169.5 %all-gather.26.cloned.1.call-start = ((), (), s32[]{:S(2)}) async-start(), calls=%async_computation.16 | async-start | bytes 1806336 | tf_op jit(solution)/shard_map/all_gather | solution.py:53
  29.8 211.4 %all-gather.28.cloned.1.call-start = ((), (), s32[]{:S(2)}) async-start(), calls=%async_computation.17 | async-start | bytes 9805824 | tf_op jit(solution)/shard_map/all_gather | solution.py:54
  42.5 35.2 %copy-start.32 = (bf16[224]{0:T(256)(128)(2,1)S(1)}, bf16[224]{0:T(256)(128)(2,1)}, u32[]{:S(2)}) copy-start(bf16[224]{0:T(256)(128)(2,1)} %param.23) | copy-start | bytes 1348
  42.5 35.7 %copy-start.33 = (bf16[224]{0:T(256)(128)(2,1)S(1)}, bf16[224]{0:T(256)(128)(2,1)}, u32[]{:S(2)}) copy-start(bf16[224]{0:T(256)(128)(2,1)} %param.27) | copy-start | bytes 1348
  42.5 35.7 %copy-start.34 = (u32[32]{0:T(128)S(1)}, u32[32]{0:T(128)}, u32[]{:S(2)}) copy-start(u32[32]{0:T(128)} %constant.149) | copy-start | bytes 388
  42.5 38.1 %copy-start.31 = (bf16[288]{0:T(512)(128)(2,1)S(1)}, bf16[288]{0:T(512)(128)(2,1)}, u32[]{:S(2)}) copy-start(bf16[288]{0:T(512)(128)(2,1)} %param.25) | copy-start | bytes 1732
  42.5 46.5 %copy-start.5 = (bf16[1,512,896]{2,1,0:T(8,128)(2,1)S(1)}, bf16[1,512,896]{2,1,0:T(8,128)(2,1)}, u32[]{:S(2)}) copy-start(bf16[1,512,896]{2,1,0:T(8,128)(2,1)} %param.22) | copy-start | bytes 2752516
  42.6 283.6 %all-gather.30.cloned.1.call-start = ((), (), s32[]{:S(2)}) async-start(), calls=%async_computation.18 | async-start | bytes 9805824 | tf_op jit(solution)/shard_map/all_gather | solution.py:55
  71.8 339.3 %all-gather.34.cloned.1.call-start = ((), (), s32[]{:S(2)}) async-start(), calls=%async_computation.20 | async-start | bytes 9805824 | tf_op jit(solution)/shard_map/all_gather | solution.py:56
  89.0 42.6 %copy-start.26 = (f32[896]{0:T(1024)}, f32[896]{0:T(1024)S(1)}, u32[]{:S(2)}) copy-start(f32[896]{0:T(1024)S(1)} %convert_element_type.439) | copy-start | bytes 10756
  89.1 42.5 %copy-start.28 = (f32[32]{0:T(128)}, f32[32]{0:T(128)S(1)}, u32[]{:S(2)}) copy-start(f32[32]{0:T(128)S(1)} %multiply_power_fusion) | copy-start | bytes 388
  89.4 42.3 %copy-start.22 = (f32[512]{0:T(512)}, f32[512]{0:T(512)S(1)}, u32[]{:S(2)}) copy-start(f32[512]{0:T(512)S(1)} %add_rsqrt_fusion.1) | copy-start | bytes 6148
  90.3 53.5 %copy-start.10 = (f32[512,32]{0,1:T(8,128)}, f32[512,32]{0,1:T(8,128)S(1)}, u32[]{:S(2)}) copy-start(f32[512,32]{0,1:T(8,128)S(1)} %get-tuple-element.550) | copy-start | bytes 196612
  90.3 53.4 %copy-start.12 = (f32[512,32]{0,1:T(8,128)}, f32[512,32]{0,1:T(8,128)S(1)}, u32[]{:S(2)}) copy-start(f32[512,32]{0,1:T(8,128)S(1)} %get-tuple-element.551) | copy-start | bytes 196612
  99.9 348.0 %all-gather.36.cloned.1.call-start = ((), (), s32[]{:S(2)}) async-start(), calls=%async_computation.21 | async-start | bytes 1433600 | tf_op jit(solution)/shard_map/all_gather | solution.py:46
  193.8 132.3 %copy-start.14 = (bf16[512,896]{1,0:T(8,128)(2,1)}, bf16[512,896]{1,0:T(8,128)(2,1)S(1)}, u32[]{:S(2)}) copy-start(bf16[512,896]{1,0:T(8,128)(2,1)S(1)} %fusion.207) | copy-start | bytes 2752516
  421.9 55.2 %all-gather.52.cloned.1.call-start = ((), (), s32[]{:S(2)}) async-start(), calls=%async_computation.36 | async-start | bytes 1433600 | tf_op jit(solution)/shard_map/all_gather | solution.py:44
  422.5 84.0 %all-gather.54.cloned.1.call-start = ((), (), s32[]{:S(2)}) async-start(), calls=%async_computation.37 | async-start | bytes 1433600 | tf_op jit(solution)/shard_map/all_gather | solution.py:45
  423.2 169.6 %all-gather.38.cloned.1.call-start = ((), (), s32[]{:S(2)}) async-start(), calls=%async_computation.22 | async-start | bytes 9805824 | tf_op jit(solution)/shard_map/all_gather | solution.py:56
  450.4 227.4 %all-gather.40.cloned.1.call-start = ((), (), s32[]{:S(2)}) async-start(), calls=%async_computation.23 | async-start | bytes 9805824 | tf_op jit(solution)/shard_map/all_gather | solution.py:54
  480.8 281.8 %all-gather.42.cloned.1.call-start = ((), (), s32[]{:S(2)}) async-start(), calls=%async_computation.24 | async-start | bytes 9805824 | tf_op jit(solution)/shard_map/all_gather | solution.py:55
  510.1 278.3 %all-gather.44.cloned.1.call-start = ((), (), s32[]{:S(2)}) async-start(), calls=%async_computation.25 | async-start | bytes 1806336 | tf_op jit(solution)/shard_map/all_gather | solution.py:53
  530.8 409.8 %reduce-scatter.32.cloned.1.call-start = ((), (), s32[]{:S(2)}) async-start(), calls=%async_computation.26 | async-start | bytes 655360 | tf_op jit(solution)/shard_map/reduce_scatter | solution.py:385
  849.9 74.3 %copy-start.19 = (bf16[1,256,2,7,64]{1,4,3,2,0:T(8,128)(2,1)S(1)}, bf16[1,256,2,7,64]{1,4,3,2,0:T(8,128)(2,1)}, u32[]{:S(2)}) copy-start(bf16[1,256,2,7,64]{1,4,3,2,0:T(8,128)(2,1)} %convert_element_type.388) | copy-start | bytes 1376260
  852.1 111.6 %reduce-scatter.34.cloned.1.call-start = ((), (), s32[]{:S(2)}) async-start(), calls=%async_computation.27 | async-start | bytes 655360 | tf_op jit(solution)/shard_map/reduce_scatter | solution.py:388
  854.2 139.9 %all-gather.46.cloned.1.call-start = ((), (), s32[]{:S(2)}) async-start(), calls=%async_computation.28 | async-start | bytes 2322432 | tf_op jit(solution)/shard_map/all_gather | solution.py:52
  924.2 103.5 %reduce-scatter.38.cloned.1.call-start = ((), (), s32[]{:S(2)}) async-start(), calls=%async_computation.30 | async-start | bytes 2007040 | tf_op jit(solution)/shard_map/reduce_scatter | solution.py:421
  928.3 191.4 %reduce-scatter.44.cloned.1.call-start = ((), (), s32[]{:S(2)}) async-start(), calls=%async_computation.33 | async-start | bytes 10895360 | tf_op jit(solution)/shard_map/reduce_scatter | solution.py:430
  939.2 218.6 %reduce-scatter.36.cloned.1.call-start = ((), (), s32[]{:S(2)}) async-start(), calls=%async_computation.29 | async-start | bytes 2580480 | tf_op jit(solution)/shard_map/reduce_scatter | solution.py:418
  940.3 23.4 %copy-start.6 = (bf16[1,512,896]{2,1,0:T(8,128)(2,1)S(1)}, bf16[1,512,896]{2,1,0:T(8,128)(2,1)}, u32[]{:S(2)}) copy-start(bf16[1,512,896]{2,1,0:T(8,128)(2,1)} %param.22) | copy-start | bytes 2752516
  940.3 23.4 %copy-start.23 = (f32[512]{0:T(512)S(1)}, f32[512]{0:T(512)}, u32[]{:S(2)}) copy-start(f32[512]{0:T(512)} %copy-done.22) | copy-start | bytes 6148
  940.4 23.4 %copy-start.27 = (f32[896]{0:T(1024)S(1)}, f32[896]{0:T(1024)}, u32[]{:S(2)}) copy-start(f32[896]{0:T(1024)} %copy-done.26) | copy-start | bytes 10756
  967.6 282.7 %reduce-scatter.40.cloned.1.call-start = ((), (), s32[]{:S(2)}) async-start(), calls=%async_computation.31 | async-start | bytes 10895360 | tf_op jit(solution)/shard_map/reduce_scatter | solution.py:424
  977.6 365.3 %reduce-scatter.42.cloned.1.call-start = ((), (), s32[]{:S(2)}) async-start(), calls=%async_computation.32 | async-start | bytes 10895360 | tf_op jit(solution)/shard_map/reduce_scatter | solution.py:427
  987.9 381.9 %reduce-scatter.54.cloned.1.call-start = ((), (), s32[]{:S(2)}) async-start(), calls=%async_computation.42 | async-start | bytes 286720
  989.5 407.7 %reduce-scatter.46.cloned.1.call-start = ((), (), s32[]{:S(2)}) async-start(), calls=%async_computation.38 | async-start | bytes 286720
  999.5 425.4 %reduce-scatter.50.cloned.1.call-start = ((), (), s32[]{:S(2)}) async-start(), calls=%async_computation.40 | async-start | bytes 368640
  1000.7 457.8 %reduce-scatter.52.cloned.1.call-start = ((), (), s32[]{:S(2)}) async-start(), calls=%async_computation.41 | async-start | bytes 516096
  1029.7 466.2 %reduce-scatter.60.cloned.1.call-start = ((), (), s32[]{:S(2)}) async-start(), calls=%async_computation.45 | async-start | bytes 2801664
  1124.0 404.8 %reduce-scatter.48.cloned.1.call-start = ((), (), s32[]{:S(2)}) async-start(), calls=%async_computation.39 | async-start | bytes 774144
  1160.0 405.7 %reduce-scatter.56.cloned.1.call-start = ((), (), s32[]{:S(2)}) async-start(), calls=%async_computation.43 | async-start | bytes 2580480
  1254.5 348.9 %reduce-scatter.58.cloned.1.call-start = ((), (), s32[]{:S(2)}) async-start(), calls=%async_computation.44 | async-start | bytes 2580480
  1342.9 27.8 %copy-start.7 = (bf16[1,512,896]{2,1,0:T(8,128)(2,1)S(1)}, bf16[1,512,896]{2,1,0:T(8,128)(2,1)}, u32[]{:S(2)}) copy-start(bf16[1,512,896]{2,1,0:T(8,128)(2,1)} %param.22) | copy-start | bytes 2752516
  1347.1 23.6 %copy-start.2 = (f32[1,512,896]{2,1,0:T(8,128)S(1)}, f32[1,512,896]{2,1,0:T(8,128)}, u32[]{:S(2)}) copy-start(f32[1,512,896]{2,1,0:T(8,128)} %fusion.201) | copy-start | bytes 5505028
  (20 other events, 59.7 us)
Sparse Core Ops, SparseCore 0:
  9.8 28.9 all-gather.47
  40.7 27.4 all-gather.49
  70.0 27.4 all-gather.31
  99.6 28.8 all-gather.23
  130.5 24.7 all-gather.25
  156.8 84.3 all-gather.27
  242.8 83.2 all-gather.29
  327.8 83.2 all-gather.33
  422.0 25.8 all-gather.35
  449.6 27.4 all-gather.51
  479.0 27.4 all-gather.53
  508.0 84.8 all-gather.37
  594.4 83.2 all-gather.39
  679.2 83.2 all-gather.41
  764.6 23.6 all-gather.43
  852.2 83.2 reduce-scatter.31
  938.9 24.7 reduce-scatter.33
  965.2 28.8 all-gather.45
  997.1 30.5 reduce-scatter.37
  1030.7 89.0 reduce-scatter.43
  1122.7 34.9 reduce-scatter.35
  1161.2 89.0 reduce-scatter.39
  1253.7 89.0 reduce-scatter.41
  1345.7 24.0 reduce-scatter.53
  1373.2 24.0 reduce-scatter.45
  1400.7 24.1 reduce-scatter.49
  1427.7 30.8 reduce-scatter.51
  1460.9 34.9 reduce-scatter.59
  1498.3 30.5 reduce-scatter.47
  1531.1 34.5 reduce-scatter.55
  1568.1 35.1 reduce-scatter.57
where the time goes:
time: 1630 us; the launch traced here: 1610 us
  waiting for transfers between devices  1140 us (70%)
  matrix products  193 us (12%)
  blocking collectives  156 us (10%)
  local copies, waits for them, and re-layouts  66.3 us (4%)
  other arithmetic  29.5 us (2%)
  between operations  22.3 us (1%)
    unnamed x39, waiting for transfers between devices  229 us
    all_gather x2, waiting for transfers between devices, collect(): lax.all_gather(widened[3], 'seq', axis=0, tiled=True)  148 us
    all_gather x2, waiting for transfers between devices, collect(): lax.all_gather(widened[4], 'seq', axis=0, tiled=True)  133 us
    all_gather x2, waiting for transfers between devices, collect(): lax.all_gather(widened[2], 'seq', axis=0, tiled=True)  116 us
    reduce_scatter x1, waiting for transfers between devices, on_device(): lax.psum_scatter(grad_gate_weight.astype(jnp.bfloat16), 'ctx', scatter_di...  90.2 us
    reduce_scatter x1, waiting for transfers between devices, on_device(): lax.psum_scatter(grad_down_weight.astype(jnp.bfloat16), 'ctx', scatter_di...  90 us
    reduce_scatter x1, waiting for transfers between devices, on_device(): lax.psum_scatter(grad_up_weight.astype(jnp.bfloat16), 'ctx', scatter_dime...  88.4 us
    all_gather x2, blocking collectives, collect(): lax.all_gather(shards[0], 'ctx', axis=1, tiled=True)  78.1 us
  transfers between devices with their start and end apart: 31, of which 29 were waited for; matrix products, arithmetic and copies ran while one was open for 13% of the time, Pallas kernels for 0%

commit v1 on v0

v1 whole, which is shorter than its diff:
```python
import math
import jax
import jax.numpy as jnp
from jax import lax
from jax.experimental import pallas as pl
from jax.experimental.pallas import tpu as pltpu
from jax.sharding import PartitionSpec as P

HEADS = 14
KV_HEADS = 2
HEAD_DIM = 64
GROUP = HEADS // KV_HEADS
PAIRS = HEADS // 2
PAIR = 2 * HEAD_DIM
Q_WIDTH = HEADS * HEAD_DIM
K_WIDTH = KV_HEADS * HEAD_DIM

norm_eps = 1e-06
rope_base = 1000000.0
masked_value = -1e30
score_scale = HEAD_DIM ** (-0.5)
log2_e = math.log2(math.e)
bf16 = jnp.bfloat16
f32 = jnp.float32


def inverse_rms(tensor):
    return lax.rsqrt(jnp.mean(tensor * tensor, axis=-1, keepdims=True) + norm_eps)


def rotate(tensor, positions, forward):
    half_width = tensor.shape[-1] // 2
    steps_up = jnp.arange(half_width).astype(f32)
    frequency = jnp.power(jnp.asarray(rope_base, f32), -2.0 * steps_up / tensor.shape[-1])
    angles = positions.astype(f32)[:, None] * frequency[None, :]
    cosine = jnp.cos(angles)[:, None, :]
    sine_part = jnp.sin(angles)[:, None, :]
    if not forward:
        sine_part = -sine_part
    first_half = tensor[..., :half_width]
    second = tensor[..., half_width:]
    return jnp.concatenate(
        [first_half * cosine - second * sine_part, second * cosine + first_half * sine_part],
        axis=-1,
    )


def dot(a, b, dims):
    return lax.dot_general(a, b, (dims, ((), ())), preferred_element_type=f32)


NN = ((1,), (0,))
NT = ((1,), (1,))
TN = ((0,), (0,))


def pair_sides(x, x_swapped):
    low = lax.broadcasted_iota(jnp.int32, x.shape, 1) < HEAD_DIM
    zero = jnp.zeros_like(x)
    left = (jnp.where(low, x, zero), jnp.where(low, x_swapped, zero))
    right = (jnp.where(low, zero, x_swapped), jnp.where(low, zero, x))
    sides = {}
    for pair in range(PAIRS):
        key = (2 * pair // GROUP, (2 * pair + 1) // GROUP)
        if key not in sides:
            sides[key] = jnp.concatenate([left[key[0]], right[key[1]]], axis=0)
    return sides


def forward_kernel(place_ref, q_ref, k_ref, vt_ref, o_ref, lse_ref, top_ref, total_ref, acc_ref):
    block = q_ref.shape[1]
    last = place_ref[pl.program_id(0) % 2]
    top_ref[...] = jnp.full_like(top_ref, masked_value)
    total_ref[...] = jnp.zeros_like(total_ref)
    acc_ref[...] = jnp.zeros_like(acc_ref)
    scale = score_scale * log2_e

    def step(index, diagonal):
        start = pl.multiple_of(index * block, block)
        sides = pair_sides(
            k_ref[0, pl.ds(start, block), :PAIR], k_ref[0, pl.ds(start, block), PAIR:]
        )
        values = vt_ref[0, index]
        if diagonal:
            key_at = lax.broadcasted_iota(jnp.int32, (block, block), 0)
            query_at = lax.broadcasted_iota(jnp.int32, (block, block), 1)
            allowed = key_at <= query_at
        for pair in range(PAIRS):
            both = dot(
                sides[(2 * pair // GROUP, (2 * pair + 1) // GROUP)],
                q_ref[0, :, pair * PAIR : (pair + 1) * PAIR],
                NT,
            )
            for odd in range(2):
                head = 2 * pair + odd
                kv = head // GROUP
                scores = both[odd * block : (odd + 1) * block] * scale
                if diagonal:
                    scores = jnp.where(allowed, scores, masked_value)
                old = top_ref[head : head + 1, :]
                new = jnp.maximum(old, jnp.max(scores, axis=0, keepdims=True))
                shrink = jnp.exp2(old - new)
                weights = jnp.exp2(scores - new)
                top_ref[head : head + 1, :] = new
                total_ref[head : head + 1, :] = total_ref[
                    head : head + 1, :
                ] * shrink + jnp.sum(weights, axis=0, keepdims=True)
                rows = slice(head * HEAD_DIM, (head + 1) * HEAD_DIM)
                acc_ref[rows, :] = acc_ref[rows, :] * shrink + dot(
                    values[kv * HEAD_DIM : (kv + 1) * HEAD_DIM], weights.astype(bf16), NN
                )

    def body(index, carry):
        step(index, False)
        return carry

    lax.fori_loop(0, last, body, 0)
    step(last, True)
    for pair in range(PAIRS):
        parts = []
        for odd in range(2):
            head = 2 * pair + odd
            parts.append(
                acc_ref[head * HEAD_DIM : (head + 1) * HEAD_DIM, :]
                / total_ref[head : head + 1, :]
            )
        o_ref[0, :, pair * PAIR : (pair + 1) * PAIR] = jnp.transpose(
            jnp.concatenate(parts, axis=0)
        ).astype(bf16)
    lse_ref[0] = top_ref[...] + jnp.log2(total_ref[...])


def backward_kernel(
    place_ref, q_ref, k_ref, v_ref, kt_ref, o_ref, g_ref, lse_ref, dq_ref, dk_ref, dv_ref, acc_ref
):
    block = q_ref.shape[1]
    last = place_ref[pl.program_id(0) % 2]
    scale = score_scale * log2_e

    @pl.when(pl.program_id(0) % 2 == 0)
    def _():
        dk_ref[...] = jnp.zeros_like(dk_ref)
        dv_ref[...] = jnp.zeros_like(dv_ref)

    acc_ref[...] = jnp.zeros_like(acc_ref)
    product = g_ref[0].astype(f32) * o_ref[0].astype(f32)
    coarse = product.astype(bf16)
    fine = (product - coarse.astype(f32)).astype(bf16)
    head_of = lax.broadcasted_iota(jnp.int32, (16, Q_WIDTH), 1) // HEAD_DIM
    picks = (head_of == lax.broadcasted_iota(jnp.int32, (16, Q_WIDTH), 0)).astype(bf16)
    delta = dot(picks, coarse, NT) + dot(picks, fine, NT)

    def step(index, diagonal):
        start = pl.multiple_of(index * block, block)
        key_sides = pair_sides(
            k_ref[0, pl.ds(start, block), :PAIR], k_ref[0, pl.ds(start, block), PAIR:]
        )
        value_sides = pair_sides(
            v_ref[0, pl.ds(start, block), :PAIR], v_ref[0, pl.ds(start, block), PAIR:]
        )
        keys_turned = kt_ref[0, index]
        if diagonal:
            key_at = lax.broadcasted_iota(jnp.int32, (block, block), 0)
            query_at = lax.broadcasted_iota(jnp.int32, (block, block), 1)
            allowed = key_at <= query_at
        key_sum = [[None, None], [None, None]]
        value_sum = [[None, None], [None, None]]

        def add(sums, odd, kv, part):
            sums[odd][kv] = part if sums[odd][kv] is None else sums[odd][kv] + part

        for pair in range(PAIRS):
            which = (2 * pair // GROUP, (2 * pair + 1) // GROUP)
            lanes = slice(pair * PAIR, (pair + 1) * PAIR)
            queries = q_ref[0, :, lanes]
            grads = g_ref[0, :, lanes]
            both = dot(key_sides[which], queries, NT)
            both_grads = dot(value_sides[which], grads, NT)
            low_weights = []
            low_scores = []
            for odd in range(2):
                head = 2 * pair + odd
                part = slice(odd * block, (odd + 1) * block)
                weights = jnp.exp2(both[part] * scale - lse_ref[0, head : head + 1, :])
                if diagonal:
                    weights = jnp.where(allowed, weights, 0.0)
                change = weights * (both_grads[part] - delta[head : head + 1, :])
                low_weights.append(weights.astype(bf16))
                low_scores.append(change.astype(bf16))
                rows = slice(head * HEAD_DIM, (head + 1) * HEAD_DIM)
                acc_ref[rows, :] += dot(
                    keys_turned[which[odd] * HEAD_DIM : (which[odd] + 1) * HEAD_DIM],
                    low_scores[odd],
                    NN,
                )
            value_part = dot(jnp.concatenate(low_weights, axis=0), grads, NN)
            key_part = dot(jnp.concatenate(low_scores, axis=0), queries, NN)
            for odd in range(2):
                part = slice(odd * block, (odd + 1) * block)
                add(value_sum, odd, which[odd], value_part[part])
                add(key_sum, odd, which[odd], key_part[part])
        low = lax.broadcasted_iota(jnp.int32, (block, PAIR), 1) < HEAD_DIM
        rows = pl.ds(start, block)
        for sums, out_ref, factor in ((key_sum, dk_ref, score_scale), (value_sum, dv_ref, 1.0)):
            straight = jnp.where(low, sums[0][0], sums[1][1])
            crossed = jnp.where(low, sums[0][1], sums[1][0])
            out_ref[0, rows, :PAIR] += straight * factor
            out_ref[0, rows, PAIR:] += crossed * factor

    def body(index, carry):
        step(index, False)
        return carry

    lax.fori_loop(0, last, body, 0)
    step(last, True)
    for pair in range(PAIRS):
        dq_ref[0, :, pair * PAIR : (pair + 1) * PAIR] = (
            jnp.transpose(acc_ref[pair * PAIR : (pair + 1) * PAIR, :]) * score_scale
        )


def swap_heads(x):
    return jnp.concatenate([x[..., HEAD_DIM:], x[..., :HEAD_DIM]], axis=-1)


def attention_specs(count, block, length):
    def rows(width):
        return pl.BlockSpec((1, block, width), lambda i, place: (i, 0, 0))

    def whole(height, width):
        return pl.BlockSpec((1, height, width), lambda i, place: (i // 2, 0, 0))

    turned = pl.BlockSpec((1, length // block, PAIR, block), lambda i, place: (i // 2, 0, 0, 0))
    stats = pl.BlockSpec((1, 16, block), lambda i, place: (i, 0, 0))
    return rows, whole, turned, stats


def attend_forward(places, queries, keys_both, values_turned):
    count, block, _ = queries.shape
    length = keys_both.shape[1]
    rows, whole, turned, stats = attention_specs(count, block, length)
    pairs_done = count * block * (length // 2 + block) * HEADS
    return pl.pallas_call(
        forward_kernel,
        grid_spec=pltpu.PrefetchScalarGridSpec(
            num_scalar_prefetch=1,
            grid=(count,),
            in_specs=[rows(Q_WIDTH), whole(length, 2 * PAIR), turned],
            out_specs=[rows(Q_WIDTH), stats],
            scratch_shapes=[
                pltpu.VMEM((16, block), f32),
                pltpu.VMEM((16, block), f32),
                pltpu.VMEM((Q_WIDTH, block), f32),
            ],
        ),
        out_shape=[
            jax.ShapeDtypeStruct((count, block, Q_WIDTH), bf16),
            jax.ShapeDtypeStruct((count, 16, block), f32),
        ],
        cost_estimate=pl.CostEstimate(
            flops=pairs_done * 4 * 256, bytes_accessed=4 << 20, transcendentals=pairs_done
        ),
        name="attend_forward",
    )(places, queries, keys_both, values_turned)


def attend_backward(places, queries, keys_both, values_both, keys_turned, mixed, grads, stats_in):
    count, block, _ = queries.shape
    length = keys_both.shape[1]
    rows, whole, turned, stats = attention_specs(count, block, length)
    pairs_done = count * block * (length // 2 + block) * HEADS
    return pl.pallas_call(
        backward_kernel,
        grid_spec=pltpu.PrefetchScalarGridSpec(
            num_scalar_prefetch=1,
            grid=(count,),
            in_specs=[
                rows(Q_WIDTH),
                whole(length, 2 * PAIR),
                whole(length, 2 * PAIR),
                turned,
                rows(Q_WIDTH),
                rows(Q_WIDTH),
                stats,
            ],
            out_specs=[rows(Q_WIDTH), whole(length, 2 * PAIR), whole(length, 2 * PAIR)],
            scratch_shapes=[pltpu.VMEM((Q_WIDTH, block), f32)],
        ),
        out_shape=[
            jax.ShapeDtypeStruct((count, block, Q_WIDTH), f32),
            jax.ShapeDtypeStruct((count // 2, length, 2 * PAIR), f32),
            jax.ShapeDtypeStruct((count // 2, length, 2 * PAIR), f32),
        ],
        cost_estimate=pl.CostEstimate(
            flops=pairs_done * 10 * 256, bytes_accessed=8 << 20, transcendentals=pairs_done
        ),
        name="attend_backward",
    )(places, queries, keys_both, values_both, keys_turned, mixed, grads, stats_in)


def hop(x, ctx_size, mask):
    return lax.ppermute(x, "ctx", [(i, i ^ mask) for i in range(ctx_size)])


def gather_pieces(x, ctx_size):
    if ctx_size != 4:
        return [x] + [hop(x, ctx_size, k) for k in range(1, ctx_size)]
    half = x.shape[0] // 2
    front, back = x[:half], x[half:]
    front_1 = hop(front, 4, 1)
    back_2 = hop(back, 4, 2)
    front_far = hop(jnp.concatenate([front, front_1], axis=0), 4, 2)
    back_far = hop(jnp.concatenate([back, back_2], axis=0), 4, 1)
    return [
        x,
        jnp.concatenate([front_1, back_far[:half]], axis=0),
        jnp.concatenate([front_far[:half], back_2], axis=0),
        jnp.concatenate([front_far[half:], back_far[half:]], axis=0),
    ]


def sum_pieces(pieces, ctx_size):
    if ctx_size != 4:
        total = pieces[0]
        for k in range(1, ctx_size):
            total = total + hop(pieces[k].astype(bf16), ctx_size, k).astype(f32)
        return total
    half = pieces[0].shape[0] // 2
    front = [piece[:half] for piece in pieces]
    back = [piece[half:] for piece in pieces]
    front_got = hop(jnp.concatenate([front[1], front[3]], axis=0).astype(bf16), 4, 1)
    back_got = hop(jnp.concatenate([back[2], back[3]], axis=0).astype(bf16), 4, 2)
    front_next = front[2] + front_got[half:].astype(f32)
    back_next = back[1] + back_got[half:].astype(f32)
    front_last = hop(front_next.astype(bf16), 4, 2).astype(f32)
    back_last = hop(back_next.astype(bf16), 4, 1).astype(f32)
    return jnp.concatenate(
        [
            front[0] + front_got[:half].astype(f32) + front_last,
            back[0] + back_got[:half].astype(f32) + back_last,
        ],
        axis=0,
    )


def in_order(pieces, place, ctx_size):
    result = jnp.zeros((ctx_size,) + pieces[0].shape, pieces[0].dtype)
    for k, piece in enumerate(pieces):
        result = lax.dynamic_update_index_in_dim(result, piece, place ^ k, 0)
    return result


def on_device(
    seq_size,
    ctx_size,
    tokens,
    attention_gain,
    project_weight,
    project_bias,
    output_weight,
    feedforward_gain,
    gate_weight,
    up_weight,
    down_weight,
    cotangent,
):
    sequences, block_rows, width = tokens.shape
    place = lax.axis_index("ctx")
    half = block_rows // 2
    length = block_rows * ctx_size
    rows = sequences * block_rows
    fold = seq_size // ctx_size
    mirror = [(i, ctx_size - 1 - i) for i in range(ctx_size)]
    turn = [
        ((c * fold + r) * ctx_size + q, (q * fold + r) * ctx_size + c)
        for c in range(ctx_size)
        for r in range(fold)
        for q in range(ctx_size)
    ]

    def zigzag(x):
        return jnp.concatenate([x[:, :half], lax.ppermute(x[:, half:], "ctx", mirror)], axis=1)

    places = jnp.stack([2 * place, 2 * (ctx_size - 1 - place) + 1]).astype(jnp.int32)
    positions = (places[:, None] * half + jnp.arange(half, dtype=jnp.int32)[None, :]).reshape(-1)

    def columns_whole(shard):
        pieces = [shard] + [hop(shard, ctx_size, k) for k in range(1, ctx_size)]
        ordered = in_order(pieces, place, ctx_size)
        return jnp.moveaxis(ordered, 0, 1).reshape(shard.shape[0], -1)

    def rows_whole(shard):
        return lax.all_gather(shard, "seq", axis=0, tiled=True)

    gain_width = attention_gain.shape[0]
    bias_width = project_bias.shape[0]
    vectors = jnp.concatenate([attention_gain, project_bias, feedforward_gain])[None, :]
    vector_pieces = [vectors] + [hop(vectors, ctx_size, k) for k in range(1, ctx_size)]
    vectors_all = in_order(vector_pieces, place, ctx_size)[:, 0, :].astype(f32)
    attention_full = vectors_all[:, :gain_width].reshape(-1)
    bias_full = vectors_all[:, gain_width : gain_width + bias_width].reshape(-1)
    feedforward_full = vectors_all[:, gain_width + bias_width :].reshape(-1)

    project_full = rows_whole(columns_whole(project_weight))
    output_full = rows_whole(columns_whole(output_weight))
    gate_mine = rows_whole(gate_weight)
    up_mine = rows_whole(up_weight)
    down_rows, down_columns = down_weight.shape
    down_turned = lax.ppermute(down_weight, ("seq", "ctx"), turn)
    down_mine = (
        lax.all_gather(down_turned, "seq", axis=0)
        .reshape(ctx_size, fold, down_rows, down_columns)
        .transpose(1, 2, 0, 3)
        .reshape(fold * down_rows, width)
    )

    inputs = zigzag(tokens).reshape(rows, width).astype(f32)
    grad_low = zigzag(cotangent).reshape(rows, width)
    grad_pieces = gather_pieces(grad_low, ctx_size)

    inverse_attention = inverse_rms(inputs)
    normed = (inputs * inverse_attention * attention_full).astype(bf16)
    projected = dot(normed, project_full, NN) + bias_full
    queries = rotate(
        projected[:, :Q_WIDTH].reshape(rows, HEADS, HEAD_DIM), jnp.tile(positions, sequences), True
    ).astype(bf16)
    queries = queries.reshape(sequences * 2, half, Q_WIDTH)
    keys_mine = (
        rotate(
            projected[:, Q_WIDTH : Q_WIDTH + K_WIDTH].reshape(rows, KV_HEADS, HEAD_DIM),
            jnp.tile(positions, sequences),
            True,
        )
        .astype(bf16)
        .reshape(rows, K_WIDTH)
    )
    values_mine = projected[:, Q_WIDTH + K_WIDTH :].astype(bf16)
    pairs_mine = jnp.concatenate([keys_mine, values_mine], axis=-1).reshape(
        sequences, 2, half, 2 * K_WIDTH
    )
    pair_pieces = [pairs_mine] + [hop(pairs_mine, ctx_size, k) for k in range(1, ctx_size)]
    pairs_all = jnp.zeros((sequences, 2 * ctx_size, half, 2 * K_WIDTH), bf16)
    for k, piece in enumerate(pair_pieces):
        owner = place ^ k
        pairs_all = lax.dynamic_update_slice_in_dim(pairs_all, piece[:, :1], 2 * owner, 1)
        pairs_all = lax.dynamic_update_slice_in_dim(
            pairs_all, piece[:, 1:], 2 * (ctx_size - 1 - owner) + 1, 1
        )
    pairs_all = pairs_all.reshape(sequences, length, 2 * K_WIDTH)
    keys_all = pairs_all[..., :K_WIDTH]
    values_all = pairs_all[..., K_WIDTH:]
    keys_both = jnp.concatenate([keys_all, swap_heads(keys_all)], axis=-1)
    values_both = jnp.concatenate([values_all, swap_heads(values_all)], axis=-1)


    def turned(x):
        return jnp.swapaxes(x.reshape(sequences, 2 * ctx_size, half, K_WIDTH), 2, 3)

    keys_turned = turned(keys_all)
    values_turned = turned(values_all)
    mixed, row_stats = attend_forward(places, queries, keys_both, values_turned)
    mixed_rows = mixed.reshape(rows, Q_WIDTH)
    hidden = inputs + dot(mixed_rows, output_full, NN)
    inverse_ffn = inverse_rms(hidden)
    normed_ffn = (hidden * inverse_ffn * feedforward_full).astype(bf16)

    normed_pieces = gather_pieces(normed_ffn, ctx_size)
    active_pieces = []
    grad_gate_pieces = []
    grad_up_pieces = []
    output_pieces = []
    grad_normed_pieces = []
    for piece, grad_piece in zip(normed_pieces, grad_pieces):
        gate_value = dot(piece, gate_mine, NN)
        up_value = dot(piece, up_mine, NN)
        grad_active = dot(grad_piece, down_mine, NT)
        sigmoid_gate = jax.nn.sigmoid(gate_value)
        active = (gate_value * sigmoid_gate * up_value).astype(bf16)
        grad_gate = (
            grad_active * up_value * sigmoid_gate * (1.0 + gate_value * (1.0 - sigmoid_gate))
        ).astype(bf16)
        grad_up = (grad_active * gate_value * sigmoid_gate).astype(bf16)
        grad_normed_pieces.append(dot(grad_gate, gate_mine, NT) + dot(grad_up, up_mine, NT))
        output_pieces.append(dot(active, down_mine, NN))
        active_pieces.append(active)
        grad_gate_pieces.append(grad_gate)
        grad_up_pieces.append(grad_up)
    grad_normed_ffn = sum_pieces(grad_normed_pieces, ctx_size)
    output_zigzag = hidden + sum_pieces(output_pieces, ctx_size)
    layer_output = zigzag(output_zigzag.astype(bf16).reshape(tokens.shape))

    normed_tokens = jnp.concatenate(normed_pieces, axis=0)
    grad_tokens = jnp.concatenate(grad_pieces, axis=0)
    active_tokens = jnp.concatenate(active_pieces, axis=0)
    grad_gate_weight = dot(normed_tokens, jnp.concatenate(grad_gate_pieces, axis=0), TN)
    grad_up_weight = dot(normed_tokens, jnp.concatenate(grad_up_pieces, axis=0), TN)
    grad_down_weight = dot(active_tokens, grad_tokens, TN)

    def rows_summed(whole):
        return lax.psum_scatter(whole.astype(bf16), "seq", scatter_dimension=0, tiled=True)

    gate_out = rows_summed(grad_gate_weight).astype(f32)
    up_out = rows_summed(grad_up_weight).astype(f32)
    down_parts = (
        grad_down_weight.astype(bf16)
        .reshape(fold, down_rows, ctx_size, down_columns)
        .transpose(2, 0, 1, 3)
        .reshape(seq_size * down_rows, down_columns)
    )
    down_out = lax.ppermute(
        rows_summed(down_parts), ("seq", "ctx"), [(b, a) for a, b in turn]
    ).astype(f32)

    grad_ffn_gain = jnp.sum(grad_normed_ffn * hidden * inverse_ffn, axis=0)
    weighted_ffn = grad_normed_ffn * feedforward_full
    grad_hidden = (
        grad_low.astype(f32)
        + inverse_ffn * weighted_ffn
        - hidden
        * inverse_ffn
        * inverse_ffn
        * inverse_ffn
        * jnp.mean(weighted_ffn * hidden, axis=-1, keepdims=True)
    )
    hidden_low = grad_hidden.astype(bf16)
    grad_output_weight = dot(mixed_rows, hidden_low, TN)
    grad_mixed = dot(hidden_low, output_full, NT).astype(bf16)

    grad_queries, key_grads, value_grads = attend_backward(
        places,
        queries,
        keys_both,
        values_both,
        keys_turned,
        mixed,
        grad_mixed.reshape(sequences * 2, half, Q_WIDTH),
        row_stats,
    )
    key_total = key_grads[..., :K_WIDTH] + swap_heads(key_grads[..., K_WIDTH:])
    value_total = value_grads[..., :K_WIDTH] + swap_heads(value_grads[..., K_WIDTH:])
    both_total = jnp.concatenate([key_total, value_total], axis=-1).reshape(
        sequences, 2 * ctx_size, half, 2 * K_WIDTH
    )
    both_pieces = []
    for k in range(ctx_size):
        owner = place ^ k
        both_pieces.append(
            jnp.concatenate(
                [
                    lax.dynamic_slice_in_dim(both_total, 2 * owner, 1, 1),
                    lax.dynamic_slice_in_dim(both_total, 2 * (ctx_size - 1 - owner) + 1, 1, 1),
                ],
                axis=1,
            )
        )
    both_sum = both_pieces[0]
    for k in range(1, ctx_size):
        both_sum = both_sum + hop(both_pieces[k].astype(bf16), ctx_size, k).astype(f32)
    both_sum = both_sum.reshape(rows, 2 * K_WIDTH)

    def unrotate(x, heads):
        return (
            rotate(x.reshape(rows, heads, HEAD_DIM), jnp.tile(positions, sequences), False)
            .astype(bf16)
            .reshape(rows, heads * HEAD_DIM)
        )

    grad_projected = jnp.concatenate(
        [
            unrotate(grad_queries, HEADS),
            unrotate(both_sum[:, :K_WIDTH], KV_HEADS),
            both_sum[:, K_WIDTH:].astype(bf16),
        ],
        axis=-1,
    )
    grad_project_weight = dot(normed, grad_projected, TN)
    grad_project_bias = jnp.sum(grad_projected.astype(f32), axis=0)
    grad_normed = dot(grad_projected, project_full, NT)
    grad_attention_gain = jnp.sum(grad_normed * inputs * inverse_attention, axis=0)
    weighted_attention = grad_normed * attention_full
    tokens_grad = (
        grad_hidden
        + inverse_attention * weighted_attention
        - inputs
        * inverse_attention
        * inverse_attention
        * inverse_attention
        * jnp.mean(weighted_attention * inputs, axis=-1, keepdims=True)
    ).reshape(tokens.shape)
    tokens_gradient = jnp.concatenate(
        [
            tokens_grad[:, :half],
            lax.ppermute(tokens_grad[:, half:].astype(bf16), "ctx", mirror).astype(f32),
        ],
        axis=1,
    )

    def columns_summed(partial):
        own = partial.shape[1] // ctx_size

        def part(k):
            return lax.dynamic_slice_in_dim(partial, (place ^ k) * own, own, 1)

        total = part(0).astype(f32)
        for k in range(1, ctx_size):
            total = total + hop(part(k), ctx_size, k).astype(f32)
        return total

    output_out = columns_summed(rows_summed(grad_output_weight))
    project_out = columns_summed(rows_summed(grad_project_weight))
    sums = lax.psum(
        jnp.concatenate([grad_attention_gain, grad_project_bias, grad_ffn_gain]), ("seq", "ctx")
    )

    def my_part(start, whole):
        own = whole // ctx_size
        return lax.dynamic_slice_in_dim(sums, start + place * own, own, 0)

    project_width = bias_width * ctx_size
    return (
        layer_output,
        tokens_gradient,
        my_part(0, width),
        project_out,
        my_part(width, project_width),
        output_out,
        my_part(width + project_width, width),
        gate_out,
        up_out,
        down_out,
    )


def solution(mesh):
    matrix = P("seq", "ctx")
    vector = P("ctx")
    activation = P("seq", "ctx", None)

    def step(*arrays):
        return on_device(mesh.shape["seq"], mesh.shape["ctx"], *arrays)

    return jax.shard_map(
        step,
        mesh=mesh,
        in_specs=(
            activation,
            vector,
            matrix,
            vector,
            matrix,
            vector,
            matrix,
            matrix,
            matrix,
            activation,
        ),
        out_specs=(
            activation,
            activation,
            vector,
            matrix,
            vector,
            matrix,
            vector,
            matrix,
            matrix,
            matrix,
        ),
        check_vma=False,
    )
```

time: 1630 us -> 566 us (0.35)
  the two profiles are of different devices: /device:TPU:2 before, /device:TPU:0 now
where the time goes in v1:
time: 566 us; the launch traced here: 557 us
  matrix products  110 us (19%)
  local copies, waits for them, and re-layouts  108 us (19%)
  waiting for transfers between devices  98.2 us (17%)
  starting transfers between devices  66.6 us (12%)
  Pallas kernels  63.3 us (11%)
  other arithmetic  50 us (9%)
  blocking collectives  45.4 us (8%)
  between operations  15.7 us (3%)
    dot_general x33, matrix products, dot(): return lax.dot_general(a, b, (dims, ((), ())), preferred_element_type=f32)  110 us
    ppermute x37, waiting for transfers between devices, hop(): return lax.ppermute(x, 'ctx', [(i, i ^ mask) for i in range(ctx_size)])  89.7 us
    ppermute x37, starting transfers between devices, hop(): return lax.ppermute(x, 'ctx', [(i, i ^ mask) for i in range(ctx_size)])  54.7 us
    psum x1, blocking collectives, on_device(): lax.psum(jnp.concatenate([grad_attention_gain, grad_project_bias, grad_ff...  45.4 us
    pallas_call x1, Pallas kernels, attend_backward(): pl.pallas_call(backward_kernel, grid_spec=pltpu.PrefetchScalarGridSpec(nu...  36.1 us
    unnamed x168, local copies, waits for them, and re-layouts  30.2 us
    pallas_call x1, Pallas kernels, attend_forward(): pl.pallas_call(forward_kernel, grid_spec=pltpu.PrefetchScalarGridSpec(num...  27.2 us
  transfers between devices with their start and end apart: 53, of which 18 were waited for; matrix products, arithmetic and copies ran while one was open for 35% of the time, Pallas kernels for 11%

profile of v1, /device:TPU:0, one launch (start us, length us, event | category | flops | bytes accessed | tf_op | source)
XLA Modules:
  0.0 556.8 jit_solution(8039068800082628366)
XLA Ops:
  7.2 3.0 collective-permute-start.4
  37.8 7.2 %collective-permute-done.23 = bf16[1,256,896]{2,1,0:T(8,128)(2,1)S(1)} collective-permute-done((bf16[1,256,896]{2,1,0:T(8,128)(2,1)S(1)}, bf16[1,256,896]{2,1,0:T(8,128)(2,1)S(1)}, u32[]{:S(2)}, u32[]{:S(2)}) %collective-permute-start.23) | collective-permute-done | bytes 458784 | tf_op jit(solution)/shard_map/ppermute | solution.py:382
  51.2 13.4 %collective-permute-done.25 = bf16[256,896]{1,0:T(8,128)(2,1)S(1)} collective-permute-done((bf16[256,896]{1,0:T(8,128)(2,1)S(1)}, bf16[256,896]{1,0:T(8,128)(2,1)S(1)}, u32[]{:S(2)}, u32[]{:S(2)}) %collective-permute-start.25) | collective-permute-done | bytes 458784 | tf_op jit(solution)/shard_map/ppermute | solution.py:302
  69.5 3.7 collective-permute-start.13
  73.3 22.9 %collective-permute-done.3 = bf16[1,736]{1,0:T(2,128)(2,1)S(1)} collective-permute-done((bf16[1,736]{1,0:T(2,128)(2,1)S(1)}, bf16[1,736]{1,0:T(2,128)(2,1)S(1)}, u32[]{:S(2)}, u32[]{:S(2)}) %collective-permute-start.3) | collective-permute-done | bytes 1504 | tf_op jit(solution)/shard_map/ppermute | solution.py:302
  102.4 14.3 %collective-permute-done.27 = bf16[512,896]{1,0:T(8,128)(2,1)S(1)} collective-permute-done((bf16[512,896]{1,0:T(8,128)(2,1)}, bf16[512,896]{1,0:T(8,128)(2,1)S(1)}, u32[]{:S(2)}, u32[]{:S(2)}) %collective-permute-start.27) | collective-permute-done | bytes 917536 | tf_op jit(solution)/shard_map/ppermute | solution.py:302
  120.8 3.3 broadcast_add_fusion
  127.6 2.6 collective-permute-start.7
  135.6 2.7 subtract_convert_fusion.1
  141.0 3.7 copy.114.q_ref
  153.7 27.2 %attend_forward.1 = (bf16[2,256,896]{2,1,0:T(8,128)(2,1)}, f32[2,16,256]{2,1,0:T(8,128)}) custom-call(s32[2]{0:T(128)} %get-tuple-element.77.place_ref, bf16[2,256,896]{2,1,0:T(8,128)(2,1)} %copy.114.q_ref, bf16[1,2048,256]{2,1,0:T(8,128)(2,1)} %get-tuple-element.171.k_ref, bf16[1,8,128,256]{3,2,1,0:T(8,128)(2,1)} %bitcast.161), custom_call_target="tpu_custom_call" | custom-call | flops 9395240960 | bytes 4194304 | tf_op jit(solution)/shard_map/attend_forward/pallas_call | solution.py:243
  181.0 3.1 multiply_reduce_fusion.2
  190.7 4.9 fusion.110
  195.5 4.9 fusion.111
  200.4 4.8 copy.137
  205.2 5.8 %reshape.351 = bf16[1216,896]{0,1:T(8,128)(2,1)} reshape(bf16[2,608,4,224]{1,0,3,2:T(2,128)(2,1)} %bitcast.138) | data formatting | bytes 4358144 | tf_op jit(solution)/shard_map/reshape | solution.py:414
  214.4 6.1 %multiply_convert_fusion.6 = (bf16[512,1216]{0,1:T(8,128)(2,1)}, bf16[512,1216]{0,1:T(8,128)(2,1)}, bf16[512,1216]{0,1:T(8,128)(2,1)S(1)}) fusion(f32[512,1216]{0,1:T(8,128)} %fusion.110, f32[512,1216]{0,1:T(8,128)} %fusion.111, bf16[1216,896]{0,1:T(8,128)(2,1)S(1)} %copy-done.12, bf16[1,256,896]{2,1,0:T(8,128)(2,1)S(1)} %collective-permute-done.23, ...), kind=kOutput, calls=%fused_computation.39 | convolution fusion | flops 1127481344 | bytes 11812864 | tf_op jit(solution)/shard_map/dot_general | solution.py:49
  222.6 7.9 %collective-permute-done.16 = bf16[512,896]{1,0:T(8,128)(2,1)S(1)} collective-permute-done((bf16[512,896]{1,0:T(8,128)(2,1)S(1)}, bf16[512,896]{1,0:T(8,128)(2,1)S(1)}, u32[]{:S(2)}, u32[]{:S(2)}) %collective-permute-start.16) | collective-permute-done | bytes 917536 | tf_op jit(solution)/shard_map/ppermute | solution.py:302
  239.0 4.3 multiply_convert_fusion.2
  243.3 2.8 fusion.66
  246.2 2.5 fusion.67
  248.7 2.5 fusion.68
  251.2 2.6 fusion.69
  253.9 4.8 multiply_convert_fusion.4
  258.7 4.3 multiply_convert_fusion
  264.0 8.6 %fusion.24 = bf16[1216,896]{1,0:T(8,128)(2,1)} fusion(bf16[2048,896]{1,0:T(8,128)(2,1)} %get-tuple-element.118, bf16[512,1216]{0,1:T(8,128)(2,1)S(1)} %get-tuple-element.83, bf16[512,1216]{0,1:T(8,128)(2,1)S(1)} %get-tuple-element.80, bf16[512,1216]{0,1:T(8,128)(2,1)S(1)} %get-tuple-element.86, bf16[512,1216]{0,1:T(8,128)(2,1)S(1)} %get-tuple-element.89), kind=kOutput, calls=%fused_computation.29 | convolution fusion | flops 4483751936 | bytes 10829824 | tf_op jit(solution)/shard_map/dot_general | solution.py:49
  272.6 6.7 %reshape.369 = bf16[2,608,4,224]{3,2,1,0:T(4,128)(2,1)} reshape(bf16[1216,896]{1,0:T(8,128)(2,1)} %fusion.24) | data formatting | bytes 4358144 | tf_op jit(solution)/shard_map/reshape | solution.py:506
  279.3 7.7 %copy.129 = bf16[2,608,4,224]{1,0,2,3:T(2,128)(2,1)} copy(bf16[2,608,4,224]{3,2,1,0:T(4,128)(2,1)} %reshape.369) | data formatting | bytes 4358144 | tf_op jit(solution)/shard_map/transpose | solution.py:507
  287.0 7.4 %copy.132 = bf16[4,2,608,224]{3,2,1,0:T(8,128)(2,1)} copy(bf16[4,2,608,224]{2,1,0,3:T(2,128)(2,1)} %bitcast.139) | data formatting | bytes 4358144
  295.6 5.0 fusion.112
  302.9 2.8 convolution_add_fusion.2
  315.2 6.8 %fusion.27 = bf16[896,1216]{1,0:T(8,128)(2,1)} fusion(bf16[2048,896]{1,0:T(8,128)(2,1)S(1)} %copy-done.40, bf16[512,1216]{0,1:T(8,128)(2,1)S(1)} %copy-done.72, bf16[512,1216]{0,1:T(8,128)(2,1)S(1)} %copy-done.70, bf16[512,1216]{0,1:T(8,128)(2,1)S(1)} %copy-done.68, bf16[512,1216]{0,1:T(8,128)(2,1)S(1)} %copy-done.67), kind=kOutput, calls=%fused_computation.30 | convolution fusion | flops 4483751936 | bytes 10829824 | tf_op jit(solution)/shard_map/dot_general | solution.py:49
  324.4 3.4 fusion.118
  341.4 6.5 %fusion.30 = bf16[896,1216]{1,0:T(8,128)(2,1)} fusion(bf16[2048,896]{1,0:T(8,128)(2,1)S(1)} %copy-done.41, bf16[512,1216]{0,1:T(8,128)(2,1)S(1)} %copy-done.59, bf16[512,1216]{0,1:T(8,128)(2,1)S(1)} %copy-done.61, bf16[512,1216]{0,1:T(8,128)(2,1)S(1)} %copy-done.60, bf16[512,1216]{0,1:T(8,128)(2,1)S(1)} %copy-done.58), kind=kOutput, calls=%fused_computation.31 | convolution fusion | flops 4483751936 | bytes 10829824 | tf_op jit(solution)/shard_map/dot_general | solution.py:49
  352.3 11.0 %collective-permute-done.28 = bf16[512,896]{1,0:T(8,128)(2,1)} collective-permute-done((bf16[512,896]{1,0:T(8,128)(2,1)}, bf16[512,896]{1,0:T(8,128)(2,1)}, u32[]{:S(2)}, u32[]{:S(2)}) %collective-permute-start.28) | collective-permute-done | bytes 917536 | tf_op jit(solution)/shard_map/ppermute | solution.py:302
  375.7 2.9 collective-permute-done.21
  384.1 36.1 %attend_backward.1 = (f32[2,256,896]{2,1,0:T(8,128)}, f32[1,2048,256]{2,1,0:T(8,128)}, f32[1,2048,256]{2,1,0:T(8,128)}) custom-call(s32[2]{0:T(128)} %get-tuple-element.77.place_ref, bf16[2,256,896]{2,1,0:T(8,128)(2,1)} %copy.114.q_ref, bf16[1,2048,256]{2,1,0:T(8,128)(2,1)} %get-tuple-element.171.k_ref, bf16[1,2048,256]{2,1,0:T(8,128)(2,1)} %get-tuple-element.172.v_ref, ...), custom_call_target="tpu_custom_call" | custom-call | flops 23488102400 | bytes 8388608 | tf_op jit(solution)/shard_map/attend_backward/pallas_call | solution.py:272
  420.1 3.0 copy.122
  423.2 2.7 reshape.356
  425.9 3.8 convolution_convert_fusion.1
  429.7 3.4 fusion.96
  441.9 2.6 collective-permute-done.32
  444.5 3.7 collective-permute-done.33
  449.2 4.0 convolution_convert_fusion
  456.4 3.5 fusion.43
  464.6 45.4 %psum.7 = f32[2944]{0:T(1024)S(1)} all-reduce(f32[2944]{0:T(1024)S(1)} %pad_maximum_fusion.34), channel_id=1, replica_groups=mesh['seq'=8,'ctx'=4] {'seq','ctx'}, use_global_device_ids=true, to_apply=%region_7.8 | all-reduce | flops 2944 | bytes 23552 | tf_op jit(solution)/shard_map/psum | solution.py:611
  522.4 4.9 collective-permute-start.39
  531.5 11.1 %collective-permute-start.36 = (bf16[112,288]{1,0:T(8,128)(2,1)S(1)}, bf16[112,288]{1,0:T(8,128)(2,1)S(1)}, u32[]{:S(2)}, u32[]{:S(2)}) collective-permute-start(bf16[112,288]{1,0:T(8,128)(2,1)S(1)} %get-tuple-element.155), channel_id=1, source_target_pairs={{0,1},{1,0},{2,3},{3,2},{4,5},{5,4},{6,7},{7,6},{8,9},{9,8},{10,11... | collective-permute-start | bytes 193544 | tf_op jit(solution)/shard_map/ppermute | solution.py:302
  (420 shorter events, 183.0 us)
Async XLA Ops:
  7.2 113.6 %all-gather.8.cloned.1.call-start = ((), (), s32[]{:S(2)}) async-start(), calls=%async_computation.5 | async-start | bytes 2322432 | tf_op jit(solution)/shard_map/all_gather | solution.py:393
  18.1 162.8 %all-gather.10.cloned.1.call-start = ((), (), s32[]{:S(2)}) async-start(), calls=%async_computation.6 | async-start | bytes 1806336 | tf_op jit(solution)/shard_map/all_gather | solution.py:393
  18.2 6.7 %collective-permute-start.10 = (bf16[112,224]{1,0:T(8,128)(2,1)}, bf16[112,224]{1,0:T(8,128)(2,1)S(1)}, u32[]{:S(2)}, u32[]{:S(2)}) collective-permute-start(bf16[112,224]{1,0:T(8,128)(2,1)} %param.14), channel_id=1, source_target_pairs={{0,1},{1,0},{2,3},{3,2},{4,5},{5,4},{6,7},{7,6},{8,9},{9,8},{10,11... | collective-permute-start | bytes 150536 | tf_op jit(solution)/shard_map/ppermute | solution.py:302
  18.8 6.2 %collective-permute-start.11 = (bf16[112,224]{1,0:T(8,128)(2,1)}, bf16[112,224]{1,0:T(8,128)(2,1)S(1)}, u32[]{:S(2)}, u32[]{:S(2)}) collective-permute-start(bf16[112,224]{1,0:T(8,128)(2,1)} %param.14), channel_id=1, source_target_pairs={{0,2},{1,3},{2,0},{3,1},{4,6},{5,7},{6,4},{7,5},{8,10},{9,11},{10,... | collective-permute-start | bytes 150536 | tf_op jit(solution)/shard_map/ppermute | solution.py:302
  19.3 5.9 %collective-permute-start.12 = (bf16[112,224]{1,0:T(8,128)(2,1)}, bf16[112,224]{1,0:T(8,128)(2,1)S(1)}, u32[]{:S(2)}, u32[]{:S(2)}) collective-permute-start(bf16[112,224]{1,0:T(8,128)(2,1)} %param.14), channel_id=1, source_target_pairs={{0,3},{1,2},{2,1},{3,0},{4,7},{5,6},{6,5},{7,4},{8,11},{9,10},{10,... | collective-permute-start | bytes 150536 | tf_op jit(solution)/shard_map/ppermute | solution.py:302
  32.7 158.0 %all-gather.12.cloned.1.call-start = ((), (), s32[]{:S(2)}) async-start(), calls=%async_computation.7 | async-start | bytes 2580480 | tf_op jit(solution)/shard_map/all_gather | solution.py:393
  33.4 162.1 %all-gather.14.cloned.1.call-start = ((), (), s32[]{:S(2)}) async-start(), calls=%async_computation.8 | async-start | bytes 2580480 | tf_op jit(solution)/shard_map/all_gather | solution.py:393
  34.0 166.4 %all-gather.16.cloned.1.call-start = ((), (), s32[]{:S(2)}) async-start(), calls=%async_computation.13 | async-start | bytes 2580480 | tf_op jit(solution)/shard_map/all_gather | solution.py:411
  34.2 10.8 %collective-permute-start.23 = (bf16[1,256,896]{2,1,0:T(8,128)(2,1)S(1)}, bf16[1,256,896]{2,1,0:T(8,128)(2,1)S(1)}, u32[]{:S(2)}, u32[]{:S(2)}) collective-permute-start(bf16[1,256,896]{2,1,0:T(8,128)(2,1)S(1)} %get-tuple-element.133), channel_id=1, source_target_pairs={{0,3},{1,2},{2,1},{3,0},{4,7},{5,6},{6,5},{7,4},{8,11},{9,10},{10,... | collective-permute-start | bytes 1376264 | tf_op jit(solution)/shard_map/ppermute | solution.py:382
  36.2 32.1 %collective-permute-start.1 = (bf16[1,736]{1,0:T(2,128)(2,1)S(1)}, bf16[1,736]{1,0:T(2,128)(2,1)S(1)}, u32[]{:S(2)}, u32[]{:S(2)}) collective-permute-start(bf16[1,736]{1,0:T(2,128)(2,1)S(1)} %squeeze.6), channel_id=1, source_target_pairs={{0,1},{1,0},{2,3},{3,2},{4,5},{5,4},{6,7},{7,6},{8,9},{9,8},{10,11... | collective-permute-start | bytes 4424 | tf_op jit(solution)/shard_map/ppermute | solution.py:302
  36.8 32.7 %collective-permute-start.2 = (bf16[1,736]{1,0:T(2,128)(2,1)S(1)}, bf16[1,736]{1,0:T(2,128)(2,1)S(1)}, u32[]{:S(2)}, u32[]{:S(2)}) collective-permute-start(bf16[1,736]{1,0:T(2,128)(2,1)S(1)} %squeeze.6), channel_id=1, source_target_pairs={{0,2},{1,3},{2,0},{3,1},{4,6},{5,7},{6,4},{7,5},{8,10},{9,11},{10,... | collective-permute-start | bytes 4424 | tf_op jit(solution)/shard_map/ppermute | solution.py:302
  45.0 19.6 %collective-permute-start.25 = (bf16[256,896]{1,0:T(8,128)(2,1)S(1)}, bf16[256,896]{1,0:T(8,128)(2,1)S(1)}, u32[]{:S(2)}, u32[]{:S(2)}) collective-permute-start(bf16[256,896]{1,0:T(8,128)(2,1)S(1)} %bitcast.145), channel_id=1, source_target_pairs={{0,2},{1,3},{2,0},{3,1},{4,6},{5,7},{6,4},{7,5},{8,10},{9,11},{10,... | collective-permute-start | bytes 1376264 | tf_op jit(solution)/shard_map/ppermute | solution.py:302
  47.5 50.9 %collective-permute-start = (bf16[1,256,896]{2,1,0:T(8,128)(2,1)}, bf16[1,256,896]{2,1,0:T(8,128)(2,1)}, u32[]{:S(2)}, u32[]{:S(2)}) collective-permute-start(bf16[1,256,896]{2,1,0:T(8,128)(2,1)} %get-tuple-element.142), channel_id=1, source_target_pairs={{0,3},{1,2},{2,1},{3,0},{4,7},{5,6},{6,5},{7,4},{8,11},{9,10},{10,... | collective-permute-start | bytes 1376264 | tf_op jit(solution)/shard_map/ppermute | solution.py:382
  49.4 46.9 %collective-permute-start.24 = (bf16[256,896]{1,0:T(8,128)(2,1)S(1)}, bf16[256,896]{1,0:T(8,128)(2,1)S(1)}, u32[]{:S(2)}, u32[]{:S(2)}) collective-permute-start(bf16[256,896]{1,0:T(8,128)(2,1)S(1)} %get-tuple-element.132), channel_id=1, source_target_pairs={{0,1},{1,0},{2,3},{3,2},{4,5},{5,4},{6,7},{7,6},{8,9},{9,8},{10,11... | collective-permute-start | bytes 1376264 | tf_op jit(solution)/shard_map/ppermute | solution.py:302
  66.4 35.1 %collective-permute-start.26 = (bf16[512,896]{1,0:T(8,128)(2,1)}, bf16[512,896]{1,0:T(8,128)(2,1)S(1)}, u32[]{:S(2)}, u32[]{:S(2)}) collective-permute-start(bf16[512,896]{1,0:T(8,128)(2,1)} %pad_maximum_fusion.9), channel_id=1, source_target_pairs={{0,1},{1,0},{2,3},{3,2},{4,5},{5,4},{6,7},{7,6},{8,9},{9,8},{10,11... | collective-permute-start | bytes 2752520 | tf_op jit(solution)/shard_map/ppermute | solution.py:302
  68.3 27.8 %collective-permute-start.3 = (bf16[1,736]{1,0:T(2,128)(2,1)S(1)}, bf16[1,736]{1,0:T(2,128)(2,1)S(1)}, u32[]{:S(2)}, u32[]{:S(2)}) collective-permute-start(bf16[1,736]{1,0:T(2,128)(2,1)S(1)} %squeeze.6), channel_id=1, source_target_pairs={{0,3},{1,2},{2,1},{3,0},{4,7},{5,6},{6,5},{7,4},{8,11},{9,10},{10,... | collective-permute-start | bytes 4424 | tf_op jit(solution)/shard_map/ppermute | solution.py:302
  69.5 28.8 %collective-permute-start.13 = (bf16[608,224]{0,1:T(8,128)(2,1)}, bf16[608,224]{0,1:T(8,128)(2,1)}, u32[]{:S(2)}, u32[]{:S(2)}) collective-permute-start(bf16[608,224]{0,1:T(8,128)(2,1)} %param.18), channel_id=1, source_target_pairs={{0,0},{1,8},{2,16},{3,24},{4,4},{5,12},{6,20},{7,28},{8,1},{9,9},{... | collective-permute-start | bytes 817160 | tf_op jit(solution)/shard_map/ppermute | solution.py:409
  98.1 18.6 %collective-permute-start.27 = (bf16[512,896]{1,0:T(8,128)(2,1)}, bf16[512,896]{1,0:T(8,128)(2,1)S(1)}, u32[]{:S(2)}, u32[]{:S(2)}) collective-permute-start(bf16[512,896]{1,0:T(8,128)(2,1)} %pad_maximum_fusion.18), channel_id=1, source_target_pairs={{0,2},{1,3},{2,0},{3,1},{4,6},{5,7},{6,4},{7,5},{8,10},{9,11},{10,... | collective-permute-start | bytes 2752520 | tf_op jit(solution)/shard_map/ppermute | solution.py:302
  98.3 416.2 %reduce-scatter.16.cloned.1.call-start = ((), (), s32[]{:S(2)}) async-start(), calls=%async_computation.14 | async-start | bytes 2801664
  127.6 17.0 %collective-permute-start.7 = (bf16[1,2,256,256]{2,1,3,0:T(2,128)(2,1)}, bf16[1,2,256,256]{2,1,3,0:T(2,128)(2,1)}, u32[]{:S(2)}, u32[]{:S(2)}) collective-permute-start(bf16[1,2,256,256]{2,1,3,0:T(2,128)(2,1)} %pad_maximum_fusion.31), channel_id=1, source_target_pairs={{0,1},{1,0},{2,3},{3,2},{4,5},{5,4},{6,7},{7,6},{8,9},{9,8},{10,11... | collective-permute-start | bytes 786440 | tf_op jit(solution)/shard_map/ppermute | solution.py:302
  130.2 16.2 %collective-permute-start.8 = (bf16[1,2,256,256]{2,1,3,0:T(2,128)(2,1)}, bf16[1,2,256,256]{2,1,3,0:T(2,128)(2,1)}, u32[]{:S(2)}, u32[]{:S(2)}) collective-permute-start(bf16[1,2,256,256]{2,1,3,0:T(2,128)(2,1)} %pad_maximum_fusion.31), channel_id=1, source_target_pairs={{0,2},{1,3},{2,0},{3,1},{4,6},{5,7},{6,4},{7,5},{8,10},{9,11},{10,... | collective-permute-start | bytes 786440 | tf_op jit(solution)/shard_map/ppermute | solution.py:302
  132.0 16.3 %collective-permute-start.9 = (bf16[1,2,256,256]{2,1,3,0:T(2,128)(2,1)}, bf16[1,2,256,256]{2,1,3,0:T(2,128)(2,1)}, u32[]{:S(2)}, u32[]{:S(2)}) collective-permute-start(bf16[1,2,256,256]{2,1,3,0:T(2,128)(2,1)} %pad_maximum_fusion.31), channel_id=1, source_target_pairs={{0,3},{1,2},{2,1},{3,0},{4,7},{5,6},{6,5},{7,4},{8,11},{9,10},{10,... | collective-permute-start | bytes 786440 | tf_op jit(solution)/shard_map/ppermute | solution.py:302
  187.2 23.8 %collective-permute-start.14 = (bf16[256,896]{1,0:T(8,128)(2,1)}, bf16[256,896]{1,0:T(8,128)(2,1)}, u32[]{:S(2)}, u32[]{:S(2)}) collective-permute-start(bf16[256,896]{1,0:T(8,128)(2,1)} %get-tuple-element.139), channel_id=1, source_target_pairs={{0,1},{1,0},{2,3},{3,2},{4,5},{5,4},{6,7},{7,6},{8,9},{9,8},{10,11... | collective-permute-start | bytes 1376264 | tf_op jit(solution)/shard_map/ppermute | solution.py:302
  188.9 23.9 %collective-permute-start.15 = (bf16[256,896]{1,0:T(8,128)(2,1)}, bf16[256,896]{1,0:T(8,128)(2,1)}, u32[]{:S(2)}, u32[]{:S(2)}) collective-permute-start(bf16[256,896]{1,0:T(8,128)(2,1)} %get-tuple-element.140), channel_id=1, source_target_pairs={{0,2},{1,3},{2,0},{3,1},{4,6},{5,7},{6,4},{7,5},{8,10},{9,11},{10,... | collective-permute-start | bytes 1376264 | tf_op jit(solution)/shard_map/ppermute | solution.py:302
  212.4 18.9 %collective-permute-start.17 = (bf16[512,896]{1,0:T(8,128)(2,1)S(1)}, bf16[512,896]{1,0:T(8,128)(2,1)S(1)}, u32[]{:S(2)}, u32[]{:S(2)}) collective-permute-start(bf16[512,896]{1,0:T(8,128)(2,1)S(1)} %pad_maximum_fusion.13), channel_id=1, source_target_pairs={{0,2},{1,3},{2,0},{3,1},{4,6},{5,7},{6,4},{7,5},{8,10},{9,11},{10,... | collective-permute-start | bytes 2752520 | tf_op jit(solution)/shard_map/ppermute | solution.py:302
  214.0 16.5 %collective-permute-start.16 = (bf16[512,896]{1,0:T(8,128)(2,1)S(1)}, bf16[512,896]{1,0:T(8,128)(2,1)S(1)}, u32[]{:S(2)}, u32[]{:S(2)}) collective-permute-start(bf16[512,896]{1,0:T(8,128)(2,1)S(1)} %pad_maximum_fusion.7), channel_id=1, source_target_pairs={{0,1},{1,0},{2,3},{3,2},{4,5},{5,4},{6,7},{7,6},{8,9},{9,8},{10,11... | collective-permute-start | bytes 2752520 | tf_op jit(solution)/shard_map/ppermute | solution.py:302
  294.4 223.3 %reduce-scatter.14.cloned.1.call-start = ((), (), s32[]{:S(2)}) async-start(), calls=%async_computation.12 | async-start | bytes 2580480 | tf_op jit(solution)/shard_map/reduce_scatter | solution.py:500
  310.1 55.9 %collective-permute-start.20 = (bf16[512,896]{1,0:T(8,128)(2,1)}, bf16[512,896]{1,0:T(8,128)(2,1)}, u32[]{:S(2)}, u32[]{:S(2)}) collective-permute-start(bf16[512,896]{1,0:T(8,128)(2,1)} %pad_maximum_fusion.16), channel_id=1, source_target_pairs={{0,2},{1,3},{2,0},{3,1},{4,6},{5,7},{6,4},{7,5},{8,10},{9,11},{10,... | collective-permute-start | bytes 2752520 | tf_op jit(solution)/shard_map/ppermute | solution.py:302
  322.1 197.4 %reduce-scatter.12.cloned.1.call-start = ((), (), s32[]{:S(2)}) async-start(), calls=%async_computation.11 | async-start | bytes 2580480 | tf_op jit(solution)/shard_map/reduce_scatter | solution.py:500
  324.3 44.8 %collective-permute-start.18 = (bf16[512,896]{1,0:T(8,128)(2,1)}, bf16[512,896]{1,0:T(8,128)(2,1)}, u32[]{:S(2)}, u32[]{:S(2)}) collective-permute-start(bf16[512,896]{1,0:T(8,128)(2,1)} %pad_maximum_fusion.15), channel_id=1, source_target_pairs={{0,1},{1,0},{2,3},{3,2},{4,5},{5,4},{6,7},{7,6},{8,9},{9,8},{10,11... | collective-permute-start | bytes 2752520 | tf_op jit(solution)/shard_map/ppermute | solution.py:302
  334.1 15.2 %collective-permute-start.30 = (bf16[512,896]{1,0:T(8,128)(2,1)}, bf16[512,896]{1,0:T(8,128)(2,1)}, u32[]{:S(2)}, u32[]{:S(2)}) collective-permute-start(bf16[512,896]{1,0:T(8,128)(2,1)} %pad_maximum_fusion.20), channel_id=1, source_target_pairs={{0,2},{1,3},{2,0},{3,1},{4,6},{5,7},{6,4},{7,5},{8,10},{9,11},{10,... | collective-permute-start | bytes 2752520 | tf_op jit(solution)/shard_map/ppermute | solution.py:302
  339.5 23.8 %collective-permute-start.28 = (bf16[512,896]{1,0:T(8,128)(2,1)}, bf16[512,896]{1,0:T(8,128)(2,1)}, u32[]{:S(2)}, u32[]{:S(2)}) collective-permute-start(bf16[512,896]{1,0:T(8,128)(2,1)} %pad_maximum_fusion.19), channel_id=1, source_target_pairs={{0,1},{1,0},{2,3},{3,2},{4,5},{5,4},{6,7},{7,6},{8,9},{9,8},{10,11... | collective-permute-start | bytes 2752520 | tf_op jit(solution)/shard_map/ppermute | solution.py:302
  347.9 173.4 %reduce-scatter.10.cloned.1.call-start = ((), (), s32[]{:S(2)}) async-start(), calls=%async_computation.10 | async-start | bytes 1806336 | tf_op jit(solution)/shard_map/reduce_scatter | solution.py:500
  350.8 22.2 %collective-permute-start.31 = (bf16[256,896]{1,0:T(8,128)(2,1)S(1)}, bf16[256,896]{1,0:T(8,128)(2,1)S(1)}, u32[]{:S(2)}, u32[]{:S(2)}) collective-permute-start(bf16[256,896]{1,0:T(8,128)(2,1)S(1)} %fusion.47), channel_id=1, source_target_pairs={{0,1},{1,0},{2,3},{3,2},{4,5},{5,4},{6,7},{7,6},{8,9},{9,8},{10,11... | collective-permute-start | bytes 1376264 | tf_op jit(solution)/shard_map/ppermute | solution.py:302
  364.7 8.9 %collective-permute-start.29 = (bf16[256,896]{1,0:T(8,128)(2,1)S(1)}, bf16[256,896]{1,0:T(8,128)(2,1)S(1)}, u32[]{:S(2)}, u32[]{:S(2)}) collective-permute-start(bf16[256,896]{1,0:T(8,128)(2,1)S(1)} %fusion.49), channel_id=1, source_target_pairs={{0,2},{1,3},{2,0},{3,1},{4,6},{5,7},{6,4},{7,5},{8,10},{9,11},{10,... | collective-permute-start | bytes 1376264 | tf_op jit(solution)/shard_map/ppermute | solution.py:302
  367.1 11.5 %collective-permute-start.21 = (bf16[256,896]{1,0:T(8,128)(2,1)S(1)}, bf16[256,896]{1,0:T(8,128)(2,1)S(1)}, u32[]{:S(2)}, u32[]{:S(2)}) collective-permute-start(bf16[256,896]{1,0:T(8,128)(2,1)S(1)} %fusion.51), channel_id=1, source_target_pairs={{0,1},{1,0},{2,3},{3,2},{4,5},{5,4},{6,7},{7,6},{8,9},{9,8},{10,11... | collective-permute-start | bytes 1376264 | tf_op jit(solution)/shard_map/ppermute | solution.py:302
  370.1 8.5 %collective-permute-start.19 = (bf16[256,896]{1,0:T(8,128)(2,1)S(1)}, bf16[256,896]{1,0:T(8,128)(2,1)S(1)}, u32[]{:S(2)}, u32[]{:S(2)}) collective-permute-start(bf16[256,896]{1,0:T(8,128)(2,1)S(1)} %fusion.53), channel_id=1, source_target_pairs={{0,2},{1,3},{2,0},{3,1},{4,6},{5,7},{6,4},{7,5},{8,10},{9,11},{10,... | collective-permute-start | bytes 1376264 | tf_op jit(solution)/shard_map/ppermute | solution.py:302
  434.4 96.0 %reduce-scatter.8.cloned.1.call-start = ((), (), s32[]{:S(2)}) async-start(), calls=%async_computation.9 | async-start | bytes 2322432 | tf_op jit(solution)/shard_map/reduce_scatter | solution.py:500
  437.7 6.8 %collective-permute-start.32 = (bf16[1,2,256,256]{3,2,1,0:T(8,128)(2,1)S(1)}, bf16[1,2,256,256]{3,2,1,0:T(8,128)(2,1)S(1)}, u32[]{:S(2)}, u32[]{:S(2)}) collective-permute-start(bf16[1,2,256,256]{3,2,1,0:T(8,128)(2,1)S(1)} %pad_maximum_fusion.28), channel_id=1, source_target_pairs={{0,1},{1,0},{2,3},{3,2},{4,5},{5,4},{6,7},{7,6},{8,9},{9,8},{10,11... | collective-permute-start | bytes 786440 | tf_op jit(solution)/shard_map/ppermute | solution.py:302
  438.9 9.2 %collective-permute-start.33 = (bf16[1,2,256,256]{3,2,1,0:T(8,128)(2,1)S(1)}, bf16[1,2,256,256]{3,2,1,0:T(8,128)(2,1)S(1)}, u32[]{:S(2)}, u32[]{:S(2)}) collective-permute-start(bf16[1,2,256,256]{3,2,1,0:T(8,128)(2,1)S(1)} %pad_maximum_fusion.29), channel_id=1, source_target_pairs={{0,2},{1,3},{2,0},{3,1},{4,6},{5,7},{6,4},{7,5},{8,10},{9,11},{10,... | collective-permute-start | bytes 786440 | tf_op jit(solution)/shard_map/ppermute | solution.py:302
  440.5 7.7 %collective-permute-start.34 = (bf16[1,2,256,256]{3,2,1,0:T(8,128)(2,1)S(1)}, bf16[1,2,256,256]{3,2,1,0:T(8,128)(2,1)S(1)}, u32[]{:S(2)}, u32[]{:S(2)}) collective-permute-start(bf16[1,2,256,256]{3,2,1,0:T(8,128)(2,1)S(1)} %pad_maximum_fusion.30), channel_id=1, source_target_pairs={{0,3},{1,2},{2,1},{3,0},{4,7},{5,6},{6,5},{7,4},{8,11},{9,10},{10,... | collective-permute-start | bytes 786440 | tf_op jit(solution)/shard_map/ppermute | solution.py:302
  455.4 55.9 %collective-permute-start.22 = (bf16[1,256,896]{2,1,0:T(8,128)(2,1)}, bf16[1,256,896]{2,1,0:T(8,128)(2,1)}, u32[]{:S(2)}, u32[]{:S(2)}) collective-permute-start(bf16[1,256,896]{2,1,0:T(8,128)(2,1)} %get-tuple-element.136), channel_id=1, source_target_pairs={{0,3},{1,2},{2,1},{3,0},{4,7},{5,6},{6,5},{7,4},{8,11},{9,10},{10,... | collective-permute-start | bytes 1376264 | tf_op jit(solution)/shard_map/ppermute | solution.py:382
  462.5 50.9 %collective-permute-start.35 = (bf16[1,256,896]{2,1,0:T(8,128)(2,1)}, bf16[1,256,896]{2,1,0:T(8,128)(2,1)}, u32[]{:S(2)}, u32[]{:S(2)}) collective-permute-start(bf16[1,256,896]{2,1,0:T(8,128)(2,1)} %slice.482), channel_id=1, source_target_pairs={{0,3},{1,2},{2,1},{3,0},{4,7},{5,6},{6,5},{7,4},{8,11},{9,10},{10,... | collective-permute-start | bytes 1376264 | tf_op jit(solution)/shard_map/ppermute | solution.py:593
  515.7 13.8 %collective-permute-start.42 = (bf16[608,224]{0,1:T(8,128)(2,1)S(1)}, bf16[608,224]{0,1:T(8,128)(2,1)S(1)}, u32[]{:S(2)}, u32[]{:S(2)}) collective-permute-start(bf16[608,224]{0,1:T(8,128)(2,1)S(1)} %copy.131), channel_id=1, source_target_pairs={{0,0},{8,1},{16,2},{24,3},{4,4},{12,5},{20,6},{28,7},{1,8},{9,9},{... | collective-permute-start | bytes 817160 | tf_op jit(solution)/shard_map/ppermute | solution.py:510
  522.4 20.2 %collective-permute-start.39 = (bf16[112,224]{1,0:T(8,128)(2,1)S(1)}, bf16[112,224]{1,0:T(8,128)(2,1)S(1)}, u32[]{:S(2)}, u32[]{:S(2)}) collective-permute-start(bf16[112,224]{1,0:T(8,128)(2,1)S(1)} %get-tuple-element.158), channel_id=1, source_target_pairs={{0,1},{1,0},{2,3},{3,2},{4,5},{5,4},{6,7},{7,6},{8,9},{9,8},{10,11... | collective-permute-start | bytes 150536 | tf_op jit(solution)/shard_map/ppermute | solution.py:302
  527.3 16.8 %collective-permute-start.40 = (bf16[112,224]{1,0:T(8,128)(2,1)S(1)}, bf16[112,224]{1,0:T(8,128)(2,1)S(1)}, u32[]{:S(2)}, u32[]{:S(2)}) collective-permute-start(bf16[112,224]{1,0:T(8,128)(2,1)S(1)} %get-tuple-element.160), channel_id=1, source_target_pairs={{0,2},{1,3},{2,0},{3,1},{4,6},{5,7},{6,4},{7,5},{8,10},{9,11},{10,... | collective-permute-start | bytes 150536 | tf_op jit(solution)/shard_map/ppermute | solution.py:302
  528.5 15.6 %collective-permute-start.41 = (bf16[112,224]{1,0:T(8,128)(2,1)S(1)}, bf16[112,224]{1,0:T(8,128)(2,1)S(1)}, u32[]{:S(2)}, u32[]{:S(2)}) collective-permute-start(bf16[112,224]{1,0:T(8,128)(2,1)S(1)} %get-tuple-element.159), channel_id=1, source_target_pairs={{0,3},{1,2},{2,1},{3,0},{4,7},{5,6},{6,5},{7,4},{8,11},{9,10},{10,... | collective-permute-start | bytes 150536 | tf_op jit(solution)/shard_map/ppermute | solution.py:302
  531.5 14.2 %collective-permute-start.36 = (bf16[112,288]{1,0:T(8,128)(2,1)S(1)}, bf16[112,288]{1,0:T(8,128)(2,1)S(1)}, u32[]{:S(2)}, u32[]{:S(2)}) collective-permute-start(bf16[112,288]{1,0:T(8,128)(2,1)S(1)} %get-tuple-element.155), channel_id=1, source_target_pairs={{0,1},{1,0},{2,3},{3,2},{4,5},{5,4},{6,7},{7,6},{8,9},{9,8},{10,11... | collective-permute-start | bytes 193544 | tf_op jit(solution)/shard_map/ppermute | solution.py:302
  (82 other events, 764.9 us)
Sparse Core Ops, SparseCore 0:
  18.3 28.1 all-gather.7
  48.1 24.7 all-gather.9
  74.5 35.2 all-gather.11
  111.3 32.2 all-gather.13
  145.1 30.1 all-gather.15
  294.5 38.0 reduce-scatter.15
  335.0 35.6 reduce-scatter.13
  373.1 35.3 reduce-scatter.11
  434.5 35.8 reduce-scatter.9
  472.7 34.1 reduce-scatter.7

commit v2 on v1

v2 whole, which is shorter than its diff:
```python
import math
import jax
import jax.numpy as jnp
from jax import lax
from jax.experimental import pallas as pl
from jax.experimental.pallas import tpu as pltpu
from jax.sharding import PartitionSpec as P

HEADS = 14
KV_HEADS = 2
HEAD_DIM = 64
GROUP = HEADS // KV_HEADS
PAIRS = HEADS // 2
PAIR = 2 * HEAD_DIM
Q_WIDTH = HEADS * HEAD_DIM
K_WIDTH = KV_HEADS * HEAD_DIM

norm_eps = 1e-06
rope_base = 1000000.0
masked_value = -1e30
score_scale = HEAD_DIM ** (-0.5)
log2_e = math.log2(math.e)
bf16 = jnp.bfloat16
f32 = jnp.float32


def inverse_rms(tensor):
    return lax.rsqrt(jnp.mean(tensor * tensor, axis=-1, keepdims=True) + norm_eps)


def dot(a, b, dims):
    return lax.dot_general(a, b, (dims, ((), ())), preferred_element_type=f32)


NN = ((1,), (0,))
NT = ((1,), (1,))
TN = ((0,), (0,))


def rotation_tables(positions):
    half_width = HEAD_DIM // 2
    steps_up = jnp.arange(half_width).astype(f32)
    frequency = jnp.power(jnp.asarray(rope_base, f32), -2.0 * steps_up / HEAD_DIM)
    angles = positions.astype(f32)[:, None] * frequency[None, :]
    cosine = jnp.cos(angles)
    sine = jnp.sin(angles)
    return (
        jnp.concatenate([cosine, cosine, cosine, cosine], axis=-1),
        jnp.concatenate([-sine, sine, -sine, sine], axis=-1),
    )


def turn_pair(x, cosine, sine):
    lane = lax.broadcasted_iota(jnp.int32, x.shape, 1)
    quarter = HEAD_DIM // 2
    other = jnp.where(
        (lane // quarter) % 2 == 0,
        pltpu.roll(x, PAIR - quarter, 1),
        pltpu.roll(x, quarter, 1),
    )
    return x * cosine + other * sine


def swap_pair(x):
    return pltpu.roll(x.astype(f32), HEAD_DIM, 1)


def params():
    return pltpu.CompilerParams(vmem_limit_bytes=60 << 20)


def project_kernel(x_ref, gain_ref, w_ref, bias_ref, cos_ref, sin_ref, normed_ref, q_ref, kv_ref):
    x = x_ref[...].astype(f32)
    normed = (x * inverse_rms(x) * gain_ref[...]).astype(bf16)
    normed_ref[...] = normed
    projected = dot(normed, w_ref[...], NN) + bias_ref[...]
    cosine = cos_ref[...]
    sine = sin_ref[...]
    for pair in range(PAIRS + 1):
        lanes = slice(pair * PAIR, (pair + 1) * PAIR)
        turned = turn_pair(projected[:, lanes], cosine, sine).astype(bf16)
        if pair < PAIRS:
            q_ref[:, lanes] = turned
        else:
            kv_ref[:, :K_WIDTH] = turned
    kv_ref[:, K_WIDTH:] = projected[:, Q_WIDTH + K_WIDTH :].astype(bf16)


def row_spec(tile, width):
    return pl.BlockSpec((tile, width), lambda i: (i, 0))


def full_spec(*shape):
    return pl.BlockSpec(shape, lambda i: (0,) * len(shape))


def project_forward(tokens, gain, weight, bias, cosine, sine):
    rows, width = tokens.shape
    tile = rows // 2
    columns = weight.shape[1]
    return pl.pallas_call(
        project_kernel,
        grid=(2,),
        in_specs=[
            row_spec(tile, width),
            full_spec(1, width),
            full_spec(width, columns),
            full_spec(1, columns),
            row_spec(tile, PAIR),
            row_spec(tile, PAIR),
        ],
        out_specs=[row_spec(tile, width), row_spec(tile, Q_WIDTH), row_spec(tile, 2 * K_WIDTH)],
        out_shape=[
            jax.ShapeDtypeStruct((rows, width), bf16),
            jax.ShapeDtypeStruct((rows, Q_WIDTH), bf16),
            jax.ShapeDtypeStruct((rows, 2 * K_WIDTH), bf16),
        ],
        cost_estimate=pl.CostEstimate(
            flops=4 * rows * width * columns, bytes_accessed=5 << 20, transcendentals=0
        ),
        compiler_params=params(),
        name="project_forward",
    )(tokens, gain, weight, bias, cosine, sine)


def project_back_kernel(
    gq_ref, w_ref, x_ref, gain_ref, hidden_ref, cos_ref, sin_ref, *rest
):
    parts = rest[:-4]
    gkv_ref, tokens_ref, gain_sum_ref, bias_sum_ref = rest[-4:]
    total = parts[0][...].astype(f32)
    for part in parts[1:]:
        total = total + part[...].astype(f32)
    turned = turn_pair(total[:, :K_WIDTH], cos_ref[...], -sin_ref[...]).astype(bf16)
    gkv_ref[:, :K_WIDTH] = turned
    gkv_ref[:, K_WIDTH:] = total[:, K_WIDTH:].astype(bf16)
    grads = jnp.concatenate([gq_ref[...], gkv_ref[...]], axis=1)
    grad_normed = dot(grads, w_ref[...], NT)
    x = x_ref[...].astype(f32)
    inverse = inverse_rms(x)
    weighted = grad_normed * gain_ref[...]
    tokens_ref[...] = (
        hidden_ref[...]
        + inverse * weighted
        - x * (inverse * inverse * inverse * jnp.mean(weighted * x, axis=-1, keepdims=True))
    )

    @pl.when(pl.program_id(0) == 0)
    def _():
        gain_sum_ref[...] = jnp.zeros_like(gain_sum_ref)
        bias_sum_ref[...] = jnp.zeros_like(bias_sum_ref)

    gain_sum_ref[...] += jnp.sum(grad_normed * x * inverse, axis=0, keepdims=True)
    bias_sum_ref[...] += jnp.sum(grads.astype(f32), axis=0, keepdims=True)


def project_backward(grad_queries, weight, tokens, gain, grad_hidden, cosine, sine, parts):
    rows, width = tokens.shape
    tile = rows // 2
    columns = weight.shape[1]
    return pl.pallas_call(
        project_back_kernel,
        grid=(2,),
        in_specs=[
            row_spec(tile, Q_WIDTH),
            full_spec(width, columns),
            row_spec(tile, width),
            full_spec(1, width),
            row_spec(tile, width),
            row_spec(tile, PAIR),
            row_spec(tile, PAIR),
        ]
        + [row_spec(tile, 2 * K_WIDTH)] * len(parts),
        out_specs=[
            row_spec(tile, 2 * K_WIDTH),
            row_spec(tile, width),
            full_spec(1, width),
            full_spec(1, columns),
        ],
        out_shape=[
            jax.ShapeDtypeStruct((rows, 2 * K_WIDTH), bf16),
            jax.ShapeDtypeStruct((rows, width), f32),
            jax.ShapeDtypeStruct((1, width), f32),
            jax.ShapeDtypeStruct((1, columns), f32),
        ],
        cost_estimate=pl.CostEstimate(
            flops=4 * rows * width * columns, bytes_accessed=8 << 20, transcendentals=0
        ),
        compiler_params=params(),
        name="project_backward",
    )(grad_queries, weight, tokens, gain, grad_hidden, cosine, sine, *parts)


def pair_sides(both):
    x, x_swapped = both[:, :PAIR], both[:, PAIR:]
    low = lax.broadcasted_iota(jnp.int32, x.shape, 1) < HEAD_DIM
    zero = jnp.zeros_like(x)
    left = (jnp.where(low, x, zero), jnp.where(low, x_swapped, zero))
    right = (jnp.where(low, zero, x_swapped), jnp.where(low, zero, x))
    sides = {}
    for pair in range(PAIRS):
        key = (2 * pair // GROUP, (2 * pair + 1) // GROUP)
        if key not in sides:
            sides[key] = jnp.concatenate([left[key[0]], right[key[1]]], axis=0)
    return sides


def causal(block):
    key_at = lax.broadcasted_iota(jnp.int32, (block, block), 0)
    query_at = lax.broadcasted_iota(jnp.int32, (block, block), 1)
    return key_at <= query_at


def forward_kernel(order_ref, q_ref, *rest):
    parts = rest[:-7]
    o_ref, lse_ref, keys_ref, turned_ref, top_ref, total_ref, acc_ref = rest[-7:]
    block = q_ref.shape[1]
    turn = pl.program_id(0) % 2
    last = order_ref[turn]

    @pl.when(turn == 0)
    def _():
        for number, part in enumerate(parts):
            for half in range(2):
                at = order_ref[2 * number + half]
                keys = part[0, half, :, :K_WIDTH]
                keys_ref[at, :, :PAIR] = keys
                keys_ref[at, :, PAIR:] = swap_pair(keys).astype(bf16)
                turned_ref[at] = jnp.transpose(part[0, half, :, K_WIDTH:].astype(f32)).astype(
                    bf16
                )

    top_ref[...] = jnp.full_like(top_ref, masked_value)
    total_ref[...] = jnp.zeros_like(total_ref)
    acc_ref[...] = jnp.zeros_like(acc_ref)
    scale = score_scale * log2_e

    def step(index, diagonal):
        sides = pair_sides(keys_ref[index])
        values = turned_ref[index]
        if diagonal:
            allowed = causal(block)
        for pair in range(PAIRS):
            both = dot(
                sides[(2 * pair // GROUP, (2 * pair + 1) // GROUP)],
                q_ref[0, :, pair * PAIR : (pair + 1) * PAIR],
                NT,
            )
            for odd in range(2):
                head = 2 * pair + odd
                kv = head // GROUP
                scores = both[odd * block : (odd + 1) * block] * scale
                if diagonal:
                    scores = jnp.where(allowed, scores, masked_value)
                old = top_ref[head : head + 1, :]
                new = jnp.maximum(old, jnp.max(scores, axis=0, keepdims=True))
                shrink = jnp.exp2(old - new)
                weights = jnp.exp2(scores - new)
                top_ref[head : head + 1, :] = new
                total_ref[head : head + 1, :] = total_ref[
                    head : head + 1, :
                ] * shrink + jnp.sum(weights, axis=0, keepdims=True)
                rows = slice(head * HEAD_DIM, (head + 1) * HEAD_DIM)
                acc_ref[rows, :] = acc_ref[rows, :] * shrink + dot(
                    values[kv * HEAD_DIM : (kv + 1) * HEAD_DIM], weights.astype(bf16), NN
                )

    def body(index, carry):
        step(index, False)
        return carry

    lax.fori_loop(0, last, body, 0)
    step(last, True)
    for pair in range(PAIRS):
        halves = []
        for odd in range(2):
            head = 2 * pair + odd
            halves.append(
                acc_ref[head * HEAD_DIM : (head + 1) * HEAD_DIM, :]
                / total_ref[head : head + 1, :]
            )
        o_ref[0, :, pair * PAIR : (pair + 1) * PAIR] = jnp.transpose(
            jnp.concatenate(halves, axis=0)
        ).astype(bf16)
    lse_ref[0] = top_ref[...] + jnp.log2(total_ref[...])


def backward_kernel(order_ref, q_ref, o_ref, g_ref, lse_ref, cos_ref, sin_ref, *rest):
    parts = rest[:-8]
    dq_ref, dkv_ref, keys_ref, values_ref, turned_ref, dk_ref, dv_ref, acc_ref = rest[-8:]
    block = q_ref.shape[1]
    turn = pl.program_id(0) % 2
    last = order_ref[turn]
    scale = score_scale * log2_e

    @pl.when(turn == 0)
    def _():
        dk_ref[...] = jnp.zeros_like(dk_ref)
        dv_ref[...] = jnp.zeros_like(dv_ref)
        for number, part in enumerate(parts):
            for half in range(2):
                at = order_ref[2 * number + half]
                keys = part[0, half, :, :K_WIDTH]
                values = part[0, half, :, K_WIDTH:]
                keys_ref[at, :, :PAIR] = keys
                keys_ref[at, :, PAIR:] = swap_pair(keys).astype(bf16)
                values_ref[at, :, :PAIR] = values
                values_ref[at, :, PAIR:] = swap_pair(values).astype(bf16)
                turned_ref[at] = jnp.transpose(keys.astype(f32)).astype(bf16)

    acc_ref[...] = jnp.zeros_like(acc_ref)
    product = g_ref[0].astype(f32) * o_ref[0].astype(f32)
    coarse = product.astype(bf16)
    fine = (product - coarse.astype(f32)).astype(bf16)
    head_of = lax.broadcasted_iota(jnp.int32, (16, Q_WIDTH), 1) // HEAD_DIM
    picks = (head_of == lax.broadcasted_iota(jnp.int32, (16, Q_WIDTH), 0)).astype(bf16)
    delta = dot(picks, coarse, NT) + dot(picks, fine, NT)

    def step(index, diagonal):
        key_sides = pair_sides(keys_ref[index])
        value_sides = pair_sides(values_ref[index])
        keys_turned = turned_ref[index]
        if diagonal:
            allowed = causal(block)
        key_sum = [[None, None], [None, None]]
        value_sum = [[None, None], [None, None]]

        def add(sums, odd, kv, part):
            sums[odd][kv] = part if sums[odd][kv] is None else sums[odd][kv] + part

        for pair in range(PAIRS):
            which = (2 * pair // GROUP, (2 * pair + 1) // GROUP)
            lanes = slice(pair * PAIR, (pair + 1) * PAIR)
            queries = q_ref[0, :, lanes]
            grads = g_ref[0, :, lanes]
            both = dot(key_sides[which], queries, NT)
            both_grads = dot(value_sides[which], grads, NT)
            low_weights = []
            low_scores = []
            for odd in range(2):
                head = 2 * pair + odd
                part = slice(odd * block, (odd + 1) * block)
                weights = jnp.exp2(both[part] * scale - lse_ref[0, head : head + 1, :])
                if diagonal:
                    weights = jnp.where(allowed, weights, 0.0)
                change = weights * (both_grads[part] - delta[head : head + 1, :])
                low_weights.append(weights.astype(bf16))
                low_scores.append(change.astype(bf16))
                rows = slice(head * HEAD_DIM, (head + 1) * HEAD_DIM)
                acc_ref[rows, :] += dot(
                    keys_turned[which[odd] * HEAD_DIM : (which[odd] + 1) * HEAD_DIM],
                    low_scores[odd],
                    NN,
                )
            value_part = dot(jnp.concatenate(low_weights, axis=0), grads, NN)
            key_part = dot(jnp.concatenate(low_scores, axis=0), queries, NN)
            for odd in range(2):
                part = slice(odd * block, (odd + 1) * block)
                add(value_sum, odd, which[odd], value_part[part])
                add(key_sum, odd, which[odd], key_part[part])
        low = lax.broadcasted_iota(jnp.int32, (block, PAIR), 1) < HEAD_DIM
        for sums, out_ref in ((key_sum, dk_ref), (value_sum, dv_ref)):
            out_ref[index, :, :PAIR] += jnp.where(low, sums[0][0], sums[1][1])
            out_ref[index, :, PAIR:] += jnp.where(low, sums[0][1], sums[1][0])

    def body(index, carry):
        step(index, False)
        return carry

    lax.fori_loop(0, last, body, 0)
    step(last, True)
    for pair in range(PAIRS):
        straight = jnp.transpose(acc_ref[pair * PAIR : (pair + 1) * PAIR, :]) * score_scale
        dq_ref[0, :, pair * PAIR : (pair + 1) * PAIR] = turn_pair(
            straight, cos_ref[0], -sin_ref[0]
        ).astype(bf16)

    @pl.when(turn == 1)
    def _():
        for slot in range(2 * len(parts)):
            at = order_ref[slot]
            keys = dk_ref[at, :, :PAIR] + swap_pair(dk_ref[at, :, PAIR:])
            dkv_ref[0, slot, :, :K_WIDTH] = (keys * score_scale).astype(bf16)
            values = dv_ref[at, :, :PAIR] + swap_pair(dv_ref[at, :, PAIR:])
            dkv_ref[0, slot, :, K_WIDTH:] = values.astype(bf16)


def attention_specs(block, parts):
    def rows(width):
        return pl.BlockSpec((1, block, width), lambda i, order: (i, 0, 0))

    def halves(number):
        return pl.BlockSpec((1, number, block, 2 * K_WIDTH), lambda i, order: (i // 2, 0, 0, 0))

    stats = pl.BlockSpec((1, 16, block), lambda i, order: (i, 0, 0))
    return rows, halves, stats


def attend_forward(order, queries, parts):
    count, block, _ = queries.shape
    slots = 2 * len(parts)
    rows, halves, stats = attention_specs(block, parts)
    pairs_done = count * block * (slots // 2 + 1) * block * HEADS
    return pl.pallas_call(
        forward_kernel,
        grid_spec=pltpu.PrefetchScalarGridSpec(
            num_scalar_prefetch=1,
            grid=(count,),
            in_specs=[rows(Q_WIDTH)] + [halves(2)] * len(parts),
            out_specs=[rows(Q_WIDTH), stats],
            scratch_shapes=[
                pltpu.VMEM((slots, block, 2 * PAIR), bf16),
                pltpu.VMEM((slots, PAIR, block), bf16),
                pltpu.VMEM((16, block), f32),
                pltpu.VMEM((16, block), f32),
                pltpu.VMEM((Q_WIDTH, block), f32),
            ],
        ),
        out_shape=[
            jax.ShapeDtypeStruct((count, block, Q_WIDTH), bf16),
            jax.ShapeDtypeStruct((count, 16, block), f32),
        ],
        cost_estimate=pl.CostEstimate(
            flops=pairs_done * 4 * 256, bytes_accessed=4 << 20, transcendentals=pairs_done
        ),
        compiler_params=params(),
        name="attend_forward",
    )(order, queries, *parts)


def attend_backward(order, queries, parts, mixed, grads, stats_in, cosine, sine):
    count, block, _ = queries.shape
    slots = 2 * len(parts)
    rows, halves, stats = attention_specs(block, parts)
    pairs_done = count * block * (slots // 2 + 1) * block * HEADS
    return pl.pallas_call(
        backward_kernel,
        grid_spec=pltpu.PrefetchScalarGridSpec(
            num_scalar_prefetch=1,
            grid=(count,),
            in_specs=[
                rows(Q_WIDTH),
                rows(Q_WIDTH),
                rows(Q_WIDTH),
                stats,
                rows(PAIR),
                rows(PAIR),
            ]
            + [halves(2)] * len(parts),
            out_specs=[rows(Q_WIDTH), halves(slots)],
            scratch_shapes=[
                pltpu.VMEM((slots, block, 2 * PAIR), bf16),
                pltpu.VMEM((slots, block, 2 * PAIR), bf16),
                pltpu.VMEM((slots, PAIR, block), bf16),
                pltpu.VMEM((slots, block, 2 * PAIR), f32),
                pltpu.VMEM((slots, block, 2 * PAIR), f32),
                pltpu.VMEM((Q_WIDTH, block), f32),
            ],
        ),
        out_shape=[
            jax.ShapeDtypeStruct((count, block, Q_WIDTH), bf16),
            jax.ShapeDtypeStruct((count // 2, slots, block, 2 * K_WIDTH), bf16),
        ],
        cost_estimate=pl.CostEstimate(
            flops=pairs_done * 10 * 256, bytes_accessed=8 << 20, transcendentals=pairs_done
        ),
        compiler_params=params(),
        name="attend_backward",
    )(order, queries, mixed, grads, stats_in, cosine, sine, *parts)


def ffn_kernel(x_ref, c_ref, w_ref, *rest):
    out_ref, grad_ref, x_all, c_all, active_all, gate_all, up_all = rest[-7:]
    seq_size, _, depth, columns = w_ref.shape
    width = seq_size * depth
    x = x_ref[...]
    c = c_ref[...]
    x_all[0] = x
    c_all[0] = c
    gate_w = w_ref[:, 0].reshape(width, columns)
    up_w = w_ref[:, 1].reshape(width, columns)
    down_w = w_ref[:, 2].reshape(width, columns)
    gate = dot(x, gate_w, NN)
    up = dot(x, up_w, NN)
    grad_active = dot(c, down_w, NN)
    sigmoid = jax.nn.sigmoid(gate)
    silu = gate * sigmoid
    active = (silu * up).astype(bf16)
    grad_gate = (grad_active * up * sigmoid * (1.0 + gate * (1.0 - sigmoid))).astype(bf16)
    grad_up = (grad_active * silu).astype(bf16)
    active_all[0] = active
    gate_all[0] = grad_gate
    up_all[0] = grad_up
    grad_ref[...] = (dot(grad_gate, gate_w, NT) + dot(grad_up, up_w, NT)).astype(bf16)
    out_ref[...] = dot(active, down_w, NT).astype(bf16)


def ffn(number, count, x, c, weights, buffers):
    rows, width = x.shape
    columns = weights.shape[3]
    tile = rows // 2

    def slot(columns):
        return pl.BlockSpec((1, tile, columns), lambda i: (number, i, 0))

    wide = jax.ShapeDtypeStruct((count, rows, width), bf16)
    inner = jax.ShapeDtypeStruct((count, rows, columns), bf16)
    return pl.pallas_call(
        ffn_kernel,
        grid=(2,),
        in_specs=[row_spec(tile, width), row_spec(tile, width), full_spec(*weights.shape)]
        + [pl.BlockSpec(memory_space=pl.ANY)] * len(buffers),
        out_specs=[row_spec(tile, width), row_spec(tile, width)]
        + [slot(width)] * 2
        + [slot(columns)] * 3,
        out_shape=[jax.ShapeDtypeStruct((rows, width), bf16)] * 2 + [wide] * 2 + [inner] * 3,
        input_output_aliases={3 + i: 2 + i for i in range(len(buffers))},
        cost_estimate=pl.CostEstimate(
            flops=14 * rows * width * columns, bytes_accessed=16 << 20, transcendentals=0
        ),
        compiler_params=params(),
        name="ffn",
    )(x, c, weights, *buffers)


def ffn_weights_kernel(x_ref, c_ref, active_ref, gate_ref, up_ref, out_ref, acc_ref):
    step = pl.program_id(0)
    seq_size, _, depth, columns = out_ref.shape

    @pl.when(step == 0)
    def _():
        acc_ref[...] = jnp.zeros_like(acc_ref)

    x = x_ref[0]
    acc_ref[0] += dot(x, gate_ref[0], TN)
    acc_ref[1] += dot(x, up_ref[0], TN)
    acc_ref[2] += dot(c_ref[0], active_ref[0], TN)

    @pl.when(step == pl.num_programs(0) - 1)
    def _():
        for which in range(3):
            out_ref[:, which] = acc_ref[which].reshape(seq_size, depth, columns).astype(bf16)


def ffn_weights(seq_size, x, c, active, grad_gate, grad_up):
    count, rows, width = x.shape
    columns = active.shape[2]

    def slot(columns):
        return pl.BlockSpec((1, rows, columns), lambda i: (i, 0, 0))

    shape = (seq_size, 3, width // seq_size, columns)
    return pl.pallas_call(
        ffn_weights_kernel,
        grid=(count,),
        in_specs=[slot(width)] * 2 + [slot(columns)] * 3,
        out_specs=pl.BlockSpec(shape, lambda i: (0, 0, 0, 0)),
        out_shape=jax.ShapeDtypeStruct(shape, bf16),
        scratch_shapes=[pltpu.VMEM((3, width, columns), f32)],
        cost_estimate=pl.CostEstimate(
            flops=6 * count * rows * width * columns, bytes_accessed=30 << 20, transcendentals=0
        ),
        compiler_params=params(),
        name="ffn_weights",
    )(x, c, active, grad_gate, grad_up)


def hop(x, ctx_size, mask):
    return lax.ppermute(x, "ctx", [(i, i ^ mask) for i in range(ctx_size)])


def spread(x, ctx_size):
    if ctx_size != 4:
        return [x] + [hop(x, ctx_size, k) for k in range(1, ctx_size)]
    half = x.shape[0] // 2
    front, back = x[:half], x[half:]
    front_1 = hop(front, 4, 1)
    back_2 = hop(back, 4, 2)
    front_far = hop(jnp.concatenate([front, front_1], axis=0), 4, 2)
    back_far = hop(jnp.concatenate([back, back_2], axis=0), 4, 1)
    return [x, jnp.concatenate([front_1, back_2], axis=0), front_far, back_far]


def gathered_sum(parts, ctx_size):
    if ctx_size != 4:
        total = parts[0].astype(f32)
        for k in range(1, ctx_size):
            total = total + hop(parts[k], ctx_size, k).astype(f32)
        return total
    own, near, front_far, back_far = parts
    half = own.shape[0] // 2
    front_got = hop(front_far, 4, 2)
    back_got = hop(back_far, 4, 1)
    front_next = (near[:half].astype(f32) + front_got[half:].astype(f32)).astype(bf16)
    back_next = (near[half:].astype(f32) + back_got[half:].astype(f32)).astype(bf16)
    front_last = hop(front_next, 4, 1)
    back_last = hop(back_next, 4, 2)
    return jnp.concatenate(
        [
            own[:half].astype(f32) + front_got[:half].astype(f32) + front_last.astype(f32),
            own[half:].astype(f32) + back_got[:half].astype(f32) + back_last.astype(f32),
        ],
        axis=0,
    )


def in_order(pieces, place, ctx_size):
    result = jnp.zeros((ctx_size,) + pieces[0].shape, pieces[0].dtype)
    for k, piece in enumerate(pieces):
        result = lax.dynamic_update_index_in_dim(result, piece, place ^ k, 0)
    return result


def on_device(
    seq_size,
    ctx_size,
    tokens,
    attention_gain,
    project_weight,
    project_bias,
    output_weight,
    feedforward_gain,
    gate_weight,
    up_weight,
    down_weight,
    cotangent,
):
    sequences, block_rows, width = tokens.shape
    place = lax.axis_index("ctx")
    half = block_rows // 2
    rows = sequences * block_rows
    fold = seq_size // ctx_size
    fold_place = lax.axis_index("seq") % fold
    mirror = [(i, ctx_size - 1 - i) for i in range(ctx_size)]

    def crossed(x, j):
        return lax.ppermute(
            x,
            ("seq", "ctx"),
            [
                ((c * fold + r) * ctx_size + q, (q * fold + (r + j) % fold) * ctx_size + c)
                for c in range(ctx_size)
                for r in range(fold)
                for q in range(ctx_size)
            ],
        )

    def crossed_parts(parts):
        came = jnp.zeros_like(parts)
        for j in range(fold):
            part = lax.dynamic_index_in_dim(parts, (fold_place + j) % fold, 0, keepdims=False)
            came = lax.dynamic_update_index_in_dim(
                came, crossed(part, j), (fold_place - j) % fold, 0
            )
        return came

    def zigzag(x):
        return jnp.concatenate([x[:, :half], lax.ppermute(x[:, half:], "ctx", mirror)], axis=1)

    owners = [place ^ k for k in range(ctx_size)]
    order = jnp.stack(
        [spot for owner in owners for spot in (2 * owner, 2 * (ctx_size - 1 - owner) + 1)]
    ).astype(jnp.int32)
    positions = (order[:2, None] * half + jnp.arange(half, dtype=jnp.int32)[None, :]).reshape(-1)
    cosine, sine = rotation_tables(jnp.tile(positions, sequences))

    def columns_whole(shard):
        pieces = [shard] + [hop(shard, ctx_size, k) for k in range(1, ctx_size)]
        ordered = in_order(pieces, place, ctx_size)
        return jnp.moveaxis(ordered, 0, 1).reshape(shard.shape[0], -1)

    gain_width = attention_gain.shape[0]
    bias_width = project_bias.shape[0]
    project_full = lax.all_gather(columns_whole(project_weight), "seq", axis=0, tiled=True)
    vectors = jnp.concatenate([attention_gain, project_bias, feedforward_gain])[None, :]
    vector_pieces = [vectors] + [hop(vectors, ctx_size, k) for k in range(1, ctx_size)]
    vectors_all = in_order(vector_pieces, place, ctx_size)[:, 0, :].astype(f32)
    attention_full = vectors_all[:, :gain_width].reshape(1, -1)
    bias_full = vectors_all[:, gain_width : gain_width + bias_width].reshape(1, -1)
    feedforward_full = vectors_all[:, gain_width + bias_width :].reshape(1, -1)

    output_columns = columns_whole(output_weight)
    down_rows, down_columns = down_weight.shape
    depth = down_columns // fold
    down_turned = crossed_parts(down_weight.T.reshape(fold, depth, down_rows))
    down_turned = jnp.moveaxis(down_turned, 0, 1).reshape(depth, fold * down_rows)
    output_full = lax.all_gather(output_columns, "seq", axis=0, tiled=True)
    weights_mine = lax.all_gather(
        jnp.stack([gate_weight, up_weight, down_turned]), "seq", axis=0
    )

    tokens_mine = zigzag(tokens).reshape(rows, width)
    normed, queries, pairs_mine = project_forward(
        tokens_mine, attention_full, project_full, bias_full, cosine, sine
    )
    queries = queries.reshape(sequences * 2, half, Q_WIDTH)
    pairs_mine = pairs_mine.reshape(sequences, 2, half, 2 * K_WIDTH)
    pair_parts = [pairs_mine] + [hop(pairs_mine, ctx_size, k) for k in range(1, ctx_size)]
    cotangent_late = lax.optimization_barrier((cotangent, pair_parts[-1]))[0]
    grad_low = zigzag(cotangent_late).reshape(rows, width)
    grad_parts = spread(grad_low, ctx_size)
    mixed, row_stats = attend_forward(order, queries, pair_parts)
    mixed_rows = mixed.reshape(rows, Q_WIDTH)
    hidden = tokens_mine.astype(f32) + dot(mixed_rows, output_full, NN)
    inverse_ffn = inverse_rms(hidden)
    normed_ffn = (hidden * inverse_ffn * feedforward_full).astype(bf16)

    normed_parts = spread(normed_ffn, ctx_size)
    output_parts = []
    grad_normed_parts = []
    buffers = []
    for number, (part, grad_part) in enumerate(zip(normed_parts, grad_parts)):
        output_part, grad_normed_part, *buffers = ffn(
            number, ctx_size, part, grad_part, weights_mine, buffers
        )
        output_parts.append(output_part)
        grad_normed_parts.append(grad_normed_part)
    grad_normed_ffn = gathered_sum(grad_normed_parts, ctx_size)
    weight_grads = lax.psum_scatter(ffn_weights(seq_size, *buffers), "seq", scatter_dimension=0)

    grad_ffn_gain = jnp.sum(grad_normed_ffn * hidden * inverse_ffn, axis=0)
    weighted_ffn = grad_normed_ffn * feedforward_full
    grad_hidden = (
        grad_low.astype(f32)
        + inverse_ffn * weighted_ffn
        - hidden
        * inverse_ffn
        * inverse_ffn
        * inverse_ffn
        * jnp.mean(weighted_ffn * hidden, axis=-1, keepdims=True)
    )
    hidden_low = grad_hidden.astype(bf16)
    grad_mixed = dot(hidden_low, output_full, NT).astype(bf16)

    grad_queries, pair_grads = attend_backward(
        order,
        queries,
        pair_parts,
        mixed,
        grad_mixed.reshape(sequences * 2, half, Q_WIDTH),
        row_stats,
        cosine.reshape(sequences * 2, half, PAIR),
        sine.reshape(sequences * 2, half, PAIR),
    )
    pair_sums = [pair_grads[:, :2].reshape(rows, 2 * K_WIDTH)]
    for k in range(1, ctx_size):
        pair_sums.append(
            hop(pair_grads[:, 2 * k : 2 * k + 2], ctx_size, k).reshape(rows, 2 * K_WIDTH)
        )
    grad_queries = grad_queries.reshape(rows, Q_WIDTH)
    grad_pairs, tokens_grad, gain_sum, bias_sum = project_backward(
        grad_queries,
        project_full,
        tokens_mine,
        attention_full,
        grad_hidden,
        cosine,
        sine,
        pair_sums,
    )

    def columns_then_rows_summed(turned):
        parts = turned.astype(bf16).reshape(ctx_size, turned.shape[0] // ctx_size, turned.shape[1])

        def part(k):
            return lax.dynamic_index_in_dim(parts, place ^ k, 0, keepdims=False)

        total = part(0).astype(f32)
        for k in range(1, ctx_size):
            total = total + hop(part(k), ctx_size, k).astype(f32)
        return lax.psum_scatter(
            total.astype(bf16).T, "seq", scatter_dimension=0, tiled=True
        ).astype(f32)

    output_out = columns_then_rows_summed(dot(hidden_low, mixed_rows, TN))
    project_out = columns_then_rows_summed(
        dot(jnp.concatenate([grad_queries, grad_pairs], axis=1), normed, TN)
    )

    tokens_grad = tokens_grad.reshape(tokens.shape)
    tokens_gradient = jnp.concatenate(
        [
            tokens_grad[:, :half],
            lax.ppermute(tokens_grad[:, half:].astype(bf16), "ctx", mirror).astype(f32),
        ],
        axis=1,
    )
    output_late = lax.optimization_barrier((tuple(output_parts), grad_mixed))[0]
    output_zigzag = hidden + gathered_sum(list(output_late), ctx_size)
    layer_output = zigzag(output_zigzag.astype(bf16).reshape(tokens.shape))

    down_grads = weight_grads[2].reshape(depth, fold, down_rows)
    down_out = crossed_parts(jnp.moveaxis(down_grads, 1, 0)).reshape(down_columns, down_rows).T

    sums = lax.psum(
        jnp.concatenate([gain_sum[0], bias_sum[0], grad_ffn_gain]), ("seq", "ctx")
    )

    def my_part(start, whole):
        own = whole // ctx_size
        return lax.dynamic_slice_in_dim(sums, start + place * own, own, 0)

    project_width = bias_width * ctx_size
    return (
        layer_output,
        tokens_gradient,
        my_part(0, width),
        project_out,
        my_part(width, project_width),
        output_out,
        my_part(width + project_width, width),
        weight_grads[0].astype(f32),
        weight_grads[1].astype(f32),
        down_out.astype(f32),
    )


def solution(mesh):
    matrix = P("seq", "ctx")
    vector = P("ctx")
    activation = P("seq", "ctx", None)

    def step(*arrays):
        return on_device(mesh.shape["seq"], mesh.shape["ctx"], *arrays)

    return jax.shard_map(
        step,
        mesh=mesh,
        in_specs=(
            activation,
            vector,
            matrix,
            vector,
            matrix,
            vector,
            matrix,
            matrix,
            matrix,
            activation,
        ),
        out_specs=(
            activation,
            activation,
            vector,
            matrix,
            vector,
            matrix,
            vector,
            matrix,
            matrix,
            matrix,
        ),
        check_vma=False,
    )
```

time: 566 us -> 523 us (0.924)
  the two profiles are of different devices: /device:TPU:0 before, /device:TPU:2 now
where the time goes in v2:
time: 523 us; the launch traced here: 516 us
  waiting for transfers between devices  154 us (29%)
  Pallas kernels  153 us (29%)
  blocking collectives  57.6 us (11%)
  starting transfers between devices  49.9 us (10%)
  local copies, waits for them, and re-layouts  41.6 us (8%)
  other arithmetic  33.7 us (6%)
  between operations  15.1 us (3%)
  matrix products  10.8 us (2%)
    ppermute x37, waiting for transfers between devices, hop(): return lax.ppermute(x, 'ctx', [(i, i ^ mask) for i in range(ctx_size)])  90.6 us
    psum x1, blocking collectives, on_device(): lax.psum(jnp.concatenate([gain_sum[0], bias_sum[0], grad_ffn_gain]), ('se...  57.6 us
    pallas_call x4, Pallas kernels, ffn(): pl.pallas_call(ffn_kernel, grid=(2,), in_specs=[row_spec(tile, width), ro...  55.2 us
    ppermute x37, starting transfers between devices, hop(): return lax.ppermute(x, 'ctx', [(i, i ^ mask) for i in range(ctx_size)])  39.9 us
    pallas_call x1, Pallas kernels, attend_backward(): pl.pallas_call(backward_kernel, grid_spec=pltpu.PrefetchScalarGridSpec(nu...  36.3 us
    ppermute x4, waiting for transfers between devices, crossed(): lax.ppermute(x, ('seq', 'ctx'), [((c * fold + r) * ctx_size + q, (q * fol...  36.3 us
    pallas_call x1, Pallas kernels, attend_forward(): pl.pallas_call(forward_kernel, grid_spec=pltpu.PrefetchScalarGridSpec(num...  27.3 us
    pallas_call x1, Pallas kernels, ffn_weights(): pl.pallas_call(ffn_weights_kernel, grid=(count,), in_specs=[slot(width)]...  22.7 us
  transfers between devices with their start and end apart: 51, of which 26 were waited for; matrix products, arithmetic and copies ran while one was open for 16% of the time, Pallas kernels for 23%

profile of v2, /device:TPU:2, one launch (start us, length us, event | category | flops | bytes accessed | tf_op | source)
XLA Modules:
  0.0 516.0 jit_solution(14249245591245320939)
XLA Ops:
  7.3 2.0 collective-permute-start.5
  20.3 2.2 dynamic_update_slice.64
  23.2 2.2 dynamic_update_slice.65
  25.4 2.2 dynamic_update_slice.66
  27.5 2.2 dynamic_update_slice.67
  30.8 4.0 collective-permute-start.14
  34.9 23.5 %collective-permute-done.14 = bf16[112,608]{1,0:T(8,128)(2,1)S(1)} collective-permute-done((bf16[112,608]{1,0:T(8,128)(2,1)S(1)}, bf16[112,608]{1,0:T(8,128)(2,1)S(1)}, u32[]{:S(2)}, u32[]{:S(2)}) %collective-permute-start.14) | collective-permute-done | bytes 136224 | tf_op jit(solution)/shard_map/ppermute | solution.py:637
  58.7 2.2 collective-permute-done.15
  61.3 3.1 dynamic_update_slice.68
  64.5 3.1 dynamic_update_slice.69
  69.1 3.4 collective-permute-start.3
  76.8 8.7 %collective-permute-done = bf16[1,256,896]{2,1,0:T(8,128)(2,1)S(1)} collective-permute-done((bf16[1,256,896]{2,1,0:T(8,128)(2,1)S(1)}, bf16[1,256,896]{2,1,0:T(8,128)(2,1)S(1)}, u32[]{:S(2)}, u32[]{:S(2)}) %collective-permute-start) | collective-permute-done | bytes 458784 | tf_op jit(solution)/shard_map/ppermute | solution.py:658
  86.5 5.1 project_forward.1
  95.8 6.2 %collective-permute-done.9.rest_3_ = bf16[1,2,256,256]{3,2,1,0:T(8,128)(2,1)S(1)} collective-permute-done((bf16[1,2,256,256]{3,2,1,0:T(8,128)(2,1)}, bf16[1,2,256,256]{3,2,1,0:T(8,128)(2,1)S(1)}, u32[]{:S(2)}, u32[]{:S(2)}) %collective-permute-start.9) | collective-permute-done | bytes 262176 | tf_op jit(solution)/shard_map/ppermute | solution.py:569
  103.4 3.1 collective-permute-done.7.rest_1_
  108.3 27.3 %attend_forward.1 = (bf16[2,256,896]{2,1,0:T(8,128)(2,1)}, f32[2,16,256]{2,1,0:T(8,128)}) custom-call(s32[8]{0:T(128)} %stack.46.order_ref, bf16[2,256,896]{2,1,0:T(8,128)(2,1)} %bitcast.152, bf16[1,2,256,256]{3,2,1,0:T(8,128)(2,1)} %bitcast.150, bf16[1,2,256,256]{3,2,1,0:T(8,128)(2,1)} %copy-done.20, bf16[1,2,256,256]{3,2,1,0:T(8,128)(2,1)} %copy-done.21, ...), custom_call_target="tpu_custom_call" | custom-call | flops 9395240960 | bytes 4194304 | tf_op jit(solution)/shard_map/attend_forward/pallas_call | solution.py:404
  135.6 3.2 multiply_reduce_fusion.2
  143.2 9.3 %collective-permute-done.16 = bf16[256,896]{1,0:T(8,128)(2,1)S(1)} collective-permute-done((bf16[256,896]{1,0:T(8,128)(2,1)S(1)}, bf16[256,896]{1,0:T(8,128)(2,1)S(1)}, u32[]{:S(2)}, u32[]{:S(2)}) %collective-permute-start.16) | collective-permute-done | bytes 458784 | tf_op jit(solution)/shard_map/ppermute | solution.py:569
  158.1 4.3 collective-permute-done.18
  166.8 13.7 %ffn.4 = (bf16[512,896]{1,0:T(8,128)(2,1)}, bf16[512,896]{1,0:T(8,128)(2,1)}, bf16[4,512,896]{2,1,0:T(8,128)(2,1)}, bf16[4,512,896]{2,1,0:T(8,128)(2,1)}, bf16[4...) custom-call(bf16[512,896]{1,0:T(8,128)(2,1)} %copy-done.1, ...), custom_call_target="tpu_custom_call" | custom-call | flops 7809794048 | bytes 16777216 | tf_op jit(solution)/shard_map/ffn/pallas_call | solution.py:508
  180.5 14.0 %ffn.5 = (bf16[512,896]{1,0:T(8,128)(2,1)}, bf16[512,896]{1,0:T(8,128)(2,1)}, bf16[4,512,896]{2,1,0:T(8,128)(2,1)}, bf16[4,512,896]{2,1,0:T(8,128)(2,1)}, bf16[4...) custom-call(bf16[512,896]{1,0:T(8,128)(2,1)} %get-tuple-element.137., ...), custom_call_target="tpu_custom_call", output_to_operand_aliasing={{2}: (3, {}), {3}: (4, {}), {4}: (5, {}), {5}: (6, {}), {6}... | custom-call | flops 7809794048 | bytes 16777216 | tf_op jit(solution)/shard_map/ffn/pallas_call | solution.py:508
  194.5 6.4 %collective-permute-done.21.c_ref = bf16[512,896]{1,0:T(8,128)(2,1)} collective-permute-done((bf16[512,896]{1,0:T(8,128)(2,1)}, bf16[512,896]{1,0:T(8,128)(2,1)}, u32[]{:S(2)}, u32[]{:S(2)}) %collective-permute-start.21) | collective-permute-done | bytes 917536 | tf_op jit(solution)/shard_map/ppermute | solution.py:569
  201.0 13.8 %ffn.6 = (bf16[512,896]{1,0:T(8,128)(2,1)}, bf16[512,896]{1,0:T(8,128)(2,1)}, bf16[4,512,896]{2,1,0:T(8,128)(2,1)}, bf16[4,512,896]{2,1,0:T(8,128)(2,1)}, bf16[4...) custom-call(bf16[512,896]{1,0:T(8,128)(2,1)} %collective-permute-don, ...), custom_call_target="tpu_custom_call", output_to_operand_aliasing={{2}: (3, {}), {3}: (4, {}), {4}: (5, {}), {5}: (6, {}), {6}... | custom-call | flops 7809794048 | bytes 16777216 | tf_op jit(solution)/shard_map/ffn/pallas_call | solution.py:508
  214.8 13.7 %ffn.7 = (bf16[512,896]{1,0:T(8,128)(2,1)}, bf16[512,896]{1,0:T(8,128)(2,1)}, bf16[4,512,896]{2,1,0:T(8,128)(2,1)}, bf16[4,512,896]{2,1,0:T(8,128)(2,1)}, bf16[4...) custom-call(bf16[512,896]{1,0:T(8,128)(2,1)} %collective-permute-don, ...), custom_call_target="tpu_custom_call", output_to_operand_aliasing={{2}: (3, {}), {3}: (4, {}), {4}: (5, {}), {5}: (6, {}), {6}... | custom-call | flops 7809794048 | bytes 16777216 | tf_op jit(solution)/shard_map/ffn/pallas_call | solution.py:508
  228.5 22.7 %ffn_weights.1 = bf16[8,3,112,1216]{3,2,1,0:T(8,128)(2,1)} custom-call(bf16[4,512,896]{2,1,0:T(8,128)(2,1)} %get-tuple-element.93.x_ref, bf16[4,512,896]{2,1,0:T(8,128)(2,1)} %get-tuple-element.94.c_ref, bf16[4,512,1216]{2,1,0:T(8,128)(2,1)} %get-tuple-element.95.active_ref, bf16[4,512,1216]{2,1,0:T(8,128)(2,1)} %get-tuple-element.96.gate_ref, ...), custom_call_target="tpu_custom_call" | custom-call | flops 13388218368 | bytes 31457280 | tf_op jit(solution)/shard_map/ffn_weights/pallas_call | solution.py:553
  253.3 19.4 %collective-permute-done.26 = bf16[512,896]{1,0:T(8,128)(2,1)S(1)} collective-permute-done((bf16[512,896]{1,0:T(8,128)(2,1)}, bf16[512,896]{1,0:T(8,128)(2,1)S(1)}, u32[]{:S(2)}, u32[]{:S(2)}) %collective-permute-start.26) | collective-permute-done | bytes 917536 | tf_op jit(solution)/shard_map/ppermute | solution.py:569
  278.5 7.3 %collective-permute-done.25 = bf16[256,896]{1,0:T(8,128)(2,1)S(1)} collective-permute-done((bf16[256,896]{1,0:T(8,128)(2,1)S(1)}, bf16[256,896]{1,0:T(8,128)(2,1)S(1)}, u32[]{:S(2)}, u32[]{:S(2)}) %collective-permute-start.25) | collective-permute-done | bytes 458784 | tf_op jit(solution)/shard_map/ppermute | solution.py:569
  288.3 2.2 convolution_convert_fusion.2
  290.4 36.3 %attend_backward.1 = (bf16[2,256,896]{2,1,0:T(8,128)(2,1)}, bf16[1,8,256,256]{3,2,1,0:T(8,128)(2,1)}) custom-call(s32[8]{0:T(128)} %stack.46.order_ref, bf16[2,256,896]{2,1,0:T(8,128)(2,1)} %bitcast.153, bf16[2,256,896]{2,1,0:T(8,128)(2,1)} %get-tuple-element.56.o_ref, bf16[2,256,896]{2,1,0:T(8,128)(2,1)} %bitcast.158, ...), custom_call_target="tpu_custom_call" | custom-call | flops 23488102400 | bytes 8388608 | tf_op jit(solution)/shard_map/attend_backward/pallas_call | solution.py:436
  326.7 2.4 fusion.21
  340.6 2.3 collective-permute-done.34
  345.4 6.3 %project_backward.1 = (bf16[512,256]{1,0:T(8,128)(2,1)}, f32[512,896]{1,0:T(8,128)}, f32[1,896]{1,0:T(1,128)}, f32[1,1152]{1,0:T(1,128)}) custom-call(bf16[512,896]{1,0:T(8,128)(2,1)} %bitcast.156, bf16[896,1152]{1,0:T(8,128)(2,1)} %all-gather.5.cloned.1.call-done.w_ref, bf16[512,896]{1,0:T(8,128)(2,1)} %maximum_bitcast_fusion.x_ref, ...), custom_call_target="tpu_custom_call" | custom-call | flops 2113929216 | bytes 8388608 | tf_op jit(solution)/shard_map/project_backward/pallas_call | solution.py:161
  351.8 2.0 slice.204
  353.8 4.3 convolution_convert_fusion
  359.9 2.7 collective-permute-done.41
  363.7 2.1 fusion.12
  365.9 2.4 dynamic-slice_bitcast_fusion.2
  371.5 20.4 %collective-permute-done.28 = bf16[512,896]{1,0:T(8,128)(2,1)S(1)} collective-permute-done((bf16[512,896]{1,0:T(8,128)(2,1)}, bf16[512,896]{1,0:T(8,128)(2,1)S(1)}, u32[]{:S(2)}, u32[]{:S(2)}) %collective-permute-start.28) | collective-permute-done | bytes 917536 | tf_op jit(solution)/shard_map/ppermute | solution.py:569
  394.2 2.6 add_convert_fusion.1
  396.8 2.6 collective-permute-start.31
  399.3 57.6 %psum.7 = f32[2944]{0:T(1024)S(1)} all-reduce(f32[2944]{0:T(1024)S(1)} %pad_maximum_fusion.14), channel_id=1, replica_groups=mesh['seq'=8,'ctx'=4] {'seq','ctx'}, use_global_device_ids=true, to_apply=%region_3.4 | all-reduce | flops 2944 | bytes 23552 | tf_op jit(solution)/shard_map/psum | solution.py:795
  458.3 2.0 convert_element_type.220
  463.2 2.0 convert_add_fusion.4
  467.2 2.2 fusion.25
  470.4 1.9 collective-permute-start.43
  475.1 18.5 %reduce-scatter.10.cloned.1.call-done = bf16[112,288]{1,0:T(8,128)(2,1)} async-done(((bf16[896,288]{1,0:T(8,128)(2,1)}), bf16[112,288]{1,0:T(8,128)(2,1)}) %reduce-scatter.10.cloned.1.call-update) | async-done | bytes 64528
  495.3 2.0 pad_maximum_fusion.8
  497.5 10.5 %collective-permute-done.44 = bf16[112,608]{1,0:T(8,128)(2,1)S(1)} collective-permute-done((bf16[112,608]{1,0:T(8,128)(2,1)S(1)}, bf16[112,608]{1,0:T(8,128)(2,1)S(1)}, u32[]{:S(2)}, u32[]{:S(2)}) %collective-permute-start.44) | collective-permute-done | bytes 136224 | tf_op jit(solution)/shard_map/ppermute | solution.py:637
  (215 shorter events, 87.1 us)
Async XLA Ops:
  7.2 79.4 %all-gather.5.cloned.1.call-start = ((), (), s32[]{:S(2)}) async-start(), calls=%async_computation.3 | async-start | bytes 2322432 | tf_op jit(solution)/shard_map/all_gather | solution.py:674
  7.3 5.6 %collective-permute-start.5 = (bf16[112,288]{0,1:T(8,128)(2,1)}, bf16[112,288]{0,1:T(8,128)(2,1)S(1)}, u32[]{:S(2)}, u32[]{:S(2)}) collective-permute-start(bf16[112,288]{0,1:T(8,128)(2,1)} %param.12), channel_id=1, source_target_pairs={{0,2},{1,3},{2,0},{3,1},{4,6},{5,7},{6,4},{7,5},{8,10},{9,11},{10,... | collective-permute-start | bytes 193544 | tf_op jit(solution)/shard_map/ppermute | solution.py:569
  9.3 5.5 %collective-permute-start.6 = (bf16[112,288]{0,1:T(8,128)(2,1)}, bf16[112,288]{0,1:T(8,128)(2,1)S(1)}, u32[]{:S(2)}, u32[]{:S(2)}) collective-permute-start(bf16[112,288]{0,1:T(8,128)(2,1)} %param.12), channel_id=1, source_target_pairs={{0,3},{1,2},{2,1},{3,0},{4,7},{5,6},{6,5},{7,4},{8,11},{9,10},{10,... | collective-permute-start | bytes 193544 | tf_op jit(solution)/shard_map/ppermute | solution.py:569
  15.7 119.9 %all-gather.7.cloned.1.call-start = ((), (), s32[]{:S(2)}) async-start(), calls=%async_computation.4 | async-start | bytes 1806336 | tf_op jit(solution)/shard_map/all_gather | solution.py:687
  15.8 6.7 %collective-permute-start.10 = (bf16[112,224]{1,0:T(8,128)(2,1)}, bf16[112,224]{1,0:T(8,128)(2,1)S(1)}, u32[]{:S(2)}, u32[]{:S(2)}) collective-permute-start(bf16[112,224]{1,0:T(8,128)(2,1)} %param.14), channel_id=1, source_target_pairs={{0,1},{1,0},{2,3},{3,2},{4,5},{5,4},{6,7},{7,6},{8,9},{9,8},{10,11... | collective-permute-start | bytes 150536 | tf_op jit(solution)/shard_map/ppermute | solution.py:569
  30.6 136.2 %all-gather.9.cloned.1.call-start = ((), (), s32[]{:S(2)}) async-start(), calls=%async_computation.7 | async-start | bytes 7741440 | tf_op jit(solution)/shard_map/all_gather | solution.py:688
  30.8 27.7 %collective-permute-start.14 = (bf16[112,608]{1,0:T(8,128)(2,1)S(1)}, bf16[112,608]{1,0:T(8,128)(2,1)S(1)}, u32[]{:S(2)}, u32[]{:S(2)}) collective-permute-start(bf16[112,608]{1,0:T(8,128)(2,1)S(1)} %get-tuple-element.142), channel_id=1, source_target_pairs={{0,0},{1,8},{2,16},{3,24},{4,4},{5,12},{6,20},{7,28},{8,1},{9,9},{... | collective-permute-start | bytes 408584 | tf_op jit(solution)/shard_map/ppermute | solution.py:637
  34.8 26.1 %collective-permute-start.15 = (bf16[112,608]{1,0:T(8,128)(2,1)S(1)}, bf16[112,608]{1,0:T(8,128)(2,1)S(1)}, u32[]{:S(2)}, u32[]{:S(2)}) collective-permute-start(bf16[112,608]{1,0:T(8,128)(2,1)S(1)} %get-tuple-element.141), channel_id=1, source_target_pairs={{0,4},{1,12},{2,20},{3,28},{4,0},{5,8},{6,16},{7,24},{8,5},{9,13},... | collective-permute-start | bytes 408584 | tf_op jit(solution)/shard_map/ppermute | solution.py:637
  68.8 398.3 %reduce-scatter.8.cloned.1.call-start = ((), (), s32[]{:S(2)}) async-start(), calls=%async_computation.6 | async-start | bytes 7741440 | tf_op jit(solution)/shard_map/reduce_scatter | solution.py:719
  69.0 6.2 %collective-permute-start.1 = (bf16[1,736]{1,0:T(2,128)(2,1)S(1)}, bf16[1,736]{1,0:T(2,128)(2,1)S(1)}, u32[]{:S(2)}, u32[]{:S(2)}) collective-permute-start(bf16[1,736]{1,0:T(2,128)(2,1)S(1)} %squeeze.49), channel_id=1, source_target_pairs={{0,1},{1,0},{2,3},{3,2},{4,5},{5,4},{6,7},{7,6},{8,9},{9,8},{10,11... | collective-permute-start | bytes 4424 | tf_op jit(solution)/shard_map/ppermute | solution.py:569
  69.0 6.2 %collective-permute-start.2 = (bf16[1,736]{1,0:T(2,128)(2,1)S(1)}, bf16[1,736]{1,0:T(2,128)(2,1)S(1)}, u32[]{:S(2)}, u32[]{:S(2)}) collective-permute-start(bf16[1,736]{1,0:T(2,128)(2,1)S(1)} %squeeze.49), channel_id=1, source_target_pairs={{0,2},{1,3},{2,0},{3,1},{4,6},{5,7},{6,4},{7,5},{8,10},{9,11},{10,... | collective-permute-start | bytes 4424 | tf_op jit(solution)/shard_map/ppermute | solution.py:569
  69.1 6.2 %collective-permute-start.3 = (bf16[1,736]{1,0:T(2,128)(2,1)S(1)}, bf16[1,736]{1,0:T(2,128)(2,1)S(1)}, u32[]{:S(2)}, u32[]{:S(2)}) collective-permute-start(bf16[1,736]{1,0:T(2,128)(2,1)S(1)} %squeeze.49), channel_id=1, source_target_pairs={{0,3},{1,2},{2,1},{3,0},{4,7},{5,6},{6,5},{7,4},{8,11},{9,10},{10,... | collective-permute-start | bytes 4424 | tf_op jit(solution)/shard_map/ppermute | solution.py:569
  72.6 12.9 %collective-permute-start = (bf16[1,256,896]{2,1,0:T(8,128)(2,1)S(1)}, bf16[1,256,896]{2,1,0:T(8,128)(2,1)S(1)}, u32[]{:S(2)}, u32[]{:S(2)}) collective-permute-start(bf16[1,256,896]{2,1,0:T(8,128)(2,1)S(1)} %get-tuple-element.129), channel_id=1, source_target_pairs={{0,3},{1,2},{2,1},{3,0},{4,7},{5,6},{6,5},{7,4},{8,11},{9,10},{10,... | collective-permute-start | bytes 1376264 | tf_op jit(solution)/shard_map/ppermute | solution.py:658
  91.7 10.4 %collective-permute-start.9 = (bf16[1,2,256,256]{3,2,1,0:T(8,128)(2,1)}, bf16[1,2,256,256]{3,2,1,0:T(8,128)(2,1)S(1)}, u32[]{:S(2)}, u32[]{:S(2)}) collective-permute-start(bf16[1,2,256,256]{3,2,1,0:T(8,128)(2,1)} %bitcast.147), channel_id=1, source_target_pairs={{0,3},{1,2},{2,1},{3,0},{4,7},{5,6},{6,5},{7,4},{8,11},{9,10},{10,... | collective-permute-start | bytes 786440 | tf_op jit(solution)/shard_map/ppermute | solution.py:569
  92.0 14.5 %collective-permute-start.7 = (bf16[1,2,256,256]{3,2,1,0:T(8,128)(2,1)}, bf16[1,2,256,256]{3,2,1,0:T(8,128)(2,1)S(1)}, u32[]{:S(2)}, u32[]{:S(2)}) collective-permute-start(bf16[1,2,256,256]{3,2,1,0:T(8,128)(2,1)} %bitcast.148), channel_id=1, source_target_pairs={{0,1},{1,0},{2,3},{3,2},{4,5},{5,4},{6,7},{7,6},{8,9},{9,8},{10,11... | collective-permute-start | bytes 786440 | tf_op jit(solution)/shard_map/ppermute | solution.py:569
  93.4 14.2 %collective-permute-start.8 = (bf16[1,2,256,256]{3,2,1,0:T(8,128)(2,1)}, bf16[1,2,256,256]{3,2,1,0:T(8,128)(2,1)S(1)}, u32[]{:S(2)}, u32[]{:S(2)}) collective-permute-start(bf16[1,2,256,256]{3,2,1,0:T(8,128)(2,1)} %bitcast.149), channel_id=1, source_target_pairs={{0,2},{1,3},{2,0},{3,1},{4,6},{5,7},{6,4},{7,5},{8,10},{9,11},{10,... | collective-permute-start | bytes 786440 | tf_op jit(solution)/shard_map/ppermute | solution.py:569
  103.1 38.8 %collective-permute-start.13 = (bf16[1,256,896]{2,1,0:T(8,128)(2,1)}, bf16[1,256,896]{2,1,0:T(8,128)(2,1)S(1)}, u32[]{:S(2)}, u32[]{:S(2)}) collective-permute-start(bf16[1,256,896]{2,1,0:T(8,128)(2,1)} %get-tuple-element.124), channel_id=1, source_target_pairs={{0,3},{1,2},{2,1},{3,0},{4,7},{5,6},{6,5},{7,4},{8,11},{9,10},{10,... | collective-permute-start | bytes 1376264 | tf_op jit(solution)/shard_map/ppermute | solution.py:658
  139.1 13.4 %collective-permute-start.16 = (bf16[256,896]{1,0:T(8,128)(2,1)S(1)}, bf16[256,896]{1,0:T(8,128)(2,1)S(1)}, u32[]{:S(2)}, u32[]{:S(2)}) collective-permute-start(bf16[256,896]{1,0:T(8,128)(2,1)S(1)} %get-tuple-element.126), channel_id=1, source_target_pairs={{0,1},{1,0},{2,3},{3,2},{4,5},{5,4},{6,7},{7,6},{8,9},{9,8},{10,11... | collective-permute-start | bytes 1376264 | tf_op jit(solution)/shard_map/ppermute | solution.py:569
  139.5 13.4 %collective-permute-start.17 = (bf16[256,896]{1,0:T(8,128)(2,1)S(1)}, bf16[256,896]{1,0:T(8,128)(2,1)S(1)}, u32[]{:S(2)}, u32[]{:S(2)}) collective-permute-start(bf16[256,896]{1,0:T(8,128)(2,1)S(1)} %get-tuple-element.127), channel_id=1, source_target_pairs={{0,2},{1,3},{2,0},{3,1},{4,6},{5,7},{6,4},{7,5},{8,10},{9,11},{10,... | collective-permute-start | bytes 1376264 | tf_op jit(solution)/shard_map/ppermute | solution.py:569
  140.3 22.1 %collective-permute-start.18 = (bf16[256,896]{1,0:T(8,128)(2,1)S(1)}, bf16[256,896]{1,0:T(8,128)(2,1)S(1)}, u32[]{:S(2)}, u32[]{:S(2)}) collective-permute-start(bf16[256,896]{1,0:T(8,128)(2,1)S(1)} %copy-done.2), channel_id=1, source_target_pairs={{0,1},{1,0},{2,3},{3,2},{4,5},{5,4},{6,7},{7,6},{8,9},{9,8},{10,11... | collective-permute-start | bytes 1376264 | tf_op jit(solution)/shard_map/ppermute | solution.py:569
  141.9 20.9 %collective-permute-start.19 = (bf16[256,896]{1,0:T(8,128)(2,1)S(1)}, bf16[256,896]{1,0:T(8,128)(2,1)S(1)}, u32[]{:S(2)}, u32[]{:S(2)}) collective-permute-start(bf16[256,896]{1,0:T(8,128)(2,1)S(1)} %bitcast.122), channel_id=1, source_target_pairs={{0,2},{1,3},{2,0},{3,1},{4,6},{5,7},{6,4},{7,5},{8,10},{9,11},{10,... | collective-permute-start | bytes 1376264 | tf_op jit(solution)/shard_map/ppermute | solution.py:569
  154.6 39.9 %collective-permute-start.20 = (bf16[512,896]{1,0:T(8,128)(2,1)}, bf16[512,896]{1,0:T(8,128)(2,1)}, u32[]{:S(2)}, u32[]{:S(2)}) collective-permute-start(bf16[512,896]{1,0:T(8,128)(2,1)} %get-tuple-element.138), channel_id=1, source_target_pairs={{0,2},{1,3},{2,0},{3,1},{4,6},{5,7},{6,4},{7,5},{8,10},{9,11},{10,... | collective-permute-start | bytes 2752520 | tf_op jit(solution)/shard_map/ppermute | solution.py:569
  155.4 59.4 %collective-permute-start.22 = (bf16[512,896]{1,0:T(8,128)(2,1)}, bf16[512,896]{1,0:T(8,128)(2,1)}, u32[]{:S(2)}, u32[]{:S(2)}) collective-permute-start(bf16[512,896]{1,0:T(8,128)(2,1)} %get-tuple-element.136), channel_id=1, source_target_pairs={{0,1},{1,0},{2,3},{3,2},{4,5},{5,4},{6,7},{7,6},{8,9},{9,8},{10,11... | collective-permute-start | bytes 2752520 | tf_op jit(solution)/shard_map/ppermute | solution.py:569
  164.4 36.5 %collective-permute-start.21 = (bf16[512,896]{1,0:T(8,128)(2,1)}, bf16[512,896]{1,0:T(8,128)(2,1)}, u32[]{:S(2)}, u32[]{:S(2)}) collective-permute-start(bf16[512,896]{1,0:T(8,128)(2,1)} %get-tuple-element.135), channel_id=1, source_target_pairs={{0,2},{1,3},{2,0},{3,1},{4,6},{5,7},{6,4},{7,5},{8,10},{9,11},{10,... | collective-permute-start | bytes 2752520 | tf_op jit(solution)/shard_map/ppermute | solution.py:569
  165.2 49.6 %collective-permute-start.23 = (bf16[512,896]{1,0:T(8,128)(2,1)}, bf16[512,896]{1,0:T(8,128)(2,1)}, u32[]{:S(2)}, u32[]{:S(2)}) collective-permute-start(bf16[512,896]{1,0:T(8,128)(2,1)} %get-tuple-element.133), channel_id=1, source_target_pairs={{0,1},{1,0},{2,3},{3,2},{4,5},{5,4},{6,7},{7,6},{8,9},{9,8},{10,11... | collective-permute-start | bytes 2752520 | tf_op jit(solution)/shard_map/ppermute | solution.py:569
  251.2 222.4 %reduce-scatter.6.cloned.1.call-start = ((), (), s32[]{:S(2)}) async-start(), calls=%async_computation.5 | async-start | bytes 516096 | tf_op jit(solution)/shard_map/reduce_scatter | solution.py:771
  251.3 21.4 %collective-permute-start.26 = (bf16[512,896]{1,0:T(8,128)(2,1)}, bf16[512,896]{1,0:T(8,128)(2,1)S(1)}, u32[]{:S(2)}, u32[]{:S(2)}) collective-permute-start(bf16[512,896]{1,0:T(8,128)(2,1)} %get-tuple-element.80), channel_id=1, source_target_pairs={{0,1},{1,0},{2,3},{3,2},{4,5},{5,4},{6,7},{7,6},{8,9},{9,8},{10,11... | collective-permute-start | bytes 2752520 | tf_op jit(solution)/shard_map/ppermute | solution.py:569
  253.0 21.0 %collective-permute-start.24 = (bf16[512,896]{1,0:T(8,128)(2,1)}, bf16[512,896]{1,0:T(8,128)(2,1)S(1)}, u32[]{:S(2)}, u32[]{:S(2)}) collective-permute-start(bf16[512,896]{1,0:T(8,128)(2,1)} %get-tuple-element.78), channel_id=1, source_target_pairs={{0,2},{1,3},{2,0},{3,1},{4,6},{5,7},{6,4},{7,5},{8,10},{9,11},{10,... | collective-permute-start | bytes 2752520 | tf_op jit(solution)/shard_map/ppermute | solution.py:569
  275.5 10.2 %collective-permute-start.25 = (bf16[256,896]{1,0:T(8,128)(2,1)S(1)}, bf16[256,896]{1,0:T(8,128)(2,1)S(1)}, u32[]{:S(2)}, u32[]{:S(2)}) collective-permute-start(bf16[256,896]{1,0:T(8,128)(2,1)S(1)} %get-tuple-element.121), channel_id=1, source_target_pairs={{0,1},{1,0},{2,3},{3,2},{4,5},{5,4},{6,7},{7,6},{8,9},{9,8},{10,11... | collective-permute-start | bytes 1376264 | tf_op jit(solution)/shard_map/ppermute | solution.py:569
  276.0 10.1 %collective-permute-start.27 = (bf16[256,896]{1,0:T(8,128)(2,1)S(1)}, bf16[256,896]{1,0:T(8,128)(2,1)S(1)}, u32[]{:S(2)}, u32[]{:S(2)}) collective-permute-start(bf16[256,896]{1,0:T(8,128)(2,1)S(1)} %get-tuple-element.122), channel_id=1, source_target_pairs={{0,2},{1,3},{2,0},{3,1},{4,6},{5,7},{6,4},{7,5},{8,10},{9,11},{10,... | collective-permute-start | bytes 1376264 | tf_op jit(solution)/shard_map/ppermute | solution.py:569
  329.1 9.7 %collective-permute-start.33 = (bf16[1,2,256,256]{3,2,1,0:T(8,128)(2,1)}, bf16[1,2,256,256]{3,2,1,0:T(8,128)(2,1)}, u32[]{:S(2)}, u32[]{:S(2)}) collective-permute-start(bf16[1,2,256,256]{3,2,1,0:T(8,128)(2,1)} %get-tuple-element.111), channel_id=1, source_target_pairs={{0,1},{1,0},{2,3},{3,2},{4,5},{5,4},{6,7},{7,6},{8,9},{9,8},{10,11... | collective-permute-start | bytes 786440 | tf_op jit(solution)/shard_map/ppermute | solution.py:569
  330.6 12.3 %collective-permute-start.34 = (bf16[1,2,256,256]{3,2,1,0:T(8,128)(2,1)}, bf16[1,2,256,256]{3,2,1,0:T(8,128)(2,1)}, u32[]{:S(2)}, u32[]{:S(2)}) collective-permute-start(bf16[1,2,256,256]{3,2,1,0:T(8,128)(2,1)} %get-tuple-element.110), channel_id=1, source_target_pairs={{0,2},{1,3},{2,0},{3,1},{4,6},{5,7},{6,4},{7,5},{8,10},{9,11},{10,... | collective-permute-start | bytes 786440 | tf_op jit(solution)/shard_map/ppermute | solution.py:569
  330.8 13.2 %collective-permute-start.35 = (bf16[1,2,256,256]{3,2,1,0:T(8,128)(2,1)}, bf16[1,2,256,256]{3,2,1,0:T(8,128)(2,1)}, u32[]{:S(2)}, u32[]{:S(2)}) collective-permute-start(bf16[1,2,256,256]{3,2,1,0:T(8,128)(2,1)} %get-tuple-element.109), channel_id=1, source_target_pairs={{0,3},{1,2},{2,1},{3,0},{4,7},{5,6},{6,5},{7,4},{8,11},{9,10},{10,... | collective-permute-start | bytes 786440 | tf_op jit(solution)/shard_map/ppermute | solution.py:569
  334.9 23.3 %collective-permute-start.40 = (bf16[224,896]{0,1:T(8,128)(2,1)}, bf16[224,896]{0,1:T(8,128)(2,1)}, u32[]{:S(2)}, u32[]{:S(2)}) collective-permute-start(bf16[224,896]{0,1:T(8,128)(2,1)} %bitcast.132), channel_id=1, source_target_pairs={{0,1},{1,0},{2,3},{3,2},{4,5},{5,4},{6,7},{7,6},{8,9},{9,8},{10,11... | collective-permute-start | bytes 1204232 | tf_op jit(solution)/shard_map/ppermute | solution.py:569
  337.4 25.2 %collective-permute-start.41 = (bf16[224,896]{0,1:T(8,128)(2,1)}, bf16[224,896]{0,1:T(8,128)(2,1)}, u32[]{:S(2)}, u32[]{:S(2)}) collective-permute-start(bf16[224,896]{0,1:T(8,128)(2,1)} %bitcast.54), channel_id=1, source_target_pairs={{0,2},{1,3},{2,0},{3,1},{4,6},{5,7},{6,4},{7,5},{8,10},{9,11},{10,... | collective-permute-start | bytes 1204232 | tf_op jit(solution)/shard_map/ppermute | solution.py:569
  338.8 24.8 %collective-permute-start.42 = (bf16[224,896]{0,1:T(8,128)(2,1)}, bf16[224,896]{0,1:T(8,128)(2,1)S(1)}, u32[]{:S(2)}, u32[]{:S(2)}) collective-permute-start(bf16[224,896]{0,1:T(8,128)(2,1)} %bitcast.133), channel_id=1, source_target_pairs={{0,3},{1,2},{2,1},{3,0},{4,7},{5,6},{6,5},{7,4},{8,11},{9,10},{10,... | collective-permute-start | bytes 1204232 | tf_op jit(solution)/shard_map/ppermute | solution.py:569
  343.0 49.0 %collective-permute-start.28 = (bf16[512,896]{1,0:T(8,128)(2,1)}, bf16[512,896]{1,0:T(8,128)(2,1)S(1)}, u32[]{:S(2)}, u32[]{:S(2)}) collective-permute-start(bf16[512,896]{1,0:T(8,128)(2,1)} %get-tuple-element.82), channel_id=1, source_target_pairs={{0,2},{1,3},{2,0},{3,1},{4,6},{5,7},{6,4},{7,5},{8,10},{9,11},{10,... | collective-permute-start | bytes 2752520 | tf_op jit(solution)/shard_map/ppermute | solution.py:569
  344.1 50.1 %collective-permute-start.30 = (bf16[512,896]{1,0:T(8,128)(2,1)}, bf16[512,896]{1,0:T(8,128)(2,1)}, u32[]{:S(2)}, u32[]{:S(2)}) collective-permute-start(bf16[512,896]{1,0:T(8,128)(2,1)} %get-tuple-element.84), channel_id=1, source_target_pairs={{0,1},{1,0},{2,3},{3,2},{4,5},{5,4},{6,7},{7,6},{8,9},{9,8},{10,11... | collective-permute-start | bytes 2752520 | tf_op jit(solution)/shard_map/ppermute | solution.py:569
  358.1 38.6 %collective-permute-start.36 = (bf16[1,256,896]{2,1,0:T(8,128)(2,1)}, bf16[1,256,896]{2,1,0:T(8,128)(2,1)}, u32[]{:S(2)}, u32[]{:S(2)}) collective-permute-start(bf16[1,256,896]{2,1,0:T(8,128)(2,1)} %slice.204), channel_id=1, source_target_pairs={{0,3},{1,2},{2,1},{3,0},{4,7},{5,6},{6,5},{7,4},{8,11},{9,10},{10,... | collective-permute-start | bytes 1376264 | tf_op jit(solution)/shard_map/ppermute | solution.py:784
  365.8 127.8 %reduce-scatter.10.cloned.1.call-start = ((), (), s32[]{:S(2)}) async-start(), calls=%async_computation.8 | async-start | bytes 774144
  368.3 91.9 %collective-permute-start.37 = (bf16[288,896]{1,0:T(8,128)(2,1)}, bf16[288,896]{1,0:T(8,128)(2,1)}, u32[]{:S(2)}, u32[]{:S(2)}) collective-permute-start(bf16[288,896]{1,0:T(8,128)(2,1)} %get-tuple-element.102), channel_id=1, source_target_pairs={{0,1},{1,0},{2,3},{3,2},{4,5},{5,4},{6,7},{7,6},{8,9},{9,8},{10,11... | collective-permute-start | bytes 1548296 | tf_op jit(solution)/shard_map/ppermute | solution.py:569
  369.7 90.5 %collective-permute-start.38 = (bf16[288,896]{1,0:T(8,128)(2,1)}, bf16[288,896]{1,0:T(8,128)(2,1)}, u32[]{:S(2)}, u32[]{:S(2)}) collective-permute-start(bf16[288,896]{1,0:T(8,128)(2,1)} %get-tuple-element.104), channel_id=1, source_target_pairs={{0,2},{1,3},{2,0},{3,1},{4,6},{5,7},{6,4},{7,5},{8,10},{9,11},{10,... | collective-permute-start | bytes 1548296 | tf_op jit(solution)/shard_map/ppermute | solution.py:569
  391.9 68.4 %collective-permute-start.39 = (bf16[288,896]{1,0:T(8,128)(2,1)S(1)}, bf16[288,896]{1,0:T(8,128)(2,1)}, u32[]{:S(2)}, u32[]{:S(2)}) collective-permute-start(bf16[288,896]{1,0:T(8,128)(2,1)S(1)} %get-tuple-element.103), channel_id=1, source_target_pairs={{0,3},{1,2},{2,1},{3,0},{4,7},{5,6},{6,5},{7,4},{8,11},{9,10},{10,... | collective-permute-start | bytes 1548296 | tf_op jit(solution)/shard_map/ppermute | solution.py:569
  396.8 66.5 %collective-permute-start.29 = (bf16[256,896]{1,0:T(8,128)(2,1)}, bf16[256,896]{1,0:T(8,128)(2,1)}, u32[]{:S(2)}, u32[]{:S(2)}) collective-permute-start(bf16[256,896]{1,0:T(8,128)(2,1)} %get-tuple-element.117), channel_id=1, source_target_pairs={{0,1},{1,0},{2,3},{3,2},{4,5},{5,4},{6,7},{7,6},{8,9},{9,8},{10,11... | collective-permute-start | bytes 1376264 | tf_op jit(solution)/shard_map/ppermute | solution.py:569
  396.8 66.5 %collective-permute-start.31 = (bf16[256,896]{1,0:T(8,128)(2,1)}, bf16[256,896]{1,0:T(8,128)(2,1)}, u32[]{:S(2)}, u32[]{:S(2)}) collective-permute-start(bf16[256,896]{1,0:T(8,128)(2,1)} %get-tuple-element.118), channel_id=1, source_target_pairs={{0,2},{1,3},{2,0},{3,1},{4,6},{5,7},{6,4},{7,5},{8,10},{9,11},{10,... | collective-permute-start | bytes 1376264 | tf_op jit(solution)/shard_map/ppermute | solution.py:569
  465.6 29.7 %collective-permute-start.32 = (bf16[1,256,896]{2,1,0:T(8,128)(2,1)S(1)}, bf16[1,256,896]{2,1,0:T(8,128)(2,1)}, u32[]{:S(2)}, u32[]{:S(2)}) collective-permute-start(bf16[1,256,896]{2,1,0:T(8,128)(2,1)S(1)} %get-tuple-element.114), channel_id=1, source_target_pairs={{0,3},{1,2},{2,1},{3,0},{4,7},{5,6},{6,5},{7,4},{8,11},{9,10},{10,... | collective-permute-start | bytes 1376264 | tf_op jit(solution)/shard_map/ppermute | solution.py:658
  470.4 27.1 %collective-permute-start.43 = (bf16[112,608]{1,0:T(8,128)(2,1)S(1)}, bf16[112,608]{1,0:T(8,128)(2,1)S(1)}, u32[]{:S(2)}, u32[]{:S(2)}) collective-permute-start(bf16[112,608]{1,0:T(8,128)(2,1)S(1)} %bitcast.140), channel_id=1, source_target_pairs={{0,0},{1,8},{2,16},{3,24},{4,4},{5,12},{6,20},{7,28},{8,1},{9,9},{... | collective-permute-start | bytes 408584 | tf_op jit(solution)/shard_map/ppermute | solution.py:637
  497.3 10.6 %collective-permute-start.44 = (bf16[112,608]{1,0:T(8,128)(2,1)S(1)}, bf16[112,608]{1,0:T(8,128)(2,1)S(1)}, u32[]{:S(2)}, u32[]{:S(2)}) collective-permute-start(bf16[112,608]{1,0:T(8,128)(2,1)S(1)} %bitcast.141), channel_id=1, source_target_pairs={{0,4},{1,12},{2,20},{3,28},{4,0},{5,8},{6,16},{7,24},{8,5},{9,13},... | collective-permute-start | bytes 408584 | tf_op jit(solution)/shard_map/ppermute | solution.py:637
  (26 other events, 286.0 us)
Sparse Core Ops, SparseCore 0:
  15.8 40.3 all-gather.4
  58.5 30.0 all-gather.6
  90.2 69.1 all-gather.8
  251.3 76.3 reduce-scatter.7
  365.9 31.7 reduce-scatter.5
  463.3 30.2 reduce-scatter.9

commit v3 on v2

--- a/solution.py
+++ b/solution.py
@@ -97,7 +97,7 @@
 def project_forward(tokens, gain, weight, bias, cosine, sine):
     rows, width = tokens.shape
     tile = rows // 2
-    columns = weight.shape[1]
+    columns = Q_WIDTH + 2 * K_WIDTH
     return pl.pallas_call(
         project_kernel,
         grid=(2,),
@@ -157,7 +157,7 @@
 def project_backward(grad_queries, weight, tokens, gain, grad_hidden, cosine, sine, parts):
     rows, width = tokens.shape
     tile = rows // 2
-    columns = weight.shape[1]
+    columns = Q_WIDTH + 2 * K_WIDTH
     return pl.pallas_call(
         project_back_kernel,
         grid=(2,),
@@ -189,6 +189,35 @@
         compiler_params=params(),
         name="project_backward",
     )(grad_queries, weight, tokens, gain, grad_hidden, cosine, sine, *parts)
+
+
+def pieces_kernel(lhs_ref, *rest):
+    rhs_refs = rest[:-1]
+    out_ref = rest[-1]
+    ranks, owners, depth, own = out_ref.shape
+    rhs = jnp.concatenate([ref[...] for ref in rhs_refs], axis=1)
+    whole = dot(lhs_ref[...], rhs, TN)
+    for rank in range(ranks):
+        part = whole[:, rank * own : (rank + 1) * own]
+        out_ref[rank] = part.reshape(owners, depth, own).astype(bf16)
+
+
+def weight_pieces(ctx_size, seq_size, lhs, *rhs):
+    rows, width = lhs.shape
+    columns = sum(x.shape[1] for x in rhs)
+    shape = (ctx_size, seq_size, width // seq_size, columns // ctx_size)
+    return pl.pallas_call(
+        pieces_kernel,
+        grid=(1,),
+        in_specs=[full_spec(*x.shape) for x in (lhs, *rhs)],
+        out_specs=full_spec(*shape),
+        out_shape=jax.ShapeDtypeStruct(shape, bf16),
+        cost_estimate=pl.CostEstimate(
+            flops=4 * rows * width * columns, bytes_accessed=5 << 20, transcendentals=0
+        ),
+        compiler_params=params(),
+        name="weight_pieces",
+    )(lhs, *rhs)
 
 
 def pair_sides(both):
@@ -581,16 +610,21 @@
     return [x, jnp.concatenate([front_1, back_2], axis=0), front_far, back_far]
 
 
-def gathered_sum(parts, ctx_size):
+def first_hops(parts, ctx_size):
+    if ctx_size != 4:
+        return [hop(parts[k], ctx_size, k) for k in range(1, ctx_size)]
+    return [hop(parts[2], 4, 2), hop(parts[3], 4, 1)]
+
+
+def gathered_sum(parts, got, ctx_size):
     if ctx_size != 4:
         total = parts[0].astype(f32)
-        for k in range(1, ctx_size):
-            total = total + hop(parts[k], ctx_size, k).astype(f32)
+        for part in got:
+            total = total + part.astype(f32)
         return total
-    own, near, front_far, back_far = parts
+    own, near = parts[:2]
+    front_got, back_got = got
     half = own.shape[0] // 2
-    front_got = hop(front_far, 4, 2)
-    back_got = hop(back_far, 4, 1)
     front_next = (near[:half].astype(f32) + front_got[half:].astype(f32)).astype(bf16)
     back_next = (near[half:].astype(f32) + back_got[half:].astype(f32)).astype(bf16)
     front_last = hop(front_next, 4, 1)
@@ -604,11 +638,8 @@
     )
 
 
-def in_order(pieces, place, ctx_size):
-    result = jnp.zeros((ctx_size,) + pieces[0].shape, pieces[0].dtype)
-    for k, piece in enumerate(pieces):
-        result = lax.dynamic_update_index_in_dim(result, piece, place ^ k, 0)
-    return result
+def pick(index, cases):
+    return cases[0] if len(cases) == 1 else lax.select_n(index, *cases)
 
 
 def on_device(
@@ -630,7 +661,8 @@
     half = block_rows // 2
     rows = sequences * block_rows
     fold = seq_size // ctx_size
-    fold_place = lax.axis_index("seq") % fold
+    seq_place = lax.axis_index("seq")
+    fold_place = seq_place % fold
     mirror = [(i, ctx_size - 1 - i) for i in range(ctx_size)]
 
     def crossed(x, j):
@@ -646,13 +678,13 @@
         )
 
     def crossed_parts(parts):
-        came = jnp.zeros_like(parts)
-        for j in range(fold):
-            part = lax.dynamic_index_in_dim(parts, (fold_place + j) % fold, 0, keepdims=False)
-            came = lax.dynamic_update_index_in_dim(
-                came, crossed(part, j), (fold_place - j) % fold, 0
-            )
-        return came
+        came = [
+            crossed(pick(fold_place, [parts[(f + j) % fold] for f in range(fold)]), j)
+            for j in range(fold)
+        ]
+        return [
+            pick(fold_place, [came[(f - t) % fold] for f in range(fold)]) for t in range(fold)
+        ]
 
     def zigzag(x):
         return jnp.concatenate([x[:, :half], lax.ppermute(x[:, half:], "ctx", mirror)], axis=1)
@@ -664,34 +696,48 @@
     positions = (order[:2, None] * half + jnp.arange(half, dtype=jnp.int32)[None, :]).reshape(-1)
     cosine, sine = rotation_tables(jnp.tile(positions, sequences))
 
-    def columns_whole(shard):
-        pieces = [shard] + [hop(shard, ctx_size, k) for k in range(1, ctx_size)]
-        ordered = in_order(pieces, place, ctx_size)
-        return jnp.moveaxis(ordered, 0, 1).reshape(shard.shape[0], -1)
-
     gain_width = attention_gain.shape[0]
     bias_width = project_bias.shape[0]
-    project_full = lax.all_gather(columns_whole(project_weight), "seq", axis=0, tiled=True)
-    vectors = jnp.concatenate([attention_gain, project_bias, feedforward_gain])[None, :]
-    vector_pieces = [vectors] + [hop(vectors, ctx_size, k) for k in range(1, ctx_size)]
-    vectors_all = in_order(vector_pieces, place, ctx_size)[:, 0, :].astype(f32)
-    attention_full = vectors_all[:, :gain_width].reshape(1, -1)
-    bias_full = vectors_all[:, gain_width : gain_width + bias_width].reshape(1, -1)
-    feedforward_full = vectors_all[:, gain_width + bias_width :].reshape(1, -1)
-
-    output_columns = columns_whole(output_weight)
+    depth_mine, own_width = project_weight.shape
+    vectors = jnp.concatenate([attention_gain, project_bias, feedforward_gain])
+    both = jnp.concatenate([project_weight, output_weight], axis=1)
+    spare = -vectors.shape[0] % both.shape[1]
+    payload = jnp.concatenate(
+        [both, jnp.pad(vectors, (0, spare)).reshape(-1, both.shape[1])], axis=0
+    )
+    pieces = [payload] + [hop(payload, ctx_size, k) for k in range(1, ctx_size)]
+    ordered = [
+        pick(place, [pieces[rank ^ p] for p in range(ctx_size)]) for rank in range(ctx_size)
+    ]
+    both_columns = jnp.concatenate(
+        [piece[:depth_mine, :own_width] for piece in ordered]
+        + [piece[:depth_mine, own_width:] for piece in ordered],
+        axis=1,
+    )
+    vectors_all = [piece[depth_mine:].reshape(-1).astype(f32) for piece in ordered]
+
+    def vector_whole(start, size):
+        return jnp.concatenate([v[start : start + size] for v in vectors_all])[None, :]
+
+    attention_full = vector_whole(0, gain_width)
+    bias_full = vector_whole(gain_width, bias_width)
+    feedforward_full = vector_whole(gain_width + bias_width, gain_width)
+    both_full = lax.all_gather(both_columns, "seq", axis=0, tiled=True)
+    output_full = both_full[:, Q_WIDTH + 2 * K_WIDTH :]
+
+    tokens_late, down_late = lax.optimization_barrier((tokens, down_weight, both_columns))[:2]
     down_rows, down_columns = down_weight.shape
     depth = down_columns // fold
-    down_turned = crossed_parts(down_weight.T.reshape(fold, depth, down_rows))
-    down_turned = jnp.moveaxis(down_turned, 0, 1).reshape(depth, fold * down_rows)
-    output_full = lax.all_gather(output_columns, "seq", axis=0, tiled=True)
+    down_turned = jnp.concatenate(
+        crossed_parts(list(down_late.T.reshape(fold, depth, down_rows))), axis=1
+    )
     weights_mine = lax.all_gather(
         jnp.stack([gate_weight, up_weight, down_turned]), "seq", axis=0
     )
 
-    tokens_mine = zigzag(tokens).reshape(rows, width)
+    tokens_mine = zigzag(tokens_late).reshape(rows, width)
     normed, queries, pairs_mine = project_forward(
-        tokens_mine, attention_full, project_full, bias_full, cosine, sine
+        tokens_mine, attention_full, both_full, bias_full, cosine, sine
     )
     queries = queries.reshape(sequences * 2, half, Q_WIDTH)
     pairs_mine = pairs_mine.reshape(sequences, 2, half, 2 * K_WIDTH)
@@ -715,8 +761,11 @@
         )
         output_parts.append(output_part)
         grad_normed_parts.append(grad_normed_part)
-    grad_normed_ffn = gathered_sum(grad_normed_parts, ctx_size)
-    weight_grads = lax.psum_scatter(ffn_weights(seq_size, *buffers), "seq", scatter_dimension=0)
+    ffn_grads, normed_got = lax.optimization_barrier(
+        (ffn_weights(seq_size, *buffers), first_hops(grad_normed_parts, ctx_size))
+    )
+    grad_normed_ffn = gathered_sum(grad_normed_parts, normed_got, ctx_size)
+    weight_grads = lax.psum_scatter(ffn_grads, "seq", scatter_dimension=0)
 
     grad_ffn_gain = jnp.sum(grad_normed_ffn * hidden * inverse_ffn, axis=0)
     weighted_ffn = grad_normed_ffn * feedforward_full
@@ -732,6 +781,9 @@
     hidden_low = grad_hidden.astype(bf16)
     grad_mixed = dot(hidden_low, output_full, NT).astype(bf16)
 
+    output_late = lax.optimization_barrier((output_parts, grad_mixed))[0]
+    output_got = first_hops(output_late, ctx_size)
+
     grad_queries, pair_grads = attend_backward(
         order,
         queries,
@@ -742,6 +794,7 @@
         cosine.reshape(sequences * 2, half, PAIR),
         sine.reshape(sequences * 2, half, PAIR),
     )
+    pair_grads, output_got = lax.optimization_barrier((pair_grads, output_got))
     pair_sums = [pair_grads[:, :2].reshape(rows, 2 * K_WIDTH)]
     for k in range(1, ctx_size):
         pair_sums.append(
@@ -750,7 +803,7 @@
     grad_queries = grad_queries.reshape(rows, Q_WIDTH)
     grad_pairs, tokens_grad, gain_sum, bias_sum = project_backward(
         grad_queries,
-        project_full,
+        both_full,
         tokens_mine,
         attention_full,
         grad_hidden,
@@ -759,22 +812,35 @@
         pair_sums,
     )
 
-    def columns_then_rows_summed(turned):
-        parts = turned.astype(bf16).reshape(ctx_size, turned.shape[0] // ctx_size, turned.shape[1])
+    def owners_sum(parts):
+        _, owners, deep, own = parts.shape
+        parts = parts.reshape(ctx_size, owners // 2, 2, deep, own)
+        core = seq_place % 2
+        mine = pick(core, [parts[:, :, 0], parts[:, :, 1]])
+        other = pick(core, [parts[:, :, 1], parts[:, :, 0]])
+        swapped = lax.ppermute(other, "seq", [(i, i ^ 1) for i in range(seq_size)])
+        chip = (mine.astype(f32) + swapped.astype(f32)).astype(bf16)
 
         def part(k):
-            return lax.dynamic_index_in_dim(parts, place ^ k, 0, keepdims=False)
+            return lax.dynamic_index_in_dim(chip, place ^ k, 0, keepdims=False)
 
         total = part(0).astype(f32)
         for k in range(1, ctx_size):
             total = total + hop(part(k), ctx_size, k).astype(f32)
-        return lax.psum_scatter(
-            total.astype(bf16).T, "seq", scatter_dimension=0, tiled=True
-        ).astype(f32)
-
-    output_out = columns_then_rows_summed(dot(hidden_low, mixed_rows, TN))
-    project_out = columns_then_rows_summed(
-        dot(jnp.concatenate([grad_queries, grad_pairs], axis=1), normed, TN)
+        column = total.astype(bf16)
+        floor = seq_place // 2
+        floors = seq_size // 2
+        total = lax.dynamic_index_in_dim(column, floor, 0, keepdims=False).astype(f32)
+        for step in range(1, floors):
+            sent = lax.dynamic_index_in_dim(column, (floor + step) % floors, 0, keepdims=False)
+            total = total + lax.ppermute(
+                sent, "seq", [(i, (i + 2 * step) % seq_size) for i in range(seq_size)]
+            ).astype(f32)
+        return total
+
+    output_out = owners_sum(weight_pieces(ctx_size, seq_size, mixed_rows, hidden_low))
+    project_out = owners_sum(
+        weight_pieces(ctx_size, seq_size, normed, grad_queries, grad_pairs)
     )
 
     tokens_grad = tokens_grad.reshape(tokens.shape)
@@ -785,30 +851,45 @@
         ],
         axis=1,
     )
-    output_late = lax.optimization_barrier((tuple(output_parts), grad_mixed))[0]
-    output_zigzag = hidden + gathered_sum(list(output_late), ctx_size)
+    output_zigzag = hidden + gathered_sum(output_late, output_got, ctx_size)
     layer_output = zigzag(output_zigzag.astype(bf16).reshape(tokens.shape))
 
     down_grads = weight_grads[2].reshape(depth, fold, down_rows)
-    down_out = crossed_parts(jnp.moveaxis(down_grads, 1, 0)).reshape(down_columns, down_rows).T
-
-    sums = lax.psum(
-        jnp.concatenate([gain_sum[0], bias_sum[0], grad_ffn_gain]), ("seq", "ctx")
-    )
-
-    def my_part(start, whole):
-        own = whole // ctx_size
-        return lax.dynamic_slice_in_dim(sums, start + place * own, own, 0)
-
-    project_width = bias_width * ctx_size
+    down_out = jnp.concatenate(
+        crossed_parts([down_grads[:, t] for t in range(fold)]), axis=0
+    ).T
+
+    sums = jnp.concatenate(
+        [
+            gain_sum.reshape(ctx_size, gain_width),
+            bias_sum.reshape(ctx_size, bias_width),
+            grad_ffn_gain.reshape(ctx_size, gain_width),
+        ],
+        axis=1,
+    )
+
+    def sums_for(k):
+        return lax.dynamic_index_in_dim(sums, place ^ k, 0)
+
+    vector_sum = sums_for(0)
+    for k in range(1, ctx_size):
+        vector_sum = vector_sum + hop(sums_for(k), ctx_size, k)
+    mask = 1
+    while mask < seq_size:
+        vector_sum = vector_sum + lax.ppermute(
+            vector_sum, "seq", [(i, i ^ mask) for i in range(seq_size)]
+        )
+        mask *= 2
+    vector_sum = vector_sum[0]
+
     return (
         layer_output,
         tokens_gradient,
-        my_part(0, width),
+        vector_sum[:gain_width],
         project_out,
-        my_part(width, project_width),
+        vector_sum[gain_width : gain_width + bias_width],
         output_out,
-        my_part(width + project_width, width),
+        vector_sum[gain_width + bias_width :],
         weight_grads[0].astype(f32),
         weight_grads[1].astype(f32),
         down_out.astype(f32),

time: 523 us -> 458 us (0.88)
  blocking collectives: 57.6 us -> 0 us
  local copies, waits for them, and re-layouts: 41.6 us -> 22.4 us
  Pallas kernels: 153 us -> 162 us
  starting transfers between devices: 49.9 us -> 57.5 us
  other arithmetic: 33.7 us -> 40.1 us
    psum x1 -> x0, blocking collectives: 57.6 us -> none  [on_device(): lax.psum(jnp.concatenate([gain_sum[0], bias_sum[0], grad_ffn_gain]), ('se...]
    unnamed x7 -> x3, waiting for transfers between devices: 18.6 us -> 0.05 us
    dynamic_update_slice x16 -> x0, local copies, waits for them, and re-layouts: 16 us -> none  [the longest x12 9.77 us: in_order(): result = lax.dynamic_update_index_in_dim(result, piece, place ^ k, 0)]
    ppermute x4, waiting for transfers between devices: 36.3 us -> 51.7 us  [crossed(): lax.ppermute(x, ('seq', 'ctx'), [((c * fold + r) * ctx_size + q, (q * fol...]
    ppermute x37 -> x34, waiting for transfers between devices: 90.6 us -> 78.8 us  [hop(): return lax.ppermute(x, 'ctx', [(i, i ^ mask) for i in range(ctx_size)])]
    ppermute x0 -> x11, starting transfers between devices: none -> 10.1 us  [the longest x6 4.9 us: owners_sum(): lax.ppermute(sent, 'seq', [(i, (i + 2 * step) % seq_size) for i in range(...]
    ppermute x3, waiting for transfers between devices: 8.68 us -> 18.5 us  [zigzag(): lax.ppermute(x[:, half:], 'ctx', mirror)]
    pallas_call x0 -> x2, Pallas kernels: none -> 8.95 us  [weight_pieces(): pl.pallas_call(pieces_kernel, grid=(1,), in_specs=[full_spec(*x.shape) fo...]
  transfers between devices with their start and end apart: 51 -> 56, of which waited for: 26 -> 27; matrix products, arithmetic and copies ran while one was open for 16% -> 14% of each run, Pallas kernels for 23% -> 36%
where the time goes in v3:
time: 458 us; the launch traced here: 453 us
  Pallas kernels  162 us (35%)
  waiting for transfers between devices  149 us (33%)
  starting transfers between devices  57.5 us (13%)
  other arithmetic  40.1 us (9%)
  local copies, waits for them, and re-layouts  22.4 us (5%)
  between operations  14.6 us (3%)
  matrix products  7.1 us (2%)
    ppermute x34, waiting for transfers between devices, hop(): return lax.ppermute(x, 'ctx', [(i, i ^ mask) for i in range(ctx_size)])  78.8 us
    pallas_call x4, Pallas kernels, ffn(): pl.pallas_call(ffn_kernel, grid=(2,), in_specs=[row_spec(tile, width), ro...  55 us
    ppermute x4, waiting for transfers between devices, crossed(): lax.ppermute(x, ('seq', 'ctx'), [((c * fold + r) * ctx_size + q, (q * fol...  51.7 us
    ppermute x34, starting transfers between devices, hop(): return lax.ppermute(x, 'ctx', [(i, i ^ mask) for i in range(ctx_size)])  37.2 us
    pallas_call x1, Pallas kernels, attend_backward(): pl.pallas_call(backward_kernel, grid_spec=pltpu.PrefetchScalarGridSpec(nu...  36.3 us
    pallas_call x1, Pallas kernels, attend_forward(): pl.pallas_call(forward_kernel, grid_spec=pltpu.PrefetchScalarGridSpec(num...  27.4 us
    pallas_call x1, Pallas kernels, ffn_weights(): pl.pallas_call(ffn_weights_kernel, grid=(count,), in_specs=[slot(width)]...  22.5 us
    ppermute x3, waiting for transfers between devices, zigzag(): lax.ppermute(x[:, half:], 'ctx', mirror)  18.5 us
  transfers between devices with their start and end apart: 56, of which 27 were waited for; matrix products, arithmetic and copies ran while one was open for 14% of the time, Pallas kernels for 36%

profile of v3, /device:TPU:2, one launch (start us, length us, event | category | flops | bytes accessed | tf_op | source)
XLA Modules:
  0.0 452.7 jit_solution(10710082194076570661)
XLA Ops:
  10.0 3.0 collective-permute-start.2
  13.5 2.7 collective-permute-done
  16.2 2.5 collective-permute-done.2
  22.8 3.5 collective-permute-start.8
  26.3 21.9 %collective-permute-done.8 = bf16[112,608]{1,0:T(8,128)(2,1)S(1)} collective-permute-done((bf16[112,608]{1,0:T(8,128)(2,1)S(1)}, bf16[112,608]{1,0:T(8,128)(2,1)S(1)}, u32[]{:S(2)}, u32[]{:S(2)}) %collective-permute-start.8) | collective-permute-done | bytes 136224 | tf_op jit(solution)/shard_map/ppermute | solution.py:669
  48.3 11.9 %collective-permute-done.9 = bf16[112,608]{1,0:T(8,128)(2,1)S(1)} collective-permute-done((bf16[112,608]{1,0:T(8,128)(2,1)S(1)}, bf16[112,608]{1,0:T(8,128)(2,1)S(1)}, u32[]{:S(2)}, u32[]{:S(2)}) %collective-permute-start.9) | collective-permute-done | bytes 136224 | tf_op jit(solution)/shard_map/ppermute | solution.py:669
  65.8 12.1 %collective-permute-done.3 = bf16[1,256,896]{2,1,0:T(8,128)(2,1)S(1)} collective-permute-done((bf16[1,256,896]{2,1,0:T(8,128)(2,1)S(1)}, bf16[1,256,896]{2,1,0:T(8,128)(2,1)S(1)}, u32[]{:S(2)}, u32[]{:S(2)}) %collective-permute-start.3) | collective-permute-done | bytes 458784 | tf_op jit(solution)/shard_map/ppermute | solution.py:690
  79.0 5.4 %project_forward.1 = (bf16[512,896]{1,0:T(8,128)(2,1)}, bf16[512,896]{1,0:T(8,128)(2,1)}, bf16[512,256]{1,0:T(8,128)(2,1)}) custom-call(bf16[512,896]{1,0:T(8,128)(2,1)} %maximum_bitcast_fusion.x_ref, f32[1,896]{1,0:T(1,128)} %broadcast_in_dim.4.gain_ref, bf16[896,2048]{1,0:T(8,128)(2,1)} %all-gather.4.cloned.1.call-done.w_ref, ...), custom_call_target="tpu_custom_call" | custom-call | flops 2113929216 | bytes 5242880 | tf_op jit(solution)/shard_map/project_forward/pallas_call | solution.py:101
  85.3 3.2 collective-permute-start.5
  88.6 6.2 %collective-permute-done.6.rest_3_ = bf16[1,2,256,256]{3,2,1,0:T(8,128)(2,1)S(1)} collective-permute-done((bf16[1,2,256,256]{3,2,1,0:T(8,128)(2,1)}, bf16[1,2,256,256]{3,2,1,0:T(8,128)(2,1)S(1)}, u32[]{:S(2)}, u32[]{:S(2)}) %collective-permute-start.6) | collective-permute-done | bytes 262176 | tf_op jit(solution)/shard_map/ppermute | solution.py:598
  97.4 2.9 collective-permute-done.5.rest_2_
  101.0 27.4 %attend_forward.1 = (bf16[2,256,896]{2,1,0:T(8,128)(2,1)}, f32[2,16,256]{2,1,0:T(8,128)}) custom-call(s32[8]{0:T(128)} %stack.49.order_ref, bf16[2,256,896]{2,1,0:T(8,128)(2,1)} %bitcast.171, bf16[1,2,256,256]{3,2,1,0:T(8,128)(2,1)} %bitcast.169, bf16[1,2,256,256]{3,2,1,0:T(8,128)(2,1)} %copy-done.20, bf16[1,2,256,256]{3,2,1,0:T(8,128)(2,1)} %copy-done.21, ...), custom_call_target="tpu_custom_call" | custom-call | flops 9395240960 | bytes 4194304 | tf_op jit(solution)/shard_map/attend_forward/pallas_call | solution.py:433
  128.3 3.2 multiply_reduce_fusion.2
  132.7 2.0 collective-permute-start.12
  136.0 9.3 %collective-permute-done.11 = bf16[256,896]{1,0:T(8,128)(2,1)S(1)} collective-permute-done((bf16[256,896]{1,0:T(8,128)(2,1)S(1)}, bf16[256,896]{1,0:T(8,128)(2,1)S(1)}, u32[]{:S(2)}, u32[]{:S(2)}) %collective-permute-start.11) | collective-permute-done | bytes 458784 | tf_op jit(solution)/shard_map/ppermute | solution.py:598
  150.0 5.9 %collective-permute-done.12 = bf16[256,896]{1,0:T(8,128)(2,1)S(1)} collective-permute-done((bf16[256,896]{1,0:T(8,128)(2,1)S(1)}, bf16[256,896]{1,0:T(8,128)(2,1)S(1)}, u32[]{:S(2)}, u32[]{:S(2)}) %collective-permute-start.12) | collective-permute-done | bytes 458784 | tf_op jit(solution)/shard_map/ppermute | solution.py:598
  158.8 13.7 %ffn.4 = (bf16[512,896]{1,0:T(8,128)(2,1)}, bf16[512,896]{1,0:T(8,128)(2,1)}, bf16[4,512,896]{2,1,0:T(8,128)(2,1)}, bf16[4,512,896]{2,1,0:T(8,128)(2,1)}, bf16[4...) custom-call(bf16[512,896]{1,0:T(8,128)(2,1)} %copy-done.2, ...), custom_call_target="tpu_custom_call" | custom-call | flops 7809794048 | bytes 16777216 | tf_op jit(solution)/shard_map/ffn/pallas_call | solution.py:537
  172.5 13.9 %ffn.5 = (bf16[512,896]{1,0:T(8,128)(2,1)}, bf16[512,896]{1,0:T(8,128)(2,1)}, bf16[4,512,896]{2,1,0:T(8,128)(2,1)}, bf16[4,512,896]{2,1,0:T(8,128)(2,1)}, bf16[4...) custom-call(bf16[512,896]{1,0:T(8,128)(2,1)} %get-tuple-element.159., ...), custom_call_target="tpu_custom_call", output_to_operand_aliasing={{2}: (3, {}), {3}: (4, {}), {4}: (5, {}), {5}: (6, {}), {6}... | custom-call | flops 7809794048 | bytes 16777216 | tf_op jit(solution)/shard_map/ffn/pallas_call | solution.py:537
  186.4 7.2 %collective-permute-done.15.c_ref = bf16[512,896]{1,0:T(8,128)(2,1)} collective-permute-done((bf16[512,896]{1,0:T(8,128)(2,1)}, bf16[512,896]{1,0:T(8,128)(2,1)}, u32[]{:S(2)}, u32[]{:S(2)}) %collective-permute-start.15) | collective-permute-done | bytes 917536 | tf_op jit(solution)/shard_map/ppermute | solution.py:598
  193.6 13.7 %ffn.6 = (bf16[512,896]{1,0:T(8,128)(2,1)}, bf16[512,896]{1,0:T(8,128)(2,1)}, bf16[4,512,896]{2,1,0:T(8,128)(2,1)}, bf16[4,512,896]{2,1,0:T(8,128)(2,1)}, bf16[4...) custom-call(bf16[512,896]{1,0:T(8,128)(2,1)} %collective-permute-don, ...), custom_call_target="tpu_custom_call", output_to_operand_aliasing={{2}: (3, {}), {3}: (4, {}), {4}: (5, {}), {5}: (6, {}), {6}... | custom-call | flops 7809794048 | bytes 16777216 | tf_op jit(solution)/shard_map/ffn/pallas_call | solution.py:537
  207.7 13.7 %ffn.7 = (bf16[512,896]{1,0:T(8,128)(2,1)}, bf16[512,896]{1,0:T(8,128)(2,1)}, bf16[4,512,896]{2,1,0:T(8,128)(2,1)}, bf16[4,512,896]{2,1,0:T(8,128)(2,1)}, bf16[4...) custom-call(bf16[512,896]{1,0:T(8,128)(2,1)} %collective-permute-don, ...), custom_call_target="tpu_custom_call", output_to_operand_aliasing={{2}: (3, {}), {3}: (4, {}), {4}: (5, {}), {5}: (6, {}), {6}... | custom-call | flops 7809794048 | bytes 16777216 | tf_op jit(solution)/shard_map/ffn/pallas_call | solution.py:537
  222.0 22.5 %ffn_weights.1 = bf16[8,3,112,1216]{3,2,1,0:T(8,128)(2,1)} custom-call(bf16[4,512,896]{2,1,0:T(8,128)(2,1)} %get-tuple-element.88.x_ref, bf16[4,512,896]{2,1,0:T(8,128)(2,1)} %get-tuple-element.89.c_ref, bf16[4,512,1216]{2,1,0:T(8,128)(2,1)} %get-tuple-element.90.active_ref, bf16[4,512,1216]{2,1,0:T(8,128)(2,1)} %get-tuple-element.91.gate_ref, ...), custom_call_target="tpu_custom_call" | custom-call | flops 13388218368 | bytes 31457280 | tf_op jit(solution)/shard_map/ffn_weights/pallas_call | solution.py:582
  244.5 2.6 add_convert_fusion.3
  252.6 5.7 %collective-permute-done.20 = bf16[256,896]{1,0:T(8,128)(2,1)S(1)} collective-permute-done((bf16[256,896]{1,0:T(8,128)(2,1)}, bf16[256,896]{1,0:T(8,128)(2,1)S(1)}, u32[]{:S(2)}, u32[]{:S(2)}) %collective-permute-start.20) | collective-permute-done | bytes 458784 | tf_op jit(solution)/shard_map/ppermute | solution.py:598
  263.6 3.9 convolution_convert_fusion
  269.5 4.1 weight_pieces.3
  273.7 2.5 select_bitcast_fusion.1
  276.2 36.3 %attend_backward.1 = (bf16[2,256,896]{2,1,0:T(8,128)(2,1)}, bf16[1,8,256,256]{3,2,1,0:T(8,128)(2,1)}) custom-call(s32[8]{0:T(128)} %stack.49.order_ref, bf16[2,256,896]{2,1,0:T(8,128)(2,1)} %bitcast.172, bf16[2,256,896]{2,1,0:T(8,128)(2,1)} %get-tuple-element.65.o_ref, bf16[2,256,896]{2,1,0:T(8,128)(2,1)} %bitcast.175, ...), custom_call_target="tpu_custom_call" | custom-call | flops 23488102400 | bytes 8388608 | tf_op jit(solution)/shard_map/attend_backward/pallas_call | solution.py:465
  312.6 2.2 fusion.2
  318.5 2.5 add_convert_fusion.1
  325.9 2.9 collective-permute-done.46
  329.4 2.4 collective-permute-start.29
  331.9 11.8 %collective-permute-done.27 = bf16[1,2,256,256]{3,2,1,0:T(8,128)(2,1)S(1)} collective-permute-done((bf16[1,2,256,256]{3,2,1,0:T(8,128)(2,1)S(1)}, bf16[1,2,256,256]{3,2,1,0:T(8,128)(2,1)S(1)}, u32[]{:S(2)}, u32[]{:S(2)}) %collective-permute-start.27) | collective-permute-done | bytes 262176 | tf_op jit(solution)/shard_map/ppermute | solution.py:598
  345.3 4.6 %collective-permute-done.29 = bf16[1,2,256,256]{3,2,1,0:T(8,128)(2,1)S(1)} collective-permute-done((bf16[1,2,256,256]{3,2,1,0:T(8,128)(2,1)S(1)}, bf16[1,2,256,256]{3,2,1,0:T(8,128)(2,1)S(1)}, u32[]{:S(2)}, u32[]{:S(2)}) %collective-permute-start.29) | collective-permute-done | bytes 262176 | tf_op jit(solution)/shard_map/ppermute | solution.py:598
  350.6 6.3 %project_backward.1 = (bf16[512,256]{1,0:T(8,128)(2,1)}, f32[512,896]{1,0:T(8,128)}, f32[1,896]{1,0:T(1,128)}, f32[1,1152]{1,0:T(1,128)}) custom-call(bf16[512,896]{1,0:T(8,128)(2,1)} %bitcast.147, bf16[896,2048]{1,0:T(8,128)(2,1)} %all-gather.4.cloned.1.call-done.w_ref, bf16[512,896]{1,0:T(8,128)(2,1)} %maximum_bitcast_fusion.x_ref, ...), custom_call_target="tpu_custom_call" | custom-call | flops 2113929216 | bytes 8388608 | tf_op jit(solution)/shard_map/project_backward/pallas_call | solution.py:161
  362.8 2.0 slice.378
  364.8 2.2 slice.319
  368.6 4.8 %weight_pieces.2 = bf16[4,8,112,288]{3,2,1,0:T(8,128)(2,1)} custom-call(bf16[512,896]{1,0:T(8,128)(2,1)} %get-tuple-element.111.lhs_ref, bf16[512,896]{1,0:T(8,128)(2,1)} %bitcast.148, bf16[512,256]{1,0:T(8,128)(2,1)} %get-tuple-element.112.rest_1_), custom_call_target="tpu_custom_call" | custom-call | flops 2113929216 | bytes 5242880 | tf_op jit(solution)/shard_map/weight_pieces/pallas_call | solution.py:209
  374.1 3.6 fusion.33
  379.5 2.5 copy.57
  382.0 3.2 collective-permute-start.36
  397.9 6.4 %collective-permute-done.26 = bf16[1,256,896]{2,1,0:T(8,128)(2,1)S(1)} collective-permute-done((bf16[1,256,896]{2,1,0:T(8,128)(2,1)S(1)}, bf16[1,256,896]{2,1,0:T(8,128)(2,1)S(1)}, u32[]{:S(2)}, u32[]{:S(2)}) %collective-permute-start.26) | collective-permute-done | bytes 458784 | tf_op jit(solution)/shard_map/ppermute | solution.py:690
  405.3 5.3 %collective-permute-done.40 = bf16[4,112,288]{1,2,0:T(8,128)(2,1)S(1)} collective-permute-done((bf16[4,112,288]{1,2,0:T(8,128)(2,1)S(1)}, bf16[4,112,288]{1,2,0:T(8,128)(2,1)S(1)}, u32[]{:S(2)}, u32[]{:S(2)}) %collective-permute-start.40) | collective-permute-done | bytes 258080 | tf_op jit(solution)/shard_map/ppermute | solution.py:598
  410.6 5.1 %collective-permute-done.39 = bf16[4,112,288]{1,2,0:T(8,128)(2,1)S(1)} collective-permute-done((bf16[4,112,288]{1,2,0:T(8,128)(2,1)S(1)}, bf16[4,112,288]{1,2,0:T(8,128)(2,1)S(1)}, u32[]{:S(2)}, u32[]{:S(2)}) %collective-permute-start.39) | collective-permute-done | bytes 258080 | tf_op jit(solution)/shard_map/ppermute | solution.py:598
  418.4 1.9 collective-permute-start.41
  420.3 2.2 fusion.39
  423.4 2.9 collective-permute-start.51
  427.3 16.8 %collective-permute-done.51 = bf16[112,608]{1,0:T(8,128)(2,1)S(1)} collective-permute-done((bf16[112,608]{1,0:T(8,128)(2,1)S(1)}, bf16[112,608]{1,0:T(8,128)(2,1)S(1)}, u32[]{:S(2)}, u32[]{:S(2)}) %collective-permute-start.51) | collective-permute-done | bytes 136224 | tf_op jit(solution)/shard_map/ppermute | solution.py:669
  (228 shorter events, 83.5 us)
Async XLA Ops:
  7.2 71.8 %all-gather.4.cloned.1.call-start = ((), (), s32[]{:S(2)}) async-start(), calls=%async_computation.1 | async-start | bytes 4128768 | tf_op jit(solution)/shard_map/all_gather | solution.py:725
  10.0 8.7 %collective-permute-start.2 = (bf16[114,512]{1,0:T(8,128)(2,1)S(1)}, bf16[114,512]{1,0:T(8,128)(2,1)S(1)}, u32[]{:S(2)}, u32[]{:S(2)}) collective-permute-start(bf16[114,512]{1,0:T(8,128)(2,1)S(1)} %pad_maximum_fusion.14), channel_id=1, source_target_pairs={{0,3},{1,2},{2,1},{3,0},{4,7},{5,6},{6,5},{7,4},{8,11},{9,10},{10,... | collective-permute-start | bytes 350216 | tf_op jit(solution)/shard_map/ppermute | solution.py:598
  22.7 136.1 %all-gather.6.cloned.1.call-start = ((), (), s32[]{:S(2)}) async-start(), calls=%async_computation.3 | async-start | bytes 7741440 | tf_op jit(solution)/shard_map/all_gather | solution.py:734
  22.8 25.5 %collective-permute-start.8 = (bf16[112,608]{1,0:T(8,128)(2,1)S(1)}, bf16[112,608]{1,0:T(8,128)(2,1)S(1)}, u32[]{:S(2)}, u32[]{:S(2)}) collective-permute-start(bf16[112,608]{1,0:T(8,128)(2,1)S(1)} %get-tuple-element.171), channel_id=1, source_target_pairs={{0,0},{1,8},{2,16},{3,24},{4,4},{5,12},{6,20},{7,28},{8,1},{9,9},{... | collective-permute-start | bytes 408584 | tf_op jit(solution)/shard_map/ppermute | solution.py:669
  26.3 33.9 %collective-permute-start.9 = (bf16[112,608]{1,0:T(8,128)(2,1)S(1)}, bf16[112,608]{1,0:T(8,128)(2,1)S(1)}, u32[]{:S(2)}, u32[]{:S(2)}) collective-permute-start(bf16[112,608]{1,0:T(8,128)(2,1)S(1)} %get-tuple-element.172), channel_id=1, source_target_pairs={{0,4},{1,12},{2,20},{3,28},{4,0},{5,8},{6,16},{7,24},{8,5},{9,13},... | collective-permute-start | bytes 408584 | tf_op jit(solution)/shard_map/ppermute | solution.py:669
  61.4 358.9 %reduce-scatter.2.cloned.1.call-start = ((), (), s32[]{:S(2)}) async-start(), calls=%async_computation.2 | async-start | bytes 7741440 | tf_op jit(solution)/shard_map/reduce_scatter | solution.py:768
  64.0 13.9 %collective-permute-start.3 = (bf16[1,256,896]{2,1,0:T(8,128)(2,1)S(1)}, bf16[1,256,896]{2,1,0:T(8,128)(2,1)S(1)}, u32[]{:S(2)}, u32[]{:S(2)}) collective-permute-start(bf16[1,256,896]{2,1,0:T(8,128)(2,1)S(1)} %get-tuple-element.146), channel_id=1, source_target_pairs={{0,3},{1,2},{2,1},{3,0},{4,7},{5,6},{6,5},{7,4},{8,11},{9,10},{10,... | collective-permute-start | bytes 1376264 | tf_op jit(solution)/shard_map/ppermute | solution.py:690
  84.3 10.4 %collective-permute-start.6 = (bf16[1,2,256,256]{3,2,1,0:T(8,128)(2,1)}, bf16[1,2,256,256]{3,2,1,0:T(8,128)(2,1)S(1)}, u32[]{:S(2)}, u32[]{:S(2)}) collective-permute-start(bf16[1,2,256,256]{3,2,1,0:T(8,128)(2,1)} %bitcast.166), channel_id=1, source_target_pairs={{0,3},{1,2},{2,1},{3,0},{4,7},{5,6},{6,5},{7,4},{8,11},{9,10},{10,... | collective-permute-start | bytes 786440 | tf_op jit(solution)/shard_map/ppermute | solution.py:598
  85.3 12.1 %collective-permute-start.4 = (bf16[1,2,256,256]{3,2,1,0:T(8,128)(2,1)}, bf16[1,2,256,256]{3,2,1,0:T(8,128)(2,1)S(1)}, u32[]{:S(2)}, u32[]{:S(2)}) collective-permute-start(bf16[1,2,256,256]{3,2,1,0:T(8,128)(2,1)} %bitcast.167), channel_id=1, source_target_pairs={{0,1},{1,0},{2,3},{3,2},{4,5},{5,4},{6,7},{7,6},{8,9},{9,8},{10,11... | collective-permute-start | bytes 786440 | tf_op jit(solution)/shard_map/ppermute | solution.py:598
  85.3 15.0 %collective-permute-start.5 = (bf16[1,2,256,256]{3,2,1,0:T(8,128)(2,1)}, bf16[1,2,256,256]{3,2,1,0:T(8,128)(2,1)S(1)}, u32[]{:S(2)}, u32[]{:S(2)}) collective-permute-start(bf16[1,2,256,256]{3,2,1,0:T(8,128)(2,1)} %bitcast.168), channel_id=1, source_target_pairs={{0,2},{1,3},{2,0},{3,1},{4,6},{5,7},{6,4},{7,5},{8,10},{9,11},{10,... | collective-permute-start | bytes 786440 | tf_op jit(solution)/shard_map/ppermute | solution.py:598
  95.6 39.0 %collective-permute-start.7 = (bf16[1,256,896]{2,1,0:T(8,128)(2,1)}, bf16[1,256,896]{2,1,0:T(8,128)(2,1)S(1)}, u32[]{:S(2)}, u32[]{:S(2)}) collective-permute-start(bf16[1,256,896]{2,1,0:T(8,128)(2,1)} %get-tuple-element.142), channel_id=1, source_target_pairs={{0,3},{1,2},{2,1},{3,0},{4,7},{5,6},{6,5},{7,4},{8,11},{9,10},{10,... | collective-permute-start | bytes 1376264 | tf_op jit(solution)/shard_map/ppermute | solution.py:690
  131.9 13.4 %collective-permute-start.11 = (bf16[256,896]{1,0:T(8,128)(2,1)S(1)}, bf16[256,896]{1,0:T(8,128)(2,1)S(1)}, u32[]{:S(2)}, u32[]{:S(2)}) collective-permute-start(bf16[256,896]{1,0:T(8,128)(2,1)S(1)} %get-tuple-element.144), channel_id=1, source_target_pairs={{0,2},{1,3},{2,0},{3,1},{4,6},{5,7},{6,4},{7,5},{8,10},{9,11},{10,... | collective-permute-start | bytes 1376264 | tf_op jit(solution)/shard_map/ppermute | solution.py:598
  132.6 13.5 %collective-permute-start.10 = (bf16[256,896]{1,0:T(8,128)(2,1)S(1)}, bf16[256,896]{1,0:T(8,128)(2,1)S(1)}, u32[]{:S(2)}, u32[]{:S(2)}) collective-permute-start(bf16[256,896]{1,0:T(8,128)(2,1)S(1)} %get-tuple-element.143), channel_id=1, source_target_pairs={{0,1},{1,0},{2,3},{3,2},{4,5},{5,4},{6,7},{7,6},{8,9},{9,8},{10,11... | collective-permute-start | bytes 1376264 | tf_op jit(solution)/shard_map/ppermute | solution.py:598
  132.7 23.2 %collective-permute-start.12 = (bf16[256,896]{1,0:T(8,128)(2,1)S(1)}, bf16[256,896]{1,0:T(8,128)(2,1)S(1)}, u32[]{:S(2)}, u32[]{:S(2)}) collective-permute-start(bf16[256,896]{1,0:T(8,128)(2,1)S(1)} %get-tuple-element.141), channel_id=1, source_target_pairs={{0,1},{1,0},{2,3},{3,2},{4,5},{5,4},{6,7},{7,6},{8,9},{9,8},{10,11... | collective-permute-start | bytes 1376264 | tf_op jit(solution)/shard_map/ppermute | solution.py:598
  134.6 21.3 %collective-permute-start.13 = (bf16[256,896]{1,0:T(8,128)(2,1)S(1)}, bf16[256,896]{1,0:T(8,128)(2,1)S(1)}, u32[]{:S(2)}, u32[]{:S(2)}) collective-permute-start(bf16[256,896]{1,0:T(8,128)(2,1)S(1)} %bitcast.141), channel_id=1, source_target_pairs={{0,2},{1,3},{2,0},{3,1},{4,6},{5,7},{6,4},{7,5},{8,10},{9,11},{10,... | collective-permute-start | bytes 1376264 | tf_op jit(solution)/shard_map/ppermute | solution.py:598
  147.7 60.0 %collective-permute-start.16 = (bf16[512,896]{1,0:T(8,128)(2,1)}, bf16[512,896]{1,0:T(8,128)(2,1)}, u32[]{:S(2)}, u32[]{:S(2)}) collective-permute-start(bf16[512,896]{1,0:T(8,128)(2,1)} %get-tuple-element.161), channel_id=1, source_target_pairs={{0,1},{1,0},{2,3},{3,2},{4,5},{5,4},{6,7},{7,6},{8,9},{9,8},{10,11... | collective-permute-start | bytes 2752520 | tf_op jit(solution)/shard_map/ppermute | solution.py:598
  147.7 38.7 %collective-permute-start.14 = (bf16[512,896]{1,0:T(8,128)(2,1)}, bf16[512,896]{1,0:T(8,128)(2,1)}, u32[]{:S(2)}, u32[]{:S(2)}) collective-permute-start(bf16[512,896]{1,0:T(8,128)(2,1)} %get-tuple-element.160), channel_id=1, source_target_pairs={{0,2},{1,3},{2,0},{3,1},{4,6},{5,7},{6,4},{7,5},{8,10},{9,11},{10,... | collective-permute-start | bytes 2752520 | tf_op jit(solution)/shard_map/ppermute | solution.py:598
  157.5 50.2 %collective-permute-start.17 = (bf16[512,896]{1,0:T(8,128)(2,1)}, bf16[512,896]{1,0:T(8,128)(2,1)}, u32[]{:S(2)}, u32[]{:S(2)}) collective-permute-start(bf16[512,896]{1,0:T(8,128)(2,1)} %get-tuple-element.158), channel_id=1, source_target_pairs={{0,1},{1,0},{2,3},{3,2},{4,5},{5,4},{6,7},{7,6},{8,9},{9,8},{10,11... | collective-permute-start | bytes 2752520 | tf_op jit(solution)/shard_map/ppermute | solution.py:598
  157.5 36.1 %collective-permute-start.15 = (bf16[512,896]{1,0:T(8,128)(2,1)}, bf16[512,896]{1,0:T(8,128)(2,1)}, u32[]{:S(2)}, u32[]{:S(2)}) collective-permute-start(bf16[512,896]{1,0:T(8,128)(2,1)} %get-tuple-element.157), channel_id=1, source_target_pairs={{0,2},{1,3},{2,0},{3,1},{4,6},{5,7},{6,4},{7,5},{8,10},{9,11},{10,... | collective-permute-start | bytes 2752520 | tf_op jit(solution)/shard_map/ppermute | solution.py:598
  207.3 37.1 %collective-permute-start.18 = (bf16[512,896]{1,0:T(8,128)(2,1)}, bf16[512,896]{1,0:T(8,128)(2,1)}, u32[]{:S(2)}, u32[]{:S(2)}) collective-permute-start(bf16[512,896]{1,0:T(8,128)(2,1)} %get-tuple-element.93), channel_id=1, source_target_pairs={{0,2},{1,3},{2,0},{3,1},{4,6},{5,7},{6,4},{7,5},{8,10},{9,11},{10,... | collective-permute-start | bytes 2752520 | tf_op jit(solution)/shard_map/ppermute | solution.py:598
  221.4 23.0 %collective-permute-start.19 = (bf16[512,896]{1,0:T(8,128)(2,1)}, bf16[512,896]{1,0:T(8,128)(2,1)}, u32[]{:S(2)}, u32[]{:S(2)}) collective-permute-start(bf16[512,896]{1,0:T(8,128)(2,1)} %get-tuple-element.94), channel_id=1, source_target_pairs={{0,1},{1,0},{2,3},{3,2},{4,5},{5,4},{6,7},{7,6},{8,9},{9,8},{10,11... | collective-permute-start | bytes 2752520 | tf_op jit(solution)/shard_map/ppermute | solution.py:598
  247.1 11.3 %collective-permute-start.20 = (bf16[256,896]{1,0:T(8,128)(2,1)}, bf16[256,896]{1,0:T(8,128)(2,1)S(1)}, u32[]{:S(2)}, u32[]{:S(2)}) collective-permute-start(bf16[256,896]{1,0:T(8,128)(2,1)} %get-tuple-element.138), channel_id=1, source_target_pairs={{0,1},{1,0},{2,3},{3,2},{4,5},{5,4},{6,7},{7,6},{8,9},{9,8},{10,11... | collective-permute-start | bytes 1376264 | tf_op jit(solution)/shard_map/ppermute | solution.py:598
  248.6 11.1 %collective-permute-start.21 = (bf16[256,896]{1,0:T(8,128)(2,1)}, bf16[256,896]{1,0:T(8,128)(2,1)}, u32[]{:S(2)}, u32[]{:S(2)}) collective-permute-start(bf16[256,896]{1,0:T(8,128)(2,1)} %get-tuple-element.139), channel_id=1, source_target_pairs={{0,2},{1,3},{2,0},{3,1},{4,6},{5,7},{6,4},{7,5},{8,10},{9,11},{10,... | collective-permute-start | bytes 1376264 | tf_op jit(solution)/shard_map/ppermute | solution.py:598
  267.5 50.9 %collective-permute-start.22 = (bf16[512,896]{1,0:T(8,128)(2,1)}, bf16[512,896]{1,0:T(8,128)(2,1)S(1)}, u32[]{:S(2)}, u32[]{:S(2)}) collective-permute-start(bf16[512,896]{1,0:T(8,128)(2,1)} %get-tuple-element.101), channel_id=1, source_target_pairs={{0,2},{1,3},{2,0},{3,1},{4,6},{5,7},{6,4},{7,5},{8,10},{9,11},{10,... | collective-permute-start | bytes 2752520 | tf_op jit(solution)/shard_map/ppermute | solution.py:598
  269.2 49.2 %collective-permute-start.23 = (bf16[512,896]{1,0:T(8,128)(2,1)}, bf16[512,896]{1,0:T(8,128)(2,1)}, u32[]{:S(2)}, u32[]{:S(2)}) collective-permute-start(bf16[512,896]{1,0:T(8,128)(2,1)} %get-tuple-element.102), channel_id=1, source_target_pairs={{0,1},{1,0},{2,3},{3,2},{4,5},{5,4},{6,7},{7,6},{8,9},{9,8},{10,11... | collective-permute-start | bytes 2752520 | tf_op jit(solution)/shard_map/ppermute | solution.py:598
  276.2 36.4 %collective-permute-start.44 = (bf16[4,4,112,224]{3,2,1,0:T(8,128)(2,1)}, bf16[4,4,112,224]{3,2,1,0:T(8,128)(2,1)}, u32[]{:S(2)}, u32[]{:S(2)}) collective-permute-start(bf16[4,4,112,224]{3,2,1,0:T(8,128)(2,1)} %select_bitcast_fusion.1), channel_id=1, source_target_pairs={{0,4},{4,0},{8,12},{12,8},{16,20},{20,16},{24,28},{28,24},{1,5},{5... | collective-permute-start | bytes 2408456 | tf_op jit(solution)/shard_map/ppermute | solution.py:821
  314.9 9.4 %collective-permute-start.47 = (bf16[4,112,224]{2,1,0:T(8,128)(2,1)S(1)}, bf16[4,112,224]{2,1,0:T(8,128)(2,1)S(1)}, u32[]{:S(2)}, u32[]{:S(2)}) collective-permute-start(bf16[4,112,224]{2,1,0:T(8,128)(2,1)S(1)} %get-tuple-element.128), channel_id=1, source_target_pairs={{0,3},{1,2},{2,1},{3,0},{4,7},{5,6},{6,5},{7,4},{8,11},{9,10},{10,... | collective-permute-start | bytes 602120 | tf_op jit(solution)/shard_map/ppermute | solution.py:598
  316.4 12.5 %collective-permute-start.46 = (bf16[4,112,224]{2,1,0:T(8,128)(2,1)S(1)}, bf16[4,112,224]{2,1,0:T(8,128)(2,1)S(1)}, u32[]{:S(2)}, u32[]{:S(2)}) collective-permute-start(bf16[4,112,224]{2,1,0:T(8,128)(2,1)S(1)} %get-tuple-element.129), channel_id=1, source_target_pairs={{0,2},{1,3},{2,0},{3,1},{4,6},{5,7},{6,4},{7,5},{8,10},{9,11},{10,... | collective-permute-start | bytes 602120 | tf_op jit(solution)/shard_map/ppermute | solution.py:598
  318.1 11.3 %collective-permute-start.45 = (bf16[4,112,224]{2,1,0:T(8,128)(2,1)S(1)}, bf16[4,112,224]{2,1,0:T(8,128)(2,1)S(1)}, u32[]{:S(2)}, u32[]{:S(2)}) collective-permute-start(bf16[4,112,224]{2,1,0:T(8,128)(2,1)S(1)} %get-tuple-element.127), channel_id=1, source_target_pairs={{0,1},{1,0},{2,3},{3,2},{4,5},{5,4},{6,7},{7,6},{8,9},{9,8},{10,11... | collective-permute-start | bytes 602120 | tf_op jit(solution)/shard_map/ppermute | solution.py:598
  321.0 67.0 %collective-permute-start.24 = (bf16[256,896]{1,0:T(8,128)(2,1)}, bf16[256,896]{1,0:T(8,128)(2,1)S(1)}, u32[]{:S(2)}, u32[]{:S(2)}) collective-permute-start(bf16[256,896]{1,0:T(8,128)(2,1)} %get-tuple-element.134), channel_id=1, source_target_pairs={{0,1},{1,0},{2,3},{3,2},{4,5},{5,4},{6,7},{7,6},{8,9},{9,8},{10,11... | collective-permute-start | bytes 1376264 | tf_op jit(solution)/shard_map/ppermute | solution.py:598
  322.6 65.4 %collective-permute-start.25 = (bf16[256,896]{1,0:T(8,128)(2,1)}, bf16[256,896]{1,0:T(8,128)(2,1)}, u32[]{:S(2)}, u32[]{:S(2)}) collective-permute-start(bf16[256,896]{1,0:T(8,128)(2,1)} %get-tuple-element.135), channel_id=1, source_target_pairs={{0,2},{1,3},{2,0},{3,1},{4,6},{5,7},{6,4},{7,5},{8,10},{9,11},{10,... | collective-permute-start | bytes 1376264 | tf_op jit(solution)/shard_map/ppermute | solution.py:598
  324.3 19.4 %collective-permute-start.27 = (bf16[1,2,256,256]{3,2,1,0:T(8,128)(2,1)S(1)}, bf16[1,2,256,256]{3,2,1,0:T(8,128)(2,1)S(1)}, u32[]{:S(2)}, u32[]{:S(2)}) collective-permute-start(bf16[1,2,256,256]{3,2,1,0:T(8,128)(2,1)S(1)} %get-tuple-element.125), channel_id=1, source_target_pairs={{0,1},{1,0},{2,3},{3,2},{4,5},{5,4},{6,7},{7,6},{8,9},{9,8},{10,11... | collective-permute-start | bytes 786440 | tf_op jit(solution)/shard_map/ppermute | solution.py:598
  328.8 15.7 %collective-permute-start.28 = (bf16[1,2,256,256]{3,2,1,0:T(8,128)(2,1)S(1)}, bf16[1,2,256,256]{3,2,1,0:T(8,128)(2,1)S(1)}, u32[]{:S(2)}, u32[]{:S(2)}) collective-permute-start(bf16[1,2,256,256]{3,2,1,0:T(8,128)(2,1)S(1)} %get-tuple-element.124), channel_id=1, source_target_pairs={{0,2},{1,3},{2,0},{3,1},{4,6},{5,7},{6,4},{7,5},{8,10},{9,11},{10,... | collective-permute-start | bytes 786440 | tf_op jit(solution)/shard_map/ppermute | solution.py:598
  329.4 20.5 %collective-permute-start.29 = (bf16[1,2,256,256]{3,2,1,0:T(8,128)(2,1)S(1)}, bf16[1,2,256,256]{3,2,1,0:T(8,128)(2,1)S(1)}, u32[]{:S(2)}, u32[]{:S(2)}) collective-permute-start(bf16[1,2,256,256]{3,2,1,0:T(8,128)(2,1)S(1)} %get-tuple-element.123), channel_id=1, source_target_pairs={{0,3},{1,2},{2,1},{3,0},{4,7},{5,6},{6,5},{7,4},{8,11},{9,10},{10,... | collective-permute-start | bytes 786440 | tf_op jit(solution)/shard_map/ppermute | solution.py:598
  343.7 14.9 %collective-permute-start.50 = (bf16[112,224]{1,0:T(8,128)(2,1)S(1)}, bf16[112,224]{1,0:T(8,128)(2,1)S(1)}, u32[]{:S(2)}, u32[]{:S(2)}) collective-permute-start(bf16[112,224]{1,0:T(8,128)(2,1)S(1)} %get-tuple-element.174), channel_id=1, source_target_pairs={{0,24},{4,28},{8,0},{12,4},{16,8},{20,12},{24,16},{28,20},{1,25},{... | collective-permute-start | bytes 150536 | tf_op jit(solution)/shard_map/ppermute | solution.py:836
  344.6 15.6 %collective-permute-start.49 = (bf16[112,224]{1,0:T(8,128)(2,1)S(1)}, bf16[112,224]{1,0:T(8,128)(2,1)S(1)}, u32[]{:S(2)}, u32[]{:S(2)}) collective-permute-start(bf16[112,224]{1,0:T(8,128)(2,1)S(1)} %get-tuple-element.175), channel_id=1, source_target_pairs={{0,16},{4,20},{8,24},{12,28},{16,0},{20,4},{24,8},{28,12},{1,17},{... | collective-permute-start | bytes 150536 | tf_op jit(solution)/shard_map/ppermute | solution.py:836
  349.9 11.9 %collective-permute-start.48 = (bf16[112,224]{1,0:T(8,128)(2,1)S(1)}, bf16[112,224]{1,0:T(8,128)(2,1)S(1)}, u32[]{:S(2)}, u32[]{:S(2)}) collective-permute-start(bf16[112,224]{1,0:T(8,128)(2,1)S(1)} %get-tuple-element.173), channel_id=1, source_target_pairs={{0,8},{4,12},{8,16},{12,20},{16,24},{20,28},{24,0},{28,4},{1,9},{5... | collective-permute-start | bytes 150536 | tf_op jit(solution)/shard_map/ppermute | solution.py:836
  358.6 8.4 %collective-permute-start.33 = (f32[1,736]{1,0:T(1,128)S(1)}, f32[1,736]{1,0:T(1,128)S(1)}, u32[]{:S(2)}, u32[]{:S(2)}) collective-permute-start(f32[1,736]{1,0:T(1,128)S(1)} %get-tuple-element.177), channel_id=1, source_target_pairs={{0,3},{1,2},{2,1},{3,0},{4,7},{5,6},{6,5},{7,4},{8,11},{9,10},{10,... | collective-permute-start | bytes 8840 | tf_op jit(solution)/shard_map/ppermute | solution.py:598
  367.0 24.4 %collective-permute-start.30 = (bf16[1,256,896]{2,1,0:T(8,128)(2,1)}, bf16[1,256,896]{2,1,0:T(8,128)(2,1)}, u32[]{:S(2)}, u32[]{:S(2)}) collective-permute-start(bf16[1,256,896]{2,1,0:T(8,128)(2,1)} %slice.378), channel_id=1, source_target_pairs={{0,3},{1,2},{2,1},{3,0},{4,7},{5,6},{6,5},{7,4},{8,11},{9,10},{10,... | collective-permute-start | bytes 1376264 | tf_op jit(solution)/shard_map/ppermute | solution.py:850
  373.4 8.6 %collective-permute-start.35 = (f32[1,736]{1,0:T(1,128)S(1)}, f32[1,736]{1,0:T(1,128)S(1)}, u32[]{:S(2)}, u32[]{:S(2)}) collective-permute-start(f32[1,736]{1,0:T(1,128)S(1)} %add.256), channel_id=1, source_target_pairs={{0,8},{4,12},{8,0},{12,4},{16,24},{20,28},{24,16},{28,20},{1,9},{5... | collective-permute-start | bytes 8840 | tf_op jit(solution)/shard_map/ppermute | solution.py:879
  389.8 14.5 %collective-permute-start.26 = (bf16[1,256,896]{2,1,0:T(8,128)(2,1)S(1)}, bf16[1,256,896]{2,1,0:T(8,128)(2,1)S(1)}, u32[]{:S(2)}, u32[]{:S(2)}) collective-permute-start(bf16[1,256,896]{2,1,0:T(8,128)(2,1)S(1)} %get-tuple-element.131), channel_id=1, source_target_pairs={{0,3},{1,2},{2,1},{3,0},{4,7},{5,6},{6,5},{7,4},{8,11},{9,10},{10,... | collective-permute-start | bytes 1376264 | tf_op jit(solution)/shard_map/ppermute | solution.py:690
  393.0 17.6 %collective-permute-start.40 = (bf16[4,112,288]{1,2,0:T(8,128)(2,1)S(1)}, bf16[4,112,288]{1,2,0:T(8,128)(2,1)S(1)}, u32[]{:S(2)}, u32[]{:S(2)}) collective-permute-start(bf16[4,112,288]{1,2,0:T(8,128)(2,1)S(1)} %get-tuple-element.121), channel_id=1, source_target_pairs={{0,3},{1,2},{2,1},{3,0},{4,7},{5,6},{6,5},{7,4},{8,11},{9,10},{10,... | collective-permute-start | bytes 774152 | tf_op jit(solution)/shard_map/ppermute | solution.py:598
  394.5 21.2 %collective-permute-start.39 = (bf16[4,112,288]{1,2,0:T(8,128)(2,1)S(1)}, bf16[4,112,288]{1,2,0:T(8,128)(2,1)S(1)}, u32[]{:S(2)}, u32[]{:S(2)}) collective-permute-start(bf16[4,112,288]{1,2,0:T(8,128)(2,1)S(1)} %get-tuple-element.122), channel_id=1, source_target_pairs={{0,2},{1,3},{2,0},{3,1},{4,6},{5,7},{6,4},{7,5},{8,10},{9,11},{10,... | collective-permute-start | bytes 774152 | tf_op jit(solution)/shard_map/ppermute | solution.py:598
  396.2 19.7 %collective-permute-start.38 = (bf16[4,112,288]{1,2,0:T(8,128)(2,1)S(1)}, bf16[4,112,288]{1,2,0:T(8,128)(2,1)S(1)}, u32[]{:S(2)}, u32[]{:S(2)}) collective-permute-start(bf16[4,112,288]{1,2,0:T(8,128)(2,1)S(1)} %get-tuple-element.120), channel_id=1, source_target_pairs={{0,1},{1,0},{2,3},{3,2},{4,5},{5,4},{6,7},{7,6},{8,9},{9,8},{10,11... | collective-permute-start | bytes 774152 | tf_op jit(solution)/shard_map/ppermute | solution.py:598
  416.1 10.5 %collective-permute-start.43 = (bf16[112,288]{0,1:T(8,128)(2,1)S(1)}, bf16[112,288]{0,1:T(8,128)(2,1)S(1)}, u32[]{:S(2)}, u32[]{:S(2)}) collective-permute-start(bf16[112,288]{0,1:T(8,128)(2,1)S(1)} %get-tuple-element.163), channel_id=1, source_target_pairs={{0,24},{4,28},{8,0},{12,4},{16,8},{20,12},{24,16},{28,20},{1,25},{... | collective-permute-start | bytes 193544 | tf_op jit(solution)/shard_map/ppermute | solution.py:836
  418.0 8.5 %collective-permute-start.42 = (bf16[112,288]{0,1:T(8,128)(2,1)S(1)}, bf16[112,288]{0,1:T(8,128)(2,1)S(1)}, u32[]{:S(2)}, u32[]{:S(2)}) collective-permute-start(bf16[112,288]{0,1:T(8,128)(2,1)S(1)} %get-tuple-element.164), channel_id=1, source_target_pairs={{0,16},{4,20},{8,24},{12,28},{16,0},{20,4},{24,8},{28,12},{1,17},{... | collective-permute-start | bytes 193544 | tf_op jit(solution)/shard_map/ppermute | solution.py:836
  423.4 20.8 %collective-permute-start.51 = (bf16[112,608]{1,0:T(8,128)(2,1)S(1)}, bf16[112,608]{1,0:T(8,128)(2,1)S(1)}, u32[]{:S(2)}, u32[]{:S(2)}) collective-permute-start(bf16[112,608]{1,0:T(8,128)(2,1)S(1)} %get-tuple-element.150), channel_id=1, source_target_pairs={{0,0},{1,8},{2,16},{3,24},{4,4},{5,12},{6,20},{7,28},{8,1},{9,9},{... | collective-permute-start | bytes 408584 | tf_op jit(solution)/shard_map/ppermute | solution.py:669
  426.3 18.8 %collective-permute-start.52 = (bf16[112,608]{1,0:T(8,128)(2,1)S(1)}, bf16[112,608]{1,0:T(8,128)(2,1)S(1)}, u32[]{:S(2)}, u32[]{:S(2)}) collective-permute-start(bf16[112,608]{1,0:T(8,128)(2,1)S(1)} %get-tuple-element.151), channel_id=1, source_target_pairs={{0,4},{1,12},{2,20},{3,28},{4,0},{5,8},{6,16},{7,24},{8,5},{9,13},... | collective-permute-start | bytes 408584 | tf_op jit(solution)/shard_map/ppermute | solution.py:669
  (30 other events, 240.8 us)
Sparse Core Ops, SparseCore 0:
  22.8 47.8 all-gather.3
  72.3 75.4 all-gather.5
  244.6 73.9 reduce-scatter.1

commit v4 on v3

--- a/solution.py
+++ b/solution.py
@@ -191,33 +191,42 @@
     )(grad_queries, weight, tokens, gain, grad_hidden, cosine, sine, *parts)
 
 
-def pieces_kernel(lhs_ref, *rest):
-    rhs_refs = rest[:-1]
-    out_ref = rest[-1]
-    ranks, owners, depth, own = out_ref.shape
+def pieces_kernel(core_ref, lhs_ref, *rest):
+    rhs_refs = rest[:-2]
+    mine_ref, other_ref = rest[-2:]
+    ranks, floors, depth, own = mine_ref.shape
     rhs = jnp.concatenate([ref[...] for ref in rhs_refs], axis=1)
     whole = dot(lhs_ref[...], rhs, TN)
+    first = core_ref[0] == 0
     for rank in range(ranks):
-        part = whole[:, rank * own : (rank + 1) * own]
-        out_ref[rank] = part.reshape(owners, depth, own).astype(bf16)
-
-
-def weight_pieces(ctx_size, seq_size, lhs, *rhs):
+        part = whole[:, rank * own : (rank + 1) * own].reshape(floors, 2, depth, own)
+        mine_ref[rank] = jnp.where(first, part[:, 0], part[:, 1]).astype(bf16)
+        other_ref[rank] = jnp.where(first, part[:, 1], part[:, 0]).astype(bf16)
+
+
+def weight_pieces(core, ctx_size, seq_size, lhs, *rhs):
     rows, width = lhs.shape
     columns = sum(x.shape[1] for x in rhs)
-    shape = (ctx_size, seq_size, width // seq_size, columns // ctx_size)
+    shape = (ctx_size, seq_size // 2, width // seq_size, columns // ctx_size)
+
+    def full(*shape):
+        return pl.BlockSpec(shape, lambda i, core: (0,) * len(shape))
+
     return pl.pallas_call(
         pieces_kernel,
-        grid=(1,),
-        in_specs=[full_spec(*x.shape) for x in (lhs, *rhs)],
-        out_specs=full_spec(*shape),
-        out_shape=jax.ShapeDtypeStruct(shape, bf16),
+        grid_spec=pltpu.PrefetchScalarGridSpec(
+            num_scalar_prefetch=1,
+            grid=(1,),
+            in_specs=[full(*x.shape) for x in (lhs, *rhs)],
+            out_specs=[full(*shape)] * 2,
+        ),
+        out_shape=[jax.ShapeDtypeStruct(shape, bf16)] * 2,
         cost_estimate=pl.CostEstimate(
             flops=4 * rows * width * columns, bytes_accessed=5 << 20, transcendentals=0
         ),
         compiler_params=params(),
         name="weight_pieces",
-    )(lhs, *rhs)
+    )(core.astype(jnp.int32)[None], lhs, *rhs)
 
 
 def pair_sides(both):
@@ -498,7 +507,7 @@
     )(order, queries, mixed, grads, stats_in, cosine, sine, *parts)
 
 
-def ffn_kernel(x_ref, c_ref, w_ref, *rest):
+def ffn_kernel(x_ref, c_ref, w_ref, d_ref, *rest):
     out_ref, grad_ref, x_all, c_all, active_all, gate_all, up_all = rest[-7:]
     seq_size, _, depth, columns = w_ref.shape
     width = seq_size * depth
@@ -508,7 +517,7 @@
     c_all[0] = c
     gate_w = w_ref[:, 0].reshape(width, columns)
     up_w = w_ref[:, 1].reshape(width, columns)
-    down_w = w_ref[:, 2].reshape(width, columns)
+    down_w = d_ref[...].reshape(width, columns)
     gate = dot(x, gate_w, NN)
     up = dot(x, up_w, NN)
     grad_active = dot(c, down_w, NN)
@@ -524,7 +533,7 @@
     out_ref[...] = dot(active, down_w, NT).astype(bf16)
 
 
-def ffn(number, count, x, c, weights, buffers):
+def ffn(number, count, x, c, weights, down, buffers):
     rows, width = x.shape
     columns = weights.shape[3]
     tile = rows // 2
@@ -537,19 +546,24 @@
     return pl.pallas_call(
         ffn_kernel,
         grid=(2,),
-        in_specs=[row_spec(tile, width), row_spec(tile, width), full_spec(*weights.shape)]
+        in_specs=[
+            row_spec(tile, width),
+            row_spec(tile, width),
+            full_spec(*weights.shape),
+            full_spec(*down.shape),
+        ]
         + [pl.BlockSpec(memory_space=pl.ANY)] * len(buffers),
         out_specs=[row_spec(tile, width), row_spec(tile, width)]
         + [slot(width)] * 2
         + [slot(columns)] * 3,
         out_shape=[jax.ShapeDtypeStruct((rows, width), bf16)] * 2 + [wide] * 2 + [inner] * 3,
-        input_output_aliases={3 + i: 2 + i for i in range(len(buffers))},
+        input_output_aliases={4 + i: 2 + i for i in range(len(buffers))},
         cost_estimate=pl.CostEstimate(
             flops=14 * rows * width * columns, bytes_accessed=16 << 20, transcendentals=0
         ),
         compiler_params=params(),
         name="ffn",
-    )(x, c, weights, *buffers)
+    )(x, c, weights, down, *buffers)
 
 
 def ffn_weights_kernel(x_ref, c_ref, active_ref, gate_ref, up_ref, out_ref, acc_ref):
@@ -598,16 +612,25 @@
     return lax.ppermute(x, "ctx", [(i, i ^ mask) for i in range(ctx_size)])
 
 
-def spread(x, ctx_size):
+def spread_near(x, ctx_size):
     if ctx_size != 4:
-        return [x] + [hop(x, ctx_size, k) for k in range(1, ctx_size)]
+        return [hop(x, ctx_size, k) for k in range(1, ctx_size)]
     half = x.shape[0] // 2
-    front, back = x[:half], x[half:]
-    front_1 = hop(front, 4, 1)
-    back_2 = hop(back, 4, 2)
-    front_far = hop(jnp.concatenate([front, front_1], axis=0), 4, 2)
-    back_far = hop(jnp.concatenate([back, back_2], axis=0), 4, 1)
-    return [x, jnp.concatenate([front_1, back_2], axis=0), front_far, back_far]
+    return [hop(x[:half], 4, 1), hop(x[half:], 4, 2)]
+
+
+def spread_far(x, near, ctx_size):
+    if ctx_size != 4:
+        return []
+    half = x.shape[0] // 2
+    return [
+        hop(jnp.concatenate([x[:half], near[0]], axis=0), 4, 2),
+        hop(jnp.concatenate([x[half:], near[1]], axis=0), 4, 1),
+    ]
+
+
+def spread_parts(x, near, far, ctx_size):
+    return [x, *near] if ctx_size != 4 else [x, jnp.concatenate(near, axis=0), *far]
 
 
 def first_hops(parts, ctx_size):
@@ -663,6 +686,9 @@
     fold = seq_size // ctx_size
     seq_place = lax.axis_index("seq")
     fold_place = seq_place % fold
+    core = seq_place % 2
+    floor = seq_place // 2
+    floors = seq_size // 2
     mirror = [(i, ctx_size - 1 - i) for i in range(ctx_size)]
 
     def crossed(x, j):
@@ -696,68 +722,102 @@
     positions = (order[:2, None] * half + jnp.arange(half, dtype=jnp.int32)[None, :]).reshape(-1)
     cosine, sine = rotation_tables(jnp.tile(positions, sequences))
 
+    def from_floors(x):
+        came = [x] + [
+            lax.ppermute(x, "seq", [(i, (i + 2 * step) % seq_size) for i in range(seq_size)])
+            for step in range(1, floors)
+        ]
+        return jnp.concatenate(
+            [
+                pick(floor, [came[(mine - theirs) % floors] for mine in range(floors)])
+                for theirs in range(floors)
+            ],
+            axis=0,
+        )
+
+    def from_ranks(x):
+        return [x] + [hop(x, ctx_size, k) for k in range(1, ctx_size)]
+
+    def by_rank(came):
+        return [pick(place, [came[rank ^ p] for p in range(ctx_size)]) for rank in range(ctx_size)]
+
+    def from_other_core(x):
+        return lax.ppermute(x, "seq", [(i, i ^ 1) for i in range(seq_size)])
+
+    def by_core(x, other):
+        first, second = pick(core, [x, other]), pick(core, [other, x])
+        shape = (floors, x.shape[0] // floors, x.shape[1])
+        return jnp.stack([first.reshape(shape), second.reshape(shape)], axis=1).reshape(
+            2 * x.shape[0], x.shape[1]
+        )
+
+    gate_up = lax.all_gather(jnp.stack([gate_weight, up_weight]), "seq", axis=0)
     gain_width = attention_gain.shape[0]
-    bias_width = project_bias.shape[0]
-    depth_mine, own_width = project_weight.shape
+    own_width = project_weight.shape[1]
     vectors = jnp.concatenate([attention_gain, project_bias, feedforward_gain])
-    both = jnp.concatenate([project_weight, output_weight], axis=1)
-    spare = -vectors.shape[0] % both.shape[1]
-    payload = jnp.concatenate(
-        [both, jnp.pad(vectors, (0, spare)).reshape(-1, both.shape[1])], axis=0
-    )
-    pieces = [payload] + [hop(payload, ctx_size, k) for k in range(1, ctx_size)]
-    ordered = [
-        pick(place, [pieces[rank ^ p] for p in range(ctx_size)]) for rank in range(ctx_size)
-    ]
-    both_columns = jnp.concatenate(
-        [piece[:depth_mine, :own_width] for piece in ordered]
-        + [piece[:depth_mine, own_width:] for piece in ordered],
-        axis=1,
-    )
-    vectors_all = [piece[depth_mine:].reshape(-1).astype(f32) for piece in ordered]
+    spare = -vectors.shape[0] % own_width
+    project_rows = from_floors(project_weight)
+    held = project_rows.shape[0]
+    tokens_mine = zigzag(tokens).reshape(rows, width)
+    project_rows, tokens_mine = lax.optimization_barrier((project_rows, tokens_mine))
+    project_came = from_ranks(
+        jnp.concatenate(
+            [project_rows, jnp.pad(vectors, (0, spare)).reshape(-1, own_width)], axis=0
+        )
+    )
+    output_late = lax.optimization_barrier((output_weight, project_rows))[0]
+    output_rows = from_floors(output_late)
+    ordered = by_rank(project_came)
+    vectors_all = [piece[held:].reshape(-1).astype(f32) for piece in ordered]
 
     def vector_whole(start, size):
         return jnp.concatenate([v[start : start + size] for v in vectors_all])[None, :]
 
     attention_full = vector_whole(0, gain_width)
-    bias_full = vector_whole(gain_width, bias_width)
-    feedforward_full = vector_whole(gain_width + bias_width, gain_width)
-    both_full = lax.all_gather(both_columns, "seq", axis=0, tiled=True)
-    output_full = both_full[:, Q_WIDTH + 2 * K_WIDTH :]
-
-    tokens_late, down_late = lax.optimization_barrier((tokens, down_weight, both_columns))[:2]
+    bias_full = vector_whole(gain_width, own_width)
+    feedforward_full = vector_whole(gain_width + own_width, gain_width)
+    project_columns = jnp.concatenate([piece[:held] for piece in ordered], axis=1)
+    project_full = by_core(project_columns, from_other_core(project_columns))
+
+    down_late, grad_late = lax.optimization_barrier((down_weight, cotangent, project_columns))[:2]
+    grad_low = zigzag(grad_late).reshape(rows, width)
+    grad_near = spread_near(grad_low, ctx_size)
     down_rows, down_columns = down_weight.shape
     depth = down_columns // fold
     down_turned = jnp.concatenate(
         crossed_parts(list(down_late.T.reshape(fold, depth, down_rows))), axis=1
     )
-    weights_mine = lax.all_gather(
-        jnp.stack([gate_weight, up_weight, down_turned]), "seq", axis=0
-    )
-
-    tokens_mine = zigzag(tokens_late).reshape(rows, width)
     normed, queries, pairs_mine = project_forward(
-        tokens_mine, attention_full, both_full, bias_full, cosine, sine
-    )
+        tokens_mine, attention_full, project_full, bias_full, cosine, sine
+    )
+    down_turned, gate_up = lax.optimization_barrier((down_turned, gate_up, queries))[:2]
+    down_mine = lax.all_gather(down_turned, "seq", axis=0)
     queries = queries.reshape(sequences * 2, half, Q_WIDTH)
     pairs_mine = pairs_mine.reshape(sequences, 2, half, 2 * K_WIDTH)
     pair_parts = [pairs_mine] + [hop(pairs_mine, ctx_size, k) for k in range(1, ctx_size)]
-    cotangent_late = lax.optimization_barrier((cotangent, pair_parts[-1]))[0]
-    grad_low = zigzag(cotangent_late).reshape(rows, width)
-    grad_parts = spread(grad_low, ctx_size)
+    grad_near, output_rows = lax.optimization_barrier((grad_near, output_rows, pair_parts))[:2]
+    grad_far = spread_far(grad_low, grad_near, ctx_size)
+    output_came = from_ranks(output_rows)
+    queries = lax.optimization_barrier((queries, down_turned))[0]
     mixed, row_stats = attend_forward(order, queries, pair_parts)
+    mixed, grad_far, output_came = lax.optimization_barrier((mixed, grad_far, output_came))
+    grad_parts = spread_parts(grad_low, grad_near, grad_far, ctx_size)
+    output_columns = jnp.concatenate(by_rank(output_came), axis=1)
+    output_full = by_core(output_columns, from_other_core(output_columns))
     mixed_rows = mixed.reshape(rows, Q_WIDTH)
     hidden = tokens_mine.astype(f32) + dot(mixed_rows, output_full, NN)
     inverse_ffn = inverse_rms(hidden)
     normed_ffn = (hidden * inverse_ffn * feedforward_full).astype(bf16)
 
-    normed_parts = spread(normed_ffn, ctx_size)
+    normed_near = spread_near(normed_ffn, ctx_size)
+    normed_far = spread_far(normed_ffn, normed_near, ctx_size)
+    normed_parts = spread_parts(normed_ffn, normed_near, normed_far, ctx_size)
     output_parts = []
     grad_normed_parts = []
     buffers = []
     for number, (part, grad_part) in enumerate(zip(normed_parts, grad_parts)):
         output_part, grad_normed_part, *buffers = ffn(
-            number, ctx_size, part, grad_part, weights_mine, buffers
+            number, ctx_size, part, grad_part, gate_up, down_mine, buffers
         )
         output_parts.append(output_part)
         grad_normed_parts.append(grad_normed_part)
@@ -781,8 +841,8 @@
     hidden_low = grad_hidden.astype(bf16)
     grad_mixed = dot(hidden_low, output_full, NT).astype(bf16)
 
-    output_late = lax.optimization_barrier((output_parts, grad_mixed))[0]
-    output_got = first_hops(output_late, ctx_size)
+    output_parts = lax.optimization_barrier((output_parts, grad_mixed))[0]
+    output_got = first_hops(output_parts, ctx_size)
 
     grad_queries, pair_grads = attend_backward(
         order,
@@ -800,10 +860,14 @@
         pair_sums.append(
             hop(pair_grads[:, 2 * k : 2 * k + 2], ctx_size, k).reshape(rows, 2 * K_WIDTH)
         )
+    hidden_late = lax.optimization_barrier((hidden_low, pair_grads))[0]
+    output_pieces = weight_pieces(core, ctx_size, seq_size, mixed_rows, hidden_late)
+    output_got = lax.optimization_barrier((output_got, pair_sums))[0]
+    output_sum = gathered_sum(output_parts, output_got, ctx_size)
     grad_queries = grad_queries.reshape(rows, Q_WIDTH)
     grad_pairs, tokens_grad, gain_sum, bias_sum = project_backward(
         grad_queries,
-        both_full,
+        project_full,
         tokens_mine,
         attention_full,
         grad_hidden,
@@ -812,24 +876,20 @@
         pair_sums,
     )
 
-    def owners_sum(parts):
-        _, owners, deep, own = parts.shape
-        parts = parts.reshape(ctx_size, owners // 2, 2, deep, own)
-        core = seq_place % 2
-        mine = pick(core, [parts[:, :, 0], parts[:, :, 1]])
-        other = pick(core, [parts[:, :, 1], parts[:, :, 0]])
-        swapped = lax.ppermute(other, "seq", [(i, i ^ 1) for i in range(seq_size)])
-        chip = (mine.astype(f32) + swapped.astype(f32)).astype(bf16)
-
+    def core_sum(mine, other):
+        return (mine.astype(f32) + from_other_core(other).astype(f32)).astype(bf16)
+
+    def ctx_sum(parts):
         def part(k):
-            return lax.dynamic_index_in_dim(chip, place ^ k, 0, keepdims=False)
+            return lax.dynamic_index_in_dim(parts, place ^ k, 0, keepdims=False)
 
         total = part(0).astype(f32)
         for k in range(1, ctx_size):
             total = total + hop(part(k), ctx_size, k).astype(f32)
-        column = total.astype(bf16)
-        floor = seq_place // 2
-        floors = seq_size // 2
+        return total
+
+    def floor_sum(column):
+        column = column.astype(bf16).reshape(floors, -1, column.shape[1])
         total = lax.dynamic_index_in_dim(column, floor, 0, keepdims=False).astype(f32)
         for step in range(1, floors):
             sent = lax.dynamic_index_in_dim(column, (floor + step) % floors, 0, keepdims=False)
@@ -838,10 +898,40 @@
             ).astype(f32)
         return total
 
-    output_out = owners_sum(weight_pieces(ctx_size, seq_size, mixed_rows, hidden_low))
-    project_out = owners_sum(
-        weight_pieces(ctx_size, seq_size, normed, grad_queries, grad_pairs)
-    )
+    def by_owner(parts):
+        return parts.reshape(ctx_size, -1, parts.shape[-1])
+
+    output_chip = by_owner(core_sum(*output_pieces))
+    output_chip = lax.optimization_barrier((output_chip, pair_sums))[0]
+    output_total = ctx_sum(output_chip)
+
+    project_pieces = weight_pieces(core, ctx_size, seq_size, normed, grad_queries, grad_pairs)
+    sums = jnp.concatenate(
+        [
+            gain_sum.reshape(ctx_size, gain_width),
+            bias_sum.reshape(ctx_size, own_width),
+            grad_ffn_gain.reshape(ctx_size, gain_width),
+        ],
+        axis=1,
+    )
+    sums = jnp.pad(sums, ((0, 0), (0, spare))).reshape(ctx_size, -1, own_width).astype(bf16)
+    project_chip = by_owner(core_sum(*project_pieces))
+    project_chip, output_total, output_sum = lax.optimization_barrier(
+        (project_chip, output_total, output_sum)
+    )
+    output_out = floor_sum(output_total)
+    down_late = lax.optimization_barrier((weight_grads[2], project_pieces))[0]
+    down_late = down_late.reshape(depth, fold, down_rows)
+    down_came = crossed_parts([down_late[:, t] for t in range(fold)])
+    project_total = ctx_sum(jnp.concatenate([project_chip, sums], axis=1))
+    project_out = floor_sum(project_total[:held])
+    vector_sum = project_total[held:].reshape(-1)
+    mask = 1
+    while mask < seq_size:
+        vector_sum = vector_sum + lax.ppermute(
+            vector_sum, "seq", [(i, i ^ mask) for i in range(seq_size)]
+        )
+        mask *= 2
 
     tokens_grad = tokens_grad.reshape(tokens.shape)
     tokens_gradient = jnp.concatenate(
@@ -851,45 +941,19 @@
         ],
         axis=1,
     )
-    output_zigzag = hidden + gathered_sum(output_late, output_got, ctx_size)
+    output_zigzag = hidden + output_sum
     layer_output = zigzag(output_zigzag.astype(bf16).reshape(tokens.shape))
 
-    down_grads = weight_grads[2].reshape(depth, fold, down_rows)
-    down_out = jnp.concatenate(
-        crossed_parts([down_grads[:, t] for t in range(fold)]), axis=0
-    ).T
-
-    sums = jnp.concatenate(
-        [
-            gain_sum.reshape(ctx_size, gain_width),
-            bias_sum.reshape(ctx_size, bias_width),
-            grad_ffn_gain.reshape(ctx_size, gain_width),
-        ],
-        axis=1,
-    )
-
-    def sums_for(k):
-        return lax.dynamic_index_in_dim(sums, place ^ k, 0)
-
-    vector_sum = sums_for(0)
-    for k in range(1, ctx_size):
-        vector_sum = vector_sum + hop(sums_for(k), ctx_size, k)
-    mask = 1
-    while mask < seq_size:
-        vector_sum = vector_sum + lax.ppermute(
-            vector_sum, "seq", [(i, i ^ mask) for i in range(seq_size)]
-        )
-        mask *= 2
-    vector_sum = vector_sum[0]
+    down_out = jnp.concatenate(down_came, axis=0).T
 
     return (
         layer_output,
         tokens_gradient,
         vector_sum[:gain_width],
         project_out,
-        vector_sum[gain_width : gain_width + bias_width],
+        vector_sum[gain_width : gain_width + own_width],
         output_out,
-        vector_sum[gain_width + bias_width :],
+        vector_sum[gain_width + own_width : vectors.shape[0]],
         weight_grads[0].astype(f32),
         weight_grads[1].astype(f32),
         down_out.astype(f32),

time: 458 us -> 437 us (0.954)
  waiting for transfers between devices: 149 us -> 82.5 us
  starting transfers between devices: 57.5 us -> 87.3 us
  other arithmetic: 40.1 us -> 48.5 us
  local copies, waits for them, and re-layouts: 22.4 us -> 30.3 us
    ppermute x34, waiting for transfers between devices: 78.8 us -> 40.1 us  [hop(): return lax.ppermute(x, 'ctx', [(i, i ^ mask) for i in range(ctx_size)])]
    ppermute x4, waiting for transfers between devices: 51.7 us -> 18.4 us  [crossed(): lax.ppermute(x, ('seq', 'ctx'), [((c * fold + r) * ctx_size + q, (q * fol...]
    ppermute x8 -> x16, starting transfers between devices: 6.17 us -> 22.9 us  [the longest x6 13.9 us: floor_sum(): lax.ppermute(sent, 'seq', [(i, (i + 2 * step) % seq_size) for i in range(...]
    ppermute x8 -> x16, waiting for transfers between devices: 0.02 us -> 10.2 us  [the longest x6 7.99 us: from_floors(): lax.ppermute(x, 'seq', [(i, (i + 2 * step) % seq_size) for i in range(seq...]
    ppermute x3, waiting for transfers between devices: 18.5 us -> 9.89 us  [zigzag(): lax.ppermute(x[:, half:], 'ctx', mirror)]
    ppermute x34, starting transfers between devices: 37.2 us -> 42.1 us  [hop(): return lax.ppermute(x, 'ctx', [(i, i ^ mask) for i in range(ctx_size)])]
  transfers between devices with their start and end apart: 56 -> 64, of which waited for: 27 -> 24; matrix products, arithmetic and copies ran while one was open for 14% -> 18% of each run, Pallas kernels for 36% -> 38%
where the time goes in v4:
time: 437 us; the launch traced here: 429 us
  Pallas kernels  162 us (37%)
  starting transfers between devices  87.3 us (20%)
  waiting for transfers between devices  82.5 us (19%)
  other arithmetic  48.5 us (11%)
  local copies, waits for them, and re-layouts  30.3 us (7%)
  between operations  15.1 us (3%)
    pallas_call x4, Pallas kernels, ffn(): pl.pallas_call(ffn_kernel, grid=(2,), in_specs=[row_spec(tile, width), ro...  55.5 us
    ppermute x34, starting transfers between devices, hop(): return lax.ppermute(x, 'ctx', [(i, i ^ mask) for i in range(ctx_size)])  42.1 us
    ppermute x34, waiting for transfers between devices, hop(): return lax.ppermute(x, 'ctx', [(i, i ^ mask) for i in range(ctx_size)])  40.1 us
    pallas_call x1, Pallas kernels, attend_backward(): pl.pallas_call(backward_kernel, grid_spec=pltpu.PrefetchScalarGridSpec(nu...  36.1 us
    pallas_call x1, Pallas kernels, attend_forward(): pl.pallas_call(forward_kernel, grid_spec=pltpu.PrefetchScalarGridSpec(num...  27.3 us
    pallas_call x1, Pallas kernels, ffn_weights(): pl.pallas_call(ffn_weights_kernel, grid=(count,), in_specs=[slot(width)]...  22.5 us
    ppermute x4, waiting for transfers between devices, crossed(): lax.ppermute(x, ('seq', 'ctx'), [((c * fold + r) * ctx_size + q, (q * fol...  18.4 us
    ppermute x6, starting transfers between devices, floor_sum(): lax.ppermute(sent, 'seq', [(i, (i + 2 * step) % seq_size) for i in range(...  13.9 us
  transfers between devices with their start and end apart: 64, of which 24 were waited for; matrix products, arithmetic and copies ran while one was open for 18% of the time, Pallas kernels for 38%

profile of v4, /device:TPU:2, one launch (start us, length us, event | category | flops | bytes accessed | tf_op | source)
XLA Modules:
  0.0 428.8 jit_solution(6749762596390359004)
XLA Ops:
  7.2 2.0 pad_maximum_fusion.13
  10.3 2.7 collective-permute-start.1
  20.8 6.7 %collective-permute-done.3 = bf16[1,256,896]{2,1,0:T(8,128)(2,1)S(1)} collective-permute-done((bf16[1,256,896]{2,1,0:T(8,128)(2,1)S(1)}, bf16[1,256,896]{2,1,0:T(8,128)(2,1)S(1)}, u32[]{:S(2)}, u32[]{:S(2)}) %collective-permute-start.3) | collective-permute-done | bytes 458784 | tf_op jit(solution)/shard_map/ppermute | solution.py:716
  33.3 2.6 collective-permute-start.18
  40.0 4.6 %collective-permute-done.16 = bf16[112,224]{1,0:T(8,128)(2,1)S(1)} collective-permute-done((bf16[112,224]{1,0:T(8,128)(2,1)S(1)}, bf16[112,224]{1,0:T(8,128)(2,1)S(1)}, u32[]{:S(2)}, u32[]{:S(2)}) %collective-permute-start.16) | collective-permute-done | bytes 50208 | tf_op jit(solution)/shard_map/ppermute | solution.py:727
  48.5 2.2 concatenate.94
  58.5 5.0 %collective-permute-start.8 = (bf16[112,608]{1,0:T(8,128)(2,1)}, bf16[112,608]{1,0:T(8,128)(2,1)S(1)}, u32[]{:S(2)}, u32[]{:S(2)}) collective-permute-start(bf16[112,608]{1,0:T(8,128)(2,1)} %get-tuple-element.236), channel_id=1, source_target_pairs={{0,0},{1,8},{2,16},{3,24},{4,4},{5,12},{6,20},{7,28},{8,1},{9,9},{... | collective-permute-start | bytes 408584 | tf_op jit(solution)/shard_map/ppermute | solution.py:695
  63.6 3.2 collective-permute-done.14
  66.8 5.0 %collective-permute-start.15 = (bf16[256,896]{1,0:T(8,128)(2,1)S(1)}, bf16[256,896]{1,0:T(8,128)(2,1)S(1)}, u32[]{:S(2)}, u32[]{:S(2)}) collective-permute-start(bf16[256,896]{1,0:T(8,128)(2,1)S(1)} %bitcast.120), channel_id=1, source_target_pairs={{0,2},{1,3},{2,0},{3,1},{4,6},{5,7},{6,4},{7,5},{8,10},{9,11},{10,... | collective-permute-start | bytes 1376264 | tf_op jit(solution)/shard_map/ppermute | solution.py:612
  75.0 4.9 %project_forward.1 = (bf16[512,896]{1,0:T(8,128)(2,1)}, bf16[512,896]{1,0:T(8,128)(2,1)}, bf16[512,256]{1,0:T(8,128)(2,1)}) custom-call(bf16[512,896]{1,0:T(8,128)(2,1)} %maximum_bitcast_fusion.x_ref, f32[1,896]{1,0:T(1,128)} %broadcast_in_dim.6.gain_ref, bf16[896,1152]{1,0:T(8,128)(2,1)} %bitcast.128, f32[1,1152]{1,0:T(1,128)} %broadcast_in_dim.7.bias_ref, ...), custom_call_target="tpu_custom_call" | custom-call | flops 2113929216 | bytes 5242880 | tf_op jit(solution)/shard_map/project_forward/pallas_call | solution.py:101
  80.8 3.1 collective-permute-done.9
  84.9 4.5 %collective-permute-done.13 = bf16[256,896]{1,0:T(8,128)(2,1)S(1)} collective-permute-done((bf16[256,896]{1,0:T(8,128)(2,1)S(1)}, bf16[256,896]{1,0:T(8,128)(2,1)S(1)}, u32[]{:S(2)}, u32[]{:S(2)}) %collective-permute-start.13) | collective-permute-done | bytes 458784 | tf_op jit(solution)/shard_map/ppermute | solution.py:612
  89.3 5.6 %collective-permute-done.10.rest_1_ = bf16[1,2,256,256]{3,2,1,0:T(8,128)(2,1)S(1)} collective-permute-done((bf16[1,2,256,256]{3,2,1,0:T(8,128)(2,1)}, bf16[1,2,256,256]{3,2,1,0:T(8,128)(2,1)S(1)}, u32[]{:S(2)}, u32[]{:S(2)}) %collective-permute-start.10) | collective-permute-done | bytes 262176 | tf_op jit(solution)/shard_map/ppermute | solution.py:612
  96.8 6.6 %collective-permute-start.19 = (bf16[512,896]{1,0:T(8,128)(2,1)}, bf16[512,896]{1,0:T(8,128)(2,1)S(1)}, u32[]{:S(2)}, u32[]{:S(2)}) collective-permute-start(bf16[512,896]{1,0:T(8,128)(2,1)} %get-tuple-element.217), channel_id=1, source_target_pairs={{0,2},{1,3},{2,0},{3,1},{4,6},{5,7},{6,4},{7,5},{8,10},{9,11},{10,... | collective-permute-start | bytes 2752520 | tf_op jit(solution)/shard_map/ppermute | solution.py:612
  104.3 2.0 collective-permute-start.21
  108.1 27.3 %attend_forward.1 = (bf16[2,256,896]{2,1,0:T(8,128)(2,1)}, f32[2,16,256]{2,1,0:T(8,128)}) custom-call(s32[8]{0:T(128)} %stack.52.order_ref, bf16[2,256,896]{2,1,0:T(8,128)(2,1)} %bitcast.152, bf16[1,2,256,256]{3,2,1,0:T(8,128)(2,1)} %bitcast.148, bf16[1,2,256,256]{3,2,1,0:T(8,128)(2,1)} %copy-done.37, bf16[1,2,256,256]{3,2,1,0:T(8,128)(2,1)} %copy-done.38, ...), custom_call_target="tpu_custom_call" | custom-call | flops 9395240960 | bytes 4194304 | tf_op jit(solution)/shard_map/attend_forward/pallas_call | solution.py:442
  137.4 2.2 collective-permute-done.24
  147.1 9.5 %collective-permute-done.25 = bf16[256,896]{1,0:T(8,128)(2,1)S(1)} collective-permute-done((bf16[256,896]{1,0:T(8,128)(2,1)S(1)}, bf16[256,896]{1,0:T(8,128)(2,1)S(1)}, u32[]{:S(2)}, u32[]{:S(2)}) %collective-permute-start.25) | collective-permute-done | bytes 458784 | tf_op jit(solution)/shard_map/ppermute | solution.py:612
  161.9 13.8 %ffn.4 = (bf16[512,896]{1,0:T(8,128)(2,1)}, bf16[512,896]{1,0:T(8,128)(2,1)}, bf16[4,512,896]{2,1,0:T(8,128)(2,1)}, bf16[4,512,896]{2,1,0:T(8,128)(2,1)}, bf16[4...) custom-call(bf16[512,896]{1,0:T(8,128)(2,1)} %copy-done.1, ...), custom_call_target="tpu_custom_call" | custom-call | flops 7809794048 | bytes 16777216 | tf_op jit(solution)/shard_map/ffn/pallas_call | solution.py:546
  175.7 14.2 %ffn.5 = (bf16[512,896]{1,0:T(8,128)(2,1)}, bf16[512,896]{1,0:T(8,128)(2,1)}, bf16[4,512,896]{2,1,0:T(8,128)(2,1)}, bf16[4,512,896]{2,1,0:T(8,128)(2,1)}, bf16[4...) custom-call(bf16[512,896]{1,0:T(8,128)(2,1)} %get-tuple-element.219., ...), custom_call_target="tpu_custom_call", output_to_operand_aliasing={{2}: (4, {}), {3}: (5, {}), {4}: (6, {}), {5}: (7, {}), {6}... | custom-call | flops 7809794048 | bytes 16777216 | tf_op jit(solution)/shard_map/ffn/pallas_call | solution.py:546
  189.9 13.8 %ffn.6 = (bf16[512,896]{1,0:T(8,128)(2,1)}, bf16[512,896]{1,0:T(8,128)(2,1)}, bf16[4,512,896]{2,1,0:T(8,128)(2,1)}, bf16[4,512,896]{2,1,0:T(8,128)(2,1)}, bf16[4...) custom-call(bf16[512,896]{1,0:T(8,128)(2,1)} %collective-permute-don, ...), custom_call_target="tpu_custom_call", output_to_operand_aliasing={{2}: (4, {}), {3}: (5, {}), {4}: (6, {}), {5}: (7, {}), {6}... | custom-call | flops 7809794048 | bytes 16777216 | tf_op jit(solution)/shard_map/ffn/pallas_call | solution.py:546
  204.1 13.7 %ffn.7 = (bf16[512,896]{1,0:T(8,128)(2,1)}, bf16[512,896]{1,0:T(8,128)(2,1)}, bf16[4,512,896]{2,1,0:T(8,128)(2,1)}, bf16[4,512,896]{2,1,0:T(8,128)(2,1)}, bf16[4...) custom-call(bf16[512,896]{1,0:T(8,128)(2,1)} %collective-permute-don, ...), custom_call_target="tpu_custom_call", output_to_operand_aliasing={{2}: (4, {}), {3}: (5, {}), {4}: (6, {}), {5}: (7, {}), {6}... | custom-call | flops 7809794048 | bytes 16777216 | tf_op jit(solution)/shard_map/ffn/pallas_call | solution.py:546
  218.9 22.5 %ffn_weights.1 = bf16[8,3,112,1216]{3,2,1,0:T(8,128)(2,1)} custom-call(bf16[4,512,896]{2,1,0:T(8,128)(2,1)} %get-tuple-element.127.x_ref, bf16[4,512,896]{2,1,0:T(8,128)(2,1)} %get-tuple-element.128.c_ref, bf16[4,512,1216]{2,1,0:T(8,128)(2,1)} %get-tuple-element.129.active_ref, bf16[4,512,1216]{2,1,0:T(8,128)(2,1)} %get-tuple-element.130.gate_ref, ...), custom_call_target="tpu_custom_call" | custom-call | flops 13388218368 | bytes 31457280 | tf_op jit(solution)/shard_map/ffn_weights/pallas_call | solution.py:596
  248.2 5.4 %collective-permute-done.31 = bf16[256,896]{1,0:T(8,128)(2,1)S(1)} collective-permute-done((bf16[256,896]{1,0:T(8,128)(2,1)S(1)}, bf16[256,896]{1,0:T(8,128)(2,1)S(1)}, u32[]{:S(2)}, u32[]{:S(2)}) %collective-permute-start.31) | collective-permute-done | bytes 458784 | tf_op jit(solution)/shard_map/ppermute | solution.py:612
  256.5 1.9 fusion.30
  258.4 2.2 convolution_convert_fusion
  262.5 36.1 %attend_backward.1 = (bf16[2,256,896]{2,1,0:T(8,128)(2,1)}, bf16[1,8,256,256]{3,2,1,0:T(8,128)(2,1)}) custom-call(s32[8]{0:T(128)} %stack.52.order_ref, bf16[2,256,896]{2,1,0:T(8,128)(2,1)} %bitcast.153, bf16[2,256,896]{2,1,0:T(8,128)(2,1)} %get-tuple-element.102.o_ref, bf16[2,256,896]{2,1,0:T(8,128)(2,1)} %bitcast.156, ...), custom_call_target="tpu_custom_call" | custom-call | flops 23488102400 | bytes 8388608 | tf_op jit(solution)/shard_map/attend_backward/pallas_call | solution.py:474
  298.7 2.3 fusion.31
  304.5 4.1 weight_pieces.3
  308.7 3.6 collective-permute-done.36
  312.3 6.5 %project_backward.1 = (bf16[512,256]{1,0:T(8,128)(2,1)}, f32[512,896]{1,0:T(8,128)}, f32[1,896]{1,0:T(1,128)}, f32[1,1152]{1,0:T(1,128)}) custom-call(bf16[512,896]{1,0:T(8,128)(2,1)} %bitcast.154, bf16[896,1152]{1,0:T(8,128)(2,1)} %bitcast.129, bf16[512,896]{1,0:T(8,128)(2,1)} %maximum_bitcast_fusion.x_ref, f32[1,896]{1,0:T(1,128)} %broadcast_in_dim.6.gain_ref, ...), custom_call_target="tpu_custom_call" | custom-call | flops 2113929216 | bytes 8388608 | tf_op jit(solution)/shard_map/project_backward/pallas_call | solution.py:161
  318.8 2.1 slice.314
  322.2 2.2 add_convert_fusion.4
  326.1 4.8 %weight_pieces.2 = (bf16[4,4,112,288]{3,2,1,0:T(8,128)(2,1)}, bf16[4,4,112,288]{3,2,1,0:T(8,128)(2,1)}) custom-call(s32[1]{0:T(128)} %bitcast.24.core_ref, bf16[512,896]{1,0:T(8,128)(2,1)} %get-tuple-element.107.lhs_ref, bf16[512,896]{1,0:T(8,128)(2,1)} %bitcast.155, bf16[512,256]{1,0:T(8,128)(2,1)} %get-tuple-element.147.rest_1_), custom_call_target="tpu_custom_call" | custom-call | flops 2113929216 | bytes 5242880 | tf_op jit(solution)/shard_map/weight_pieces/pallas_call | solution.py:215
  330.8 2.5 copy.88
  335.8 1.9 convert_add_fusion.2
  344.2 3.8 collective-permute-done.46
  350.4 2.3 collective-permute-done.42
  352.8 4.5 %collective-permute-done.41 = bf16[448,224]{1,0:T(8,128)(2,1)S(1)} collective-permute-done((bf16[448,224]{1,0:T(8,128)(2,1)S(1)}, bf16[448,224]{1,0:T(8,128)(2,1)S(1)}, u32[]{:S(2)}, u32[]{:S(2)}) %collective-permute-start.41) | collective-permute-done | bytes 200736 | tf_op jit(solution)/shard_map/ppermute | solution.py:612
  359.9 2.8 add_convert_fusion
  364.6 1.8 collective-permute-start.49
  370.5 3.9 collective-permute-start.57
  375.6 4.1 collective-permute-start.56
  383.8 3.8 collective-permute-start.51
  391.1 3.1 collective-permute-start.55
  396.4 2.2 slice_bitcast_fusion
  399.5 5.2 %collective-permute-start.59 = (bf16[112,608]{1,0:T(8,128)(2,1)S(1)}, bf16[112,608]{1,0:T(8,128)(2,1)S(1)}, u32[]{:S(2)}, u32[]{:S(2)}) collective-permute-start(bf16[112,608]{1,0:T(8,128)(2,1)S(1)} %get-tuple-element.214), channel_id=1, source_target_pairs={{0,0},{1,8},{2,16},{3,24},{4,4},{5,12},{6,20},{7,28},{8,1},{9,9},{... | collective-permute-start | bytes 408584 | tf_op jit(solution)/shard_map/ppermute | solution.py:695
  406.5 13.7 %collective-permute-done.59 = bf16[112,608]{1,0:T(8,128)(2,1)S(1)} collective-permute-done((bf16[112,608]{1,0:T(8,128)(2,1)S(1)}, bf16[112,608]{1,0:T(8,128)(2,1)S(1)}, u32[]{:S(2)}, u32[]{:S(2)}) %collective-permute-start.59) | collective-permute-done | bytes 136224 | tf_op jit(solution)/shard_map/ppermute | solution.py:695
  (297 shorter events, 109.1 us)
Async XLA Ops:
  7.2 100.6 %all-gather.5.cloned.1.call-start = ((), (), s32[]{:S(2)}) async-start(), calls=%async_computation.2 | async-start | bytes 5160960 | tf_op jit(solution)/shard_map/all_gather | solution.py:754
  9.2 152.7 %all-gather.7.cloned.1.call-start = ((), (), s32[]{:S(2)}) async-start(), calls=%async_computation.3 | async-start | bytes 2580480 | tf_op jit(solution)/shard_map/all_gather | solution.py:794
  15.1 12.4 %collective-permute-start.3 = (bf16[1,256,896]{2,1,0:T(8,128)(2,1)S(1)}, bf16[1,256,896]{2,1,0:T(8,128)(2,1)S(1)}, u32[]{:S(2)}, u32[]{:S(2)}) collective-permute-start(bf16[1,256,896]{2,1,0:T(8,128)(2,1)S(1)} %get-tuple-element.210), channel_id=1, source_target_pairs={{0,3},{1,2},{2,1},{3,0},{4,7},{5,6},{6,5},{7,4},{8,11},{9,10},{10,... | collective-permute-start | bytes 1376264 | tf_op jit(solution)/shard_map/ppermute | solution.py:716
  29.8 15.8 %collective-permute-start.5 = (bf16[451,288]{1,0:T(8,128)(2,1)S(1)}, bf16[451,288]{1,0:T(8,128)(2,1)S(1)}, u32[]{:S(2)}, u32[]{:S(2)}) collective-permute-start(bf16[451,288]{1,0:T(8,128)(2,1)S(1)} %constant_dynamic-update-slice_fusion), channel_id=1, source_target_pairs={{0,2},{1,3},{2,0},{3,1},{4,6},{5,7},{6,4},{7,5},{8,10},{9,11},{10,... | collective-permute-start | bytes 779336 | tf_op jit(solution)/shard_map/ppermute | solution.py:612
  31.4 14.3 %collective-permute-start.6 = (bf16[451,288]{1,0:T(8,128)(2,1)S(1)}, bf16[451,288]{1,0:T(8,128)(2,1)S(1)}, u32[]{:S(2)}, u32[]{:S(2)}) collective-permute-start(bf16[451,288]{1,0:T(8,128)(2,1)S(1)} %constant_dynamic-update-slice_fusion), channel_id=1, source_target_pairs={{0,3},{1,2},{2,1},{3,0},{4,7},{5,6},{6,5},{7,4},{8,11},{9,10},{10,... | collective-permute-start | bytes 779336 | tf_op jit(solution)/shard_map/ppermute | solution.py:612
  31.8 15.0 %collective-permute-start.4 = (bf16[451,288]{1,0:T(8,128)(2,1)S(1)}, bf16[451,288]{1,0:T(8,128)(2,1)S(1)}, u32[]{:S(2)}, u32[]{:S(2)}) collective-permute-start(bf16[451,288]{1,0:T(8,128)(2,1)S(1)} %constant_dynamic-update-slice_fusion), channel_id=1, source_target_pairs={{0,1},{1,0},{2,3},{3,2},{4,5},{5,4},{6,7},{7,6},{8,9},{9,8},{10,11... | collective-permute-start | bytes 779336 | tf_op jit(solution)/shard_map/ppermute | solution.py:612
  50.8 21.1 %collective-permute-start.7 = (bf16[448,1152]{1,0:T(8,128)(2,1)S(1)}, bf16[448,1152]{1,0:T(8,128)(2,1)}, u32[]{:S(2)}, u32[]{:S(2)}) collective-permute-start(bf16[448,1152]{1,0:T(8,128)(2,1)S(1)} %concatenate.94), channel_id=1, source_target_pairs={{0,4},{4,0},{8,12},{12,8},{16,20},{20,16},{24,28},{28,24},{1,5},{5... | collective-permute-start | bytes 3096584 | tf_op jit(solution)/shard_map/ppermute | solution.py:745
  53.0 13.9 %collective-permute-start.14 = (bf16[1,256,896]{2,1,0:T(8,128)(2,1)S(1)}, bf16[1,256,896]{2,1,0:T(8,128)(2,1)S(1)}, u32[]{:S(2)}, u32[]{:S(2)}) collective-permute-start(bf16[1,256,896]{2,1,0:T(8,128)(2,1)S(1)} %get-tuple-element.202), channel_id=1, source_target_pairs={{0,3},{1,2},{2,1},{3,0},{4,7},{5,6},{6,5},{7,4},{8,11},{9,10},{10,... | collective-permute-start | bytes 1376264 | tf_op jit(solution)/shard_map/ppermute | solution.py:716
  58.5 22.3 %collective-permute-start.8 = (bf16[112,608]{1,0:T(8,128)(2,1)}, bf16[112,608]{1,0:T(8,128)(2,1)S(1)}, u32[]{:S(2)}, u32[]{:S(2)}) collective-permute-start(bf16[112,608]{1,0:T(8,128)(2,1)} %get-tuple-element.236), channel_id=1, source_target_pairs={{0,0},{1,8},{2,16},{3,24},{4,4},{5,12},{6,20},{7,28},{8,1},{9,9},{... | collective-permute-start | bytes 408584 | tf_op jit(solution)/shard_map/ppermute | solution.py:695
  63.5 20.4 %collective-permute-start.9 = (bf16[112,608]{1,0:T(8,128)(2,1)}, bf16[112,608]{1,0:T(8,128)(2,1)}, u32[]{:S(2)}, u32[]{:S(2)}) collective-permute-start(bf16[112,608]{1,0:T(8,128)(2,1)} %get-tuple-element.237), channel_id=1, source_target_pairs={{0,4},{1,12},{2,20},{3,28},{4,0},{5,8},{6,16},{7,24},{8,5},{9,13},... | collective-permute-start | bytes 408584 | tf_op jit(solution)/shard_map/ppermute | solution.py:695
  63.5 25.8 %collective-permute-start.13 = (bf16[256,896]{1,0:T(8,128)(2,1)S(1)}, bf16[256,896]{1,0:T(8,128)(2,1)S(1)}, u32[]{:S(2)}, u32[]{:S(2)}) collective-permute-start(bf16[256,896]{1,0:T(8,128)(2,1)S(1)} %get-tuple-element.201), channel_id=1, source_target_pairs={{0,1},{1,0},{2,3},{3,2},{4,5},{5,4},{6,7},{7,6},{8,9},{9,8},{10,11... | collective-permute-start | bytes 1376264 | tf_op jit(solution)/shard_map/ppermute | solution.py:612
  66.8 22.5 %collective-permute-start.15 = (bf16[256,896]{1,0:T(8,128)(2,1)S(1)}, bf16[256,896]{1,0:T(8,128)(2,1)S(1)}, u32[]{:S(2)}, u32[]{:S(2)}) collective-permute-start(bf16[256,896]{1,0:T(8,128)(2,1)S(1)} %bitcast.120), channel_id=1, source_target_pairs={{0,2},{1,3},{2,0},{3,1},{4,6},{5,7},{6,4},{7,5},{8,10},{9,11},{10,... | collective-permute-start | bytes 1376264 | tf_op jit(solution)/shard_map/ppermute | solution.py:612
  79.8 15.1 %collective-permute-start.10 = (bf16[1,2,256,256]{3,2,1,0:T(8,128)(2,1)}, bf16[1,2,256,256]{3,2,1,0:T(8,128)(2,1)S(1)}, u32[]{:S(2)}, u32[]{:S(2)}) collective-permute-start(bf16[1,2,256,256]{3,2,1,0:T(8,128)(2,1)} %bitcast.145), channel_id=1, source_target_pairs={{0,1},{1,0},{2,3},{3,2},{4,5},{5,4},{6,7},{7,6},{8,9},{9,8},{10,11... | collective-permute-start | bytes 786440 | tf_op jit(solution)/shard_map/ppermute | solution.py:612
  80.8 14.2 %collective-permute-start.11 = (bf16[1,2,256,256]{3,2,1,0:T(8,128)(2,1)}, bf16[1,2,256,256]{3,2,1,0:T(8,128)(2,1)S(1)}, u32[]{:S(2)}, u32[]{:S(2)}) collective-permute-start(bf16[1,2,256,256]{3,2,1,0:T(8,128)(2,1)} %bitcast.146), channel_id=1, source_target_pairs={{0,2},{1,3},{2,0},{3,1},{4,6},{5,7},{6,4},{7,5},{8,10},{9,11},{10,... | collective-permute-start | bytes 786440 | tf_op jit(solution)/shard_map/ppermute | solution.py:612
  83.9 11.1 %collective-permute-start.12 = (bf16[1,2,256,256]{3,2,1,0:T(8,128)(2,1)}, bf16[1,2,256,256]{3,2,1,0:T(8,128)(2,1)S(1)}, u32[]{:S(2)}, u32[]{:S(2)}) collective-permute-start(bf16[1,2,256,256]{3,2,1,0:T(8,128)(2,1)} %bitcast.147), channel_id=1, source_target_pairs={{0,3},{1,2},{2,1},{3,0},{4,7},{5,6},{6,5},{7,4},{8,11},{9,10},{10,... | collective-permute-start | bytes 786440 | tf_op jit(solution)/shard_map/ppermute | solution.py:612
  96.8 38.6 %collective-permute-start.19 = (bf16[512,896]{1,0:T(8,128)(2,1)}, bf16[512,896]{1,0:T(8,128)(2,1)S(1)}, u32[]{:S(2)}, u32[]{:S(2)}) collective-permute-start(bf16[512,896]{1,0:T(8,128)(2,1)} %get-tuple-element.217), channel_id=1, source_target_pairs={{0,2},{1,3},{2,0},{3,1},{4,6},{5,7},{6,4},{7,5},{8,10},{9,11},{10,... | collective-permute-start | bytes 2752520 | tf_op jit(solution)/shard_map/ppermute | solution.py:612
  103.5 32.0 %collective-permute-start.20 = (bf16[512,896]{1,0:T(8,128)(2,1)}, bf16[512,896]{1,0:T(8,128)(2,1)S(1)}, u32[]{:S(2)}, u32[]{:S(2)}) collective-permute-start(bf16[512,896]{1,0:T(8,128)(2,1)} %get-tuple-element.218), channel_id=1, source_target_pairs={{0,1},{1,0},{2,3},{3,2},{4,5},{5,4},{6,7},{7,6},{8,9},{9,8},{10,11... | collective-permute-start | bytes 2752520 | tf_op jit(solution)/shard_map/ppermute | solution.py:612
  104.3 31.1 %collective-permute-start.21 = (bf16[448,224]{1,0:T(8,128)(2,1)S(1)}, bf16[448,224]{1,0:T(8,128)(2,1)S(1)}, u32[]{:S(2)}, u32[]{:S(2)}) collective-permute-start(bf16[448,224]{1,0:T(8,128)(2,1)S(1)} %pad_maximum_fusion.20), channel_id=1, source_target_pairs={{0,1},{1,0},{2,3},{3,2},{4,5},{5,4},{6,7},{7,6},{8,9},{9,8},{10,11... | collective-permute-start | bytes 602120 | tf_op jit(solution)/shard_map/ppermute | solution.py:612
  106.3 29.1 %collective-permute-start.22 = (bf16[448,224]{1,0:T(8,128)(2,1)S(1)}, bf16[448,224]{1,0:T(8,128)(2,1)S(1)}, u32[]{:S(2)}, u32[]{:S(2)}) collective-permute-start(bf16[448,224]{1,0:T(8,128)(2,1)S(1)} %pad_maximum_fusion.20), channel_id=1, source_target_pairs={{0,2},{1,3},{2,0},{3,1},{4,6},{5,7},{6,4},{7,5},{8,10},{9,11},{10,... | collective-permute-start | bytes 602120 | tf_op jit(solution)/shard_map/ppermute | solution.py:612
  106.4 29.0 %collective-permute-start.23 = (bf16[448,224]{1,0:T(8,128)(2,1)S(1)}, bf16[448,224]{1,0:T(8,128)(2,1)}, u32[]{:S(2)}, u32[]{:S(2)}) collective-permute-start(bf16[448,224]{1,0:T(8,128)(2,1)S(1)} %pad_maximum_fusion.20), channel_id=1, source_target_pairs={{0,3},{1,2},{2,1},{3,0},{4,7},{5,6},{6,5},{7,4},{8,11},{9,10},{10,... | collective-permute-start | bytes 602120 | tf_op jit(solution)/shard_map/ppermute | solution.py:612
  107.8 288.6 %reduce-scatter.2.cloned.1.call-start = ((), (), s32[]{:S(2)}) async-start(), calls=%async_computation.1 | async-start | bytes 7741440 | tf_op jit(solution)/shard_map/reduce_scatter | solution.py:828
  143.9 12.6 %collective-permute-start.25 = (bf16[256,896]{1,0:T(8,128)(2,1)S(1)}, bf16[256,896]{1,0:T(8,128)(2,1)S(1)}, u32[]{:S(2)}, u32[]{:S(2)}) collective-permute-start(bf16[256,896]{1,0:T(8,128)(2,1)S(1)} %get-tuple-element.204), channel_id=1, source_target_pairs={{0,2},{1,3},{2,0},{3,1},{4,6},{5,7},{6,4},{7,5},{8,10},{9,11},{10,... | collective-permute-start | bytes 1376264 | tf_op jit(solution)/shard_map/ppermute | solution.py:612
  145.3 12.3 %collective-permute-start.27 = (bf16[256,896]{1,0:T(8,128)(2,1)S(1)}, bf16[256,896]{1,0:T(8,128)(2,1)S(1)}, u32[]{:S(2)}, u32[]{:S(2)}) collective-permute-start(bf16[256,896]{1,0:T(8,128)(2,1)S(1)} %get-tuple-element.203), channel_id=1, source_target_pairs={{0,1},{1,0},{2,3},{3,2},{4,5},{5,4},{6,7},{7,6},{8,9},{9,8},{10,11... | collective-permute-start | bytes 1376264 | tf_op jit(solution)/shard_map/ppermute | solution.py:612
  159.2 44.9 %collective-permute-start.26 = (bf16[512,896]{1,0:T(8,128)(2,1)}, bf16[512,896]{1,0:T(8,128)(2,1)}, u32[]{:S(2)}, u32[]{:S(2)}) collective-permute-start(bf16[512,896]{1,0:T(8,128)(2,1)} %get-tuple-element.221), channel_id=1, source_target_pairs={{0,1},{1,0},{2,3},{3,2},{4,5},{5,4},{6,7},{7,6},{8,9},{9,8},{10,11... | collective-permute-start | bytes 2752520 | tf_op jit(solution)/shard_map/ppermute | solution.py:612
  160.2 29.7 %collective-permute-start.28 = (bf16[512,896]{1,0:T(8,128)(2,1)}, bf16[512,896]{1,0:T(8,128)(2,1)}, u32[]{:S(2)}, u32[]{:S(2)}) collective-permute-start(bf16[512,896]{1,0:T(8,128)(2,1)} %get-tuple-element.220), channel_id=1, source_target_pairs={{0,2},{1,3},{2,0},{3,1},{4,6},{5,7},{6,4},{7,5},{8,10},{9,11},{10,... | collective-permute-start | bytes 2752520 | tf_op jit(solution)/shard_map/ppermute | solution.py:612
  203.7 37.7 %collective-permute-start.29 = (bf16[512,896]{1,0:T(8,128)(2,1)}, bf16[512,896]{1,0:T(8,128)(2,1)}, u32[]{:S(2)}, u32[]{:S(2)}) collective-permute-start(bf16[512,896]{1,0:T(8,128)(2,1)} %get-tuple-element.132), channel_id=1, source_target_pairs={{0,2},{1,3},{2,0},{3,1},{4,6},{5,7},{6,4},{7,5},{8,10},{9,11},{10,... | collective-permute-start | bytes 2752520 | tf_op jit(solution)/shard_map/ppermute | solution.py:612
  217.8 23.6 %collective-permute-start.30 = (bf16[512,896]{1,0:T(8,128)(2,1)}, bf16[512,896]{1,0:T(8,128)(2,1)}, u32[]{:S(2)}, u32[]{:S(2)}) collective-permute-start(bf16[512,896]{1,0:T(8,128)(2,1)} %get-tuple-element.133), channel_id=1, source_target_pairs={{0,1},{1,0},{2,3},{3,2},{4,5},{5,4},{6,7},{7,6},{8,9},{9,8},{10,11... | collective-permute-start | bytes 2752520 | tf_op jit(solution)/shard_map/ppermute | solution.py:612
  260.6 38.1 %collective-permute-start.33 = (bf16[512,896]{1,0:T(8,128)(2,1)}, bf16[512,896]{1,0:T(8,128)(2,1)S(1)}, u32[]{:S(2)}, u32[]{:S(2)}) collective-permute-start(bf16[512,896]{1,0:T(8,128)(2,1)} %get-tuple-element.144), channel_id=1, source_target_pairs={{0,2},{1,3},{2,0},{3,1},{4,6},{5,7},{6,4},{7,5},{8,10},{9,11},{10,... | collective-permute-start | bytes 2752520 | tf_op jit(solution)/shard_map/ppermute | solution.py:612
  262.0 36.7 %collective-permute-start.34 = (bf16[512,896]{1,0:T(8,128)(2,1)}, bf16[512,896]{1,0:T(8,128)(2,1)}, u32[]{:S(2)}, u32[]{:S(2)}) collective-permute-start(bf16[512,896]{1,0:T(8,128)(2,1)} %get-tuple-element.145), channel_id=1, source_target_pairs={{0,1},{1,0},{2,3},{3,2},{4,5},{5,4},{6,7},{7,6},{8,9},{9,8},{10,11... | collective-permute-start | bytes 2752520 | tf_op jit(solution)/shard_map/ppermute | solution.py:612
  308.7 29.1 %collective-permute-start.39 = (bf16[4,4,112,224]{3,2,1,0:T(8,128)(2,1)}, bf16[4,4,112,224]{3,2,1,0:T(8,128)(2,1)}, u32[]{:S(2)}, u32[]{:S(2)}) collective-permute-start(bf16[4,4,112,224]{3,2,1,0:T(8,128)(2,1)} %get-tuple-element.152), channel_id=1, source_target_pairs={{0,4},{4,0},{8,12},{12,8},{16,20},{20,16},{24,28},{28,24},{1,5},{5... | collective-permute-start | bytes 2408456 | tf_op jit(solution)/shard_map/ppermute | solution.py:745
  324.3 11.5 %collective-permute-start.43 = (bf16[256,896]{1,0:T(8,128)(2,1)}, bf16[256,896]{1,0:T(8,128)(2,1)S(1)}, u32[]{:S(2)}, u32[]{:S(2)}) collective-permute-start(bf16[256,896]{1,0:T(8,128)(2,1)} %get-tuple-element.191), channel_id=1, source_target_pairs={{0,1},{1,0},{2,3},{3,2},{4,5},{5,4},{6,7},{7,6},{8,9},{9,8},{10,11... | collective-permute-start | bytes 1376264 | tf_op jit(solution)/shard_map/ppermute | solution.py:612
  325.2 10.7 %collective-permute-start.44 = (bf16[256,896]{1,0:T(8,128)(2,1)}, bf16[256,896]{1,0:T(8,128)(2,1)}, u32[]{:S(2)}, u32[]{:S(2)}) collective-permute-start(bf16[256,896]{1,0:T(8,128)(2,1)} %get-tuple-element.192), channel_id=1, source_target_pairs={{0,2},{1,3},{2,0},{3,1},{4,6},{5,7},{6,4},{7,5},{8,10},{9,11},{10,... | collective-permute-start | bytes 1376264 | tf_op jit(solution)/shard_map/ppermute | solution.py:612
  333.4 24.7 %collective-permute-start.38 = (bf16[4,4,112,288]{2,3,1,0:T(8,128)(2,1)}, bf16[4,4,112,288]{2,3,1,0:T(8,128)(2,1)}, u32[]{:S(2)}, u32[]{:S(2)}) collective-permute-start(bf16[4,4,112,288]{2,3,1,0:T(8,128)(2,1)} %copy.88), channel_id=1, source_target_pairs={{0,4},{4,0},{8,12},{12,8},{16,20},{20,16},{24,28},{28,24},{1,5},{5... | collective-permute-start | bytes 3096584 | tf_op jit(solution)/shard_map/ppermute | solution.py:745
  333.4 14.6 %collective-permute-start.46 = (bf16[1,256,896]{2,1,0:T(8,128)(2,1)}, bf16[1,256,896]{2,1,0:T(8,128)(2,1)}, u32[]{:S(2)}, u32[]{:S(2)}) collective-permute-start(bf16[1,256,896]{2,1,0:T(8,128)(2,1)} %slice.314), channel_id=1, source_target_pairs={{0,3},{1,2},{2,1},{3,0},{4,7},{5,6},{6,5},{7,4},{8,11},{9,10},{10,... | collective-permute-start | bytes 1376264 | tf_op jit(solution)/shard_map/ppermute | solution.py:940
  339.3 13.4 %collective-permute-start.42 = (bf16[448,224]{1,0:T(8,128)(2,1)S(1)}, bf16[448,224]{1,0:T(8,128)(2,1)S(1)}, u32[]{:S(2)}, u32[]{:S(2)}) collective-permute-start(bf16[448,224]{1,0:T(8,128)(2,1)S(1)} %get-tuple-element.194), channel_id=1, source_target_pairs={{0,3},{1,2},{2,1},{3,0},{4,7},{5,6},{6,5},{7,4},{8,11},{9,10},{10,... | collective-permute-start | bytes 602120 | tf_op jit(solution)/shard_map/ppermute | solution.py:612
  340.5 16.7 %collective-permute-start.41 = (bf16[448,224]{1,0:T(8,128)(2,1)S(1)}, bf16[448,224]{1,0:T(8,128)(2,1)S(1)}, u32[]{:S(2)}, u32[]{:S(2)}) collective-permute-start(bf16[448,224]{1,0:T(8,128)(2,1)S(1)} %get-tuple-element.195), channel_id=1, source_target_pairs={{0,2},{1,3},{2,0},{3,1},{4,6},{5,7},{6,4},{7,5},{8,10},{9,11},{10,... | collective-permute-start | bytes 602120 | tf_op jit(solution)/shard_map/ppermute | solution.py:612
  341.7 15.6 %collective-permute-start.40 = (bf16[448,224]{1,0:T(8,128)(2,1)S(1)}, bf16[448,224]{1,0:T(8,128)(2,1)S(1)}, u32[]{:S(2)}, u32[]{:S(2)}) collective-permute-start(bf16[448,224]{1,0:T(8,128)(2,1)S(1)} %get-tuple-element.193), channel_id=1, source_target_pairs={{0,1},{1,0},{2,3},{3,2},{4,5},{5,4},{6,7},{7,6},{8,9},{9,8},{10,11... | collective-permute-start | bytes 602120 | tf_op jit(solution)/shard_map/ppermute | solution.py:612
  364.6 11.0 %collective-permute-start.49 = (bf16[451,288]{0,1:T(8,128)(2,1)S(1)}, bf16[451,288]{0,1:T(8,128)(2,1)S(1)}, u32[]{:S(2)}, u32[]{:S(2)}) collective-permute-start(bf16[451,288]{0,1:T(8,128)(2,1)S(1)} %get-tuple-element.178), channel_id=1, source_target_pairs={{0,3},{1,2},{2,1},{3,0},{4,7},{5,6},{6,5},{7,4},{8,11},{9,10},{10,... | collective-permute-start | bytes 779336 | tf_op jit(solution)/shard_map/ppermute | solution.py:612
  366.4 14.4 %collective-permute-start.48 = (bf16[451,288]{0,1:T(8,128)(2,1)S(1)}, bf16[451,288]{0,1:T(8,128)(2,1)S(1)}, u32[]{:S(2)}, u32[]{:S(2)}) collective-permute-start(bf16[451,288]{0,1:T(8,128)(2,1)S(1)} %get-tuple-element.177), channel_id=1, source_target_pairs={{0,2},{1,3},{2,0},{3,1},{4,6},{5,7},{6,4},{7,5},{8,10},{9,11},{10,... | collective-permute-start | bytes 779336 | tf_op jit(solution)/shard_map/ppermute | solution.py:612
  367.2 13.5 %collective-permute-start.47 = (bf16[451,288]{0,1:T(8,128)(2,1)S(1)}, bf16[451,288]{0,1:T(8,128)(2,1)S(1)}, u32[]{:S(2)}, u32[]{:S(2)}) collective-permute-start(bf16[451,288]{0,1:T(8,128)(2,1)S(1)} %get-tuple-element.176), channel_id=1, source_target_pairs={{0,1},{1,0},{2,3},{3,2},{4,5},{5,4},{6,7},{7,6},{8,9},{9,8},{10,11... | collective-permute-start | bytes 779336 | tf_op jit(solution)/shard_map/ppermute | solution.py:612
  368.8 18.8 %collective-permute-start.58 = (bf16[112,224]{1,0:T(8,128)(2,1)}, bf16[112,224]{1,0:T(8,128)(2,1)S(1)}, u32[]{:S(2)}, u32[]{:S(2)}) collective-permute-start(bf16[112,224]{1,0:T(8,128)(2,1)} %get-tuple-element.239), channel_id=1, source_target_pairs={{0,24},{4,28},{8,0},{12,4},{16,8},{20,12},{24,16},{28,20},{1,25},{... | collective-permute-start | bytes 150536 | tf_op jit(solution)/shard_map/ppermute | solution.py:896
  370.5 17.0 %collective-permute-start.57 = (bf16[112,224]{1,0:T(8,128)(2,1)}, bf16[112,224]{1,0:T(8,128)(2,1)S(1)}, u32[]{:S(2)}, u32[]{:S(2)}) collective-permute-start(bf16[112,224]{1,0:T(8,128)(2,1)} %get-tuple-element.240), channel_id=1, source_target_pairs={{0,16},{4,20},{8,24},{12,28},{16,0},{20,4},{24,8},{28,12},{1,17},{... | collective-permute-start | bytes 150536 | tf_op jit(solution)/shard_map/ppermute | solution.py:896
  375.6 12.0 %collective-permute-start.56 = (bf16[112,224]{1,0:T(8,128)(2,1)S(1)}, bf16[112,224]{1,0:T(8,128)(2,1)}, u32[]{:S(2)}, u32[]{:S(2)}) collective-permute-start(bf16[112,224]{1,0:T(8,128)(2,1)S(1)} %get-tuple-element.238), channel_id=1, source_target_pairs={{0,8},{4,12},{8,16},{12,20},{16,24},{20,28},{24,0},{28,4},{1,9},{5... | collective-permute-start | bytes 150536 | tf_op jit(solution)/shard_map/ppermute | solution.py:896
  382.0 23.5 %collective-permute-start.45 = (bf16[1,256,896]{2,1,0:T(8,128)(2,1)S(1)}, bf16[1,256,896]{2,1,0:T(8,128)(2,1)S(1)}, u32[]{:S(2)}, u32[]{:S(2)}) collective-permute-start(bf16[1,256,896]{2,1,0:T(8,128)(2,1)S(1)} %get-tuple-element.188), channel_id=1, source_target_pairs={{0,3},{1,2},{2,1},{3,0},{4,7},{5,6},{6,5},{7,4},{8,11},{9,10},{10,... | collective-permute-start | bytes 1376264 | tf_op jit(solution)/shard_map/ppermute | solution.py:716
  391.1 13.7 %collective-permute-start.55 = (bf16[112,288]{0,1:T(8,128)(2,1)S(1)}, bf16[112,288]{0,1:T(8,128)(2,1)S(1)}, u32[]{:S(2)}, u32[]{:S(2)}) collective-permute-start(bf16[112,288]{0,1:T(8,128)(2,1)S(1)} %bitcast.143), channel_id=1, source_target_pairs={{0,24},{4,28},{8,0},{12,4},{16,8},{20,12},{24,16},{28,20},{1,25},{... | collective-permute-start | bytes 193544 | tf_op jit(solution)/shard_map/ppermute | solution.py:896
  394.2 10.6 %collective-permute-start.54 = (bf16[112,288]{0,1:T(8,128)(2,1)S(1)}, bf16[112,288]{0,1:T(8,128)(2,1)S(1)}, u32[]{:S(2)}, u32[]{:S(2)}) collective-permute-start(bf16[112,288]{0,1:T(8,128)(2,1)S(1)} %bitcast.141), channel_id=1, source_target_pairs={{0,16},{4,20},{8,24},{12,28},{16,0},{20,4},{24,8},{28,12},{1,17},{... | collective-permute-start | bytes 193544 | tf_op jit(solution)/shard_map/ppermute | solution.py:896
  399.5 20.7 %collective-permute-start.59 = (bf16[112,608]{1,0:T(8,128)(2,1)S(1)}, bf16[112,608]{1,0:T(8,128)(2,1)S(1)}, u32[]{:S(2)}, u32[]{:S(2)}) collective-permute-start(bf16[112,608]{1,0:T(8,128)(2,1)S(1)} %get-tuple-element.214), channel_id=1, source_target_pairs={{0,0},{1,8},{2,16},{3,24},{4,4},{5,12},{6,20},{7,28},{8,1},{9,9},{... | collective-permute-start | bytes 408584 | tf_op jit(solution)/shard_map/ppermute | solution.py:695
  404.7 16.2 %collective-permute-start.60 = (bf16[112,608]{1,0:T(8,128)(2,1)S(1)}, bf16[112,608]{1,0:T(8,128)(2,1)S(1)}, u32[]{:S(2)}, u32[]{:S(2)}) collective-permute-start(bf16[112,608]{1,0:T(8,128)(2,1)S(1)} %get-tuple-element.215), channel_id=1, source_target_pairs={{0,4},{1,12},{2,20},{3,28},{4,0},{5,8},{6,16},{7,24},{8,5},{9,13},... | collective-permute-start | bytes 408584 | tf_op jit(solution)/shard_map/ppermute | solution.py:695
  (57 other events, 319.2 us)
Sparse Core Ops, SparseCore 0:
  10.2 56.5 all-gather.4
  107.9 32.3 all-gather.6
  241.5 77.1 reduce-scatter.1

commit v5 on v4

--- a/solution.py
+++ b/solution.py
@@ -1,3 +1,4 @@
+import functools
 import math
 import jax
 import jax.numpy as jnp
@@ -191,42 +192,39 @@
     )(grad_queries, weight, tokens, gain, grad_hidden, cosine, sine, *parts)
 
 
-def pieces_kernel(core_ref, lhs_ref, *rest):
-    rhs_refs = rest[:-2]
-    mine_ref, other_ref = rest[-2:]
-    ranks, floors, depth, own = mine_ref.shape
-    rhs = jnp.concatenate([ref[...] for ref in rhs_refs], axis=1)
-    whole = dot(lhs_ref[...], rhs, TN)
-    first = core_ref[0] == 0
-    for rank in range(ranks):
-        part = whole[:, rank * own : (rank + 1) * own].reshape(floors, 2, depth, own)
-        mine_ref[rank] = jnp.where(first, part[:, 0], part[:, 1]).astype(bf16)
-        other_ref[rank] = jnp.where(first, part[:, 1], part[:, 0]).astype(bf16)
-
-
-def weight_pieces(core, ctx_size, seq_size, lhs, *rhs):
-    rows, width = lhs.shape
-    columns = sum(x.shape[1] for x in rhs)
-    shape = (ctx_size, seq_size // 2, width // seq_size, columns // ctx_size)
-
-    def full(*shape):
-        return pl.BlockSpec(shape, lambda i, core: (0,) * len(shape))
-
+def owned_weights_kernel(ctx_size, normed_ref, gq_ref, gkv_ref, mixed_ref, hidden_ref, out_ref):
+    grads = jnp.concatenate([gq_ref[...], gkv_ref[...]], axis=1)
+    project = dot(normed_ref[...], grads, TN)
+    output = dot(mixed_ref[...], hidden_ref[...], TN)
+    first = project.shape[1] // ctx_size
+    second = output.shape[1] // ctx_size
+    own = first + second
+    for rank in range(ctx_size):
+        out_ref[:, rank * own : (rank + 1) * own] = jnp.concatenate(
+            [
+                project[:, rank * first : (rank + 1) * first],
+                output[:, rank * second : (rank + 1) * second],
+            ],
+            axis=1,
+        ).astype(bf16)
+
+
+def owned_weights(ctx_size, normed, grad_queries, grad_pairs, mixed, hidden_low):
+    rows, width = normed.shape
+    columns = Q_WIDTH + 2 * K_WIDTH + hidden_low.shape[1]
+    arrays = (normed, grad_queries, grad_pairs, mixed, hidden_low)
     return pl.pallas_call(
-        pieces_kernel,
-        grid_spec=pltpu.PrefetchScalarGridSpec(
-            num_scalar_prefetch=1,
-            grid=(1,),
-            in_specs=[full(*x.shape) for x in (lhs, *rhs)],
-            out_specs=[full(*shape)] * 2,
-        ),
-        out_shape=[jax.ShapeDtypeStruct(shape, bf16)] * 2,
+        functools.partial(owned_weights_kernel, ctx_size),
+        grid=(1,),
+        in_specs=[full_spec(*x.shape) for x in arrays],
+        out_specs=full_spec(width, columns),
+        out_shape=jax.ShapeDtypeStruct((width, columns), bf16),
         cost_estimate=pl.CostEstimate(
-            flops=4 * rows * width * columns, bytes_accessed=5 << 20, transcendentals=0
+            flops=4 * rows * width * columns, bytes_accessed=8 << 20, transcendentals=0
         ),
         compiler_params=params(),
-        name="weight_pieces",
-    )(core.astype(jnp.int32)[None], lhs, *rhs)
+        name="owned_weights",
+    )(*arrays)
 
 
 def pair_sides(both):
@@ -507,12 +505,13 @@
     )(order, queries, mixed, grads, stats_in, cosine, sine, *parts)
 
 
-def ffn_kernel(x_ref, c_ref, w_ref, d_ref, *rest):
+def ffn_kernel(x_low, x_high, c_low, c_high, w_ref, d_ref, *rest):
     out_ref, grad_ref, x_all, c_all, active_all, gate_all, up_all = rest[-7:]
     seq_size, _, depth, columns = w_ref.shape
     width = seq_size * depth
-    x = x_ref[...]
-    c = c_ref[...]
+    low = pl.program_id(0) == 0
+    x = jnp.where(low, x_low[...], x_high[...])
+    c = jnp.where(low, c_low[...], c_high[...])
     x_all[0] = x
     c_all[0] = c
     gate_w = w_ref[:, 0].reshape(width, columns)
@@ -533,10 +532,13 @@
     out_ref[...] = dot(active, down_w, NT).astype(bf16)
 
 
-def ffn(number, count, x, c, weights, down, buffers):
-    rows, width = x.shape
+def ffn(number, count, rows, halves, weights, down, buffers):
+    width = halves[0][0].shape[1]
     columns = weights.shape[3]
     tile = rows // 2
+
+    def half_spec(at):
+        return pl.BlockSpec((tile, width), lambda i: (at, 0))
 
     def slot(columns):
         return pl.BlockSpec((1, tile, columns), lambda i: (number, i, 0))
@@ -546,24 +548,20 @@
     return pl.pallas_call(
         ffn_kernel,
         grid=(2,),
-        in_specs=[
-            row_spec(tile, width),
-            row_spec(tile, width),
-            full_spec(*weights.shape),
-            full_spec(*down.shape),
-        ]
+        in_specs=[half_spec(at) for _, at in halves]
+        + [full_spec(*weights.shape), full_spec(*down.shape)]
         + [pl.BlockSpec(memory_space=pl.ANY)] * len(buffers),
         out_specs=[row_spec(tile, width), row_spec(tile, width)]
         + [slot(width)] * 2
         + [slot(columns)] * 3,
         out_shape=[jax.ShapeDtypeStruct((rows, width), bf16)] * 2 + [wide] * 2 + [inner] * 3,
-        input_output_aliases={4 + i: 2 + i for i in range(len(buffers))},
+        input_output_aliases={6 + i: 2 + i for i in range(len(buffers))},
         cost_estimate=pl.CostEstimate(
             flops=14 * rows * width * columns, bytes_accessed=16 << 20, transcendentals=0
         ),
         compiler_params=params(),
         name="ffn",
-    )(x, c, weights, down, *buffers)
+    )(*[x for x, _ in halves], weights, down, *buffers)
 
 
 def ffn_weights_kernel(x_ref, c_ref, active_ref, gate_ref, up_ref, out_ref, acc_ref):
@@ -612,53 +610,15 @@
     return lax.ppermute(x, "ctx", [(i, i ^ mask) for i in range(ctx_size)])
 
 
-def spread_near(x, ctx_size):
-    if ctx_size != 4:
-        return [hop(x, ctx_size, k) for k in range(1, ctx_size)]
-    half = x.shape[0] // 2
-    return [hop(x[:half], 4, 1), hop(x[half:], 4, 2)]
-
-
-def spread_far(x, near, ctx_size):
-    if ctx_size != 4:
-        return []
-    half = x.shape[0] // 2
-    return [
-        hop(jnp.concatenate([x[:half], near[0]], axis=0), 4, 2),
-        hop(jnp.concatenate([x[half:], near[1]], axis=0), 4, 1),
-    ]
-
-
-def spread_parts(x, near, far, ctx_size):
-    return [x, *near] if ctx_size != 4 else [x, jnp.concatenate(near, axis=0), *far]
-
-
-def first_hops(parts, ctx_size):
-    if ctx_size != 4:
-        return [hop(parts[k], ctx_size, k) for k in range(1, ctx_size)]
-    return [hop(parts[2], 4, 2), hop(parts[3], 4, 1)]
-
-
-def gathered_sum(parts, got, ctx_size):
-    if ctx_size != 4:
-        total = parts[0].astype(f32)
-        for part in got:
-            total = total + part.astype(f32)
-        return total
-    own, near = parts[:2]
-    front_got, back_got = got
-    half = own.shape[0] // 2
-    front_next = (near[:half].astype(f32) + front_got[half:].astype(f32)).astype(bf16)
-    back_next = (near[half:].astype(f32) + back_got[half:].astype(f32)).astype(bf16)
-    front_last = hop(front_next, 4, 1)
-    back_last = hop(back_next, 4, 2)
-    return jnp.concatenate(
-        [
-            own[:half].astype(f32) + front_got[:half].astype(f32) + front_last.astype(f32),
-            own[half:].astype(f32) + back_got[:half].astype(f32) + back_last.astype(f32),
-        ],
-        axis=0,
-    )
+def others(x, ctx_size):
+    return [hop(x, ctx_size, k) for k in range(1, ctx_size)]
+
+
+def others_sum(parts, got):
+    total = parts[0].astype(f32)
+    for part in got:
+        total = total + part.astype(f32)
+    return total
 
 
 def pick(index, cases):
@@ -689,7 +649,19 @@
     core = seq_place % 2
     floor = seq_place // 2
     floors = seq_size // 2
-    mirror = [(i, ctx_size - 1 - i) for i in range(ctx_size)]
+    far = ctx_size - 1
+    half_rows = rows // 2
+
+    def to_rows(x):
+        shape = (sequences, 2, half, x.shape[-1])
+        return jnp.swapaxes(x.reshape(shape), 0, 1).reshape(rows, x.shape[-1])
+
+    def to_blocks(x):
+        shape = (2, sequences, half, x.shape[-1])
+        return jnp.swapaxes(x.reshape(shape), 0, 1)
+
+    def attention_blocks(x):
+        return to_blocks(x).reshape(2 * sequences, half, x.shape[-1])
 
     def crossed(x, j):
         return lax.ppermute(
@@ -712,15 +684,16 @@
             pick(fold_place, [came[(f - t) % fold] for f in range(fold)]) for t in range(fold)
         ]
 
-    def zigzag(x):
-        return jnp.concatenate([x[:, :half], lax.ppermute(x[:, half:], "ctx", mirror)], axis=1)
+    def swap_second(x):
+        return jnp.concatenate([x[:half_rows], hop(x[half_rows:], ctx_size, far)], axis=0)
 
     owners = [place ^ k for k in range(ctx_size)]
     order = jnp.stack(
         [spot for owner in owners for spot in (2 * owner, 2 * (ctx_size - 1 - owner) + 1)]
     ).astype(jnp.int32)
-    positions = (order[:2, None] * half + jnp.arange(half, dtype=jnp.int32)[None, :]).reshape(-1)
-    cosine, sine = rotation_tables(jnp.tile(positions, sequences))
+    positions = order[:2, None, None] * half + jnp.arange(half, dtype=jnp.int32)[None, None, :]
+    positions = jnp.broadcast_to(positions, (2, sequences, half)).reshape(-1)
+    cosine, sine = rotation_tables(positions)
 
     def from_floors(x):
         came = [x] + [
@@ -758,7 +731,7 @@
     spare = -vectors.shape[0] % own_width
     project_rows = from_floors(project_weight)
     held = project_rows.shape[0]
-    tokens_mine = zigzag(tokens).reshape(rows, width)
+    tokens_mine = swap_second(to_rows(tokens))
     project_rows, tokens_mine = lax.optimization_barrier((project_rows, tokens_mine))
     project_came = from_ranks(
         jnp.concatenate(
@@ -779,9 +752,12 @@
     project_columns = jnp.concatenate([piece[:held] for piece in ordered], axis=1)
     project_full = by_core(project_columns, from_other_core(project_columns))
 
-    down_late, grad_late = lax.optimization_barrier((down_weight, cotangent, project_columns))[:2]
-    grad_low = zigzag(grad_late).reshape(rows, width)
-    grad_near = spread_near(grad_low, ctx_size)
+    down_late, grad_late = lax.optimization_barrier((down_weight, cotangent, project_full))[:2]
+    grad_rows = to_rows(grad_late)
+    if ctx_size == 4:
+        grad_near = [hop(grad_rows[:half_rows], 4, 1), hop(grad_rows[half_rows:], 4, 2)]
+    else:
+        grad_near = others(grad_rows, ctx_size)
     down_rows, down_columns = down_weight.shape
     depth = down_columns // fold
     down_turned = jnp.concatenate(
@@ -792,39 +768,58 @@
     )
     down_turned, gate_up = lax.optimization_barrier((down_turned, gate_up, queries))[:2]
     down_mine = lax.all_gather(down_turned, "seq", axis=0)
-    queries = queries.reshape(sequences * 2, half, Q_WIDTH)
-    pairs_mine = pairs_mine.reshape(sequences, 2, half, 2 * K_WIDTH)
+    queries = attention_blocks(queries)
+    pairs_mine = to_blocks(pairs_mine)
     pair_parts = [pairs_mine] + [hop(pairs_mine, ctx_size, k) for k in range(1, ctx_size)]
     grad_near, output_rows = lax.optimization_barrier((grad_near, output_rows, pair_parts))[:2]
-    grad_far = spread_far(grad_low, grad_near, ctx_size)
+    if ctx_size == 4:
+        grad_far = [
+            hop(jnp.concatenate([grad_rows[:half_rows], grad_near[0]], axis=0), 4, 2),
+            hop(jnp.concatenate([grad_rows[half_rows:], grad_near[1]], axis=0), 4, 1),
+        ]
+    else:
+        grad_far = []
     output_came = from_ranks(output_rows)
     queries = lax.optimization_barrier((queries, down_turned))[0]
     mixed, row_stats = attend_forward(order, queries, pair_parts)
     mixed, grad_far, output_came = lax.optimization_barrier((mixed, grad_far, output_came))
-    grad_parts = spread_parts(grad_low, grad_near, grad_far, ctx_size)
+    if ctx_size == 4:
+        firsts = [(grad_rows, 0), (grad_near[0], 0), (grad_far[0], 0), (grad_far[0], 1)]
+        seconds = [(grad_rows, 1), (grad_far[1], 0), (grad_near[1], 0), (grad_far[1], 1)]
+        own_second = grad_far[1][half_rows:]
+    else:
+        firsts = [(x, 0) for x in (grad_rows, *grad_near)]
+        seconds = [(x, 1) for x in (grad_rows, *grad_near)]
+        own_second = grad_near[far - 1][half_rows:]
+    grad_low = jnp.concatenate([grad_rows[:half_rows], own_second], axis=0)
     output_columns = jnp.concatenate(by_rank(output_came), axis=1)
     output_full = by_core(output_columns, from_other_core(output_columns))
-    mixed_rows = mixed.reshape(rows, Q_WIDTH)
+    mixed_rows = to_rows(mixed)
     hidden = tokens_mine.astype(f32) + dot(mixed_rows, output_full, NN)
     inverse_ffn = inverse_rms(hidden)
     normed_ffn = (hidden * inverse_ffn * feedforward_full).astype(bf16)
 
-    normed_near = spread_near(normed_ffn, ctx_size)
-    normed_far = spread_far(normed_ffn, normed_near, ctx_size)
-    normed_parts = spread_parts(normed_ffn, normed_near, normed_far, ctx_size)
+    normed_parts = [normed_ffn, *others(normed_ffn, ctx_size)]
     output_parts = []
     grad_normed_parts = []
     buffers = []
-    for number, (part, grad_part) in enumerate(zip(normed_parts, grad_parts)):
+    for k, part in enumerate(normed_parts):
         output_part, grad_normed_part, *buffers = ffn(
-            number, ctx_size, part, grad_part, gate_up, down_mine, buffers
+            k,
+            ctx_size,
+            rows,
+            [(part, 0), (part, 1), firsts[k], seconds[k ^ far]],
+            gate_up,
+            down_mine,
+            buffers,
         )
         output_parts.append(output_part)
         grad_normed_parts.append(grad_normed_part)
+    normed_got = [hop(grad_normed_parts[k], ctx_size, k) for k in range(1, ctx_size)]
     ffn_grads, normed_got = lax.optimization_barrier(
-        (ffn_weights(seq_size, *buffers), first_hops(grad_normed_parts, ctx_size))
-    )
-    grad_normed_ffn = gathered_sum(grad_normed_parts, normed_got, ctx_size)
+        (ffn_weights(seq_size, *buffers), normed_got)
+    )
+    grad_normed_ffn = others_sum(grad_normed_parts, normed_got)
     weight_grads = lax.psum_scatter(ffn_grads, "seq", scatter_dimension=0)
 
     grad_ffn_gain = jnp.sum(grad_normed_ffn * hidden * inverse_ffn, axis=0)
@@ -842,29 +837,24 @@
     grad_mixed = dot(hidden_low, output_full, NT).astype(bf16)
 
     output_parts = lax.optimization_barrier((output_parts, grad_mixed))[0]
-    output_got = first_hops(output_parts, ctx_size)
+    output_got = [hop(output_parts[k], ctx_size, k) for k in range(1, ctx_size)]
 
     grad_queries, pair_grads = attend_backward(
         order,
         queries,
         pair_parts,
         mixed,
-        grad_mixed.reshape(sequences * 2, half, Q_WIDTH),
+        attention_blocks(grad_mixed),
         row_stats,
-        cosine.reshape(sequences * 2, half, PAIR),
-        sine.reshape(sequences * 2, half, PAIR),
+        attention_blocks(cosine),
+        attention_blocks(sine),
     )
     pair_grads, output_got = lax.optimization_barrier((pair_grads, output_got))
-    pair_sums = [pair_grads[:, :2].reshape(rows, 2 * K_WIDTH)]
+    pair_sums = [to_rows(pair_grads[:, :2])]
     for k in range(1, ctx_size):
-        pair_sums.append(
-            hop(pair_grads[:, 2 * k : 2 * k + 2], ctx_size, k).reshape(rows, 2 * K_WIDTH)
-        )
-    hidden_late = lax.optimization_barrier((hidden_low, pair_grads))[0]
-    output_pieces = weight_pieces(core, ctx_size, seq_size, mixed_rows, hidden_late)
-    output_got = lax.optimization_barrier((output_got, pair_sums))[0]
-    output_sum = gathered_sum(output_parts, output_got, ctx_size)
-    grad_queries = grad_queries.reshape(rows, Q_WIDTH)
+        pair_sums.append(to_rows(hop(pair_grads[:, 2 * k : 2 * k + 2], ctx_size, k)))
+    output_zigzag = hidden + others_sum(output_parts, output_got)
+    grad_queries = to_rows(grad_queries)
     grad_pairs, tokens_grad, gain_sum, bias_sum = project_backward(
         grad_queries,
         project_full,
@@ -876,36 +866,21 @@
         pair_sums,
     )
 
-    def core_sum(mine, other):
-        return (mine.astype(f32) + from_other_core(other).astype(f32)).astype(bf16)
-
-    def ctx_sum(parts):
-        def part(k):
-            return lax.dynamic_index_in_dim(parts, place ^ k, 0, keepdims=False)
-
-        total = part(0).astype(f32)
-        for k in range(1, ctx_size):
-            total = total + hop(part(k), ctx_size, k).astype(f32)
-        return total
-
-    def floor_sum(column):
-        column = column.astype(bf16).reshape(floors, -1, column.shape[1])
-        total = lax.dynamic_index_in_dim(column, floor, 0, keepdims=False).astype(f32)
-        for step in range(1, floors):
-            sent = lax.dynamic_index_in_dim(column, (floor + step) % floors, 0, keepdims=False)
-            total = total + lax.ppermute(
-                sent, "seq", [(i, (i + 2 * step) % seq_size) for i in range(seq_size)]
-            ).astype(f32)
-        return total
-
-    def by_owner(parts):
-        return parts.reshape(ctx_size, -1, parts.shape[-1])
-
-    output_chip = by_owner(core_sum(*output_pieces))
-    output_chip = lax.optimization_barrier((output_chip, pair_sums))[0]
-    output_total = ctx_sum(output_chip)
-
-    project_pieces = weight_pieces(core, ctx_size, seq_size, normed, grad_queries, grad_pairs)
+    owned = lax.psum_scatter(
+        owned_weights(ctx_size, normed, grad_queries, grad_pairs, mixed_rows, hidden_low),
+        "seq",
+        scatter_dimension=0,
+        tiled=True,
+    )
+
+    layer_output = swap_second(output_zigzag.astype(bf16))
+    tokens_gradient = jnp.concatenate(
+        [
+            tokens_grad[:half_rows],
+            hop(tokens_grad[half_rows:].astype(bf16), ctx_size, far).astype(f32),
+        ],
+        axis=0,
+    )
     sums = jnp.concatenate(
         [
             gain_sum.reshape(ctx_size, gain_width),
@@ -914,45 +889,42 @@
         ],
         axis=1,
     )
-    sums = jnp.pad(sums, ((0, 0), (0, spare))).reshape(ctx_size, -1, own_width).astype(bf16)
-    project_chip = by_owner(core_sum(*project_pieces))
-    project_chip, output_total, output_sum = lax.optimization_barrier(
-        (project_chip, output_total, output_sum)
-    )
-    output_out = floor_sum(output_total)
-    down_late = lax.optimization_barrier((weight_grads[2], project_pieces))[0]
-    down_late = down_late.reshape(depth, fold, down_rows)
-    down_came = crossed_parts([down_late[:, t] for t in range(fold)])
-    project_total = ctx_sum(jnp.concatenate([project_chip, sums], axis=1))
-    project_out = floor_sum(project_total[:held])
-    vector_sum = project_total[held:].reshape(-1)
+
+    def sums_for(k):
+        return lax.dynamic_index_in_dim(sums, place ^ k, 0)
+
+    vector_sum = sums_for(0)
+    for k in range(1, ctx_size):
+        vector_sum = vector_sum + hop(sums_for(k), ctx_size, k)
     mask = 1
     while mask < seq_size:
         vector_sum = vector_sum + lax.ppermute(
             vector_sum, "seq", [(i, i ^ mask) for i in range(seq_size)]
         )
         mask *= 2
-
-    tokens_grad = tokens_grad.reshape(tokens.shape)
-    tokens_gradient = jnp.concatenate(
-        [
-            tokens_grad[:, :half],
-            lax.ppermute(tokens_grad[:, half:].astype(bf16), "ctx", mirror).astype(f32),
-        ],
-        axis=1,
-    )
-    output_zigzag = hidden + output_sum
-    layer_output = zigzag(output_zigzag.astype(bf16).reshape(tokens.shape))
-
+    vector_sum = vector_sum[0]
+    down_late = weight_grads[2].reshape(depth, fold, down_rows)
+    down_came = crossed_parts([down_late[:, t] for t in range(fold)])
     down_out = jnp.concatenate(down_came, axis=0).T
+    owned, layer_output, tokens_gradient, vector_sum, down_out = lax.optimization_barrier(
+        (owned, layer_output, tokens_gradient, vector_sum, down_out)
+    )
+    own_columns = owned.shape[1] // ctx_size
+
+    def owned_for(k):
+        return lax.dynamic_slice_in_dim(owned, (place ^ k) * own_columns, own_columns, 1)
+
+    owned_total = owned_for(0).astype(f32)
+    for k in range(1, ctx_size):
+        owned_total = owned_total + hop(owned_for(k), ctx_size, k).astype(f32)
 
     return (
-        layer_output,
-        tokens_gradient,
+        to_blocks(layer_output).reshape(tokens.shape),
+        to_blocks(tokens_gradient).reshape(tokens.shape),
         vector_sum[:gain_width],
-        project_out,
+        owned_total[:, :own_width],
         vector_sum[gain_width : gain_width + own_width],
-        output_out,
+        owned_total[:, own_width:],
         vector_sum[gain_width + own_width : vectors.shape[0]],
         weight_grads[0].astype(f32),
         weight_grads[1].astype(f32),

time: 437 us -> 409 us (0.936)
  starting transfers between devices: 87.3 us -> 60.7 us
  waiting for transfers between devices: 82.5 us -> 107 us
  other arithmetic: 48.5 us -> 32.3 us
  local copies, waits for them, and re-layouts: 30.3 us -> 23.8 us
    ppermute x4, waiting for transfers between devices: 18.4 us -> 41.9 us  [crossed(): lax.ppermute(x, ('seq', 'ctx'), [((c * fold + r) * ctx_size + q, (q * fol...]
    ppermute x10 -> x0, starting transfers between devices: 20.5 us -> none  [the longest x6 13.9 us: floor_sum(): lax.ppermute(sent, 'seq', [(i, (i + 2 * step) % seq_size) for i in range(...]
    ppermute x10 -> x0, waiting for transfers between devices: 13.7 us -> none  [the longest x3 9.89 us: zigzag(): lax.ppermute(x[:, half:], 'ctx', mirror)]
    ppermute x34, waiting for transfers between devices: 40.1 us -> 50.3 us  [hop(): return lax.ppermute(x, 'ctx', [(i, i ^ mask) for i in range(ctx_size)])]
    ppermute x34, starting transfers between devices: 42.1 us -> 35.8 us  [hop(): return lax.ppermute(x, 'ctx', [(i, i ^ mask) for i in range(ctx_size)])]
    add x6 -> x2, other arithmetic: 6.66 us -> 0.97 us  [the longest x1 0.96 us: on_device(): owned_total = owned_total + hop(owned_for(k), ctx_size, k).astype(f32)]
    ppermute x3, waiting for transfers between devices: 0.01 us -> 4.79 us  [on_device(): lax.ppermute(vector_sum, 'seq', [(i, i ^ mask) for i in range(seq_size)])]
    convert_element_type x5 -> x3, other arithmetic: 9.26 us -> 5.58 us  [the longest x1 2.26 us: on_device(): layer_output = swap_second(output_zigzag.astype(bf16))]
  transfers between devices with their start and end apart: 64 -> 53, of which waited for: 24 -> 25; matrix products, arithmetic and copies ran while one was open for 18% -> 12% of each run, Pallas kernels for 38% -> 40%
where the time goes in v5:
time: 409 us; the launch traced here: 402 us
  Pallas kernels  160 us (39%)
  waiting for transfers between devices  107 us (26%)
  starting transfers between devices  60.7 us (15%)
  other arithmetic  32.3 us (8%)
  local copies, waits for them, and re-layouts  23.8 us (6%)
  between operations  15 us (4%)
    pallas_call x4, Pallas kernels, ffn(): pl.pallas_call(ffn_kernel, grid=(2,), in_specs=[half_spec(at) for _, at i...  56.2 us
    ppermute x34, waiting for transfers between devices, hop(): return lax.ppermute(x, 'ctx', [(i, i ^ mask) for i in range(ctx_size)])  50.3 us
    ppermute x4, waiting for transfers between devices, crossed(): lax.ppermute(x, ('seq', 'ctx'), [((c * fold + r) * ctx_size + q, (q * fol...  41.9 us
    pallas_call x1, Pallas kernels, attend_backward(): pl.pallas_call(backward_kernel, grid_spec=pltpu.PrefetchScalarGridSpec(nu...  36.3 us
    ppermute x34, starting transfers between devices, hop(): return lax.ppermute(x, 'ctx', [(i, i ^ mask) for i in range(ctx_size)])  35.8 us
    pallas_call x1, Pallas kernels, attend_forward(): pl.pallas_call(forward_kernel, grid_spec=pltpu.PrefetchScalarGridSpec(num...  27.4 us
    pallas_call x1, Pallas kernels, ffn_weights(): pl.pallas_call(ffn_weights_kernel, grid=(count,), in_specs=[slot(width)]...  22.4 us
    ppermute x3, starting transfers between devices, on_device(): lax.ppermute(vector_sum, 'seq', [(i, i ^ mask) for i in range(seq_size)])  8.7 us
  transfers between devices with their start and end apart: 53, of which 25 were waited for; matrix products, arithmetic and copies ran while one was open for 12% of the time, Pallas kernels for 40%

profile of v5, /device:TPU:2, one launch (start us, length us, event | category | flops | bytes accessed | tf_op | source)
XLA Modules:
  0.0 402.1 jit_solution(16343322137888873387)
XLA Ops:
  7.3 2.0 pad_maximum_fusion.9
  10.3 2.7 collective-permute-start.1
  20.8 6.7 %collective-permute-done.3 = bf16[256,896]{1,0:T(8,128)(2,1)S(1)} collective-permute-done((bf16[256,896]{1,0:T(8,128)(2,1)S(1)}, bf16[256,896]{1,0:T(8,128)(2,1)S(1)}, u32[]{:S(2)}, u32[]{:S(2)}) %collective-permute-start.3) | collective-permute-done | bytes 458784 | tf_op jit(solution)/shard_map/ppermute | solution.py:610
  29.8 2.6 collective-permute-start.17
  34.5 3.6 collective-permute-done.16
  41.1 6.6 %collective-permute-done.5 = bf16[451,288]{1,0:T(8,128)(2,1)S(1)} collective-permute-done((bf16[451,288]{1,0:T(8,128)(2,1)S(1)}, bf16[451,288]{1,0:T(8,128)(2,1)S(1)}, u32[]{:S(2)}, u32[]{:S(2)}) %collective-permute-start.5) | collective-permute-done | bytes 259808 | tf_op jit(solution)/shard_map/ppermute | solution.py:610
  50.0 3.2 concatenate.72
  57.8 5.0 %project_forward.1 = (bf16[512,896]{1,0:T(8,128)(2,1)}, bf16[512,896]{1,0:T(8,128)(2,1)}, bf16[512,256]{1,0:T(8,128)(2,1)}) custom-call(bf16[512,896]{1,0:T(8,128)(2,1)} %pad_maximum_fusion.5.x_ref, f32[1,896]{1,0:T(1,128)} %broadcast_in_dim.4.gain_ref, bf16[896,1152]{1,0:T(8,128)(2,1)} %bitcast.76, f32[1,1152]{1,0:T(1,128)} %broadcast_in_dim.5.bias_ref, ...), custom_call_target="tpu_custom_call" | custom-call | flops 2113929216 | bytes 5242880 | tf_op jit(solution)/shard_map/project_forward/pallas_call | solution.py:102
  66.3 3.5 collective-permute-start.8
  69.9 17.4 %collective-permute-done.8 = bf16[112,608]{1,0:T(8,128)(2,1)S(1)} collective-permute-done((bf16[112,608]{1,0:T(8,128)(2,1)S(1)}, bf16[112,608]{1,0:T(8,128)(2,1)S(1)}, u32[]{:S(2)}, u32[]{:S(2)}) %collective-permute-start.8) | collective-permute-done | bytes 136224 | tf_op jit(solution)/shard_map/ppermute | solution.py:667
  89.2 10.0 %collective-permute-done.13.c_low = bf16[256,896]{1,0:T(8,128)(2,1)S(1)} collective-permute-done((bf16[256,896]{1,0:T(8,128)(2,1)S(1)}, bf16[256,896]{1,0:T(8,128)(2,1)S(1)}, u32[]{:S(2)}, u32[]{:S(2)}) %collective-permute-start.13) | collective-permute-done | bytes 458784 | tf_op jit(solution)/shard_map/ppermute | solution.py:610
  99.2 2.5 collective-permute-done.14.c_high
  104.1 2.0 collective-permute-start.20
  106.2 2.0 collective-permute-start.21
  108.2 27.4 %attend_forward.1 = (bf16[2,256,896]{2,1,0:T(8,128)(2,1)}, f32[2,16,256]{2,1,0:T(8,128)}) custom-call(s32[8]{0:T(128)} %stack.54.order_ref, bf16[2,256,896]{2,1,0:T(8,128)(2,1)} %bitcast.95, bf16[1,2,256,256]{3,2,1,0:T(8,128)(2,1)} %bitcast.90, bf16[1,2,256,256]{3,2,1,0:T(8,128)(2,1)} %copy-done.25, ...), custom_call_target="tpu_custom_call" | custom-call | flops 9395240960 | bytes 4194304 | tf_op jit(solution)/shard_map/attend_forward/pallas_call | solution.py:440
  139.0 2.2 collective-permute-done.23
  148.2 1.7 collective-permute-start.25
  149.9 13.9 %ffn.4 = (bf16[512,896]{1,0:T(8,128)(2,1)}, bf16[512,896]{1,0:T(8,128)(2,1)}, bf16[4,512,896]{2,1,0:T(8,128)(2,1)}, bf16[4,512,896]{2,1,0:T(8,128)(2,1)}, bf16[4...) custom-call(bf16[512,896]{1,0:T(8,128)(2,1)} %multiply_convert_fusion.x_low.x_high, ...), custom_call_target="tpu_custom_call" | custom-call | flops 7809794048 | bytes 16777216 | tf_op jit(solution)/shard_map/ffn/pallas_call | solution.py:548
  163.8 6.0 %collective-permute-done.26.x_low.x_high = bf16[512,896]{1,0:T(8,128)(2,1)S(1)} collective-permute-done((bf16[512,896]{1,0:T(8,128)(2,1)}, bf16[512,896]{1,0:T(8,128)(2,1)S(1)}, u32[]{:S(2)}, u32[]{:S(2)}) %collective-permute-start.26) | collective-permute-done | bytes 917536 | tf_op jit(solution)/shard_map/ppermute | solution.py:610
  170.8 14.3 %ffn.5 = (bf16[512,896]{1,0:T(8,128)(2,1)}, bf16[512,896]{1,0:T(8,128)(2,1)}, bf16[4,512,896]{2,1,0:T(8,128)(2,1)}, bf16[4,512,896]{2,1,0:T(8,128)(2,1)}, bf16[4...) custom-call(bf16[512,896]{1,0:T(8,128)(2,1)} %copy-done.5, ...), custom_call_target="tpu_custom_call", output_to_operand_aliasing={{2}: (6, {}), {3}: (7, {}), {4}: (8, {}), {5}: (9, {}), {6}... | custom-call | flops 7809794048 | bytes 16777216 | tf_op jit(solution)/shard_map/ffn/pallas_call | solution.py:548
  185.4 4.6 %collective-permute-done.25.x_low.x_high = bf16[512,896]{1,0:T(8,128)(2,1)} collective-permute-done((bf16[512,896]{1,0:T(8,128)(2,1)}, bf16[512,896]{1,0:T(8,128)(2,1)}, u32[]{:S(2)}, u32[]{:S(2)}) %collective-permute-start.25) | collective-permute-done | bytes 917536 | tf_op jit(solution)/shard_map/ppermute | solution.py:610
  190.0 14.1 %ffn.6 = (bf16[512,896]{1,0:T(8,128)(2,1)}, bf16[512,896]{1,0:T(8,128)(2,1)}, bf16[4,512,896]{2,1,0:T(8,128)(2,1)}, bf16[4,512,896]{2,1,0:T(8,128)(2,1)}, bf16[4...) custom-call(bf16[512,896]{1,0:T(8,128)(2,1)} %collective-permute-don, ...), custom_call_target="tpu_custom_call", output_to_operand_aliasing={{2}: (6, {}), {3}: (7, {}), {4}: (8, {}), {5}: (9, {}), {6}... | custom-call | flops 7809794048 | bytes 16777216 | tf_op jit(solution)/shard_map/ffn/pallas_call | solution.py:548
  204.1 1.8 collective-permute-start.28
  205.8 14.0 %ffn.7 = (bf16[512,896]{1,0:T(8,128)(2,1)}, bf16[512,896]{1,0:T(8,128)(2,1)}, bf16[4,512,896]{2,1,0:T(8,128)(2,1)}, bf16[4,512,896]{2,1,0:T(8,128)(2,1)}, bf16[4...) custom-call(bf16[512,896]{1,0:T(8,128)(2,1)} %collective-permute-don, ...), custom_call_target="tpu_custom_call", output_to_operand_aliasing={{2}: (6, {}), {3}: (7, {}), {4}: (8, {}), {5}: (9, {}), {6}... | custom-call | flops 7809794048 | bytes 16777216 | tf_op jit(solution)/shard_map/ffn/pallas_call | solution.py:548
  221.4 22.4 %ffn_weights.1 = bf16[8,3,112,1216]{3,2,1,0:T(8,128)(2,1)} custom-call(bf16[4,512,896]{2,1,0:T(8,128)(2,1)} %get-tuple-element.122.x_ref, bf16[4,512,896]{2,1,0:T(8,128)(2,1)} %get-tuple-element.123.c_ref, bf16[4,512,1216]{2,1,0:T(8,128)(2,1)} %get-tuple-element.124.active_ref, bf16[4,512,1216]{2,1,0:T(8,128)(2,1)} %get-tuple-element.125.gate_ref, ...), custom_call_target="tpu_custom_call" | custom-call | flops 13388218368 | bytes 31457280 | tf_op jit(solution)/shard_map/ffn_weights/pallas_call | solution.py:594
  247.2 2.4 multiply_reduce_fusion
  249.6 3.8 fusion.9
  253.5 2.2 convolution_convert_fusion
  259.1 36.3 %attend_backward.1 = (bf16[2,256,896]{2,1,0:T(8,128)(2,1)}, bf16[1,8,256,256]{3,2,1,0:T(8,128)(2,1)}) custom-call(s32[8]{0:T(128)} %stack.54.order_ref, bf16[2,256,896]{2,1,0:T(8,128)(2,1)} %bitcast.96, bf16[2,256,896]{2,1,0:T(8,128)(2,1)} %get-tuple-element.98.o_ref, bf16[2,256,896]{2,1,0:T(8,128)(2,1)} %bitcast.101, ...), custom_call_target="tpu_custom_call" | custom-call | flops 23488102400 | bytes 8388608 | tf_op jit(solution)/shard_map/attend_backward/pallas_call | solution.py:472
  295.5 2.3 fusion.10
  298.1 1.7 collective-permute-start.34
  301.3 2.9 collective-permute-done.33
  304.1 3.1 collective-permute-done.34
  308.1 6.5 %project_backward.1 = (bf16[512,256]{1,0:T(8,128)(2,1)}, f32[512,896]{1,0:T(8,128)}, f32[1,896]{1,0:T(1,128)}, f32[1,1152]{1,0:T(1,128)}) custom-call(bf16[512,896]{1,0:T(8,128)(2,1)} %bitcast.99, bf16[896,1152]{1,0:T(8,128)(2,1)} %bitcast.77, bf16[512,896]{1,0:T(8,128)(2,1)} %pad_maximum_fusion.5.x_ref, f32[1,896]{1,0:T(1,128)} %broadcast_in_dim.4.gain_ref, ...), custom_call_target="tpu_custom_call" | custom-call | flops 2113929216 | bytes 8388608 | tf_op jit(solution)/shard_map/project_backward/pallas_call | solution.py:162
  314.6 6.4 %owned_weights.1 = bf16[896,2048]{1,0:T(8,128)(2,1)} custom-call(bf16[512,896]{1,0:T(8,128)(2,1)} %get-tuple-element.86.normed_ref, bf16[512,896]{1,0:T(8,128)(2,1)} %bitcast.100, bf16[512,256]{1,0:T(8,128)(2,1)} %get-tuple-element.144.gkv_ref, bf16[512,896]{1,0:T(8,128)(2,1)} %bitcast.97, bf16[512,896]{1,0:T(8,128)(2,1)} %copy-done.16), custom_call_target="tpu_custom_call" | custom-call | flops 3758096384 | bytes 8388608 | tf_op jit(solution)/shard_map/owned_weights/pallas_call | solution.py:216
  322.2 2.3 add_convert_fusion
  328.7 1.8 collective-permute-start.39
  333.0 2.8 collective-permute-done.40
  337.0 4.1 %collective-permute-start.42 = (f32[1,736]{1,0:T(1,128)S(1)}, f32[1,736]{1,0:T(1,128)S(1)}, u32[]{:S(2)}, u32[]{:S(2)}) collective-permute-start(f32[1,736]{1,0:T(1,128)S(1)} %add.171), channel_id=1, source_target_pairs={{0,8},{4,12},{8,0},{12,4},{16,24},{20,28},{24,16},{28,20},{1,9},{5... | collective-permute-start | bytes 8840 | tf_op jit(solution)/shard_map/ppermute | solution.py:901
  341.1 1.8 collective-permute-done.42
  342.9 4.5 %collective-permute-start.43 = (f32[1,736]{1,0:T(1,128)S(1)}, f32[1,736]{1,0:T(1,128)S(1)}, u32[]{:S(2)}, u32[]{:S(2)}) collective-permute-start(f32[1,736]{1,0:T(1,128)S(1)} %add.172), channel_id=1, source_target_pairs={{0,16},{4,20},{8,24},{12,28},{16,0},{20,4},{24,8},{28,12},{1,17},{... | collective-permute-start | bytes 8840 | tf_op jit(solution)/shard_map/ppermute | solution.py:901
  347.5 1.8 collective-permute-done.43
  349.4 2.0 pad_maximum_fusion.7
  352.5 2.2 fusion
  355.6 3.0 collective-permute-start.44
  360.1 21.1 %collective-permute-done.44 = bf16[112,608]{1,0:T(8,128)(2,1)S(1)} collective-permute-done((bf16[112,608]{1,0:T(8,128)(2,1)S(1)}, bf16[112,608]{1,0:T(8,128)(2,1)S(1)}, u32[]{:S(2)}, u32[]{:S(2)}) %collective-permute-start.44) | collective-permute-done | bytes 136224 | tf_op jit(solution)/shard_map/ppermute | solution.py:667
  381.1 2.4 collective-permute-done.45
  384.9 3.4 collective-permute-start.46
  (233 shorter events, 74.0 us)
Async XLA Ops:
  7.2 94.5 %all-gather.5.cloned.1.call-start = ((), (), s32[]{:S(2)}) async-start(), calls=%async_computation.4 | async-start | bytes 5160960 | tf_op jit(solution)/shard_map/all_gather | solution.py:727
  9.3 140.6 %all-gather.7.cloned.1.call-start = ((), (), s32[]{:S(2)}) async-start(), calls=%async_computation.5 | async-start | bytes 2580480 | tf_op jit(solution)/shard_map/all_gather | solution.py:770
  10.3 9.0 %collective-permute-start.1 = (bf16[112,288]{1,0:T(8,128)(2,1)S(1)}, bf16[112,288]{1,0:T(8,128)(2,1)S(1)}, u32[]{:S(2)}, u32[]{:S(2)}) collective-permute-start(bf16[112,288]{1,0:T(8,128)(2,1)S(1)} %copy.63), channel_id=1, source_target_pairs={{0,16},{4,20},{8,24},{12,28},{16,0},{20,4},{24,8},{28,12},{1,17},{... | collective-permute-start | bytes 193544 | tf_op jit(solution)/shard_map/ppermute | solution.py:700
  13.0 6.3 %collective-permute-start.2 = (bf16[112,288]{1,0:T(8,128)(2,1)S(1)}, bf16[112,288]{1,0:T(8,128)(2,1)S(1)}, u32[]{:S(2)}, u32[]{:S(2)}) collective-permute-start(bf16[112,288]{1,0:T(8,128)(2,1)S(1)} %copy.63), channel_id=1, source_target_pairs={{0,24},{4,28},{8,0},{12,4},{16,8},{20,12},{24,16},{28,20},{1,25},{... | collective-permute-start | bytes 193544 | tf_op jit(solution)/shard_map/ppermute | solution.py:700
  14.3 6.3 %collective-permute-start = (bf16[112,288]{1,0:T(8,128)(2,1)S(1)}, bf16[112,288]{1,0:T(8,128)(2,1)S(1)}, u32[]{:S(2)}, u32[]{:S(2)}) collective-permute-start(bf16[112,288]{1,0:T(8,128)(2,1)S(1)} %copy.63), channel_id=1, source_target_pairs={{0,8},{4,12},{8,16},{12,20},{16,24},{20,28},{24,0},{28,4},{1,9},{5... | collective-permute-start | bytes 193544 | tf_op jit(solution)/shard_map/ppermute | solution.py:700
  15.1 12.4 %collective-permute-start.3 = (bf16[256,896]{1,0:T(8,128)(2,1)S(1)}, bf16[256,896]{1,0:T(8,128)(2,1)S(1)}, u32[]{:S(2)}, u32[]{:S(2)}) collective-permute-start(bf16[256,896]{1,0:T(8,128)(2,1)S(1)} %get-tuple-element.223), channel_id=1, source_target_pairs={{0,3},{1,2},{2,1},{3,0},{4,7},{5,6},{6,5},{7,4},{8,11},{9,10},{10,... | collective-permute-start | bytes 1376264 | tf_op jit(solution)/shard_map/ppermute | solution.py:610
  28.5 9.6 %collective-permute-start.16 = (bf16[112,224]{1,0:T(8,128)(2,1)S(1)}, bf16[112,224]{1,0:T(8,128)(2,1)S(1)}, u32[]{:S(2)}, u32[]{:S(2)}) collective-permute-start(bf16[112,224]{1,0:T(8,128)(2,1)S(1)} %copy-done.19), channel_id=1, source_target_pairs={{0,16},{4,20},{8,24},{12,28},{16,0},{20,4},{24,8},{28,12},{1,17},{... | collective-permute-start | bytes 150536 | tf_op jit(solution)/shard_map/ppermute | solution.py:700
  29.8 8.9 %collective-permute-start.17 = (bf16[112,224]{1,0:T(8,128)(2,1)S(1)}, bf16[112,224]{1,0:T(8,128)(2,1)S(1)}, u32[]{:S(2)}, u32[]{:S(2)}) collective-permute-start(bf16[112,224]{1,0:T(8,128)(2,1)S(1)} %copy-done.19), channel_id=1, source_target_pairs={{0,24},{4,28},{8,0},{12,4},{16,8},{20,12},{24,16},{28,20},{1,25},{... | collective-permute-start | bytes 150536 | tf_op jit(solution)/shard_map/ppermute | solution.py:700
  32.4 7.9 %collective-permute-start.15 = (bf16[112,224]{1,0:T(8,128)(2,1)S(1)}, bf16[112,224]{1,0:T(8,128)(2,1)S(1)}, u32[]{:S(2)}, u32[]{:S(2)}) collective-permute-start(bf16[112,224]{1,0:T(8,128)(2,1)S(1)} %copy-done.19), channel_id=1, source_target_pairs={{0,8},{4,12},{8,16},{12,20},{16,24},{20,28},{24,0},{28,4},{1,9},{5... | collective-permute-start | bytes 150536 | tf_op jit(solution)/shard_map/ppermute | solution.py:700
  32.5 15.2 %collective-permute-start.5 = (bf16[451,288]{1,0:T(8,128)(2,1)S(1)}, bf16[451,288]{1,0:T(8,128)(2,1)S(1)}, u32[]{:S(2)}, u32[]{:S(2)}) collective-permute-start(bf16[451,288]{1,0:T(8,128)(2,1)S(1)} %constant_dynamic-update-slice_fusion), channel_id=1, source_target_pairs={{0,2},{1,3},{2,0},{3,1},{4,6},{5,7},{6,4},{7,5},{8,10},{9,11},{10,... | collective-permute-start | bytes 779336 | tf_op jit(solution)/shard_map/ppermute | solution.py:610
  34.0 13.6 %collective-permute-start.6 = (bf16[451,288]{1,0:T(8,128)(2,1)S(1)}, bf16[451,288]{1,0:T(8,128)(2,1)S(1)}, u32[]{:S(2)}, u32[]{:S(2)}) collective-permute-start(bf16[451,288]{1,0:T(8,128)(2,1)S(1)} %constant_dynamic-update-slice_fusion), channel_id=1, source_target_pairs={{0,3},{1,2},{2,1},{3,0},{4,7},{5,6},{6,5},{7,4},{8,11},{9,10},{10,... | collective-permute-start | bytes 779336 | tf_op jit(solution)/shard_map/ppermute | solution.py:610
  38.1 10.8 %collective-permute-start.4 = (bf16[451,288]{1,0:T(8,128)(2,1)S(1)}, bf16[451,288]{1,0:T(8,128)(2,1)S(1)}, u32[]{:S(2)}, u32[]{:S(2)}) collective-permute-start(bf16[451,288]{1,0:T(8,128)(2,1)S(1)} %constant_dynamic-update-slice_fusion), channel_id=1, source_target_pairs={{0,1},{1,0},{2,3},{3,2},{4,5},{5,4},{6,7},{7,6},{8,9},{9,8},{10,11... | collective-permute-start | bytes 779336 | tf_op jit(solution)/shard_map/ppermute | solution.py:610
  62.7 26.4 %collective-permute-start.10 = (bf16[1,2,256,256]{3,2,1,0:T(8,128)(2,1)}, bf16[1,2,256,256]{3,2,1,0:T(8,128)(2,1)S(1)}, u32[]{:S(2)}, u32[]{:S(2)}) collective-permute-start(bf16[1,2,256,256]{3,2,1,0:T(8,128)(2,1)} %bitcast.87), channel_id=1, source_target_pairs={{0,1},{1,0},{2,3},{3,2},{4,5},{5,4},{6,7},{7,6},{8,9},{9,8},{10,11... | collective-permute-start | bytes 786440 | tf_op jit(solution)/shard_map/ppermute | solution.py:610
  63.3 25.9 %collective-permute-start.11 = (bf16[1,2,256,256]{3,2,1,0:T(8,128)(2,1)}, bf16[1,2,256,256]{3,2,1,0:T(8,128)(2,1)}, u32[]{:S(2)}, u32[]{:S(2)}) collective-permute-start(bf16[1,2,256,256]{3,2,1,0:T(8,128)(2,1)} %bitcast.88), channel_id=1, source_target_pairs={{0,2},{1,3},{2,0},{3,1},{4,6},{5,7},{6,4},{7,5},{8,10},{9,11},{10,... | collective-permute-start | bytes 786440 | tf_op jit(solution)/shard_map/ppermute | solution.py:610
  64.8 24.4 %collective-permute-start.12 = (bf16[1,2,256,256]{3,2,1,0:T(8,128)(2,1)}, bf16[1,2,256,256]{3,2,1,0:T(8,128)(2,1)}, u32[]{:S(2)}, u32[]{:S(2)}) collective-permute-start(bf16[1,2,256,256]{3,2,1,0:T(8,128)(2,1)} %bitcast.89), channel_id=1, source_target_pairs={{0,3},{1,2},{2,1},{3,0},{4,7},{5,6},{6,5},{7,4},{8,11},{9,10},{10,... | collective-permute-start | bytes 786440 | tf_op jit(solution)/shard_map/ppermute | solution.py:610
  66.3 21.1 %collective-permute-start.8 = (bf16[112,608]{1,0:T(8,128)(2,1)S(1)}, bf16[112,608]{1,0:T(8,128)(2,1)S(1)}, u32[]{:S(2)}, u32[]{:S(2)}) collective-permute-start(bf16[112,608]{1,0:T(8,128)(2,1)S(1)} %get-tuple-element.242), channel_id=1, source_target_pairs={{0,0},{1,8},{2,16},{3,24},{4,4},{5,12},{6,20},{7,28},{8,1},{9,9},{... | collective-permute-start | bytes 408584 | tf_op jit(solution)/shard_map/ppermute | solution.py:667
  69.8 18.5 %collective-permute-start.9 = (bf16[112,608]{1,0:T(8,128)(2,1)S(1)}, bf16[112,608]{1,0:T(8,128)(2,1)S(1)}, u32[]{:S(2)}, u32[]{:S(2)}) collective-permute-start(bf16[112,608]{1,0:T(8,128)(2,1)S(1)} %get-tuple-element.243), channel_id=1, source_target_pairs={{0,4},{1,12},{2,20},{3,28},{4,0},{5,8},{6,16},{7,24},{8,5},{9,13},... | collective-permute-start | bytes 408584 | tf_op jit(solution)/shard_map/ppermute | solution.py:667
  87.4 11.8 %collective-permute-start.13 = (bf16[256,896]{1,0:T(8,128)(2,1)S(1)}, bf16[256,896]{1,0:T(8,128)(2,1)S(1)}, u32[]{:S(2)}, u32[]{:S(2)}) collective-permute-start(bf16[256,896]{1,0:T(8,128)(2,1)S(1)} %get-tuple-element.221), channel_id=1, source_target_pairs={{0,1},{1,0},{2,3},{3,2},{4,5},{5,4},{6,7},{7,6},{8,9},{9,8},{10,11... | collective-permute-start | bytes 1376264 | tf_op jit(solution)/shard_map/ppermute | solution.py:610
  88.3 13.4 %collective-permute-start.14 = (bf16[256,896]{1,0:T(8,128)(2,1)S(1)}, bf16[256,896]{1,0:T(8,128)(2,1)S(1)}, u32[]{:S(2)}, u32[]{:S(2)}) collective-permute-start(bf16[256,896]{1,0:T(8,128)(2,1)S(1)} %get-tuple-element.220), channel_id=1, source_target_pairs={{0,2},{1,3},{2,0},{3,1},{4,6},{5,7},{6,4},{7,5},{8,10},{9,11},{10,... | collective-permute-start | bytes 1376264 | tf_op jit(solution)/shard_map/ppermute | solution.py:610
  101.7 250.8 %reduce-scatter.5.cloned.1.call-start = ((), (), s32[]{:S(2)}) async-start(), calls=%async_computation.3 | async-start | bytes 7741440 | tf_op jit(solution)/shard_map/reduce_scatter | solution.py:823
  102.4 34.8 %collective-permute-start.18 = (bf16[512,896]{1,0:T(8,128)(2,1)S(1)}, bf16[512,896]{1,0:T(8,128)(2,1)S(1)}, u32[]{:S(2)}, u32[]{:S(2)}) collective-permute-start(bf16[512,896]{1,0:T(8,128)(2,1)S(1)} %pad_maximum_fusion.4), channel_id=1, source_target_pairs={{0,2},{1,3},{2,0},{3,1},{4,6},{5,7},{6,4},{7,5},{8,10},{9,11},{10,... | collective-permute-start | bytes 2752520 | tf_op jit(solution)/shard_map/ppermute | solution.py:610
  103.5 33.7 %collective-permute-start.19 = (bf16[512,896]{1,0:T(8,128)(2,1)}, bf16[512,896]{1,0:T(8,128)(2,1)S(1)}, u32[]{:S(2)}, u32[]{:S(2)}) collective-permute-start(bf16[512,896]{1,0:T(8,128)(2,1)} %pad_maximum_fusion.6), channel_id=1, source_target_pairs={{0,1},{1,0},{2,3},{3,2},{4,5},{5,4},{6,7},{7,6},{8,9},{9,8},{10,11... | collective-permute-start | bytes 2752520 | tf_op jit(solution)/shard_map/ppermute | solution.py:610
  104.1 31.4 %collective-permute-start.20 = (bf16[448,224]{1,0:T(8,128)(2,1)S(1)}, bf16[448,224]{1,0:T(8,128)(2,1)S(1)}, u32[]{:S(2)}, u32[]{:S(2)}) collective-permute-start(bf16[448,224]{1,0:T(8,128)(2,1)S(1)} %copy-done.17), channel_id=1, source_target_pairs={{0,1},{1,0},{2,3},{3,2},{4,5},{5,4},{6,7},{7,6},{8,9},{9,8},{10,11... | collective-permute-start | bytes 602120 | tf_op jit(solution)/shard_map/ppermute | solution.py:610
  106.2 29.4 %collective-permute-start.21 = (bf16[448,224]{1,0:T(8,128)(2,1)S(1)}, bf16[448,224]{1,0:T(8,128)(2,1)S(1)}, u32[]{:S(2)}, u32[]{:S(2)}) collective-permute-start(bf16[448,224]{1,0:T(8,128)(2,1)S(1)} %copy-done.17), channel_id=1, source_target_pairs={{0,2},{1,3},{2,0},{3,1},{4,6},{5,7},{6,4},{7,5},{8,10},{9,11},{10,... | collective-permute-start | bytes 602120 | tf_op jit(solution)/shard_map/ppermute | solution.py:610
  108.2 29.0 %collective-permute-start.22 = (bf16[448,224]{1,0:T(8,128)(2,1)S(1)}, bf16[448,224]{1,0:T(8,128)(2,1)}, u32[]{:S(2)}, u32[]{:S(2)}) collective-permute-start(bf16[448,224]{1,0:T(8,128)(2,1)S(1)} %copy-done.17), channel_id=1, source_target_pairs={{0,3},{1,2},{2,1},{3,0},{4,7},{5,6},{6,5},{7,4},{8,11},{9,10},{10,... | collective-permute-start | bytes 602120 | tf_op jit(solution)/shard_map/ppermute | solution.py:610
  146.4 23.4 %collective-permute-start.26 = (bf16[512,896]{1,0:T(8,128)(2,1)}, bf16[512,896]{1,0:T(8,128)(2,1)S(1)}, u32[]{:S(2)}, u32[]{:S(2)}) collective-permute-start(bf16[512,896]{1,0:T(8,128)(2,1)} %multiply_convert_fusion.x_low.x_high), channel_id=1, source_target_pairs={{0,1},{1,0},{2,3},{3,2},{4,5},{5,4},{6,7},{7,6},{8,9},{9,8},{10,11... | collective-permute-start | bytes 2752520 | tf_op jit(solution)/shard_map/ppermute | solution.py:610
  146.7 59.2 %collective-permute-start.24 = (bf16[512,896]{1,0:T(8,128)(2,1)}, bf16[512,896]{1,0:T(8,128)(2,1)}, u32[]{:S(2)}, u32[]{:S(2)}) collective-permute-start(bf16[512,896]{1,0:T(8,128)(2,1)} %multiply_convert_fusion.x_low.x_high), channel_id=1, source_target_pairs={{0,3},{1,2},{2,1},{3,0},{4,7},{5,6},{6,5},{7,4},{8,11},{9,10},{10,... | collective-permute-start | bytes 2752520 | tf_op jit(solution)/shard_map/ppermute | solution.py:610
  148.2 41.8 %collective-permute-start.25 = (bf16[512,896]{1,0:T(8,128)(2,1)}, bf16[512,896]{1,0:T(8,128)(2,1)}, u32[]{:S(2)}, u32[]{:S(2)}) collective-permute-start(bf16[512,896]{1,0:T(8,128)(2,1)} %multiply_convert_fusion.x_low.x_high), channel_id=1, source_target_pairs={{0,2},{1,3},{2,0},{3,1},{4,6},{5,7},{6,4},{7,5},{8,10},{9,11},{10,... | collective-permute-start | bytes 2752520 | tf_op jit(solution)/shard_map/ppermute | solution.py:610
  185.0 58.8 %collective-permute-start.27 = (bf16[512,896]{1,0:T(8,128)(2,1)}, bf16[512,896]{1,0:T(8,128)(2,1)S(1)}, u32[]{:S(2)}, u32[]{:S(2)}) collective-permute-start(bf16[512,896]{1,0:T(8,128)(2,1)} %get-tuple-element.127), channel_id=1, source_target_pairs={{0,1},{1,0},{2,3},{3,2},{4,5},{5,4},{6,7},{7,6},{8,9},{9,8},{10,11... | collective-permute-start | bytes 2752520 | tf_op jit(solution)/shard_map/ppermute | solution.py:610
  204.1 39.8 %collective-permute-start.28 = (bf16[512,896]{1,0:T(8,128)(2,1)}, bf16[512,896]{1,0:T(8,128)(2,1)}, u32[]{:S(2)}, u32[]{:S(2)}) collective-permute-start(bf16[512,896]{1,0:T(8,128)(2,1)} %get-tuple-element.128), channel_id=1, source_target_pairs={{0,2},{1,3},{2,0},{3,1},{4,6},{5,7},{6,4},{7,5},{8,10},{9,11},{10,... | collective-permute-start | bytes 2752520 | tf_op jit(solution)/shard_map/ppermute | solution.py:610
  219.9 23.9 %collective-permute-start.29 = (bf16[512,896]{1,0:T(8,128)(2,1)}, bf16[512,896]{1,0:T(8,128)(2,1)}, u32[]{:S(2)}, u32[]{:S(2)}) collective-permute-start(bf16[512,896]{1,0:T(8,128)(2,1)} %get-tuple-element.129), channel_id=1, source_target_pairs={{0,3},{1,2},{2,1},{3,0},{4,7},{5,6},{6,5},{7,4},{8,11},{9,10},{10,... | collective-permute-start | bytes 2752520 | tf_op jit(solution)/shard_map/ppermute | solution.py:610
  244.8 138.9 %reduce-scatter.3.cloned.1.call-start = ((), (), s32[]{:S(2)}) async-start(), calls=%async_computation.2 | async-start | bytes 4128768 | tf_op jit(solution)/shard_map/reduce_scatter | solution.py:869
  255.6 39.8 %collective-permute-start.30 = (bf16[512,896]{1,0:T(8,128)(2,1)}, bf16[512,896]{1,0:T(8,128)(2,1)S(1)}, u32[]{:S(2)}, u32[]{:S(2)}) collective-permute-start(bf16[512,896]{1,0:T(8,128)(2,1)} %get-tuple-element.140), channel_id=1, source_target_pairs={{0,1},{1,0},{2,3},{3,2},{4,5},{5,4},{6,7},{7,6},{8,9},{9,8},{10,11... | collective-permute-start | bytes 2752520 | tf_op jit(solution)/shard_map/ppermute | solution.py:610
  256.0 39.5 %collective-permute-start.31 = (bf16[512,896]{1,0:T(8,128)(2,1)}, bf16[512,896]{1,0:T(8,128)(2,1)}, u32[]{:S(2)}, u32[]{:S(2)}) collective-permute-start(bf16[512,896]{1,0:T(8,128)(2,1)} %get-tuple-element.141), channel_id=1, source_target_pairs={{0,2},{1,3},{2,0},{3,1},{4,6},{5,7},{6,4},{7,5},{8,10},{9,11},{10,... | collective-permute-start | bytes 2752520 | tf_op jit(solution)/shard_map/ppermute | solution.py:610
  257.7 37.8 %collective-permute-start.32 = (bf16[512,896]{1,0:T(8,128)(2,1)}, bf16[512,896]{1,0:T(8,128)(2,1)}, u32[]{:S(2)}, u32[]{:S(2)}) collective-permute-start(bf16[512,896]{1,0:T(8,128)(2,1)} %get-tuple-element.142), channel_id=1, source_target_pairs={{0,3},{1,2},{2,1},{3,0},{4,7},{5,6},{6,5},{7,4},{8,11},{9,10},{10,... | collective-permute-start | bytes 2752520 | tf_op jit(solution)/shard_map/ppermute | solution.py:610
  297.8 6.4 %collective-permute-start.33 = (bf16[1,2,256,256]{3,2,1,0:T(8,128)(2,1)S(1)}, bf16[1,2,256,256]{3,2,1,0:T(8,128)(2,1)S(1)}, u32[]{:S(2)}, u32[]{:S(2)}) collective-permute-start(bf16[1,2,256,256]{3,2,1,0:T(8,128)(2,1)S(1)} %get-tuple-element.212), channel_id=1, source_target_pairs={{0,1},{1,0},{2,3},{3,2},{4,5},{5,4},{6,7},{7,6},{8,9},{9,8},{10,11... | collective-permute-start | bytes 786440 | tf_op jit(solution)/shard_map/ppermute | solution.py:610
  298.1 9.2 %collective-permute-start.34 = (bf16[1,2,256,256]{3,2,1,0:T(8,128)(2,1)S(1)}, bf16[1,2,256,256]{3,2,1,0:T(8,128)(2,1)S(1)}, u32[]{:S(2)}, u32[]{:S(2)}) collective-permute-start(bf16[1,2,256,256]{3,2,1,0:T(8,128)(2,1)S(1)} %get-tuple-element.211), channel_id=1, source_target_pairs={{0,2},{1,3},{2,0},{3,1},{4,6},{5,7},{6,4},{7,5},{8,10},{9,11},{10,... | collective-permute-start | bytes 786440 | tf_op jit(solution)/shard_map/ppermute | solution.py:610
  299.8 7.4 %collective-permute-start.35 = (bf16[1,2,256,256]{3,2,1,0:T(8,128)(2,1)S(1)}, bf16[1,2,256,256]{3,2,1,0:T(8,128)(2,1)S(1)}, u32[]{:S(2)}, u32[]{:S(2)}) collective-permute-start(bf16[1,2,256,256]{3,2,1,0:T(8,128)(2,1)S(1)} %get-tuple-element.210), channel_id=1, source_target_pairs={{0,3},{1,2},{2,1},{3,0},{4,7},{5,6},{6,5},{7,4},{8,11},{9,10},{10,... | collective-permute-start | bytes 786440 | tf_op jit(solution)/shard_map/ppermute | solution.py:610
  325.4 24.0 %collective-permute-start.36 = (bf16[256,896]{1,0:T(8,128)(2,1)}, bf16[256,896]{1,0:T(8,128)(2,1)}, u32[]{:S(2)}, u32[]{:S(2)}) collective-permute-start(bf16[256,896]{1,0:T(8,128)(2,1)} %get-tuple-element.215), channel_id=1, source_target_pairs={{0,3},{1,2},{2,1},{3,0},{4,7},{5,6},{6,5},{7,4},{8,11},{9,10},{10,... | collective-permute-start | bytes 1376264 | tf_op jit(solution)/shard_map/ppermute | solution.py:610
  327.1 8.7 %collective-permute-start.40 = (f32[1,736]{1,0:T(1,128)S(1)}, f32[1,736]{1,0:T(1,128)S(1)}, u32[]{:S(2)}, u32[]{:S(2)}) collective-permute-start(f32[1,736]{1,0:T(1,128)S(1)} %get-tuple-element.249), channel_id=1, source_target_pairs={{0,3},{1,2},{2,1},{3,0},{4,7},{5,6},{6,5},{7,4},{8,11},{9,10},{10,... | collective-permute-start | bytes 8840 | tf_op jit(solution)/shard_map/ppermute | solution.py:610
  328.7 7.1 %collective-permute-start.39 = (f32[1,736]{1,0:T(1,128)S(1)}, f32[1,736]{1,0:T(1,128)S(1)}, u32[]{:S(2)}, u32[]{:S(2)}) collective-permute-start(f32[1,736]{1,0:T(1,128)S(1)} %get-tuple-element.250), channel_id=1, source_target_pairs={{0,2},{1,3},{2,0},{3,1},{4,6},{5,7},{6,4},{7,5},{8,10},{9,11},{10,... | collective-permute-start | bytes 8840 | tf_op jit(solution)/shard_map/ppermute | solution.py:610
  331.5 19.9 %collective-permute-start.37 = (bf16[256,896]{1,0:T(8,128)(2,1)}, bf16[256,896]{1,0:T(8,128)(2,1)}, u32[]{:S(2)}, u32[]{:S(2)}) collective-permute-start(bf16[256,896]{1,0:T(8,128)(2,1)} %slice.232), channel_id=1, source_target_pairs={{0,3},{1,2},{2,1},{3,0},{4,7},{5,6},{6,5},{7,4},{8,11},{9,10},{10,... | collective-permute-start | bytes 1376264 | tf_op jit(solution)/shard_map/ppermute | solution.py:610
  342.9 6.4 %collective-permute-start.43 = (f32[1,736]{1,0:T(1,128)S(1)}, f32[1,736]{1,0:T(1,128)S(1)}, u32[]{:S(2)}, u32[]{:S(2)}) collective-permute-start(f32[1,736]{1,0:T(1,128)S(1)} %add.172), channel_id=1, source_target_pairs={{0,16},{4,20},{8,24},{12,28},{16,0},{20,4},{24,8},{28,12},{1,17},{... | collective-permute-start | bytes 8840 | tf_op jit(solution)/shard_map/ppermute | solution.py:901
  355.6 25.6 %collective-permute-start.44 = (bf16[112,608]{1,0:T(8,128)(2,1)S(1)}, bf16[112,608]{1,0:T(8,128)(2,1)S(1)}, u32[]{:S(2)}, u32[]{:S(2)}) collective-permute-start(bf16[112,608]{1,0:T(8,128)(2,1)S(1)} %get-tuple-element.227), channel_id=1, source_target_pairs={{0,0},{1,8},{2,16},{3,24},{4,4},{5,12},{6,20},{7,28},{8,1},{9,9},{... | collective-permute-start | bytes 408584 | tf_op jit(solution)/shard_map/ppermute | solution.py:667
  358.6 25.0 %collective-permute-start.45 = (bf16[112,608]{1,0:T(8,128)(2,1)S(1)}, bf16[112,608]{1,0:T(8,128)(2,1)S(1)}, u32[]{:S(2)}, u32[]{:S(2)}) collective-permute-start(bf16[112,608]{1,0:T(8,128)(2,1)S(1)} %get-tuple-element.228), channel_id=1, source_target_pairs={{0,4},{1,12},{2,20},{3,28},{4,0},{5,8},{6,16},{7,24},{8,5},{9,13},... | collective-permute-start | bytes 408584 | tf_op jit(solution)/shard_map/ppermute | solution.py:667
  384.7 7.0 %collective-permute-start.48 = (bf16[112,512]{1,0:T(8,128)(2,1)S(1)}, bf16[112,512]{1,0:T(8,128)(2,1)S(1)}, u32[]{:S(2)}, u32[]{:S(2)}) collective-permute-start(bf16[112,512]{1,0:T(8,128)(2,1)S(1)} %get-tuple-element.230), channel_id=1, source_target_pairs={{0,3},{1,2},{2,1},{3,0},{4,7},{5,6},{6,5},{7,4},{8,11},{9,10},{10,... | collective-permute-start | bytes 344072 | tf_op jit(solution)/shard_map/ppermute | solution.py:610
  384.8 7.8 %collective-permute-start.47 = (bf16[112,512]{1,0:T(8,128)(2,1)S(1)}, bf16[112,512]{1,0:T(8,128)(2,1)S(1)}, u32[]{:S(2)}, u32[]{:S(2)}) collective-permute-start(bf16[112,512]{1,0:T(8,128)(2,1)S(1)} %get-tuple-element.231), channel_id=1, source_target_pairs={{0,2},{1,3},{2,0},{3,1},{4,6},{5,7},{6,4},{7,5},{8,10},{9,11},{10,... | collective-permute-start | bytes 344072 | tf_op jit(solution)/shard_map/ppermute | solution.py:610
  384.9 7.7 %collective-permute-start.46 = (bf16[112,512]{1,0:T(8,128)(2,1)S(1)}, bf16[112,512]{1,0:T(8,128)(2,1)S(1)}, u32[]{:S(2)}, u32[]{:S(2)}) collective-permute-start(bf16[112,512]{1,0:T(8,128)(2,1)S(1)} %get-tuple-element.229), channel_id=1, source_target_pairs={{0,1},{1,0},{2,3},{3,2},{4,5},{5,4},{6,7},{7,6},{8,9},{9,8},{10,11... | collective-permute-start | bytes 344072 | tf_op jit(solution)/shard_map/ppermute | solution.py:610
  (36 other events, 168.5 us)
Sparse Core Ops, SparseCore 0:
  10.2 56.6 all-gather.4
  101.8 31.2 all-gather.6
  244.9 75.9 reduce-scatter.4
  323.0 50.3 reduce-scatter.2

commit v6 on v5

--- a/solution.py
+++ b/solution.py
@@ -675,11 +675,13 @@
             ],
         )
 
-    def crossed_parts(parts):
-        came = [
+    def send_crossed(parts):
+        return [
             crossed(pick(fold_place, [parts[(f + j) % fold] for f in range(fold)]), j)
             for j in range(fold)
         ]
+
+    def crossed_parts(came):
         return [
             pick(fold_place, [came[(f - t) % fold] for f in range(fold)]) for t in range(fold)
         ]
@@ -693,7 +695,7 @@
     ).astype(jnp.int32)
     positions = order[:2, None, None] * half + jnp.arange(half, dtype=jnp.int32)[None, None, :]
     positions = jnp.broadcast_to(positions, (2, sequences, half)).reshape(-1)
-    cosine, sine = rotation_tables(positions)
+    cosine, sine = lax.optimization_barrier(rotation_tables(positions))
 
     def from_floors(x):
         came = [x] + [
@@ -738,6 +740,10 @@
             [project_rows, jnp.pad(vectors, (0, spare)).reshape(-1, own_width)], axis=0
         )
     )
+    down_rows, down_columns = down_weight.shape
+    depth = down_columns // fold
+    down_late = lax.optimization_barrier((down_weight, project_came[1]))[0]
+    down_came = send_crossed(list(down_late.T.reshape(fold, depth, down_rows)))
     output_late = lax.optimization_barrier((output_weight, project_rows))[0]
     output_rows = from_floors(output_late)
     ordered = by_rank(project_came)
@@ -750,24 +756,20 @@
     bias_full = vector_whole(gain_width, own_width)
     feedforward_full = vector_whole(gain_width + own_width, gain_width)
     project_columns = jnp.concatenate([piece[:held] for piece in ordered], axis=1)
-    project_full = by_core(project_columns, from_other_core(project_columns))
-
-    down_late, grad_late = lax.optimization_barrier((down_weight, cotangent, project_full))[:2]
+    project_other, down_came = lax.optimization_barrier(
+        (from_other_core(project_columns), down_came)
+    )
+    project_full = by_core(project_columns, project_other)
+
+    grad_late = lax.optimization_barrier((cotangent, project_full))[0]
     grad_rows = to_rows(grad_late)
     if ctx_size == 4:
         grad_near = [hop(grad_rows[:half_rows], 4, 1), hop(grad_rows[half_rows:], 4, 2)]
     else:
         grad_near = others(grad_rows, ctx_size)
-    down_rows, down_columns = down_weight.shape
-    depth = down_columns // fold
-    down_turned = jnp.concatenate(
-        crossed_parts(list(down_late.T.reshape(fold, depth, down_rows))), axis=1
-    )
     normed, queries, pairs_mine = project_forward(
         tokens_mine, attention_full, project_full, bias_full, cosine, sine
     )
-    down_turned, gate_up = lax.optimization_barrier((down_turned, gate_up, queries))[:2]
-    down_mine = lax.all_gather(down_turned, "seq", axis=0)
     queries = attention_blocks(queries)
     pairs_mine = to_blocks(pairs_mine)
     pair_parts = [pairs_mine] + [hop(pairs_mine, ctx_size, k) for k in range(1, ctx_size)]
@@ -780,6 +782,9 @@
     else:
         grad_far = []
     output_came = from_ranks(output_rows)
+    down_came, gate_up, pair_parts = lax.optimization_barrier((down_came, gate_up, pair_parts))
+    down_turned = jnp.concatenate(crossed_parts(down_came), axis=1)
+    down_mine = lax.all_gather(down_turned, "seq", axis=0)
     queries = lax.optimization_barrier((queries, down_turned))[0]
     mixed, row_stats = attend_forward(order, queries, pair_parts)
     mixed, grad_far, output_came = lax.optimization_barrier((mixed, grad_far, output_came))
@@ -890,6 +895,11 @@
         axis=1,
     )
 
+    down_late = weight_grads[2].reshape(depth, fold, down_rows)
+    grads_came = send_crossed([down_late[:, t] for t in range(fold)])
+    sums, grads_came = lax.optimization_barrier((sums, grads_came))
+    down_out = jnp.concatenate(crossed_parts(grads_came), axis=0).T
+
     def sums_for(k):
         return lax.dynamic_index_in_dim(sums, place ^ k, 0)
 
@@ -903,9 +913,6 @@
         )
         mask *= 2
     vector_sum = vector_sum[0]
-    down_late = weight_grads[2].reshape(depth, fold, down_rows)
-    down_came = crossed_parts([down_late[:, t] for t in range(fold)])
-    down_out = jnp.concatenate(down_came, axis=0).T
     owned, layer_output, tokens_gradient, vector_sum, down_out = lax.optimization_barrier(
         (owned, layer_output, tokens_gradient, vector_sum, down_out)
     )

time: 409 us -> 437 us (1.068)
  waiting for transfers between devices: 107 us -> 138 us
    ppermute x34, waiting for transfers between devices: 50.3 us -> 69.7 us  [hop(): return lax.ppermute(x, 'ctx', [(i, i ^ mask) for i in range(ctx_size)])]
    ppermute x4, waiting for transfers between devices: 41.9 us -> 53.6 us  [crossed(): lax.ppermute(x, ('seq', 'ctx'), [((c * fold + r) * ctx_size + q, (q * fol...]
    ppermute x3, starting transfers between devices: 8.7 us -> 0.14 us  [on_device(): lax.ppermute(vector_sum, 'seq', [(i, i ^ mask) for i in range(seq_size)])]
  transfers between devices with their start and end apart: 53 -> 53, of which waited for: 25 -> 24; matrix products, arithmetic and copies ran while one was open for 12% -> 11% of each run, Pallas kernels for 40% -> 34%
where the time goes in v6:
time: 437 us; the launch traced here: 430 us
  Pallas kernels  160 us (37%)
  waiting for transfers between devices  138 us (32%)
  starting transfers between devices  57.3 us (13%)
  other arithmetic  32.4 us (7%)
  local copies, waits for them, and re-layouts  23.7 us (5%)
  between operations  15.1 us (3%)
    ppermute x34, waiting for transfers between devices, hop(): return lax.ppermute(x, 'ctx', [(i, i ^ mask) for i in range(ctx_size)])  69.7 us
    pallas_call x4, Pallas kernels, ffn(): pl.pallas_call(ffn_kernel, grid=(2,), in_specs=[half_spec(at) for _, at i...  56.2 us
    ppermute x4, waiting for transfers between devices, crossed(): lax.ppermute(x, ('seq', 'ctx'), [((c * fold + r) * ctx_size + q, (q * fol...  53.6 us
    ppermute x34, starting transfers between devices, hop(): return lax.ppermute(x, 'ctx', [(i, i ^ mask) for i in range(ctx_size)])  40 us
    pallas_call x1, Pallas kernels, attend_backward(): pl.pallas_call(backward_kernel, grid_spec=pltpu.PrefetchScalarGridSpec(nu...  36.3 us
    pallas_call x1, Pallas kernels, attend_forward(): pl.pallas_call(forward_kernel, grid_spec=pltpu.PrefetchScalarGridSpec(num...  27.3 us
    pallas_call x1, Pallas kernels, ffn_weights(): pl.pallas_call(ffn_weights_kernel, grid=(count,), in_specs=[slot(width)]...  22.4 us
  transfers between devices with their start and end apart: 53, of which 24 were waited for; matrix products, arithmetic and copies ran while one was open for 11% of the time, Pallas kernels for 34%

profile of v6, /device:TPU:2, one launch (start us, length us, event | category | flops | bytes accessed | tf_op | source)
XLA Modules:
  0.0 430.4 jit_solution(13954982430102928178)
XLA Ops:
  7.3 2.0 pad_maximum_fusion.9
  10.3 3.7 collective-permute-start.2
  17.0 4.8 %collective-permute-done.1 = bf16[112,288]{1,0:T(8,128)(2,1)S(1)} collective-permute-done((bf16[112,288]{1,0:T(8,128)(2,1)S(1)}, bf16[112,288]{1,0:T(8,128)(2,1)S(1)}, u32[]{:S(2)}, u32[]{:S(2)}) %collective-permute-start.1) | collective-permute-done | bytes 64544 | tf_op jit(solution)/shard_map/ppermute | solution.py:702
  21.9 5.5 %collective-permute-done.3 = bf16[256,896]{1,0:T(8,128)(2,1)S(1)} collective-permute-done((bf16[256,896]{1,0:T(8,128)(2,1)S(1)}, bf16[256,896]{1,0:T(8,128)(2,1)S(1)}, u32[]{:S(2)}, u32[]{:S(2)}) %collective-permute-start.3) | collective-permute-done | bytes 458784 | tf_op jit(solution)/shard_map/ppermute | solution.py:610
  34.3 3.1 collective-permute-start.17
  38.3 7.1 %collective-permute-done.4 = bf16[451,288]{1,0:T(8,128)(2,1)S(1)} collective-permute-done((bf16[451,288]{1,0:T(8,128)(2,1)S(1)}, bf16[451,288]{1,0:T(8,128)(2,1)S(1)}, u32[]{:S(2)}, u32[]{:S(2)}) %collective-permute-start.4) | collective-permute-done | bytes 259808 | tf_op jit(solution)/shard_map/ppermute | solution.py:610
  46.5 3.2 concatenate.66
  50.8 2.6 collective-permute-start.9
  53.4 2.4 collective-permute-start.8
  57.8 19.9 %collective-permute-done.9 = bf16[112,608]{1,0:T(8,128)(2,1)S(1)} collective-permute-done((bf16[112,608]{1,0:T(8,128)(2,1)S(1)}, bf16[112,608]{1,0:T(8,128)(2,1)S(1)}, u32[]{:S(2)}, u32[]{:S(2)}) %collective-permute-start.9) | collective-permute-done | bytes 136224 | tf_op jit(solution)/shard_map/ppermute | solution.py:667
  77.7 3.3 collective-permute-done.8
  83.5 4.9 %project_forward.1 = (bf16[512,896]{1,0:T(8,128)(2,1)}, bf16[512,896]{1,0:T(8,128)(2,1)}, bf16[512,256]{1,0:T(8,128)(2,1)}) custom-call(bf16[512,896]{1,0:T(8,128)(2,1)} %pad_maximum_fusion.5.x_ref, f32[1,896]{1,0:T(1,128)} %broadcast_in_dim.4.gain_ref, bf16[896,1152]{1,0:T(8,128)(2,1)} %bitcast.78, f32[1,1152]{1,0:T(1,128)} %broadcast_in_dim.5.bias_ref, ...), custom_call_target="tpu_custom_call" | custom-call | flops 2113929216 | bytes 5242880 | tf_op jit(solution)/shard_map/project_forward/pallas_call | solution.py:102
  88.4 3.4 collective-permute-start.12
  93.4 10.6 %collective-permute-done.12.rest_3_ = bf16[1,2,256,256]{3,2,1,0:T(8,128)(2,1)S(1)} collective-permute-done((bf16[1,2,256,256]{3,2,1,0:T(8,128)(2,1)}, bf16[1,2,256,256]{3,2,1,0:T(8,128)(2,1)S(1)}, u32[]{:S(2)}, u32[]{:S(2)}) %collective-permute-start.12) | collective-permute-done | bytes 262176 | tf_op jit(solution)/shard_map/ppermute | solution.py:610
  104.0 3.0 collective-permute-done.11.rest_2_
  116.7 27.3 %attend_forward.1 = (bf16[2,256,896]{2,1,0:T(8,128)(2,1)}, f32[2,16,256]{2,1,0:T(8,128)}) custom-call(s32[8]{0:T(128)} %stack.54.order_ref, bf16[2,256,896]{2,1,0:T(8,128)(2,1)} %bitcast.99, bf16[1,2,256,256]{3,2,1,0:T(8,128)(2,1)} %bitcast.94, bf16[1,2,256,256]{3,2,1,0:T(8,128)(2,1)} %copy-done.25, bf16[1,2,256,256]{3,2,1,0:T(8,128)(2,1)} %copy-done.24, ...), custom_call_target="tpu_custom_call" | custom-call | flops 9395240960 | bytes 4194304 | tf_op jit(solution)/shard_map/attend_forward/pallas_call | solution.py:440
  145.9 2.2 collective-permute-done.23
  156.7 13.9 %ffn.4 = (bf16[512,896]{1,0:T(8,128)(2,1)}, bf16[512,896]{1,0:T(8,128)(2,1)}, bf16[4,512,896]{2,1,0:T(8,128)(2,1)}, bf16[4,512,896]{2,1,0:T(8,128)(2,1)}, bf16[4...) custom-call(bf16[512,896]{1,0:T(8,128)(2,1)} %multiply_convert_fusion.x_low.x_high, ...), custom_call_target="tpu_custom_call" | custom-call | flops 7809794048 | bytes 16777216 | tf_op jit(solution)/shard_map/ffn/pallas_call | solution.py:548
  170.6 6.2 %collective-permute-done.26.x_low.x_high = bf16[512,896]{1,0:T(8,128)(2,1)} collective-permute-done((bf16[512,896]{1,0:T(8,128)(2,1)}, bf16[512,896]{1,0:T(8,128)(2,1)}, u32[]{:S(2)}, u32[]{:S(2)}) %collective-permute-start.26) | collective-permute-done | bytes 917536 | tf_op jit(solution)/shard_map/ppermute | solution.py:610
  176.8 14.3 %ffn.5 = (bf16[512,896]{1,0:T(8,128)(2,1)}, bf16[512,896]{1,0:T(8,128)(2,1)}, bf16[4,512,896]{2,1,0:T(8,128)(2,1)}, bf16[4,512,896]{2,1,0:T(8,128)(2,1)}, bf16[4...) custom-call(bf16[512,896]{1,0:T(8,128)(2,1)} %collective-permute-don, ...), custom_call_target="tpu_custom_call", output_to_operand_aliasing={{2}: (6, {}), {3}: (7, {}), {4}: (8, {}), {5}: (9, {}), {6}... | custom-call | flops 7809794048 | bytes 16777216 | tf_op jit(solution)/shard_map/ffn/pallas_call | solution.py:548
  191.0 6.0 %collective-permute-done.25.x_low.x_high = bf16[512,896]{1,0:T(8,128)(2,1)} collective-permute-done((bf16[512,896]{1,0:T(8,128)(2,1)}, bf16[512,896]{1,0:T(8,128)(2,1)}, u32[]{:S(2)}, u32[]{:S(2)}) %collective-permute-start.25) | collective-permute-done | bytes 917536 | tf_op jit(solution)/shard_map/ppermute | solution.py:610
  197.1 14.1 %ffn.6 = (bf16[512,896]{1,0:T(8,128)(2,1)}, bf16[512,896]{1,0:T(8,128)(2,1)}, bf16[4,512,896]{2,1,0:T(8,128)(2,1)}, bf16[4,512,896]{2,1,0:T(8,128)(2,1)}, bf16[4...) custom-call(bf16[512,896]{1,0:T(8,128)(2,1)} %collective-permute-don, ...), custom_call_target="tpu_custom_call", output_to_operand_aliasing={{2}: (6, {}), {3}: (7, {}), {4}: (8, {}), {5}: (9, {}), {6}... | custom-call | flops 7809794048 | bytes 16777216 | tf_op jit(solution)/shard_map/ffn/pallas_call | solution.py:548
  212.1 14.0 %ffn.7 = (bf16[512,896]{1,0:T(8,128)(2,1)}, bf16[512,896]{1,0:T(8,128)(2,1)}, bf16[4,512,896]{2,1,0:T(8,128)(2,1)}, bf16[4,512,896]{2,1,0:T(8,128)(2,1)}, bf16[4...) custom-call(bf16[512,896]{1,0:T(8,128)(2,1)} %copy-done.3, ...), custom_call_target="tpu_custom_call", output_to_operand_aliasing={{2}: (6, {}), {3}: (7, {}), {4}: (8, {}), {5}: (9, {}), {6}... | custom-call | flops 7809794048 | bytes 16777216 | tf_op jit(solution)/shard_map/ffn/pallas_call | solution.py:548
  229.7 22.4 %ffn_weights.1 = bf16[8,3,112,1216]{3,2,1,0:T(8,128)(2,1)} custom-call(bf16[4,512,896]{2,1,0:T(8,128)(2,1)} %get-tuple-element.145.x_ref, bf16[4,512,896]{2,1,0:T(8,128)(2,1)} %get-tuple-element.146.c_ref, bf16[4,512,1216]{2,1,0:T(8,128)(2,1)} %get-tuple-element.147.active_ref, bf16[4,512,1216]{2,1,0:T(8,128)(2,1)} %get-tuple-element.148.gate_ref, ...), custom_call_target="tpu_custom_call" | custom-call | flops 13388218368 | bytes 31457280 | tf_op jit(solution)/shard_map/ffn_weights/pallas_call | solution.py:594
  252.1 15.4 %collective-permute-done.28 = bf16[512,896]{1,0:T(8,128)(2,1)} collective-permute-done((bf16[512,896]{1,0:T(8,128)(2,1)}, bf16[512,896]{1,0:T(8,128)(2,1)}, u32[]{:S(2)}, u32[]{:S(2)}) %collective-permute-start.28) | collective-permute-done | bytes 917536 | tf_op jit(solution)/shard_map/ppermute | solution.py:610
  267.6 2.7 multiply_reduce_fusion
  270.3 4.1 fusion.8
  274.3 2.2 convolution_convert_fusion
  278.2 1.8 collective-permute-start.32
  280.0 36.3 %attend_backward.1 = (bf16[2,256,896]{2,1,0:T(8,128)(2,1)}, bf16[1,8,256,256]{3,2,1,0:T(8,128)(2,1)}) custom-call(s32[8]{0:T(128)} %stack.54.order_ref, bf16[2,256,896]{2,1,0:T(8,128)(2,1)} %bitcast.100, bf16[2,256,896]{2,1,0:T(8,128)(2,1)} %get-tuple-element.121.o_ref, bf16[2,256,896]{2,1,0:T(8,128)(2,1)} %bitcast.105, ...), custom_call_target="tpu_custom_call" | custom-call | flops 23488102400 | bytes 8388608 | tf_op jit(solution)/shard_map/attend_backward/pallas_call | solution.py:472
  318.4 2.0 fusion.9
  320.4 1.7 collective-permute-start.35
  323.9 6.4 %collective-permute-done.35 = bf16[1,2,256,256]{3,2,1,0:T(8,128)(2,1)S(1)} collective-permute-done((bf16[1,2,256,256]{3,2,1,0:T(8,128)(2,1)S(1)}, bf16[1,2,256,256]{3,2,1,0:T(8,128)(2,1)S(1)}, u32[]{:S(2)}, u32[]{:S(2)}) %collective-permute-start.35) | collective-permute-done | bytes 262176 | tf_op jit(solution)/shard_map/ppermute | solution.py:610
  330.2 2.8 collective-permute-done.34
  333.8 6.5 %project_backward.1 = (bf16[512,256]{1,0:T(8,128)(2,1)}, f32[512,896]{1,0:T(8,128)}, f32[1,896]{1,0:T(1,128)}, f32[1,1152]{1,0:T(1,128)}) custom-call(bf16[512,896]{1,0:T(8,128)(2,1)} %bitcast.103, bf16[896,1152]{1,0:T(8,128)(2,1)} %bitcast.79, bf16[512,896]{1,0:T(8,128)(2,1)} %pad_maximum_fusion.5.x_ref, f32[1,896]{1,0:T(1,128)} %broadcast_in_dim.4.gain_ref, ...), custom_call_target="tpu_custom_call" | custom-call | flops 2113929216 | bytes 8388608 | tf_op jit(solution)/shard_map/project_backward/pallas_call | solution.py:162
  340.3 6.4 %owned_weights.1 = bf16[896,2048]{1,0:T(8,128)(2,1)} custom-call(bf16[512,896]{1,0:T(8,128)(2,1)} %get-tuple-element.103.normed_ref, bf16[512,896]{1,0:T(8,128)(2,1)} %bitcast.104, bf16[512,256]{1,0:T(8,128)(2,1)} %get-tuple-element.167.gkv_ref, bf16[512,896]{1,0:T(8,128)(2,1)} %bitcast.101, bf16[512,896]{1,0:T(8,128)(2,1)} %copy-done.14), custom_call_target="tpu_custom_call" | custom-call | flops 3758096384 | bytes 8388608 | tf_op jit(solution)/shard_map/owned_weights/pallas_call | solution.py:216
  348.0 2.2 add_convert_fusion
  351.1 2.6 collective-permute-start.36
  355.3 2.2 fusion
  359.1 2.8 collective-permute-start.38
  362.3 26.1 %collective-permute-done.39 = bf16[112,608]{1,0:T(8,128)(2,1)S(1)} collective-permute-done((bf16[112,608]{1,0:T(8,128)(2,1)}, bf16[112,608]{1,0:T(8,128)(2,1)S(1)}, u32[]{:S(2)}, u32[]{:S(2)}) %collective-permute-start.39) | collective-permute-done | bytes 136224 | tf_op jit(solution)/shard_map/ppermute | solution.py:667
  388.4 4.3 %collective-permute-done.38 = bf16[112,608]{1,0:T(8,128)(2,1)S(1)} collective-permute-done((bf16[112,608]{1,0:T(8,128)(2,1)}, bf16[112,608]{1,0:T(8,128)(2,1)S(1)}, u32[]{:S(2)}, u32[]{:S(2)}) %collective-permute-start.38) | collective-permute-done | bytes 136224 | tf_op jit(solution)/shard_map/ppermute | solution.py:667
  392.9 3.4 collective-permute-start.41
  396.3 2.0 pad_maximum_fusion.7
  401.1 3.5 collective-permute-done.44
  404.6 4.5 %collective-permute-done.45 = f32[1,736]{1,0:T(1,128)S(1)} collective-permute-done((f32[1,736]{1,0:T(1,128)S(1)}, f32[1,736]{1,0:T(1,128)S(1)}, u32[]{:S(2)}, u32[]{:S(2)}) %collective-permute-start.45) | collective-permute-done | bytes 2976 | tf_op jit(solution)/shard_map/ppermute | solution.py:911
  411.2 3.8 collective-permute-start.48
  416.9 2.9 collective-permute-done.48
  (230 shorter events, 67.0 us)
Async XLA Ops:
  7.2 100.7 %all-gather.5.cloned.1.call-start = ((), (), s32[]{:S(2)}) async-start(), calls=%async_computation.4 | async-start | bytes 5160960 | tf_op jit(solution)/shard_map/all_gather | solution.py:729
  9.3 147.5 %all-gather.7.cloned.1.call-start = ((), (), s32[]{:S(2)}) async-start(), calls=%async_computation.5 | async-start | bytes 2580480 | tf_op jit(solution)/shard_map/all_gather | solution.py:787
  10.3 6.6 %collective-permute-start.2 = (bf16[112,288]{1,0:T(8,128)(2,1)S(1)}, bf16[112,288]{1,0:T(8,128)(2,1)S(1)}, u32[]{:S(2)}, u32[]{:S(2)}) collective-permute-start(bf16[112,288]{1,0:T(8,128)(2,1)S(1)} %copy.63), channel_id=1, source_target_pairs={{0,24},{4,28},{8,0},{12,4},{16,8},{20,12},{24,16},{28,20},{1,25},{... | collective-permute-start | bytes 193544 | tf_op jit(solution)/shard_map/ppermute | solution.py:702
  14.0 7.8 %collective-permute-start.1 = (bf16[112,288]{1,0:T(8,128)(2,1)S(1)}, bf16[112,288]{1,0:T(8,128)(2,1)S(1)}, u32[]{:S(2)}, u32[]{:S(2)}) collective-permute-start(bf16[112,288]{1,0:T(8,128)(2,1)S(1)} %copy.63), channel_id=1, source_target_pairs={{0,16},{4,20},{8,24},{12,28},{16,0},{20,4},{24,8},{28,12},{1,17},{... | collective-permute-start | bytes 193544 | tf_op jit(solution)/shard_map/ppermute | solution.py:702
  14.0 7.8 %collective-permute-start = (bf16[112,288]{1,0:T(8,128)(2,1)S(1)}, bf16[112,288]{1,0:T(8,128)(2,1)S(1)}, u32[]{:S(2)}, u32[]{:S(2)}) collective-permute-start(bf16[112,288]{1,0:T(8,128)(2,1)S(1)} %copy.63), channel_id=1, source_target_pairs={{0,8},{4,12},{8,16},{12,20},{16,24},{20,28},{24,0},{28,4},{1,9},{5... | collective-permute-start | bytes 193544 | tf_op jit(solution)/shard_map/ppermute | solution.py:702
  15.1 12.4 %collective-permute-start.3 = (bf16[256,896]{1,0:T(8,128)(2,1)S(1)}, bf16[256,896]{1,0:T(8,128)(2,1)S(1)}, u32[]{:S(2)}, u32[]{:S(2)}) collective-permute-start(bf16[256,896]{1,0:T(8,128)(2,1)S(1)} %get-tuple-element.249), channel_id=1, source_target_pairs={{0,3},{1,2},{2,1},{3,0},{4,7},{5,6},{6,5},{7,4},{8,11},{9,10},{10,... | collective-permute-start | bytes 1376264 | tf_op jit(solution)/shard_map/ppermute | solution.py:610
  28.5 16.8 %collective-permute-start.6 = (bf16[451,288]{1,0:T(8,128)(2,1)S(1)}, bf16[451,288]{1,0:T(8,128)(2,1)S(1)}, u32[]{:S(2)}, u32[]{:S(2)}) collective-permute-start(bf16[451,288]{1,0:T(8,128)(2,1)S(1)} %constant_dynamic-update-slice_fusion), channel_id=1, source_target_pairs={{0,3},{1,2},{2,1},{3,0},{4,7},{5,6},{6,5},{7,4},{8,11},{9,10},{10,... | collective-permute-start | bytes 779336 | tf_op jit(solution)/shard_map/ppermute | solution.py:610
  30.1 15.3 %collective-permute-start.5 = (bf16[451,288]{1,0:T(8,128)(2,1)S(1)}, bf16[451,288]{1,0:T(8,128)(2,1)S(1)}, u32[]{:S(2)}, u32[]{:S(2)}) collective-permute-start(bf16[451,288]{1,0:T(8,128)(2,1)S(1)} %constant_dynamic-update-slice_fusion), channel_id=1, source_target_pairs={{0,2},{1,3},{2,0},{3,1},{4,6},{5,7},{6,4},{7,5},{8,10},{9,11},{10,... | collective-permute-start | bytes 779336 | tf_op jit(solution)/shard_map/ppermute | solution.py:610
  30.6 14.8 %collective-permute-start.4 = (bf16[451,288]{1,0:T(8,128)(2,1)S(1)}, bf16[451,288]{1,0:T(8,128)(2,1)S(1)}, u32[]{:S(2)}, u32[]{:S(2)}) collective-permute-start(bf16[451,288]{1,0:T(8,128)(2,1)S(1)} %constant_dynamic-update-slice_fusion), channel_id=1, source_target_pairs={{0,1},{1,0},{2,3},{3,2},{4,5},{5,4},{6,7},{7,6},{8,9},{9,8},{10,11... | collective-permute-start | bytes 779336 | tf_op jit(solution)/shard_map/ppermute | solution.py:610
  34.3 54.1 %collective-permute-start.17 = (bf16[112,224]{1,0:T(8,128)(2,1)S(1)}, bf16[112,224]{1,0:T(8,128)(2,1)}, u32[]{:S(2)}, u32[]{:S(2)}) collective-permute-start(bf16[112,224]{1,0:T(8,128)(2,1)S(1)} %copy-done.17), channel_id=1, source_target_pairs={{0,24},{4,28},{8,0},{12,4},{16,8},{20,12},{24,16},{28,20},{1,25},{... | collective-permute-start | bytes 150536 | tf_op jit(solution)/shard_map/ppermute | solution.py:702
  37.4 54.4 %collective-permute-start.16 = (bf16[112,224]{1,0:T(8,128)(2,1)S(1)}, bf16[112,224]{1,0:T(8,128)(2,1)}, u32[]{:S(2)}, u32[]{:S(2)}) collective-permute-start(bf16[112,224]{1,0:T(8,128)(2,1)S(1)} %copy-done.17), channel_id=1, source_target_pairs={{0,16},{4,20},{8,24},{12,28},{16,0},{20,4},{24,8},{28,12},{1,17},{... | collective-permute-start | bytes 150536 | tf_op jit(solution)/shard_map/ppermute | solution.py:702
  49.7 31.3 %collective-permute-start.7 = (bf16[448,1152]{1,0:T(8,128)(2,1)S(1)}, bf16[448,1152]{1,0:T(8,128)(2,1)S(1)}, u32[]{:S(2)}, u32[]{:S(2)}) collective-permute-start(bf16[448,1152]{1,0:T(8,128)(2,1)S(1)} %concatenate.66), channel_id=1, source_target_pairs={{0,4},{4,0},{8,12},{12,8},{16,20},{20,16},{24,28},{28,24},{1,5},{5... | collective-permute-start | bytes 3096584 | tf_op jit(solution)/shard_map/ppermute | solution.py:720
  50.8 26.9 %collective-permute-start.9 = (bf16[112,608]{1,0:T(8,128)(2,1)S(1)}, bf16[112,608]{1,0:T(8,128)(2,1)S(1)}, u32[]{:S(2)}, u32[]{:S(2)}) collective-permute-start(bf16[112,608]{1,0:T(8,128)(2,1)S(1)} %get-tuple-element.268), channel_id=1, source_target_pairs={{0,4},{1,12},{2,20},{3,28},{4,0},{5,8},{6,16},{7,24},{8,5},{9,13},... | collective-permute-start | bytes 408584 | tf_op jit(solution)/shard_map/ppermute | solution.py:667
  53.4 27.5 %collective-permute-start.8 = (bf16[112,608]{1,0:T(8,128)(2,1)S(1)}, bf16[112,608]{1,0:T(8,128)(2,1)S(1)}, u32[]{:S(2)}, u32[]{:S(2)}) collective-permute-start(bf16[112,608]{1,0:T(8,128)(2,1)S(1)} %get-tuple-element.269), channel_id=1, source_target_pairs={{0,0},{1,8},{2,16},{3,24},{4,4},{5,12},{6,20},{7,28},{8,1},{9,9},{... | collective-permute-start | bytes 408584 | tf_op jit(solution)/shard_map/ppermute | solution.py:667
  77.7 14.2 %collective-permute-start.15 = (bf16[112,224]{1,0:T(8,128)(2,1)S(1)}, bf16[112,224]{1,0:T(8,128)(2,1)S(1)}, u32[]{:S(2)}, u32[]{:S(2)}) collective-permute-start(bf16[112,224]{1,0:T(8,128)(2,1)S(1)} %copy-done.17), channel_id=1, source_target_pairs={{0,8},{4,12},{8,16},{12,20},{16,24},{20,28},{24,0},{28,4},{1,9},{5... | collective-permute-start | bytes 150536 | tf_op jit(solution)/shard_map/ppermute | solution.py:702
  83.4 23.8 %collective-permute-start.14 = (bf16[256,896]{1,0:T(8,128)(2,1)S(1)}, bf16[256,896]{1,0:T(8,128)(2,1)S(1)}, u32[]{:S(2)}, u32[]{:S(2)}) collective-permute-start(bf16[256,896]{1,0:T(8,128)(2,1)S(1)} %get-tuple-element.246), channel_id=1, source_target_pairs={{0,2},{1,3},{2,0},{3,1},{4,6},{5,7},{6,4},{7,5},{8,10},{9,11},{10,... | collective-permute-start | bytes 1376264 | tf_op jit(solution)/shard_map/ppermute | solution.py:610
  83.4 24.4 %collective-permute-start.13 = (bf16[256,896]{1,0:T(8,128)(2,1)S(1)}, bf16[256,896]{1,0:T(8,128)(2,1)S(1)}, u32[]{:S(2)}, u32[]{:S(2)}) collective-permute-start(bf16[256,896]{1,0:T(8,128)(2,1)S(1)} %get-tuple-element.247), channel_id=1, source_target_pairs={{0,1},{1,0},{2,3},{3,2},{4,5},{5,4},{6,7},{7,6},{8,9},{9,8},{10,11... | collective-permute-start | bytes 1376264 | tf_op jit(solution)/shard_map/ppermute | solution.py:610
  88.4 15.6 %collective-permute-start.12 = (bf16[1,2,256,256]{3,2,1,0:T(8,128)(2,1)}, bf16[1,2,256,256]{3,2,1,0:T(8,128)(2,1)S(1)}, u32[]{:S(2)}, u32[]{:S(2)}) collective-permute-start(bf16[1,2,256,256]{3,2,1,0:T(8,128)(2,1)} %bitcast.91), channel_id=1, source_target_pairs={{0,3},{1,2},{2,1},{3,0},{4,7},{5,6},{6,5},{7,4},{8,11},{9,10},{10,... | collective-permute-start | bytes 786440 | tf_op jit(solution)/shard_map/ppermute | solution.py:610
  91.8 15.2 %collective-permute-start.11 = (bf16[1,2,256,256]{3,2,1,0:T(8,128)(2,1)}, bf16[1,2,256,256]{3,2,1,0:T(8,128)(2,1)S(1)}, u32[]{:S(2)}, u32[]{:S(2)}) collective-permute-start(bf16[1,2,256,256]{3,2,1,0:T(8,128)(2,1)} %bitcast.92), channel_id=1, source_target_pairs={{0,2},{1,3},{2,0},{3,1},{4,6},{5,7},{6,4},{7,5},{8,10},{9,11},{10,... | collective-permute-start | bytes 786440 | tf_op jit(solution)/shard_map/ppermute | solution.py:610
  91.9 15.2 %collective-permute-start.10 = (bf16[1,2,256,256]{3,2,1,0:T(8,128)(2,1)}, bf16[1,2,256,256]{3,2,1,0:T(8,128)(2,1)S(1)}, u32[]{:S(2)}, u32[]{:S(2)}) collective-permute-start(bf16[1,2,256,256]{3,2,1,0:T(8,128)(2,1)} %bitcast.93), channel_id=1, source_target_pairs={{0,1},{1,0},{2,3},{3,2},{4,5},{5,4},{6,7},{7,6},{8,9},{9,8},{10,11... | collective-permute-start | bytes 786440 | tf_op jit(solution)/shard_map/ppermute | solution.py:610
  108.9 246.4 %reduce-scatter.5.cloned.1.call-start = ((), (), s32[]{:S(2)}) async-start(), calls=%async_computation.3 | async-start | bytes 7741440 | tf_op jit(solution)/shard_map/reduce_scatter | solution.py:828
  110.5 33.5 %collective-permute-start.18 = (bf16[512,896]{1,0:T(8,128)(2,1)S(1)}, bf16[512,896]{1,0:T(8,128)(2,1)S(1)}, u32[]{:S(2)}, u32[]{:S(2)}) collective-permute-start(bf16[512,896]{1,0:T(8,128)(2,1)S(1)} %pad_maximum_fusion.4), channel_id=1, source_target_pairs={{0,2},{1,3},{2,0},{3,1},{4,6},{5,7},{6,4},{7,5},{8,10},{9,11},{10,... | collective-permute-start | bytes 2752520 | tf_op jit(solution)/shard_map/ppermute | solution.py:610
  112.3 31.7 %collective-permute-start.19 = (bf16[512,896]{1,0:T(8,128)(2,1)}, bf16[512,896]{1,0:T(8,128)(2,1)S(1)}, u32[]{:S(2)}, u32[]{:S(2)}) collective-permute-start(bf16[512,896]{1,0:T(8,128)(2,1)} %pad_maximum_fusion.6), channel_id=1, source_target_pairs={{0,1},{1,0},{2,3},{3,2},{4,5},{5,4},{6,7},{7,6},{8,9},{9,8},{10,11... | collective-permute-start | bytes 2752520 | tf_op jit(solution)/shard_map/ppermute | solution.py:610
  113.2 30.8 %collective-permute-start.22 = (bf16[448,224]{1,0:T(8,128)(2,1)S(1)}, bf16[448,224]{1,0:T(8,128)(2,1)S(1)}, u32[]{:S(2)}, u32[]{:S(2)}) collective-permute-start(bf16[448,224]{1,0:T(8,128)(2,1)S(1)} %pad_maximum_fusion.14), channel_id=1, source_target_pairs={{0,3},{1,2},{2,1},{3,0},{4,7},{5,6},{6,5},{7,4},{8,11},{9,10},{10,... | collective-permute-start | bytes 602120 | tf_op jit(solution)/shard_map/ppermute | solution.py:610
  114.7 29.2 %collective-permute-start.21 = (bf16[448,224]{1,0:T(8,128)(2,1)S(1)}, bf16[448,224]{1,0:T(8,128)(2,1)S(1)}, u32[]{:S(2)}, u32[]{:S(2)}) collective-permute-start(bf16[448,224]{1,0:T(8,128)(2,1)S(1)} %pad_maximum_fusion.14), channel_id=1, source_target_pairs={{0,2},{1,3},{2,0},{3,1},{4,6},{5,7},{6,4},{7,5},{8,10},{9,11},{10,... | collective-permute-start | bytes 602120 | tf_op jit(solution)/shard_map/ppermute | solution.py:610
  116.4 27.6 %collective-permute-start.20 = (bf16[448,224]{1,0:T(8,128)(2,1)S(1)}, bf16[448,224]{1,0:T(8,128)(2,1)}, u32[]{:S(2)}, u32[]{:S(2)}) collective-permute-start(bf16[448,224]{1,0:T(8,128)(2,1)S(1)} %pad_maximum_fusion.14), channel_id=1, source_target_pairs={{0,1},{1,0},{2,3},{3,2},{4,5},{5,4},{6,7},{7,6},{8,9},{9,8},{10,11... | collective-permute-start | bytes 602120 | tf_op jit(solution)/shard_map/ppermute | solution.py:610
  153.2 23.5 %collective-permute-start.26 = (bf16[512,896]{1,0:T(8,128)(2,1)}, bf16[512,896]{1,0:T(8,128)(2,1)}, u32[]{:S(2)}, u32[]{:S(2)}) collective-permute-start(bf16[512,896]{1,0:T(8,128)(2,1)} %multiply_convert_fusion.x_low.x_high), channel_id=1, source_target_pairs={{0,1},{1,0},{2,3},{3,2},{4,5},{5,4},{6,7},{7,6},{8,9},{9,8},{10,11... | collective-permute-start | bytes 2752520 | tf_op jit(solution)/shard_map/ppermute | solution.py:610
  155.0 42.1 %collective-permute-start.25 = (bf16[512,896]{1,0:T(8,128)(2,1)}, bf16[512,896]{1,0:T(8,128)(2,1)}, u32[]{:S(2)}, u32[]{:S(2)}) collective-permute-start(bf16[512,896]{1,0:T(8,128)(2,1)} %multiply_convert_fusion.x_low.x_high), channel_id=1, source_target_pairs={{0,2},{1,3},{2,0},{3,1},{4,6},{5,7},{6,4},{7,5},{8,10},{9,11},{10,... | collective-permute-start | bytes 2752520 | tf_op jit(solution)/shard_map/ppermute | solution.py:610
  155.3 55.8 %collective-permute-start.24 = (bf16[512,896]{1,0:T(8,128)(2,1)}, bf16[512,896]{1,0:T(8,128)(2,1)S(1)}, u32[]{:S(2)}, u32[]{:S(2)}) collective-permute-start(bf16[512,896]{1,0:T(8,128)(2,1)} %multiply_convert_fusion.x_low.x_high), channel_id=1, source_target_pairs={{0,3},{1,2},{2,1},{3,0},{4,7},{5,6},{6,5},{7,4},{8,11},{9,10},{10,... | collective-permute-start | bytes 2752520 | tf_op jit(solution)/shard_map/ppermute | solution.py:610
  226.1 26.0 %collective-permute-start.29 = (bf16[512,896]{1,0:T(8,128)(2,1)}, bf16[512,896]{1,0:T(8,128)(2,1)}, u32[]{:S(2)}, u32[]{:S(2)}) collective-permute-start(bf16[512,896]{1,0:T(8,128)(2,1)} %get-tuple-element.152), channel_id=1, source_target_pairs={{0,3},{1,2},{2,1},{3,0},{4,7},{5,6},{6,5},{7,4},{8,11},{9,10},{10,... | collective-permute-start | bytes 2752520 | tf_op jit(solution)/shard_map/ppermute | solution.py:610
  226.2 41.3 %collective-permute-start.28 = (bf16[512,896]{1,0:T(8,128)(2,1)}, bf16[512,896]{1,0:T(8,128)(2,1)}, u32[]{:S(2)}, u32[]{:S(2)}) collective-permute-start(bf16[512,896]{1,0:T(8,128)(2,1)} %get-tuple-element.151), channel_id=1, source_target_pairs={{0,2},{1,3},{2,0},{3,1},{4,6},{5,7},{6,4},{7,5},{8,10},{9,11},{10,... | collective-permute-start | bytes 2752520 | tf_op jit(solution)/shard_map/ppermute | solution.py:610
  227.9 39.5 %collective-permute-start.27 = (bf16[512,896]{1,0:T(8,128)(2,1)}, bf16[512,896]{1,0:T(8,128)(2,1)}, u32[]{:S(2)}, u32[]{:S(2)}) collective-permute-start(bf16[512,896]{1,0:T(8,128)(2,1)} %get-tuple-element.150), channel_id=1, source_target_pairs={{0,1},{1,0},{2,3},{3,2},{4,5},{5,4},{6,7},{7,6},{8,9},{9,8},{10,11... | collective-permute-start | bytes 2752520 | tf_op jit(solution)/shard_map/ppermute | solution.py:610
  267.5 141.6 %reduce-scatter.3.cloned.1.call-start = ((), (), s32[]{:S(2)}) async-start(), calls=%async_computation.2 | async-start | bytes 4128768 | tf_op jit(solution)/shard_map/reduce_scatter | solution.py:874
  276.5 39.8 %collective-permute-start.30 = (bf16[512,896]{1,0:T(8,128)(2,1)}, bf16[512,896]{1,0:T(8,128)(2,1)S(1)}, u32[]{:S(2)}, u32[]{:S(2)}) collective-permute-start(bf16[512,896]{1,0:T(8,128)(2,1)} %get-tuple-element.163), channel_id=1, source_target_pairs={{0,1},{1,0},{2,3},{3,2},{4,5},{5,4},{6,7},{7,6},{8,9},{9,8},{10,11... | collective-permute-start | bytes 2752520 | tf_op jit(solution)/shard_map/ppermute | solution.py:610
  276.7 40.9 %collective-permute-start.31 = (bf16[512,896]{1,0:T(8,128)(2,1)}, bf16[512,896]{1,0:T(8,128)(2,1)}, u32[]{:S(2)}, u32[]{:S(2)}) collective-permute-start(bf16[512,896]{1,0:T(8,128)(2,1)} %get-tuple-element.164), channel_id=1, source_target_pairs={{0,2},{1,3},{2,0},{3,1},{4,6},{5,7},{6,4},{7,5},{8,10},{9,11},{10,... | collective-permute-start | bytes 2752520 | tf_op jit(solution)/shard_map/ppermute | solution.py:610
  278.2 40.2 %collective-permute-start.32 = (bf16[512,896]{1,0:T(8,128)(2,1)}, bf16[512,896]{1,0:T(8,128)(2,1)}, u32[]{:S(2)}, u32[]{:S(2)}) collective-permute-start(bf16[512,896]{1,0:T(8,128)(2,1)} %get-tuple-element.165), channel_id=1, source_target_pairs={{0,3},{1,2},{2,1},{3,0},{4,7},{5,6},{6,5},{7,4},{8,11},{9,10},{10,... | collective-permute-start | bytes 2752520 | tf_op jit(solution)/shard_map/ppermute | solution.py:610
  320.4 9.8 %collective-permute-start.35 = (bf16[1,2,256,256]{3,2,1,0:T(8,128)(2,1)S(1)}, bf16[1,2,256,256]{3,2,1,0:T(8,128)(2,1)S(1)}, u32[]{:S(2)}, u32[]{:S(2)}) collective-permute-start(bf16[1,2,256,256]{3,2,1,0:T(8,128)(2,1)S(1)} %get-tuple-element.236), channel_id=1, source_target_pairs={{0,3},{1,2},{2,1},{3,0},{4,7},{5,6},{6,5},{7,4},{8,11},{9,10},{10,... | collective-permute-start | bytes 786440 | tf_op jit(solution)/shard_map/ppermute | solution.py:610
  322.1 10.9 %collective-permute-start.34 = (bf16[1,2,256,256]{3,2,1,0:T(8,128)(2,1)S(1)}, bf16[1,2,256,256]{3,2,1,0:T(8,128)(2,1)S(1)}, u32[]{:S(2)}, u32[]{:S(2)}) collective-permute-start(bf16[1,2,256,256]{3,2,1,0:T(8,128)(2,1)S(1)} %get-tuple-element.237), channel_id=1, source_target_pairs={{0,2},{1,3},{2,0},{3,1},{4,6},{5,7},{6,4},{7,5},{8,10},{9,11},{10,... | collective-permute-start | bytes 786440 | tf_op jit(solution)/shard_map/ppermute | solution.py:610
  323.3 9.8 %collective-permute-start.33 = (bf16[1,2,256,256]{3,2,1,0:T(8,128)(2,1)S(1)}, bf16[1,2,256,256]{3,2,1,0:T(8,128)(2,1)S(1)}, u32[]{:S(2)}, u32[]{:S(2)}) collective-permute-start(bf16[1,2,256,256]{3,2,1,0:T(8,128)(2,1)S(1)} %get-tuple-element.238), channel_id=1, source_target_pairs={{0,1},{1,0},{2,3},{3,2},{4,5},{5,4},{6,7},{7,6},{8,9},{9,8},{10,11... | collective-permute-start | bytes 786440 | tf_op jit(solution)/shard_map/ppermute | solution.py:610
  351.1 45.3 %collective-permute-start.36 = (bf16[256,896]{1,0:T(8,128)(2,1)}, bf16[256,896]{1,0:T(8,128)(2,1)}, u32[]{:S(2)}, u32[]{:S(2)}) collective-permute-start(bf16[256,896]{1,0:T(8,128)(2,1)} %get-tuple-element.241), channel_id=1, source_target_pairs={{0,3},{1,2},{2,1},{3,0},{4,7},{5,6},{6,5},{7,4},{8,11},{9,10},{10,... | collective-permute-start | bytes 1376264 | tf_op jit(solution)/shard_map/ppermute | solution.py:610
  354.5 43.9 %collective-permute-start.37 = (bf16[256,896]{1,0:T(8,128)(2,1)}, bf16[256,896]{1,0:T(8,128)(2,1)}, u32[]{:S(2)}, u32[]{:S(2)}) collective-permute-start(bf16[256,896]{1,0:T(8,128)(2,1)} %slice.232), channel_id=1, source_target_pairs={{0,3},{1,2},{2,1},{3,0},{4,7},{5,6},{6,5},{7,4},{8,11},{9,10},{10,... | collective-permute-start | bytes 1376264 | tf_op jit(solution)/shard_map/ppermute | solution.py:610
  359.1 29.4 %collective-permute-start.39 = (bf16[112,608]{1,0:T(8,128)(2,1)}, bf16[112,608]{1,0:T(8,128)(2,1)S(1)}, u32[]{:S(2)}, u32[]{:S(2)}) collective-permute-start(bf16[112,608]{1,0:T(8,128)(2,1)} %get-tuple-element.253), channel_id=1, source_target_pairs={{0,4},{1,12},{2,20},{3,28},{4,0},{5,8},{6,16},{7,24},{8,5},{9,13},... | collective-permute-start | bytes 408584 | tf_op jit(solution)/shard_map/ppermute | solution.py:667
  359.1 33.7 %collective-permute-start.38 = (bf16[112,608]{1,0:T(8,128)(2,1)}, bf16[112,608]{1,0:T(8,128)(2,1)S(1)}, u32[]{:S(2)}, u32[]{:S(2)}) collective-permute-start(bf16[112,608]{1,0:T(8,128)(2,1)} %get-tuple-element.254), channel_id=1, source_target_pairs={{0,0},{1,8},{2,16},{3,24},{4,4},{5,12},{6,20},{7,28},{8,1},{9,9},{... | collective-permute-start | bytes 408584 | tf_op jit(solution)/shard_map/ppermute | solution.py:667
  392.8 6.7 %collective-permute-start.40 = (f32[1,736]{1,0:T(1,128)S(1)}, f32[1,736]{1,0:T(1,128)S(1)}, u32[]{:S(2)}, u32[]{:S(2)}) collective-permute-start(f32[1,736]{1,0:T(1,128)S(1)} %get-tuple-element.274), channel_id=1, source_target_pairs={{0,1},{1,0},{2,3},{3,2},{4,5},{5,4},{6,7},{7,6},{8,9},{9,8},{10,11... | collective-permute-start | bytes 8840 | tf_op jit(solution)/shard_map/ppermute | solution.py:610
  392.8 6.6 %collective-permute-start.42 = (f32[1,736]{1,0:T(1,128)S(1)}, f32[1,736]{1,0:T(1,128)S(1)}, u32[]{:S(2)}, u32[]{:S(2)}) collective-permute-start(f32[1,736]{1,0:T(1,128)S(1)} %get-tuple-element.275), channel_id=1, source_target_pairs={{0,3},{1,2},{2,1},{3,0},{4,7},{5,6},{6,5},{7,4},{8,11},{9,10},{10,... | collective-permute-start | bytes 8840 | tf_op jit(solution)/shard_map/ppermute | solution.py:610
  392.9 6.5 %collective-permute-start.41 = (f32[1,736]{1,0:T(1,128)S(1)}, f32[1,736]{1,0:T(1,128)S(1)}, u32[]{:S(2)}, u32[]{:S(2)}) collective-permute-start(f32[1,736]{1,0:T(1,128)S(1)} %get-tuple-element.276), channel_id=1, source_target_pairs={{0,2},{1,3},{2,0},{3,1},{4,6},{5,7},{6,4},{7,5},{8,10},{9,11},{10,... | collective-permute-start | bytes 8840 | tf_op jit(solution)/shard_map/ppermute | solution.py:610
  410.8 6.1 %collective-permute-start.46 = (bf16[112,512]{1,0:T(8,128)(2,1)S(1)}, bf16[112,512]{1,0:T(8,128)(2,1)S(1)}, u32[]{:S(2)}, u32[]{:S(2)}) collective-permute-start(bf16[112,512]{1,0:T(8,128)(2,1)S(1)} %get-tuple-element.255), channel_id=1, source_target_pairs={{0,1},{1,0},{2,3},{3,2},{4,5},{5,4},{6,7},{7,6},{8,9},{9,8},{10,11... | collective-permute-start | bytes 344072 | tf_op jit(solution)/shard_map/ppermute | solution.py:610
  411.2 8.6 %collective-permute-start.48 = (bf16[112,512]{1,0:T(8,128)(2,1)S(1)}, bf16[112,512]{1,0:T(8,128)(2,1)S(1)}, u32[]{:S(2)}, u32[]{:S(2)}) collective-permute-start(bf16[112,512]{1,0:T(8,128)(2,1)S(1)} %get-tuple-element.256), channel_id=1, source_target_pairs={{0,3},{1,2},{2,1},{3,0},{4,7},{5,6},{6,5},{7,4},{8,11},{9,10},{10,... | collective-permute-start | bytes 344072 | tf_op jit(solution)/shard_map/ppermute | solution.py:610
  (36 other events, 184.7 us)
Sparse Core Ops, SparseCore 0:
  10.2 66.0 all-gather.4
  109.0 29.8 all-gather.6
  267.6 74.2 reduce-scatter.4
  346.9 53.7 reduce-scatter.2

commit v7 on v6

--- a/solution.py
+++ b/solution.py
@@ -734,16 +734,19 @@
     project_rows = from_floors(project_weight)
     held = project_rows.shape[0]
     tokens_mine = swap_second(to_rows(tokens))
-    project_rows, tokens_mine = lax.optimization_barrier((project_rows, tokens_mine))
+    grad_rows = to_rows(cotangent)
+    if ctx_size == 4:
+        grad_near = [hop(grad_rows[:half_rows], 4, 1), hop(grad_rows[half_rows:], 4, 2)]
+    else:
+        grad_near = others(grad_rows, ctx_size)
     project_came = from_ranks(
         jnp.concatenate(
             [project_rows, jnp.pad(vectors, (0, spare)).reshape(-1, own_width)], axis=0
         )
     )
-    down_rows, down_columns = down_weight.shape
-    depth = down_columns // fold
-    down_late = lax.optimization_barrier((down_weight, project_came[1]))[0]
-    down_came = send_crossed(list(down_late.T.reshape(fold, depth, down_rows)))
+    project_came, tokens_mine, grad_near = lax.optimization_barrier(
+        (project_came, tokens_mine, grad_near)
+    )
     output_late = lax.optimization_barrier((output_weight, project_rows))[0]
     output_rows = from_floors(output_late)
     ordered = by_rank(project_came)
@@ -756,17 +759,13 @@
     bias_full = vector_whole(gain_width, own_width)
     feedforward_full = vector_whole(gain_width + own_width, gain_width)
     project_columns = jnp.concatenate([piece[:held] for piece in ordered], axis=1)
-    project_other, down_came = lax.optimization_barrier(
-        (from_other_core(project_columns), down_came)
-    )
-    project_full = by_core(project_columns, project_other)
-
-    grad_late = lax.optimization_barrier((cotangent, project_full))[0]
-    grad_rows = to_rows(grad_late)
-    if ctx_size == 4:
-        grad_near = [hop(grad_rows[:half_rows], 4, 1), hop(grad_rows[half_rows:], 4, 2)]
-    else:
-        grad_near = others(grad_rows, ctx_size)
+    project_full = by_core(project_columns, from_other_core(project_columns))
+
+    down_late = lax.optimization_barrier((down_weight, project_full))[0]
+    down_rows, down_columns = down_weight.shape
+    depth = down_columns // fold
+    down_came = send_crossed(list(down_late.T.reshape(fold, depth, down_rows)))
+
     normed, queries, pairs_mine = project_forward(
         tokens_mine, attention_full, project_full, bias_full, cosine, sine
     )
@@ -781,11 +780,11 @@
         ]
     else:
         grad_far = []
-    output_came = from_ranks(output_rows)
     down_came, gate_up, pair_parts = lax.optimization_barrier((down_came, gate_up, pair_parts))
     down_turned = jnp.concatenate(crossed_parts(down_came), axis=1)
     down_mine = lax.all_gather(down_turned, "seq", axis=0)
     queries = lax.optimization_barrier((queries, down_turned))[0]
+    output_came = from_ranks(output_rows)
     mixed, row_stats = attend_forward(order, queries, pair_parts)
     mixed, grad_far, output_came = lax.optimization_barrier((mixed, grad_far, output_came))
     if ctx_size == 4:
@@ -895,11 +894,6 @@
         axis=1,
     )
 
-    down_late = weight_grads[2].reshape(depth, fold, down_rows)
-    grads_came = send_crossed([down_late[:, t] for t in range(fold)])
-    sums, grads_came = lax.optimization_barrier((sums, grads_came))
-    down_out = jnp.concatenate(crossed_parts(grads_came), axis=0).T
-
     def sums_for(k):
         return lax.dynamic_index_in_dim(sums, place ^ k, 0)
 
@@ -913,6 +907,9 @@
         )
         mask *= 2
     vector_sum = vector_sum[0]
+    down_late = weight_grads[2].reshape(depth, fold, down_rows)
+    grads_came = send_crossed([down_late[:, t] for t in range(fold)])
+    down_out = jnp.concatenate(crossed_parts(grads_came), axis=0).T
     owned, layer_output, tokens_gradient, vector_sum, down_out = lax.optimization_barrier(
         (owned, layer_output, tokens_gradient, vector_sum, down_out)
     )

time: 437 us -> 430 us (0.984)
  waiting for transfers between devices: 138 us -> 124 us
    ppermute x4, waiting for transfers between devices: 53.6 us -> 21.6 us  [crossed(): lax.ppermute(x, ('seq', 'ctx'), [((c * fold + r) * ctx_size + q, (q * fol...]
    ppermute x34, waiting for transfers between devices: 69.7 us -> 92.5 us  [hop(): return lax.ppermute(x, 'ctx', [(i, i ^ mask) for i in range(ctx_size)])]
    ppermute x6, waiting for transfers between devices: 4.84 us -> 0.02 us  [from_floors(): lax.ppermute(x, 'seq', [(i, (i + 2 * step) % seq_size) for i in range(seq...]
  transfers between devices with their start and end apart: 53 -> 53, of which waited for: 24 -> 24; matrix products, arithmetic and copies ran while one was open for 11% -> 12% of each run, Pallas kernels for 34% -> 35%
where the time goes in v7:
time: 430 us; the launch traced here: 422 us
  Pallas kernels  160 us (37%)
  waiting for transfers between devices  124 us (29%)
  starting transfers between devices  59.6 us (14%)
  other arithmetic  33.7 us (8%)
  local copies, waits for them, and re-layouts  26.5 us (6%)
  between operations  15 us (3%)
    ppermute x34, waiting for transfers between devices, hop(): return lax.ppermute(x, 'ctx', [(i, i ^ mask) for i in range(ctx_size)])  92.5 us
    pallas_call x4, Pallas kernels, ffn(): pl.pallas_call(ffn_kernel, grid=(2,), in_specs=[half_spec(at) for _, at i...  56.2 us
    ppermute x34, starting transfers between devices, hop(): return lax.ppermute(x, 'ctx', [(i, i ^ mask) for i in range(ctx_size)])  38 us
    pallas_call x1, Pallas kernels, attend_backward(): pl.pallas_call(backward_kernel, grid_spec=pltpu.PrefetchScalarGridSpec(nu...  36.3 us
    pallas_call x1, Pallas kernels, attend_forward(): pl.pallas_call(forward_kernel, grid_spec=pltpu.PrefetchScalarGridSpec(num...  27.4 us
    pallas_call x1, Pallas kernels, ffn_weights(): pl.pallas_call(ffn_weights_kernel, grid=(count,), in_specs=[slot(width)]...  22.4 us
    ppermute x4, waiting for transfers between devices, crossed(): lax.ppermute(x, ('seq', 'ctx'), [((c * fold + r) * ctx_size + q, (q * fol...  21.6 us
    ppermute x6, starting transfers between devices, from_floors(): lax.ppermute(x, 'seq', [(i, (i + 2 * step) % seq_size) for i in range(seq...  11.2 us
  transfers between devices with their start and end apart: 53, of which 24 were waited for; matrix products, arithmetic and copies ran while one was open for 12% of the time, Pallas kernels for 35%

profile of v7, /device:TPU:2, one launch (start us, length us, event | category | flops | bytes accessed | tf_op | source)
XLA Modules:
  0.0 422.3 jit_solution(1920206215608093336)
XLA Ops:
  7.2 2.0 pad_maximum_fusion.9
  10.3 3.7 collective-permute-start.2
  15.0 2.0 slice_bitcast_fusion.3
  24.4 7.3 %collective-permute-done.6 = bf16[256,896]{1,0:T(8,128)(2,1)} collective-permute-done((bf16[256,896]{1,0:T(8,128)(2,1)}, bf16[256,896]{1,0:T(8,128)(2,1)}, u32[]{:S(2)}, u32[]{:S(2)}) %collective-permute-start.6) | collective-permute-done | bytes 458784 | tf_op jit(solution)/shard_map/ppermute | solution.py:610
  33.5 2.0 pad_maximum_fusion.5.x_ref
  35.6 13.4 %collective-permute-done.5 = bf16[451,288]{1,0:T(8,128)(2,1)S(1)} collective-permute-done((bf16[451,288]{1,0:T(8,128)(2,1)S(1)}, bf16[451,288]{1,0:T(8,128)(2,1)S(1)}, u32[]{:S(2)}, u32[]{:S(2)}) %collective-permute-start.5) | collective-permute-done | bytes 259808 | tf_op jit(solution)/shard_map/ppermute | solution.py:610
  49.0 2.8 collective-permute-start.17
  51.8 2.6 collective-permute-done.4
  54.4 2.2 collective-permute-start.16
  60.8 2.9 concatenate.64
  69.7 4.9 %project_forward.1 = (bf16[512,896]{1,0:T(8,128)(2,1)}, bf16[512,896]{1,0:T(8,128)(2,1)}, bf16[512,256]{1,0:T(8,128)(2,1)}) custom-call(bf16[512,896]{1,0:T(8,128)(2,1)} %pad_maximum_fusion.5.x_ref, f32[1,896]{1,0:T(1,128)} %broadcast_in_dim.4.gain_ref, bf16[896,1152]{1,0:T(8,128)(2,1)} %bitcast.78, f32[1,1152]{1,0:T(1,128)} %broadcast_in_dim.5.bias_ref, ...), custom_call_target="tpu_custom_call" | custom-call | flops 2113929216 | bytes 5242880 | tf_op jit(solution)/shard_map/project_forward/pallas_call | solution.py:102
  78.2 4.0 collective-permute-start.10
  84.9 9.7 %collective-permute-done.13.rest_2_ = bf16[1,2,256,256]{3,2,1,0:T(8,128)(2,1)S(1)} collective-permute-done((bf16[1,2,256,256]{3,2,1,0:T(8,128)(2,1)}, bf16[1,2,256,256]{3,2,1,0:T(8,128)(2,1)S(1)}, u32[]{:S(2)}, u32[]{:S(2)}) %collective-permute-start.13) | collective-permute-done | bytes 262176 | tf_op jit(solution)/shard_map/ppermute | solution.py:610
  94.5 7.1 %collective-permute-done.12.rest_1_ = bf16[1,2,256,256]{3,2,1,0:T(8,128)(2,1)S(1)} collective-permute-done((bf16[1,2,256,256]{3,2,1,0:T(8,128)(2,1)}, bf16[1,2,256,256]{3,2,1,0:T(8,128)(2,1)S(1)}, u32[]{:S(2)}, u32[]{:S(2)}) %collective-permute-start.12) | collective-permute-done | bytes 262176 | tf_op jit(solution)/shard_map/ppermute | solution.py:610
  105.8 3.4 collective-permute-start.22
  109.7 27.4 %attend_forward.1 = (bf16[2,256,896]{2,1,0:T(8,128)(2,1)}, f32[2,16,256]{2,1,0:T(8,128)}) custom-call(s32[8]{0:T(128)} %stack.54.order_ref, bf16[2,256,896]{2,1,0:T(8,128)(2,1)} %bitcast.99, bf16[1,2,256,256]{3,2,1,0:T(8,128)(2,1)} %bitcast.94, bf16[1,2,256,256]{3,2,1,0:T(8,128)(2,1)} %copy-done.26, bf16[1,2,256,256]{3,2,1,0:T(8,128)(2,1)} %copy-done.25, ...), custom_call_target="tpu_custom_call" | custom-call | flops 9395240960 | bytes 4194304 | tf_op jit(solution)/shard_map/attend_forward/pallas_call | solution.py:440
  139.1 2.2 collective-permute-done.23
  149.9 13.9 %ffn.4 = (bf16[512,896]{1,0:T(8,128)(2,1)}, bf16[512,896]{1,0:T(8,128)(2,1)}, bf16[4,512,896]{2,1,0:T(8,128)(2,1)}, bf16[4,512,896]{2,1,0:T(8,128)(2,1)}, bf16[4...) custom-call(bf16[512,896]{1,0:T(8,128)(2,1)} %multiply_convert_fusion.x_low.x_high, ...), custom_call_target="tpu_custom_call" | custom-call | flops 7809794048 | bytes 16777216 | tf_op jit(solution)/shard_map/ffn/pallas_call | solution.py:548
  163.8 6.2 %collective-permute-done.26.x_low.x_high = bf16[512,896]{1,0:T(8,128)(2,1)} collective-permute-done((bf16[512,896]{1,0:T(8,128)(2,1)}, bf16[512,896]{1,0:T(8,128)(2,1)}, u32[]{:S(2)}, u32[]{:S(2)}) %collective-permute-start.26) | collective-permute-done | bytes 917536 | tf_op jit(solution)/shard_map/ppermute | solution.py:610
  169.9 14.3 %ffn.5 = (bf16[512,896]{1,0:T(8,128)(2,1)}, bf16[512,896]{1,0:T(8,128)(2,1)}, bf16[4,512,896]{2,1,0:T(8,128)(2,1)}, bf16[4,512,896]{2,1,0:T(8,128)(2,1)}, bf16[4...) custom-call(bf16[512,896]{1,0:T(8,128)(2,1)} %collective-permute-don, ...), custom_call_target="tpu_custom_call", output_to_operand_aliasing={{2}: (6, {}), {3}: (7, {}), {4}: (8, {}), {5}: (9, {}), {6}... | custom-call | flops 7809794048 | bytes 16777216 | tf_op jit(solution)/shard_map/ffn/pallas_call | solution.py:548
  184.2 5.9 %collective-permute-done.25.x_low.x_high = bf16[512,896]{1,0:T(8,128)(2,1)} collective-permute-done((bf16[512,896]{1,0:T(8,128)(2,1)}, bf16[512,896]{1,0:T(8,128)(2,1)}, u32[]{:S(2)}, u32[]{:S(2)}) %collective-permute-start.25) | collective-permute-done | bytes 917536 | tf_op jit(solution)/shard_map/ppermute | solution.py:610
  190.1 14.1 %ffn.6 = (bf16[512,896]{1,0:T(8,128)(2,1)}, bf16[512,896]{1,0:T(8,128)(2,1)}, bf16[4,512,896]{2,1,0:T(8,128)(2,1)}, bf16[4,512,896]{2,1,0:T(8,128)(2,1)}, bf16[4...) custom-call(bf16[512,896]{1,0:T(8,128)(2,1)} %collective-permute-don, ...), custom_call_target="tpu_custom_call", output_to_operand_aliasing={{2}: (6, {}), {3}: (7, {}), {4}: (8, {}), {5}: (9, {}), {6}... | custom-call | flops 7809794048 | bytes 16777216 | tf_op jit(solution)/shard_map/ffn/pallas_call | solution.py:548
  205.1 14.0 %ffn.7 = (bf16[512,896]{1,0:T(8,128)(2,1)}, bf16[512,896]{1,0:T(8,128)(2,1)}, bf16[4,512,896]{2,1,0:T(8,128)(2,1)}, bf16[4,512,896]{2,1,0:T(8,128)(2,1)}, bf16[4...) custom-call(bf16[512,896]{1,0:T(8,128)(2,1)} %copy-done.3, ...), custom_call_target="tpu_custom_call", output_to_operand_aliasing={{2}: (6, {}), {3}: (7, {}), {4}: (8, {}), {5}: (9, {}), {6}... | custom-call | flops 7809794048 | bytes 16777216 | tf_op jit(solution)/shard_map/ffn/pallas_call | solution.py:548
  222.7 22.4 %ffn_weights.1 = bf16[8,3,112,1216]{3,2,1,0:T(8,128)(2,1)} custom-call(bf16[4,512,896]{2,1,0:T(8,128)(2,1)} %get-tuple-element.142.x_ref, bf16[4,512,896]{2,1,0:T(8,128)(2,1)} %get-tuple-element.143.c_ref, bf16[4,512,1216]{2,1,0:T(8,128)(2,1)} %get-tuple-element.144.active_ref, bf16[4,512,1216]{2,1,0:T(8,128)(2,1)} %get-tuple-element.145.gate_ref, ...), custom_call_target="tpu_custom_call" | custom-call | flops 13388218368 | bytes 31457280 | tf_op jit(solution)/shard_map/ffn_weights/pallas_call | solution.py:594
  245.2 14.6 %collective-permute-done.28 = bf16[512,896]{1,0:T(8,128)(2,1)} collective-permute-done((bf16[512,896]{1,0:T(8,128)(2,1)}, bf16[512,896]{1,0:T(8,128)(2,1)}, u32[]{:S(2)}, u32[]{:S(2)}) %collective-permute-start.28) | collective-permute-done | bytes 917536 | tf_op jit(solution)/shard_map/ppermute | solution.py:610
  261.7 2.7 multiply_reduce_fusion
  264.4 4.1 fusion.8
  268.5 2.2 convolution_convert_fusion
  271.5 2.6 collective-permute-start.32
  274.2 36.3 %attend_backward.1 = (bf16[2,256,896]{2,1,0:T(8,128)(2,1)}, bf16[1,8,256,256]{3,2,1,0:T(8,128)(2,1)}) custom-call(s32[8]{0:T(128)} %stack.54.order_ref, bf16[2,256,896]{2,1,0:T(8,128)(2,1)} %bitcast.100, bf16[2,256,896]{2,1,0:T(8,128)(2,1)} %get-tuple-element.118.o_ref, bf16[2,256,896]{2,1,0:T(8,128)(2,1)} %bitcast.105, ...), custom_call_target="tpu_custom_call" | custom-call | flops 23488102400 | bytes 8388608 | tf_op jit(solution)/shard_map/attend_backward/pallas_call | solution.py:472
  310.5 2.4 collective-permute-done.31
  312.9 2.0 fusion.9
  318.4 6.2 %collective-permute-done.35 = bf16[1,2,256,256]{3,2,1,0:T(8,128)(2,1)S(1)} collective-permute-done((bf16[1,2,256,256]{3,2,1,0:T(8,128)(2,1)S(1)}, bf16[1,2,256,256]{3,2,1,0:T(8,128)(2,1)S(1)}, u32[]{:S(2)}, u32[]{:S(2)}) %collective-permute-start.35) | collective-permute-done | bytes 262176 | tf_op jit(solution)/shard_map/ppermute | solution.py:610
  324.6 2.7 collective-permute-done.34
  328.1 6.5 %project_backward.1 = (bf16[512,256]{1,0:T(8,128)(2,1)}, f32[512,896]{1,0:T(8,128)}, f32[1,896]{1,0:T(1,128)}, f32[1,1152]{1,0:T(1,128)}) custom-call(bf16[512,896]{1,0:T(8,128)(2,1)} %bitcast.103, bf16[896,1152]{1,0:T(8,128)(2,1)} %bitcast.79, bf16[512,896]{1,0:T(8,128)(2,1)} %pad_maximum_fusion.5.x_ref, f32[1,896]{1,0:T(1,128)} %broadcast_in_dim.4.gain_ref, ...), custom_call_target="tpu_custom_call" | custom-call | flops 2113929216 | bytes 8388608 | tf_op jit(solution)/shard_map/project_backward/pallas_call | solution.py:162
  334.6 6.4 %owned_weights.1 = bf16[896,2048]{1,0:T(8,128)(2,1)} custom-call(bf16[512,896]{1,0:T(8,128)(2,1)} %get-tuple-element.101.normed_ref, bf16[512,896]{1,0:T(8,128)(2,1)} %bitcast.104, bf16[512,256]{1,0:T(8,128)(2,1)} %get-tuple-element.164.gkv_ref, bf16[512,896]{1,0:T(8,128)(2,1)} %bitcast.101, bf16[512,896]{1,0:T(8,128)(2,1)} %copy-done.17), custom_call_target="tpu_custom_call" | custom-call | flops 3758096384 | bytes 8388608 | tf_op jit(solution)/shard_map/owned_weights/pallas_call | solution.py:216
  342.2 2.2 add_convert_fusion
  347.6 2.7 collective-permute-start.40
  352.9 6.0 %collective-permute-done.38 = f32[1,736]{1,0:T(1,128)S(1)} collective-permute-done((f32[1,736]{1,0:T(1,128)S(1)}, f32[1,736]{1,0:T(1,128)S(1)}, u32[]{:S(2)}, u32[]{:S(2)}) %collective-permute-start.38) | collective-permute-done | bytes 2976 | tf_op jit(solution)/shard_map/ppermute | solution.py:610
  362.4 2.7 collective-permute-done.42
  366.6 3.3 collective-permute-done.43
  369.9 2.0 pad_maximum_fusion.7
  373.1 2.2 fusion
  376.1 3.0 collective-permute-start.44
  380.5 19.4 %collective-permute-done.44 = bf16[112,608]{1,0:T(8,128)(2,1)S(1)} collective-permute-done((bf16[112,608]{1,0:T(8,128)(2,1)S(1)}, bf16[112,608]{1,0:T(8,128)(2,1)S(1)}, u32[]{:S(2)}, u32[]{:S(2)}) %collective-permute-start.44) | collective-permute-done | bytes 136224 | tf_op jit(solution)/shard_map/ppermute | solution.py:667
  400.0 2.2 collective-permute-done.45
  404.1 3.4 collective-permute-start.47
  410.4 2.4 collective-permute-done.47
  (233 shorter events, 76.8 us)
Async XLA Ops:
  7.2 95.2 %all-gather.5.cloned.1.call-start = ((), (), s32[]{:S(2)}) async-start(), calls=%async_computation.4 | async-start | bytes 5160960 | tf_op jit(solution)/shard_map/all_gather | solution.py:729
  9.2 140.7 %all-gather.7.cloned.1.call-start = ((), (), s32[]{:S(2)}) async-start(), calls=%async_computation.5 | async-start | bytes 2580480 | tf_op jit(solution)/shard_map/all_gather | solution.py:785
  10.3 10.2 %collective-permute-start.2 = (bf16[112,288]{1,0:T(8,128)(2,1)S(1)}, bf16[112,288]{1,0:T(8,128)(2,1)S(1)}, u32[]{:S(2)}, u32[]{:S(2)}) collective-permute-start(bf16[112,288]{1,0:T(8,128)(2,1)S(1)} %copy.63), channel_id=1, source_target_pairs={{0,24},{4,28},{8,0},{12,4},{16,8},{20,12},{24,16},{28,20},{1,25},{... | collective-permute-start | bytes 193544 | tf_op jit(solution)/shard_map/ppermute | solution.py:702
  14.0 8.1 %collective-permute-start.1 = (bf16[112,288]{1,0:T(8,128)(2,1)S(1)}, bf16[112,288]{1,0:T(8,128)(2,1)S(1)}, u32[]{:S(2)}, u32[]{:S(2)}) collective-permute-start(bf16[112,288]{1,0:T(8,128)(2,1)S(1)} %copy.63), channel_id=1, source_target_pairs={{0,16},{4,20},{8,24},{12,28},{16,0},{20,4},{24,8},{28,12},{1,17},{... | collective-permute-start | bytes 193544 | tf_op jit(solution)/shard_map/ppermute | solution.py:702
  14.0 8.1 %collective-permute-start = (bf16[112,288]{1,0:T(8,128)(2,1)S(1)}, bf16[112,288]{1,0:T(8,128)(2,1)S(1)}, u32[]{:S(2)}, u32[]{:S(2)}) collective-permute-start(bf16[112,288]{1,0:T(8,128)(2,1)S(1)} %copy.63), channel_id=1, source_target_pairs={{0,8},{4,12},{8,16},{12,20},{16,24},{20,28},{24,0},{28,4},{1,9},{5... | collective-permute-start | bytes 193544 | tf_op jit(solution)/shard_map/ppermute | solution.py:702
  17.0 14.7 %collective-permute-start.6 = (bf16[256,896]{1,0:T(8,128)(2,1)}, bf16[256,896]{1,0:T(8,128)(2,1)}, u32[]{:S(2)}, u32[]{:S(2)}) collective-permute-start(bf16[256,896]{1,0:T(8,128)(2,1)} %get-tuple-element.245), channel_id=1, source_target_pairs={{0,3},{1,2},{2,1},{3,0},{4,7},{5,6},{6,5},{7,4},{8,11},{9,10},{10,... | collective-permute-start | bytes 1376264 | tf_op jit(solution)/shard_map/ppermute | solution.py:610
  18.6 39.5 %collective-permute-start.8 = (bf16[256,896]{1,0:T(8,128)(2,1)S(1)}, bf16[256,896]{1,0:T(8,128)(2,1)S(1)}, u32[]{:S(2)}, u32[]{:S(2)}) collective-permute-start(bf16[256,896]{1,0:T(8,128)(2,1)S(1)} %get-tuple-element.242), channel_id=1, source_target_pairs={{0,2},{1,3},{2,0},{3,1},{4,6},{5,7},{6,4},{7,5},{8,10},{9,11},{10,... | collective-permute-start | bytes 1376264 | tf_op jit(solution)/shard_map/ppermute | solution.py:610
  20.5 37.5 %collective-permute-start.7 = (bf16[256,896]{1,0:T(8,128)(2,1)S(1)}, bf16[256,896]{1,0:T(8,128)(2,1)S(1)}, u32[]{:S(2)}, u32[]{:S(2)}) collective-permute-start(bf16[256,896]{1,0:T(8,128)(2,1)S(1)} %get-tuple-element.243), channel_id=1, source_target_pairs={{0,1},{1,0},{2,3},{3,2},{4,5},{5,4},{6,7},{7,6},{8,9},{9,8},{10,11... | collective-permute-start | bytes 1376264 | tf_op jit(solution)/shard_map/ppermute | solution.py:610
  22.4 26.6 %collective-permute-start.5 = (bf16[451,288]{1,0:T(8,128)(2,1)S(1)}, bf16[451,288]{1,0:T(8,128)(2,1)S(1)}, u32[]{:S(2)}, u32[]{:S(2)}) collective-permute-start(bf16[451,288]{1,0:T(8,128)(2,1)S(1)} %constant_dynamic-update-slice_fusion), channel_id=1, source_target_pairs={{0,3},{1,2},{2,1},{3,0},{4,7},{5,6},{6,5},{7,4},{8,11},{9,10},{10,... | collective-permute-start | bytes 779336 | tf_op jit(solution)/shard_map/ppermute | solution.py:610
  23.9 30.5 %collective-permute-start.4 = (bf16[451,288]{1,0:T(8,128)(2,1)S(1)}, bf16[451,288]{1,0:T(8,128)(2,1)S(1)}, u32[]{:S(2)}, u32[]{:S(2)}) collective-permute-start(bf16[451,288]{1,0:T(8,128)(2,1)S(1)} %constant_dynamic-update-slice_fusion), channel_id=1, source_target_pairs={{0,2},{1,3},{2,0},{3,1},{4,6},{5,7},{6,4},{7,5},{8,10},{9,11},{10,... | collective-permute-start | bytes 779336 | tf_op jit(solution)/shard_map/ppermute | solution.py:610
  31.7 24.9 %collective-permute-start.3 = (bf16[451,288]{1,0:T(8,128)(2,1)S(1)}, bf16[451,288]{1,0:T(8,128)(2,1)S(1)}, u32[]{:S(2)}, u32[]{:S(2)}) collective-permute-start(bf16[451,288]{1,0:T(8,128)(2,1)S(1)} %constant_dynamic-update-slice_fusion), channel_id=1, source_target_pairs={{0,1},{1,0},{2,3},{3,2},{4,5},{5,4},{6,7},{7,6},{8,9},{9,8},{10,11... | collective-permute-start | bytes 779336 | tf_op jit(solution)/shard_map/ppermute | solution.py:610
  49.0 27.7 %collective-permute-start.17 = (bf16[112,224]{1,0:T(8,128)(2,1)}, bf16[112,224]{1,0:T(8,128)(2,1)S(1)}, u32[]{:S(2)}, u32[]{:S(2)}) collective-permute-start(bf16[112,224]{1,0:T(8,128)(2,1)} %param.14), channel_id=1, source_target_pairs={{0,24},{4,28},{8,0},{12,4},{16,8},{20,12},{24,16},{28,20},{1,25},{... | collective-permute-start | bytes 150536 | tf_op jit(solution)/shard_map/ppermute | solution.py:702
  54.4 23.9 %collective-permute-start.16 = (bf16[112,224]{1,0:T(8,128)(2,1)}, bf16[112,224]{1,0:T(8,128)(2,1)}, u32[]{:S(2)}, u32[]{:S(2)}) collective-permute-start(bf16[112,224]{1,0:T(8,128)(2,1)} %param.14), channel_id=1, source_target_pairs={{0,16},{4,20},{8,24},{12,28},{16,0},{20,4},{24,8},{28,12},{1,17},{... | collective-permute-start | bytes 150536 | tf_op jit(solution)/shard_map/ppermute | solution.py:702
  56.6 21.7 %collective-permute-start.15 = (bf16[112,224]{1,0:T(8,128)(2,1)}, bf16[112,224]{1,0:T(8,128)(2,1)}, u32[]{:S(2)}, u32[]{:S(2)}) collective-permute-start(bf16[112,224]{1,0:T(8,128)(2,1)} %param.14), channel_id=1, source_target_pairs={{0,8},{4,12},{8,16},{12,20},{16,24},{20,28},{24,0},{28,4},{1,9},{5... | collective-permute-start | bytes 150536 | tf_op jit(solution)/shard_map/ppermute | solution.py:702
  74.6 10.3 %collective-permute-start.14 = (bf16[1,2,256,256]{3,2,1,0:T(8,128)(2,1)}, bf16[1,2,256,256]{3,2,1,0:T(8,128)(2,1)S(1)}, u32[]{:S(2)}, u32[]{:S(2)}) collective-permute-start(bf16[1,2,256,256]{3,2,1,0:T(8,128)(2,1)} %bitcast.91), channel_id=1, source_target_pairs={{0,3},{1,2},{2,1},{3,0},{4,7},{5,6},{6,5},{7,4},{8,11},{9,10},{10,... | collective-permute-start | bytes 786440 | tf_op jit(solution)/shard_map/ppermute | solution.py:610
  76.1 18.4 %collective-permute-start.13 = (bf16[1,2,256,256]{3,2,1,0:T(8,128)(2,1)}, bf16[1,2,256,256]{3,2,1,0:T(8,128)(2,1)S(1)}, u32[]{:S(2)}, u32[]{:S(2)}) collective-permute-start(bf16[1,2,256,256]{3,2,1,0:T(8,128)(2,1)} %bitcast.92), channel_id=1, source_target_pairs={{0,2},{1,3},{2,0},{3,1},{4,6},{5,7},{6,4},{7,5},{8,10},{9,11},{10,... | collective-permute-start | bytes 786440 | tf_op jit(solution)/shard_map/ppermute | solution.py:610
  76.7 25.0 %collective-permute-start.12 = (bf16[1,2,256,256]{3,2,1,0:T(8,128)(2,1)}, bf16[1,2,256,256]{3,2,1,0:T(8,128)(2,1)S(1)}, u32[]{:S(2)}, u32[]{:S(2)}) collective-permute-start(bf16[1,2,256,256]{3,2,1,0:T(8,128)(2,1)} %bitcast.93), channel_id=1, source_target_pairs={{0,1},{1,0},{2,3},{3,2},{4,5},{5,4},{6,7},{7,6},{8,9},{9,8},{10,11... | collective-permute-start | bytes 786440 | tf_op jit(solution)/shard_map/ppermute | solution.py:610
  78.2 23.4 %collective-permute-start.11 = (bf16[112,608]{1,0:T(8,128)(2,1)S(1)}, bf16[112,608]{1,0:T(8,128)(2,1)S(1)}, u32[]{:S(2)}, u32[]{:S(2)}) collective-permute-start(bf16[112,608]{1,0:T(8,128)(2,1)S(1)} %get-tuple-element.260), channel_id=1, source_target_pairs={{0,4},{1,12},{2,20},{3,28},{4,0},{5,8},{6,16},{7,24},{8,5},{9,13},... | collective-permute-start | bytes 408584 | tf_op jit(solution)/shard_map/ppermute | solution.py:667
  78.2 24.1 %collective-permute-start.10 = (bf16[112,608]{1,0:T(8,128)(2,1)S(1)}, bf16[112,608]{1,0:T(8,128)(2,1)S(1)}, u32[]{:S(2)}, u32[]{:S(2)}) collective-permute-start(bf16[112,608]{1,0:T(8,128)(2,1)S(1)} %get-tuple-element.261), channel_id=1, source_target_pairs={{0,0},{1,8},{2,16},{3,24},{4,4},{5,12},{6,20},{7,28},{8,1},{9,9},{... | collective-permute-start | bytes 408584 | tf_op jit(solution)/shard_map/ppermute | solution.py:667
  103.2 269.8 %reduce-scatter.5.cloned.1.call-start = ((), (), s32[]{:S(2)}) async-start(), calls=%async_computation.3 | async-start | bytes 7741440 | tf_op jit(solution)/shard_map/reduce_scatter | solution.py:827
  104.9 32.3 %collective-permute-start.18 = (bf16[512,896]{1,0:T(8,128)(2,1)S(1)}, bf16[512,896]{1,0:T(8,128)(2,1)S(1)}, u32[]{:S(2)}, u32[]{:S(2)}) collective-permute-start(bf16[512,896]{1,0:T(8,128)(2,1)S(1)} %pad_maximum_fusion.4), channel_id=1, source_target_pairs={{0,2},{1,3},{2,0},{3,1},{4,6},{5,7},{6,4},{7,5},{8,10},{9,11},{10,... | collective-permute-start | bytes 2752520 | tf_op jit(solution)/shard_map/ppermute | solution.py:610
  105.0 32.2 %collective-permute-start.19 = (bf16[512,896]{1,0:T(8,128)(2,1)}, bf16[512,896]{1,0:T(8,128)(2,1)S(1)}, u32[]{:S(2)}, u32[]{:S(2)}) collective-permute-start(bf16[512,896]{1,0:T(8,128)(2,1)} %pad_maximum_fusion.6), channel_id=1, source_target_pairs={{0,1},{1,0},{2,3},{3,2},{4,5},{5,4},{6,7},{7,6},{8,9},{9,8},{10,11... | collective-permute-start | bytes 2752520 | tf_op jit(solution)/shard_map/ppermute | solution.py:610
  105.8 31.4 %collective-permute-start.22 = (bf16[448,224]{1,0:T(8,128)(2,1)S(1)}, bf16[448,224]{1,0:T(8,128)(2,1)S(1)}, u32[]{:S(2)}, u32[]{:S(2)}) collective-permute-start(bf16[448,224]{1,0:T(8,128)(2,1)S(1)} %pad_maximum_fusion.13), channel_id=1, source_target_pairs={{0,3},{1,2},{2,1},{3,0},{4,7},{5,6},{6,5},{7,4},{8,11},{9,10},{10,... | collective-permute-start | bytes 602120 | tf_op jit(solution)/shard_map/ppermute | solution.py:610
  109.1 28.0 %collective-permute-start.21 = (bf16[448,224]{1,0:T(8,128)(2,1)S(1)}, bf16[448,224]{1,0:T(8,128)(2,1)S(1)}, u32[]{:S(2)}, u32[]{:S(2)}) collective-permute-start(bf16[448,224]{1,0:T(8,128)(2,1)S(1)} %pad_maximum_fusion.13), channel_id=1, source_target_pairs={{0,2},{1,3},{2,0},{3,1},{4,6},{5,7},{6,4},{7,5},{8,10},{9,11},{10,... | collective-permute-start | bytes 602120 | tf_op jit(solution)/shard_map/ppermute | solution.py:610
  109.2 28.0 %collective-permute-start.20 = (bf16[448,224]{1,0:T(8,128)(2,1)S(1)}, bf16[448,224]{1,0:T(8,128)(2,1)}, u32[]{:S(2)}, u32[]{:S(2)}) collective-permute-start(bf16[448,224]{1,0:T(8,128)(2,1)S(1)} %pad_maximum_fusion.13), channel_id=1, source_target_pairs={{0,1},{1,0},{2,3},{3,2},{4,5},{5,4},{6,7},{7,6},{8,9},{9,8},{10,11... | collective-permute-start | bytes 602120 | tf_op jit(solution)/shard_map/ppermute | solution.py:610
  146.4 23.5 %collective-permute-start.26 = (bf16[512,896]{1,0:T(8,128)(2,1)}, bf16[512,896]{1,0:T(8,128)(2,1)}, u32[]{:S(2)}, u32[]{:S(2)}) collective-permute-start(bf16[512,896]{1,0:T(8,128)(2,1)} %multiply_convert_fusion.x_low.x_high), channel_id=1, source_target_pairs={{0,1},{1,0},{2,3},{3,2},{4,5},{5,4},{6,7},{7,6},{8,9},{9,8},{10,11... | collective-permute-start | bytes 2752520 | tf_op jit(solution)/shard_map/ppermute | solution.py:610
  147.8 42.3 %collective-permute-start.25 = (bf16[512,896]{1,0:T(8,128)(2,1)}, bf16[512,896]{1,0:T(8,128)(2,1)}, u32[]{:S(2)}, u32[]{:S(2)}) collective-permute-start(bf16[512,896]{1,0:T(8,128)(2,1)} %multiply_convert_fusion.x_low.x_high), channel_id=1, source_target_pairs={{0,2},{1,3},{2,0},{3,1},{4,6},{5,7},{6,4},{7,5},{8,10},{9,11},{10,... | collective-permute-start | bytes 2752520 | tf_op jit(solution)/shard_map/ppermute | solution.py:610
  149.8 54.4 %collective-permute-start.24 = (bf16[512,896]{1,0:T(8,128)(2,1)}, bf16[512,896]{1,0:T(8,128)(2,1)S(1)}, u32[]{:S(2)}, u32[]{:S(2)}) collective-permute-start(bf16[512,896]{1,0:T(8,128)(2,1)} %multiply_convert_fusion.x_low.x_high), channel_id=1, source_target_pairs={{0,3},{1,2},{2,1},{3,0},{4,7},{5,6},{6,5},{7,4},{8,11},{9,10},{10,... | collective-permute-start | bytes 2752520 | tf_op jit(solution)/shard_map/ppermute | solution.py:610
  219.2 26.0 %collective-permute-start.29 = (bf16[512,896]{1,0:T(8,128)(2,1)}, bf16[512,896]{1,0:T(8,128)(2,1)}, u32[]{:S(2)}, u32[]{:S(2)}) collective-permute-start(bf16[512,896]{1,0:T(8,128)(2,1)} %get-tuple-element.149), channel_id=1, source_target_pairs={{0,3},{1,2},{2,1},{3,0},{4,7},{5,6},{6,5},{7,4},{8,11},{9,10},{10,... | collective-permute-start | bytes 2752520 | tf_op jit(solution)/shard_map/ppermute | solution.py:610
  220.8 39.0 %collective-permute-start.28 = (bf16[512,896]{1,0:T(8,128)(2,1)}, bf16[512,896]{1,0:T(8,128)(2,1)}, u32[]{:S(2)}, u32[]{:S(2)}) collective-permute-start(bf16[512,896]{1,0:T(8,128)(2,1)} %get-tuple-element.148), channel_id=1, source_target_pairs={{0,2},{1,3},{2,0},{3,1},{4,6},{5,7},{6,4},{7,5},{8,10},{9,11},{10,... | collective-permute-start | bytes 2752520 | tf_op jit(solution)/shard_map/ppermute | solution.py:610
  221.0 40.6 %collective-permute-start.27 = (bf16[512,896]{1,0:T(8,128)(2,1)}, bf16[512,896]{1,0:T(8,128)(2,1)}, u32[]{:S(2)}, u32[]{:S(2)}) collective-permute-start(bf16[512,896]{1,0:T(8,128)(2,1)} %get-tuple-element.147), channel_id=1, source_target_pairs={{0,1},{1,0},{2,3},{3,2},{4,5},{5,4},{6,7},{7,6},{8,9},{9,8},{10,11... | collective-permute-start | bytes 2752520 | tf_op jit(solution)/shard_map/ppermute | solution.py:610
  261.7 140.5 %reduce-scatter.3.cloned.1.call-start = ((), (), s32[]{:S(2)}) async-start(), calls=%async_computation.2 | async-start | bytes 4128768 | tf_op jit(solution)/shard_map/reduce_scatter | solution.py:873
  270.7 39.8 %collective-permute-start.30 = (bf16[512,896]{1,0:T(8,128)(2,1)}, bf16[512,896]{1,0:T(8,128)(2,1)S(1)}, u32[]{:S(2)}, u32[]{:S(2)}) collective-permute-start(bf16[512,896]{1,0:T(8,128)(2,1)} %get-tuple-element.160), channel_id=1, source_target_pairs={{0,1},{1,0},{2,3},{3,2},{4,5},{5,4},{6,7},{7,6},{8,9},{9,8},{10,11... | collective-permute-start | bytes 2752520 | tf_op jit(solution)/shard_map/ppermute | solution.py:610
  270.9 42.0 %collective-permute-start.31 = (bf16[512,896]{1,0:T(8,128)(2,1)}, bf16[512,896]{1,0:T(8,128)(2,1)}, u32[]{:S(2)}, u32[]{:S(2)}) collective-permute-start(bf16[512,896]{1,0:T(8,128)(2,1)} %get-tuple-element.161), channel_id=1, source_target_pairs={{0,2},{1,3},{2,0},{3,1},{4,6},{5,7},{6,4},{7,5},{8,10},{9,11},{10,... | collective-permute-start | bytes 2752520 | tf_op jit(solution)/shard_map/ppermute | solution.py:610
  271.5 41.4 %collective-permute-start.32 = (bf16[512,896]{1,0:T(8,128)(2,1)}, bf16[512,896]{1,0:T(8,128)(2,1)}, u32[]{:S(2)}, u32[]{:S(2)}) collective-permute-start(bf16[512,896]{1,0:T(8,128)(2,1)} %get-tuple-element.162), channel_id=1, source_target_pairs={{0,3},{1,2},{2,1},{3,0},{4,7},{5,6},{6,5},{7,4},{8,11},{9,10},{10,... | collective-permute-start | bytes 2752520 | tf_op jit(solution)/shard_map/ppermute | solution.py:610
  314.9 9.7 %collective-permute-start.35 = (bf16[1,2,256,256]{3,2,1,0:T(8,128)(2,1)S(1)}, bf16[1,2,256,256]{3,2,1,0:T(8,128)(2,1)S(1)}, u32[]{:S(2)}, u32[]{:S(2)}) collective-permute-start(bf16[1,2,256,256]{3,2,1,0:T(8,128)(2,1)S(1)} %get-tuple-element.232), channel_id=1, source_target_pairs={{0,3},{1,2},{2,1},{3,0},{4,7},{5,6},{6,5},{7,4},{8,11},{9,10},{10,... | collective-permute-start | bytes 786440 | tf_op jit(solution)/shard_map/ppermute | solution.py:610
  316.0 11.2 %collective-permute-start.34 = (bf16[1,2,256,256]{3,2,1,0:T(8,128)(2,1)S(1)}, bf16[1,2,256,256]{3,2,1,0:T(8,128)(2,1)S(1)}, u32[]{:S(2)}, u32[]{:S(2)}) collective-permute-start(bf16[1,2,256,256]{3,2,1,0:T(8,128)(2,1)S(1)} %get-tuple-element.233), channel_id=1, source_target_pairs={{0,2},{1,3},{2,0},{3,1},{4,6},{5,7},{6,4},{7,5},{8,10},{9,11},{10,... | collective-permute-start | bytes 786440 | tf_op jit(solution)/shard_map/ppermute | solution.py:610
  316.6 10.7 %collective-permute-start.33 = (bf16[1,2,256,256]{3,2,1,0:T(8,128)(2,1)S(1)}, bf16[1,2,256,256]{3,2,1,0:T(8,128)(2,1)S(1)}, u32[]{:S(2)}, u32[]{:S(2)}) collective-permute-start(bf16[1,2,256,256]{3,2,1,0:T(8,128)(2,1)S(1)} %get-tuple-element.234), channel_id=1, source_target_pairs={{0,1},{1,0},{2,3},{3,2},{4,5},{5,4},{6,7},{7,6},{8,9},{9,8},{10,11... | collective-permute-start | bytes 786440 | tf_op jit(solution)/shard_map/ppermute | solution.py:610
  345.3 24.6 %collective-permute-start.36 = (bf16[256,896]{1,0:T(8,128)(2,1)}, bf16[256,896]{1,0:T(8,128)(2,1)}, u32[]{:S(2)}, u32[]{:S(2)}) collective-permute-start(bf16[256,896]{1,0:T(8,128)(2,1)} %get-tuple-element.237), channel_id=1, source_target_pairs={{0,3},{1,2},{2,1},{3,0},{4,7},{5,6},{6,5},{7,4},{8,11},{9,10},{10,... | collective-permute-start | bytes 1376264 | tf_op jit(solution)/shard_map/ppermute | solution.py:610
  347.4 11.5 %collective-permute-start.38 = (f32[1,736]{1,0:T(1,128)S(1)}, f32[1,736]{1,0:T(1,128)S(1)}, u32[]{:S(2)}, u32[]{:S(2)}) collective-permute-start(f32[1,736]{1,0:T(1,128)S(1)} %get-tuple-element.266), channel_id=1, source_target_pairs={{0,1},{1,0},{2,3},{3,2},{4,5},{5,4},{6,7},{7,6},{8,9},{9,8},{10,11... | collective-permute-start | bytes 8840 | tf_op jit(solution)/shard_map/ppermute | solution.py:610
  347.6 12.5 %collective-permute-start.40 = (f32[1,736]{1,0:T(1,128)S(1)}, f32[1,736]{1,0:T(1,128)S(1)}, u32[]{:S(2)}, u32[]{:S(2)}) collective-permute-start(f32[1,736]{1,0:T(1,128)S(1)} %get-tuple-element.267), channel_id=1, source_target_pairs={{0,3},{1,2},{2,1},{3,0},{4,7},{5,6},{6,5},{7,4},{8,11},{9,10},{10,... | collective-permute-start | bytes 8840 | tf_op jit(solution)/shard_map/ppermute | solution.py:610
  350.3 9.8 %collective-permute-start.39 = (f32[1,736]{1,0:T(1,128)S(1)}, f32[1,736]{1,0:T(1,128)S(1)}, u32[]{:S(2)}, u32[]{:S(2)}) collective-permute-start(f32[1,736]{1,0:T(1,128)S(1)} %get-tuple-element.268), channel_id=1, source_target_pairs={{0,2},{1,3},{2,0},{3,1},{4,6},{5,7},{6,4},{7,5},{8,10},{9,11},{10,... | collective-permute-start | bytes 8840 | tf_op jit(solution)/shard_map/ppermute | solution.py:610
  351.8 20.2 %collective-permute-start.37 = (bf16[256,896]{1,0:T(8,128)(2,1)}, bf16[256,896]{1,0:T(8,128)(2,1)}, u32[]{:S(2)}, u32[]{:S(2)}) collective-permute-start(bf16[256,896]{1,0:T(8,128)(2,1)} %slice.232), channel_id=1, source_target_pairs={{0,3},{1,2},{2,1},{3,0},{4,7},{5,6},{6,5},{7,4},{8,11},{9,10},{10,... | collective-permute-start | bytes 1376264 | tf_op jit(solution)/shard_map/ppermute | solution.py:610
  376.1 23.8 %collective-permute-start.44 = (bf16[112,608]{1,0:T(8,128)(2,1)S(1)}, bf16[112,608]{1,0:T(8,128)(2,1)S(1)}, u32[]{:S(2)}, u32[]{:S(2)}) collective-permute-start(bf16[112,608]{1,0:T(8,128)(2,1)S(1)} %get-tuple-element.249), channel_id=1, source_target_pairs={{0,0},{1,8},{2,16},{3,24},{4,4},{5,12},{6,20},{7,28},{8,1},{9,9},{... | collective-permute-start | bytes 408584 | tf_op jit(solution)/shard_map/ppermute | solution.py:667
  379.1 23.0 %collective-permute-start.45 = (bf16[112,608]{1,0:T(8,128)(2,1)S(1)}, bf16[112,608]{1,0:T(8,128)(2,1)S(1)}, u32[]{:S(2)}, u32[]{:S(2)}) collective-permute-start(bf16[112,608]{1,0:T(8,128)(2,1)S(1)} %get-tuple-element.250), channel_id=1, source_target_pairs={{0,4},{1,12},{2,20},{3,28},{4,0},{5,8},{6,16},{7,24},{8,5},{9,13},... | collective-permute-start | bytes 408584 | tf_op jit(solution)/shard_map/ppermute | solution.py:667
  403.9 6.0 %collective-permute-start.46 = (bf16[112,512]{1,0:T(8,128)(2,1)S(1)}, bf16[112,512]{1,0:T(8,128)(2,1)S(1)}, u32[]{:S(2)}, u32[]{:S(2)}) collective-permute-start(bf16[112,512]{1,0:T(8,128)(2,1)S(1)} %get-tuple-element.251), channel_id=1, source_target_pairs={{0,1},{1,0},{2,3},{3,2},{4,5},{5,4},{6,7},{7,6},{8,9},{9,8},{10,11... | collective-permute-start | bytes 344072 | tf_op jit(solution)/shard_map/ppermute | solution.py:610
  404.0 6.4 %collective-permute-start.48 = (bf16[112,512]{1,0:T(8,128)(2,1)S(1)}, bf16[112,512]{1,0:T(8,128)(2,1)S(1)}, u32[]{:S(2)}, u32[]{:S(2)}) collective-permute-start(bf16[112,512]{1,0:T(8,128)(2,1)S(1)} %get-tuple-element.252), channel_id=1, source_target_pairs={{0,3},{1,2},{2,1},{3,0},{4,7},{5,6},{6,5},{7,4},{8,11},{9,10},{10,... | collective-permute-start | bytes 344072 | tf_op jit(solution)/shard_map/ppermute | solution.py:610
  404.1 8.7 %collective-permute-start.47 = (bf16[112,512]{1,0:T(8,128)(2,1)S(1)}, bf16[112,512]{1,0:T(8,128)(2,1)S(1)}, u32[]{:S(2)}, u32[]{:S(2)}) collective-permute-start(bf16[112,512]{1,0:T(8,128)(2,1)S(1)} %get-tuple-element.253), channel_id=1, source_target_pairs={{0,2},{1,3},{2,0},{3,1},{4,6},{5,7},{6,4},{7,5},{8,10},{9,11},{10,... | collective-permute-start | bytes 344072 | tf_op jit(solution)/shard_map/ppermute | solution.py:610
  (37 other events, 317.4 us)
Sparse Core Ops, SparseCore 0:
  10.2 56.7 all-gather.4
  103.4 29.8 all-gather.6
  261.8 74.4 reduce-scatter.4
  341.2 49.0 reduce-scatter.2

commit v8 on v5

--- a/solution.py
+++ b/solution.py
@@ -676,10 +676,15 @@
         )
 
     def crossed_parts(parts):
-        came = [
+        return ordered_parts(send_parts(parts))
+
+    def send_parts(parts):
+        return [
             crossed(pick(fold_place, [parts[(f + j) % fold] for f in range(fold)]), j)
             for j in range(fold)
         ]
+
+    def ordered_parts(came):
         return [
             pick(fold_place, [came[(f - t) % fold] for f in range(fold)]) for t in range(fold)
         ]
@@ -866,8 +871,14 @@
         pair_sums,
     )
 
+    owned, weight_grads = lax.optimization_barrier(
+        (
+            owned_weights(ctx_size, normed, grad_queries, grad_pairs, mixed_rows, hidden_low),
+            weight_grads,
+        )
+    )
     owned = lax.psum_scatter(
-        owned_weights(ctx_size, normed, grad_queries, grad_pairs, mixed_rows, hidden_low),
+        owned,
         "seq",
         scatter_dimension=0,
         tiled=True,
@@ -904,19 +915,20 @@
         mask *= 2
     vector_sum = vector_sum[0]
     down_late = weight_grads[2].reshape(depth, fold, down_rows)
-    down_came = crossed_parts([down_late[:, t] for t in range(fold)])
-    down_out = jnp.concatenate(down_came, axis=0).T
-    owned, layer_output, tokens_gradient, vector_sum, down_out = lax.optimization_barrier(
-        (owned, layer_output, tokens_gradient, vector_sum, down_out)
+    down_came = send_parts([down_late[:, t] for t in range(fold)])
+    owned, layer_output, tokens_gradient, vector_sum = lax.optimization_barrier(
+        (owned, layer_output, tokens_gradient, vector_sum)
     )
     own_columns = owned.shape[1] // ctx_size
 
     def owned_for(k):
         return lax.dynamic_slice_in_dim(owned, (place ^ k) * own_columns, own_columns, 1)
 
-    owned_total = owned_for(0).astype(f32)
-    for k in range(1, ctx_size):
-        owned_total = owned_total + hop(owned_for(k), ctx_size, k).astype(f32)
+    owned_got, down_came = lax.optimization_barrier(
+        ([hop(owned_for(k), ctx_size, k) for k in range(1, ctx_size)], down_came)
+    )
+    owned_total = others_sum([owned_for(0)], owned_got)
+    down_out = jnp.concatenate(ordered_parts(down_came), axis=0).T
 
     return (
         to_blocks(layer_output).reshape(tokens.shape),

time: 409 us -> 409 us (level)
  the two profiles are of different devices: /device:TPU:2 before, /device:TPU:24 now
where the time goes in v8:
time: 409 us; the launch traced here: 403 us
  Pallas kernels  160 us (39%)
  starting transfers between devices  88.1 us (22%)
  waiting for transfers between devices  82.9 us (20%)
  other arithmetic  30.1 us (7%)
  local copies, waits for them, and re-layouts  23 us (6%)
  between operations  15 us (4%)
    ppermute x34, starting transfers between devices, hop(): return lax.ppermute(x, 'ctx', [(i, i ^ mask) for i in range(ctx_size)])  66.9 us
    ppermute x34, waiting for transfers between devices, hop(): return lax.ppermute(x, 'ctx', [(i, i ^ mask) for i in range(ctx_size)])  56.3 us
    pallas_call x4, Pallas kernels, ffn(): pl.pallas_call(ffn_kernel, grid=(2,), in_specs=[half_spec(at) for _, at i...  56.3 us
    pallas_call x1, Pallas kernels, attend_backward(): pl.pallas_call(backward_kernel, grid_spec=pltpu.PrefetchScalarGridSpec(nu...  36.3 us
    pallas_call x1, Pallas kernels, attend_forward(): pl.pallas_call(forward_kernel, grid_spec=pltpu.PrefetchScalarGridSpec(num...  27.5 us
    pallas_call x1, Pallas kernels, ffn_weights(): pl.pallas_call(ffn_weights_kernel, grid=(count,), in_specs=[slot(width)]...  22.5 us
    ppermute x4, starting transfers between devices, crossed(): lax.ppermute(x, ('seq', 'ctx'), [((c * fold + r) * ctx_size + q, (q * fol...  11.2 us
    ppermute x3, waiting for transfers between devices, on_device(): lax.ppermute(vector_sum, 'seq', [(i, i ^ mask) for i in range(seq_size)])  9.34 us
  transfers between devices with their start and end apart: 53, of which 21 were waited for; matrix products, arithmetic and copies ran while one was open for 11% of the time, Pallas kernels for 40%

profile of v8, /device:TPU:24, one launch (start us, length us, event | category | flops | bytes accessed | tf_op | source)
XLA Modules:
  0.0 403.0 jit_solution(8295706458723679685)
XLA Ops:
  7.3 2.0 pad_maximum_fusion.9
  10.9 3.6 collective-permute-start
  14.6 2.5 collective-permute-start.3
  19.9 7.1 %collective-permute-done.3 = bf16[256,896]{1,0:T(8,128)(2,1)S(1)} collective-permute-done((bf16[256,896]{1,0:T(8,128)(2,1)S(1)}, bf16[256,896]{1,0:T(8,128)(2,1)S(1)}, u32[]{:S(2)}, u32[]{:S(2)}) %collective-permute-start.3) | collective-permute-done | bytes 458784 | tf_op jit(solution)/shard_map/ppermute | solution.py:610
  29.2 3.4 collective-permute-start.15
  39.4 8.2 %collective-permute-done.5 = bf16[451,288]{1,0:T(8,128)(2,1)S(1)} collective-permute-done((bf16[451,288]{1,0:T(8,128)(2,1)S(1)}, bf16[451,288]{1,0:T(8,128)(2,1)S(1)}, u32[]{:S(2)}, u32[]{:S(2)}) %collective-permute-start.5) | collective-permute-done | bytes 259808 | tf_op jit(solution)/shard_map/ppermute | solution.py:610
  50.1 3.2 concatenate.72
  57.9 5.0 %project_forward.1 = (bf16[512,896]{1,0:T(8,128)(2,1)}, bf16[512,896]{1,0:T(8,128)(2,1)}, bf16[512,256]{1,0:T(8,128)(2,1)}) custom-call(bf16[512,896]{1,0:T(8,128)(2,1)} %pad_maximum_fusion.5.x_ref, f32[1,896]{1,0:T(1,128)} %broadcast_in_dim.4.gain_ref, bf16[896,1152]{1,0:T(8,128)(2,1)} %bitcast.71, f32[1,1152]{1,0:T(1,128)} %broadcast_in_dim.5.bias_ref, ...), custom_call_target="tpu_custom_call" | custom-call | flops 2113929216 | bytes 5242880 | tf_op jit(solution)/shard_map/project_forward/pallas_call | solution.py:102
  66.4 3.9 collective-permute-start.8
  70.3 2.4 collective-permute-start.9
  72.7 4.4 %collective-permute-done.8 = bf16[112,608]{1,0:T(8,128)(2,1)S(1)} collective-permute-done((bf16[112,608]{1,0:T(8,128)(2,1)S(1)}, bf16[112,608]{1,0:T(8,128)(2,1)S(1)}, u32[]{:S(2)}, u32[]{:S(2)}) %collective-permute-start.8) | collective-permute-done | bytes 136224 | tf_op jit(solution)/shard_map/ppermute | solution.py:667
  77.1 6.8 %collective-permute-start.13 = (bf16[256,896]{1,0:T(8,128)(2,1)S(1)}, bf16[256,896]{1,0:T(8,128)(2,1)S(1)}, u32[]{:S(2)}, u32[]{:S(2)}) collective-permute-start(bf16[256,896]{1,0:T(8,128)(2,1)S(1)} %get-tuple-element.233), channel_id=1, source_target_pairs={{0,1},{1,0},{2,3},{3,2},{4,5},{5,4},{6,7},{7,6},{8,9},{9,8},{10,11... | collective-permute-start | bytes 1376264 | tf_op jit(solution)/shard_map/ppermute | solution.py:610
  83.9 6.2 %collective-permute-start.14 = (bf16[256,896]{1,0:T(8,128)(2,1)S(1)}, bf16[256,896]{1,0:T(8,128)(2,1)S(1)}, u32[]{:S(2)}, u32[]{:S(2)}) collective-permute-start(bf16[256,896]{1,0:T(8,128)(2,1)S(1)} %get-tuple-element.232), channel_id=1, source_target_pairs={{0,2},{1,3},{2,0},{3,1},{4,6},{5,7},{6,4},{7,5},{8,10},{9,11},{10,... | collective-permute-start | bytes 1376264 | tf_op jit(solution)/shard_map/ppermute | solution.py:610
  92.5 8.7 %collective-permute-done.14.c_high = bf16[256,896]{1,0:T(8,128)(2,1)S(1)} collective-permute-done((bf16[256,896]{1,0:T(8,128)(2,1)S(1)}, bf16[256,896]{1,0:T(8,128)(2,1)S(1)}, u32[]{:S(2)}, u32[]{:S(2)}) %collective-permute-start.14) | collective-permute-done | bytes 458784 | tf_op jit(solution)/shard_map/ppermute | solution.py:610
  101.9 2.3 collective-permute-start.18
  105.8 2.0 collective-permute-start.20
  109.3 27.5 %attend_forward.1 = (bf16[2,256,896]{2,1,0:T(8,128)(2,1)}, f32[2,16,256]{2,1,0:T(8,128)}) custom-call(s32[8]{0:T(128)} %stack.54.order_ref, bf16[2,256,896]{2,1,0:T(8,128)(2,1)} %bitcast.91, bf16[1,2,256,256]{3,2,1,0:T(8,128)(2,1)} %bitcast.86, bf16[1,2,256,256]{3,2,1,0:T(8,128)(2,1)} %copy-done.26, ...), custom_call_target="tpu_custom_call" | custom-call | flops 9395240960 | bytes 4194304 | tf_op jit(solution)/shard_map/attend_forward/pallas_call | solution.py:440
  139.0 2.2 collective-permute-done.23
  149.9 13.9 %ffn.4 = (bf16[512,896]{1,0:T(8,128)(2,1)}, bf16[512,896]{1,0:T(8,128)(2,1)}, bf16[4,512,896]{2,1,0:T(8,128)(2,1)}, bf16[4,512,896]{2,1,0:T(8,128)(2,1)}, bf16[4...) custom-call(bf16[512,896]{1,0:T(8,128)(2,1)} %multiply_convert_fusion.x_low.x_high, ...), custom_call_target="tpu_custom_call" | custom-call | flops 7809794048 | bytes 16777216 | tf_op jit(solution)/shard_map/ffn/pallas_call | solution.py:548
  163.8 6.0 %collective-permute-done.26.x_low.x_high = bf16[512,896]{1,0:T(8,128)(2,1)S(1)} collective-permute-done((bf16[512,896]{1,0:T(8,128)(2,1)}, bf16[512,896]{1,0:T(8,128)(2,1)S(1)}, u32[]{:S(2)}, u32[]{:S(2)}) %collective-permute-start.26) | collective-permute-done | bytes 917536 | tf_op jit(solution)/shard_map/ppermute | solution.py:610
  170.7 14.3 %ffn.5 = (bf16[512,896]{1,0:T(8,128)(2,1)}, bf16[512,896]{1,0:T(8,128)(2,1)}, bf16[4,512,896]{2,1,0:T(8,128)(2,1)}, bf16[4,512,896]{2,1,0:T(8,128)(2,1)}, bf16[4...) custom-call(bf16[512,896]{1,0:T(8,128)(2,1)} %copy-done.5, ...), custom_call_target="tpu_custom_call", output_to_operand_aliasing={{2}: (6, {}), {3}: (7, {}), {4}: (8, {}), {5}: (9, {}), {6}... | custom-call | flops 7809794048 | bytes 16777216 | tf_op jit(solution)/shard_map/ffn/pallas_call | solution.py:548
  186.6 4.8 %collective-permute-done.25.x_low.x_high = bf16[512,896]{1,0:T(8,128)(2,1)} collective-permute-done((bf16[512,896]{1,0:T(8,128)(2,1)}, bf16[512,896]{1,0:T(8,128)(2,1)}, u32[]{:S(2)}, u32[]{:S(2)}) %collective-permute-start.25) | collective-permute-done | bytes 917536 | tf_op jit(solution)/shard_map/ppermute | solution.py:610
  191.4 14.1 %ffn.6 = (bf16[512,896]{1,0:T(8,128)(2,1)}, bf16[512,896]{1,0:T(8,128)(2,1)}, bf16[4,512,896]{2,1,0:T(8,128)(2,1)}, bf16[4,512,896]{2,1,0:T(8,128)(2,1)}, bf16[4...) custom-call(bf16[512,896]{1,0:T(8,128)(2,1)} %collective-permute-don, ...), custom_call_target="tpu_custom_call", output_to_operand_aliasing={{2}: (6, {}), {3}: (7, {}), {4}: (8, {}), {5}: (9, {}), {6}... | custom-call | flops 7809794048 | bytes 16777216 | tf_op jit(solution)/shard_map/ffn/pallas_call | solution.py:548
  205.9 14.0 %ffn.7 = (bf16[512,896]{1,0:T(8,128)(2,1)}, bf16[512,896]{1,0:T(8,128)(2,1)}, bf16[4,512,896]{2,1,0:T(8,128)(2,1)}, bf16[4,512,896]{2,1,0:T(8,128)(2,1)}, bf16[4...) custom-call(bf16[512,896]{1,0:T(8,128)(2,1)} %collective-permute-don, ...), custom_call_target="tpu_custom_call", output_to_operand_aliasing={{2}: (6, {}), {3}: (7, {}), {4}: (8, {}), {5}: (9, {}), {6}... | custom-call | flops 7809794048 | bytes 16777216 | tf_op jit(solution)/shard_map/ffn/pallas_call | solution.py:548
  221.4 22.5 %ffn_weights.1 = bf16[8,3,112,1216]{3,2,1,0:T(8,128)(2,1)} custom-call(bf16[4,512,896]{2,1,0:T(8,128)(2,1)} %get-tuple-element.128.x_ref, bf16[4,512,896]{2,1,0:T(8,128)(2,1)} %get-tuple-element.129.c_ref, bf16[4,512,1216]{2,1,0:T(8,128)(2,1)} %get-tuple-element.130.active_ref, bf16[4,512,1216]{2,1,0:T(8,128)(2,1)} %get-tuple-element.131.gate_ref, ...), custom_call_target="tpu_custom_call" | custom-call | flops 13388218368 | bytes 31457280 | tf_op jit(solution)/shard_map/ffn_weights/pallas_call | solution.py:594
  247.2 2.4 multiply_reduce_fusion
  249.7 3.8 fusion.7
  253.5 2.2 convolution_convert_fusion
  255.6 1.8 collective-permute-start.30
  259.1 36.3 %attend_backward.1 = (bf16[2,256,896]{2,1,0:T(8,128)(2,1)}, bf16[1,8,256,256]{3,2,1,0:T(8,128)(2,1)}) custom-call(s32[8]{0:T(128)} %stack.54.order_ref, bf16[2,256,896]{2,1,0:T(8,128)(2,1)} %bitcast.92, bf16[2,256,896]{2,1,0:T(8,128)(2,1)} %get-tuple-element.104.o_ref, bf16[2,256,896]{2,1,0:T(8,128)(2,1)} %bitcast.97, ...), custom_call_target="tpu_custom_call" | custom-call | flops 23488102400 | bytes 8388608 | tf_op jit(solution)/shard_map/attend_backward/pallas_call | solution.py:472
  295.4 2.3 fusion.8
  297.7 1.7 collective-permute-start.33
  301.2 2.9 collective-permute-done.33
  304.1 4.5 %collective-permute-done.34 = bf16[1,2,256,256]{3,2,1,0:T(8,128)(2,1)S(1)} collective-permute-done((bf16[1,2,256,256]{3,2,1,0:T(8,128)(2,1)S(1)}, bf16[1,2,256,256]{3,2,1,0:T(8,128)(2,1)S(1)}, u32[]{:S(2)}, u32[]{:S(2)}) %collective-permute-start.34) | collective-permute-done | bytes 262176 | tf_op jit(solution)/shard_map/ppermute | solution.py:610
  309.5 6.5 %project_backward.1 = (bf16[512,256]{1,0:T(8,128)(2,1)}, f32[512,896]{1,0:T(8,128)}, f32[1,896]{1,0:T(1,128)}, f32[1,1152]{1,0:T(1,128)}) custom-call(bf16[512,896]{1,0:T(8,128)(2,1)} %bitcast.95, bf16[896,1152]{1,0:T(8,128)(2,1)} %bitcast.72, bf16[512,896]{1,0:T(8,128)(2,1)} %pad_maximum_fusion.5.x_ref, f32[1,896]{1,0:T(1,128)} %broadcast_in_dim.4.gain_ref, ...), custom_call_target="tpu_custom_call" | custom-call | flops 2113929216 | bytes 8388608 | tf_op jit(solution)/shard_map/project_backward/pallas_call | solution.py:162
  316.0 6.4 %owned_weights.1 = bf16[896,2048]{1,0:T(8,128)(2,1)} custom-call(bf16[512,896]{1,0:T(8,128)(2,1)} %get-tuple-element.92.normed_ref, bf16[512,896]{1,0:T(8,128)(2,1)} %bitcast.96, bf16[512,256]{1,0:T(8,128)(2,1)} %get-tuple-element.150.gkv_ref, bf16[512,896]{1,0:T(8,128)(2,1)} %bitcast.93, bf16[512,896]{1,0:T(8,128)(2,1)} %copy-done.16), custom_call_target="tpu_custom_call" | custom-call | flops 3758096384 | bytes 8388608 | tf_op jit(solution)/shard_map/owned_weights/pallas_call | solution.py:216
  323.6 2.3 add_convert_fusion
  327.6 1.8 collective-permute-start.40
  331.9 1.7 collective-permute-start.37
  333.7 6.2 %collective-permute-done.40 = f32[1,736]{1,0:T(1,128)S(1)} collective-permute-done((f32[1,736]{1,0:T(1,128)S(1)}, f32[1,736]{1,0:T(1,128)S(1)}, u32[]{:S(2)}, u32[]{:S(2)}) %collective-permute-start.40) | collective-permute-done | bytes 2976 | tf_op jit(solution)/shard_map/ppermute | solution.py:610
  341.4 3.5 collective-permute-done.42
  345.0 4.7 %collective-permute-done.43 = f32[1,736]{1,0:T(1,128)S(1)} collective-permute-done((f32[1,736]{1,0:T(1,128)S(1)}, f32[1,736]{1,0:T(1,128)S(1)}, u32[]{:S(2)}, u32[]{:S(2)}) %collective-permute-start.43) | collective-permute-done | bytes 2976 | tf_op jit(solution)/shard_map/ppermute | solution.py:912
  355.1 3.7 collective-permute-start.47
  360.1 8.5 %reduce-scatter.5.cloned.1.call-done = bf16[112,2048]{1,0:T(8,128)(2,1)} async-done(((bf16[896,2048]{1,0:T(8,128)(2,1)}), bf16[112,2048]{1,0:T(8,128)(2,1)}) %reduce-scatter.5.cloned.1.call-update) | async-done | bytes 458768 | tf_op jit(solution)/shard_map/reduce_scatter | solution.py:880
  369.7 2.6 collective-permute-start.44
  372.3 14.6 %collective-permute-start.45 = (bf16[112,512]{1,0:T(8,128)(2,1)S(1)}, bf16[112,512]{1,0:T(8,128)(2,1)S(1)}, u32[]{:S(2)}, u32[]{:S(2)}) collective-permute-start(bf16[112,512]{1,0:T(8,128)(2,1)S(1)} %get-tuple-element.242), channel_id=1, source_target_pairs={{0,2},{1,3},{2,0},{3,1},{4,6},{5,7},{6,4},{7,5},{8,10},{9,11},{10,... | collective-permute-start | bytes 344072 | tf_op jit(solution)/shard_map/ppermute | solution.py:610
  388.2 2.3 collective-permute-done.45
  390.5 2.1 collective-permute-done.46
  (234 shorter events, 72.4 us)
Async XLA Ops:
  7.2 94.0 %all-gather.5.cloned.1.call-start = ((), (), s32[]{:S(2)}) async-start(), calls=%async_computation.4 | async-start | bytes 5160960 | tf_op jit(solution)/shard_map/all_gather | solution.py:732
  9.3 140.6 %all-gather.7.cloned.1.call-start = ((), (), s32[]{:S(2)}) async-start(), calls=%async_computation.5 | async-start | bytes 2580480 | tf_op jit(solution)/shard_map/all_gather | solution.py:775
  10.3 9.5 %collective-permute-start.1 = (bf16[112,288]{1,0:T(8,128)(2,1)S(1)}, bf16[112,288]{1,0:T(8,128)(2,1)S(1)}, u32[]{:S(2)}, u32[]{:S(2)}) collective-permute-start(bf16[112,288]{1,0:T(8,128)(2,1)S(1)} %copy.63), channel_id=1, source_target_pairs={{0,16},{4,20},{8,24},{12,28},{16,0},{20,4},{24,8},{28,12},{1,17},{... | collective-permute-start | bytes 193544 | tf_op jit(solution)/shard_map/ppermute | solution.py:705
  10.7 9.1 %collective-permute-start.2 = (bf16[112,288]{1,0:T(8,128)(2,1)S(1)}, bf16[112,288]{1,0:T(8,128)(2,1)S(1)}, u32[]{:S(2)}, u32[]{:S(2)}) collective-permute-start(bf16[112,288]{1,0:T(8,128)(2,1)S(1)} %copy.63), channel_id=1, source_target_pairs={{0,24},{4,28},{8,0},{12,4},{16,8},{20,12},{24,16},{28,20},{1,25},{... | collective-permute-start | bytes 193544 | tf_op jit(solution)/shard_map/ppermute | solution.py:705
  10.9 8.9 %collective-permute-start = (bf16[112,288]{1,0:T(8,128)(2,1)S(1)}, bf16[112,288]{1,0:T(8,128)(2,1)S(1)}, u32[]{:S(2)}, u32[]{:S(2)}) collective-permute-start(bf16[112,288]{1,0:T(8,128)(2,1)S(1)} %copy.63), channel_id=1, source_target_pairs={{0,8},{4,12},{8,16},{12,20},{16,24},{20,28},{24,0},{28,4},{1,9},{5... | collective-permute-start | bytes 193544 | tf_op jit(solution)/shard_map/ppermute | solution.py:705
  14.6 12.4 %collective-permute-start.3 = (bf16[256,896]{1,0:T(8,128)(2,1)S(1)}, bf16[256,896]{1,0:T(8,128)(2,1)S(1)}, u32[]{:S(2)}, u32[]{:S(2)}) collective-permute-start(bf16[256,896]{1,0:T(8,128)(2,1)S(1)} %get-tuple-element.235), channel_id=1, source_target_pairs={{0,3},{1,2},{2,1},{3,0},{4,7},{5,6},{6,5},{7,4},{8,11},{9,10},{10,... | collective-permute-start | bytes 1376264 | tf_op jit(solution)/shard_map/ppermute | solution.py:610
  28.0 9.1 %collective-permute-start.16 = (bf16[112,224]{1,0:T(8,128)(2,1)S(1)}, bf16[112,224]{1,0:T(8,128)(2,1)S(1)}, u32[]{:S(2)}, u32[]{:S(2)}) collective-permute-start(bf16[112,224]{1,0:T(8,128)(2,1)S(1)} %copy-done.20), channel_id=1, source_target_pairs={{0,16},{4,20},{8,24},{12,28},{16,0},{20,4},{24,8},{28,12},{1,17},{... | collective-permute-start | bytes 150536 | tf_op jit(solution)/shard_map/ppermute | solution.py:705
  28.8 9.8 %collective-permute-start.17 = (bf16[112,224]{1,0:T(8,128)(2,1)S(1)}, bf16[112,224]{1,0:T(8,128)(2,1)S(1)}, u32[]{:S(2)}, u32[]{:S(2)}) collective-permute-start(bf16[112,224]{1,0:T(8,128)(2,1)S(1)} %copy-done.20), channel_id=1, source_target_pairs={{0,24},{4,28},{8,0},{12,4},{16,8},{20,12},{24,16},{28,20},{1,25},{... | collective-permute-start | bytes 150536 | tf_op jit(solution)/shard_map/ppermute | solution.py:705
  29.2 9.4 %collective-permute-start.15 = (bf16[112,224]{1,0:T(8,128)(2,1)S(1)}, bf16[112,224]{1,0:T(8,128)(2,1)S(1)}, u32[]{:S(2)}, u32[]{:S(2)}) collective-permute-start(bf16[112,224]{1,0:T(8,128)(2,1)S(1)} %copy-done.20), channel_id=1, source_target_pairs={{0,8},{4,12},{8,16},{12,20},{16,24},{20,28},{24,0},{28,4},{1,9},{5... | collective-permute-start | bytes 150536 | tf_op jit(solution)/shard_map/ppermute | solution.py:705
  32.7 14.9 %collective-permute-start.5 = (bf16[451,288]{1,0:T(8,128)(2,1)S(1)}, bf16[451,288]{1,0:T(8,128)(2,1)S(1)}, u32[]{:S(2)}, u32[]{:S(2)}) collective-permute-start(bf16[451,288]{1,0:T(8,128)(2,1)S(1)} %constant_dynamic-update-slice_fusion), channel_id=1, source_target_pairs={{0,2},{1,3},{2,0},{3,1},{4,6},{5,7},{6,4},{7,5},{8,10},{9,11},{10,... | collective-permute-start | bytes 779336 | tf_op jit(solution)/shard_map/ppermute | solution.py:610
  34.3 13.3 %collective-permute-start.6 = (bf16[451,288]{1,0:T(8,128)(2,1)S(1)}, bf16[451,288]{1,0:T(8,128)(2,1)S(1)}, u32[]{:S(2)}, u32[]{:S(2)}) collective-permute-start(bf16[451,288]{1,0:T(8,128)(2,1)S(1)} %constant_dynamic-update-slice_fusion), channel_id=1, source_target_pairs={{0,3},{1,2},{2,1},{3,0},{4,7},{5,6},{6,5},{7,4},{8,11},{9,10},{10,... | collective-permute-start | bytes 779336 | tf_op jit(solution)/shard_map/ppermute | solution.py:610
  37.1 11.9 %collective-permute-start.4 = (bf16[451,288]{1,0:T(8,128)(2,1)S(1)}, bf16[451,288]{1,0:T(8,128)(2,1)S(1)}, u32[]{:S(2)}, u32[]{:S(2)}) collective-permute-start(bf16[451,288]{1,0:T(8,128)(2,1)S(1)} %constant_dynamic-update-slice_fusion), channel_id=1, source_target_pairs={{0,1},{1,0},{2,3},{3,2},{4,5},{5,4},{6,7},{7,6},{8,9},{9,8},{10,11... | collective-permute-start | bytes 779336 | tf_op jit(solution)/shard_map/ppermute | solution.py:610
  62.9 28.0 %collective-permute-start.10 = (bf16[1,2,256,256]{3,2,1,0:T(8,128)(2,1)}, bf16[1,2,256,256]{3,2,1,0:T(8,128)(2,1)S(1)}, u32[]{:S(2)}, u32[]{:S(2)}) collective-permute-start(bf16[1,2,256,256]{3,2,1,0:T(8,128)(2,1)} %bitcast.83), channel_id=1, source_target_pairs={{0,1},{1,0},{2,3},{3,2},{4,5},{5,4},{6,7},{7,6},{8,9},{9,8},{10,11... | collective-permute-start | bytes 786440 | tf_op jit(solution)/shard_map/ppermute | solution.py:610
  64.4 26.5 %collective-permute-start.11 = (bf16[1,2,256,256]{3,2,1,0:T(8,128)(2,1)}, bf16[1,2,256,256]{3,2,1,0:T(8,128)(2,1)}, u32[]{:S(2)}, u32[]{:S(2)}) collective-permute-start(bf16[1,2,256,256]{3,2,1,0:T(8,128)(2,1)} %bitcast.84), channel_id=1, source_target_pairs={{0,2},{1,3},{2,0},{3,1},{4,6},{5,7},{6,4},{7,5},{8,10},{9,11},{10,... | collective-permute-start | bytes 786440 | tf_op jit(solution)/shard_map/ppermute | solution.py:610
  65.9 25.0 %collective-permute-start.12 = (bf16[1,2,256,256]{3,2,1,0:T(8,128)(2,1)}, bf16[1,2,256,256]{3,2,1,0:T(8,128)(2,1)}, u32[]{:S(2)}, u32[]{:S(2)}) collective-permute-start(bf16[1,2,256,256]{3,2,1,0:T(8,128)(2,1)} %bitcast.85), channel_id=1, source_target_pairs={{0,3},{1,2},{2,1},{3,0},{4,7},{5,6},{6,5},{7,4},{8,11},{9,10},{10,... | collective-permute-start | bytes 786440 | tf_op jit(solution)/shard_map/ppermute | solution.py:610
  66.4 10.7 %collective-permute-start.8 = (bf16[112,608]{1,0:T(8,128)(2,1)S(1)}, bf16[112,608]{1,0:T(8,128)(2,1)S(1)}, u32[]{:S(2)}, u32[]{:S(2)}) collective-permute-start(bf16[112,608]{1,0:T(8,128)(2,1)S(1)} %get-tuple-element.254), channel_id=1, source_target_pairs={{0,0},{1,8},{2,16},{3,24},{4,4},{5,12},{6,20},{7,28},{8,1},{9,9},{... | collective-permute-start | bytes 408584 | tf_op jit(solution)/shard_map/ppermute | solution.py:667
  70.3 13.6 %collective-permute-start.9 = (bf16[112,608]{1,0:T(8,128)(2,1)S(1)}, bf16[112,608]{1,0:T(8,128)(2,1)S(1)}, u32[]{:S(2)}, u32[]{:S(2)}) collective-permute-start(bf16[112,608]{1,0:T(8,128)(2,1)S(1)} %get-tuple-element.255), channel_id=1, source_target_pairs={{0,4},{1,12},{2,20},{3,28},{4,0},{5,8},{6,16},{7,24},{8,5},{9,13},... | collective-permute-start | bytes 408584 | tf_op jit(solution)/shard_map/ppermute | solution.py:667
  77.1 15.4 %collective-permute-start.13 = (bf16[256,896]{1,0:T(8,128)(2,1)S(1)}, bf16[256,896]{1,0:T(8,128)(2,1)S(1)}, u32[]{:S(2)}, u32[]{:S(2)}) collective-permute-start(bf16[256,896]{1,0:T(8,128)(2,1)S(1)} %get-tuple-element.233), channel_id=1, source_target_pairs={{0,1},{1,0},{2,3},{3,2},{4,5},{5,4},{6,7},{7,6},{8,9},{9,8},{10,11... | collective-permute-start | bytes 1376264 | tf_op jit(solution)/shard_map/ppermute | solution.py:610
  83.9 17.3 %collective-permute-start.14 = (bf16[256,896]{1,0:T(8,128)(2,1)S(1)}, bf16[256,896]{1,0:T(8,128)(2,1)S(1)}, u32[]{:S(2)}, u32[]{:S(2)}) collective-permute-start(bf16[256,896]{1,0:T(8,128)(2,1)S(1)} %get-tuple-element.232), channel_id=1, source_target_pairs={{0,2},{1,3},{2,0},{3,1},{4,6},{5,7},{6,4},{7,5},{8,10},{9,11},{10,... | collective-permute-start | bytes 1376264 | tf_op jit(solution)/shard_map/ppermute | solution.py:610
  101.3 221.2 %reduce-scatter.3.cloned.1.call-start = ((), (), s32[]{:S(2)}) async-start(), calls=%async_computation.2 | async-start | bytes 7741440 | tf_op jit(solution)/shard_map/reduce_scatter | solution.py:828
  101.9 35.2 %collective-permute-start.18 = (bf16[512,896]{1,0:T(8,128)(2,1)S(1)}, bf16[512,896]{1,0:T(8,128)(2,1)S(1)}, u32[]{:S(2)}, u32[]{:S(2)}) collective-permute-start(bf16[512,896]{1,0:T(8,128)(2,1)S(1)} %pad_maximum_fusion.4), channel_id=1, source_target_pairs={{0,2},{1,3},{2,0},{3,1},{4,6},{5,7},{6,4},{7,5},{8,10},{9,11},{10,... | collective-permute-start | bytes 2752520 | tf_op jit(solution)/shard_map/ppermute | solution.py:610
  105.2 31.9 %collective-permute-start.19 = (bf16[512,896]{1,0:T(8,128)(2,1)}, bf16[512,896]{1,0:T(8,128)(2,1)S(1)}, u32[]{:S(2)}, u32[]{:S(2)}) collective-permute-start(bf16[512,896]{1,0:T(8,128)(2,1)} %pad_maximum_fusion.6), channel_id=1, source_target_pairs={{0,1},{1,0},{2,3},{3,2},{4,5},{5,4},{6,7},{7,6},{8,9},{9,8},{10,11... | collective-permute-start | bytes 2752520 | tf_op jit(solution)/shard_map/ppermute | solution.py:610
  105.8 31.0 %collective-permute-start.20 = (bf16[448,224]{1,0:T(8,128)(2,1)S(1)}, bf16[448,224]{1,0:T(8,128)(2,1)S(1)}, u32[]{:S(2)}, u32[]{:S(2)}) collective-permute-start(bf16[448,224]{1,0:T(8,128)(2,1)S(1)} %copy-done.17), channel_id=1, source_target_pairs={{0,1},{1,0},{2,3},{3,2},{4,5},{5,4},{6,7},{7,6},{8,9},{9,8},{10,11... | collective-permute-start | bytes 602120 | tf_op jit(solution)/shard_map/ppermute | solution.py:610
  107.8 29.0 %collective-permute-start.21 = (bf16[448,224]{1,0:T(8,128)(2,1)S(1)}, bf16[448,224]{1,0:T(8,128)(2,1)S(1)}, u32[]{:S(2)}, u32[]{:S(2)}) collective-permute-start(bf16[448,224]{1,0:T(8,128)(2,1)S(1)} %copy-done.17), channel_id=1, source_target_pairs={{0,2},{1,3},{2,0},{3,1},{4,6},{5,7},{6,4},{7,5},{8,10},{9,11},{10,... | collective-permute-start | bytes 602120 | tf_op jit(solution)/shard_map/ppermute | solution.py:610
  107.9 29.3 %collective-permute-start.22 = (bf16[448,224]{1,0:T(8,128)(2,1)S(1)}, bf16[448,224]{1,0:T(8,128)(2,1)}, u32[]{:S(2)}, u32[]{:S(2)}) collective-permute-start(bf16[448,224]{1,0:T(8,128)(2,1)S(1)} %copy-done.17), channel_id=1, source_target_pairs={{0,3},{1,2},{2,1},{3,0},{4,7},{5,6},{6,5},{7,4},{8,11},{9,10},{10,... | collective-permute-start | bytes 602120 | tf_op jit(solution)/shard_map/ppermute | solution.py:610
  146.4 23.4 %collective-permute-start.26 = (bf16[512,896]{1,0:T(8,128)(2,1)}, bf16[512,896]{1,0:T(8,128)(2,1)S(1)}, u32[]{:S(2)}, u32[]{:S(2)}) collective-permute-start(bf16[512,896]{1,0:T(8,128)(2,1)} %multiply_convert_fusion.x_low.x_high), channel_id=1, source_target_pairs={{0,1},{1,0},{2,3},{3,2},{4,5},{5,4},{6,7},{7,6},{8,9},{9,8},{10,11... | collective-permute-start | bytes 2752520 | tf_op jit(solution)/shard_map/ppermute | solution.py:610
  147.9 58.0 %collective-permute-start.24 = (bf16[512,896]{1,0:T(8,128)(2,1)}, bf16[512,896]{1,0:T(8,128)(2,1)}, u32[]{:S(2)}, u32[]{:S(2)}) collective-permute-start(bf16[512,896]{1,0:T(8,128)(2,1)} %multiply_convert_fusion.x_low.x_high), channel_id=1, source_target_pairs={{0,3},{1,2},{2,1},{3,0},{4,7},{5,6},{6,5},{7,4},{8,11},{9,10},{10,... | collective-permute-start | bytes 2752520 | tf_op jit(solution)/shard_map/ppermute | solution.py:610
  149.6 41.8 %collective-permute-start.25 = (bf16[512,896]{1,0:T(8,128)(2,1)}, bf16[512,896]{1,0:T(8,128)(2,1)}, u32[]{:S(2)}, u32[]{:S(2)}) collective-permute-start(bf16[512,896]{1,0:T(8,128)(2,1)} %multiply_convert_fusion.x_low.x_high), channel_id=1, source_target_pairs={{0,2},{1,3},{2,0},{3,1},{4,6},{5,7},{6,4},{7,5},{8,10},{9,11},{10,... | collective-permute-start | bytes 2752520 | tf_op jit(solution)/shard_map/ppermute | solution.py:610
  185.0 58.8 %collective-permute-start.27 = (bf16[512,896]{1,0:T(8,128)(2,1)}, bf16[512,896]{1,0:T(8,128)(2,1)S(1)}, u32[]{:S(2)}, u32[]{:S(2)}) collective-permute-start(bf16[512,896]{1,0:T(8,128)(2,1)} %get-tuple-element.133), channel_id=1, source_target_pairs={{0,1},{1,0},{2,3},{3,2},{4,5},{5,4},{6,7},{7,6},{8,9},{9,8},{10,11... | collective-permute-start | bytes 2752520 | tf_op jit(solution)/shard_map/ppermute | solution.py:610
  205.5 38.4 %collective-permute-start.28 = (bf16[512,896]{1,0:T(8,128)(2,1)}, bf16[512,896]{1,0:T(8,128)(2,1)}, u32[]{:S(2)}, u32[]{:S(2)}) collective-permute-start(bf16[512,896]{1,0:T(8,128)(2,1)} %get-tuple-element.134), channel_id=1, source_target_pairs={{0,2},{1,3},{2,0},{3,1},{4,6},{5,7},{6,4},{7,5},{8,10},{9,11},{10,... | collective-permute-start | bytes 2752520 | tf_op jit(solution)/shard_map/ppermute | solution.py:610
  219.9 24.0 %collective-permute-start.29 = (bf16[512,896]{1,0:T(8,128)(2,1)}, bf16[512,896]{1,0:T(8,128)(2,1)}, u32[]{:S(2)}, u32[]{:S(2)}) collective-permute-start(bf16[512,896]{1,0:T(8,128)(2,1)} %get-tuple-element.135), channel_id=1, source_target_pairs={{0,3},{1,2},{2,1},{3,0},{4,7},{5,6},{6,5},{7,4},{8,11},{9,10},{10,... | collective-permute-start | bytes 2752520 | tf_op jit(solution)/shard_map/ppermute | solution.py:610
  244.8 123.8 %reduce-scatter.5.cloned.1.call-start = ((), (), s32[]{:S(2)}) async-start(), calls=%async_computation.3 | async-start | bytes 4128768 | tf_op jit(solution)/shard_map/reduce_scatter | solution.py:880
  255.6 39.8 %collective-permute-start.30 = (bf16[512,896]{1,0:T(8,128)(2,1)}, bf16[512,896]{1,0:T(8,128)(2,1)S(1)}, u32[]{:S(2)}, u32[]{:S(2)}) collective-permute-start(bf16[512,896]{1,0:T(8,128)(2,1)} %get-tuple-element.146), channel_id=1, source_target_pairs={{0,1},{1,0},{2,3},{3,2},{4,5},{5,4},{6,7},{7,6},{8,9},{9,8},{10,11... | collective-permute-start | bytes 2752520 | tf_op jit(solution)/shard_map/ppermute | solution.py:610
  257.4 38.0 %collective-permute-start.31 = (bf16[512,896]{1,0:T(8,128)(2,1)}, bf16[512,896]{1,0:T(8,128)(2,1)}, u32[]{:S(2)}, u32[]{:S(2)}) collective-permute-start(bf16[512,896]{1,0:T(8,128)(2,1)} %get-tuple-element.147), channel_id=1, source_target_pairs={{0,2},{1,3},{2,0},{3,1},{4,6},{5,7},{6,4},{7,5},{8,10},{9,11},{10,... | collective-permute-start | bytes 2752520 | tf_op jit(solution)/shard_map/ppermute | solution.py:610
  257.7 37.7 %collective-permute-start.32 = (bf16[512,896]{1,0:T(8,128)(2,1)}, bf16[512,896]{1,0:T(8,128)(2,1)}, u32[]{:S(2)}, u32[]{:S(2)}) collective-permute-start(bf16[512,896]{1,0:T(8,128)(2,1)} %get-tuple-element.148), channel_id=1, source_target_pairs={{0,3},{1,2},{2,1},{3,0},{4,7},{5,6},{6,5},{7,4},{8,11},{9,10},{10,... | collective-permute-start | bytes 2752520 | tf_op jit(solution)/shard_map/ppermute | solution.py:610
  297.7 6.4 %collective-permute-start.33 = (bf16[1,2,256,256]{3,2,1,0:T(8,128)(2,1)S(1)}, bf16[1,2,256,256]{3,2,1,0:T(8,128)(2,1)S(1)}, u32[]{:S(2)}, u32[]{:S(2)}) collective-permute-start(bf16[1,2,256,256]{3,2,1,0:T(8,128)(2,1)S(1)} %get-tuple-element.224), channel_id=1, source_target_pairs={{0,1},{1,0},{2,3},{3,2},{4,5},{5,4},{6,7},{7,6},{8,9},{9,8},{10,11... | collective-permute-start | bytes 786440 | tf_op jit(solution)/shard_map/ppermute | solution.py:610
  299.5 9.2 %collective-permute-start.34 = (bf16[1,2,256,256]{3,2,1,0:T(8,128)(2,1)S(1)}, bf16[1,2,256,256]{3,2,1,0:T(8,128)(2,1)S(1)}, u32[]{:S(2)}, u32[]{:S(2)}) collective-permute-start(bf16[1,2,256,256]{3,2,1,0:T(8,128)(2,1)S(1)} %get-tuple-element.223), channel_id=1, source_target_pairs={{0,2},{1,3},{2,0},{3,1},{4,6},{5,7},{6,4},{7,5},{8,10},{9,11},{10,... | collective-permute-start | bytes 786440 | tf_op jit(solution)/shard_map/ppermute | solution.py:610
  299.8 8.9 %collective-permute-start.35 = (bf16[1,2,256,256]{3,2,1,0:T(8,128)(2,1)S(1)}, bf16[1,2,256,256]{3,2,1,0:T(8,128)(2,1)S(1)}, u32[]{:S(2)}, u32[]{:S(2)}) collective-permute-start(bf16[1,2,256,256]{3,2,1,0:T(8,128)(2,1)S(1)} %get-tuple-element.222), channel_id=1, source_target_pairs={{0,3},{1,2},{2,1},{3,0},{4,7},{5,6},{6,5},{7,4},{8,11},{9,10},{10,... | collective-permute-start | bytes 786440 | tf_op jit(solution)/shard_map/ppermute | solution.py:610
  326.0 23.7 %collective-permute-start.36 = (bf16[256,896]{1,0:T(8,128)(2,1)S(1)}, bf16[256,896]{1,0:T(8,128)(2,1)S(1)}, u32[]{:S(2)}, u32[]{:S(2)}) collective-permute-start(bf16[256,896]{1,0:T(8,128)(2,1)S(1)} %get-tuple-element.227), channel_id=1, source_target_pairs={{0,3},{1,2},{2,1},{3,0},{4,7},{5,6},{6,5},{7,4},{8,11},{9,10},{10,... | collective-permute-start | bytes 1376264 | tf_op jit(solution)/shard_map/ppermute | solution.py:610
  327.6 12.3 %collective-permute-start.40 = (f32[1,736]{1,0:T(1,128)S(1)}, f32[1,736]{1,0:T(1,128)S(1)}, u32[]{:S(2)}, u32[]{:S(2)}) collective-permute-start(f32[1,736]{1,0:T(1,128)S(1)} %get-tuple-element.261), channel_id=1, source_target_pairs={{0,3},{1,2},{2,1},{3,0},{4,7},{5,6},{6,5},{7,4},{8,11},{9,10},{10,... | collective-permute-start | bytes 8840 | tf_op jit(solution)/shard_map/ppermute | solution.py:610
  329.3 10.5 %collective-permute-start.39 = (f32[1,736]{1,0:T(1,128)S(1)}, f32[1,736]{1,0:T(1,128)S(1)}, u32[]{:S(2)}, u32[]{:S(2)}) collective-permute-start(f32[1,736]{1,0:T(1,128)S(1)} %get-tuple-element.262), channel_id=1, source_target_pairs={{0,2},{1,3},{2,0},{3,1},{4,6},{5,7},{6,4},{7,5},{8,10},{9,11},{10,... | collective-permute-start | bytes 8840 | tf_op jit(solution)/shard_map/ppermute | solution.py:610
  329.6 10.3 %collective-permute-start.38 = (f32[1,736]{1,0:T(1,128)S(1)}, f32[1,736]{1,0:T(1,128)S(1)}, u32[]{:S(2)}, u32[]{:S(2)}) collective-permute-start(f32[1,736]{1,0:T(1,128)S(1)} %get-tuple-element.260), channel_id=1, source_target_pairs={{0,1},{1,0},{2,3},{3,2},{4,5},{5,4},{6,7},{7,6},{8,9},{9,8},{10,11... | collective-permute-start | bytes 8840 | tf_op jit(solution)/shard_map/ppermute | solution.py:610
  331.9 18.7 %collective-permute-start.37 = (bf16[256,896]{1,0:T(8,128)(2,1)}, bf16[256,896]{1,0:T(8,128)(2,1)}, u32[]{:S(2)}, u32[]{:S(2)}) collective-permute-start(bf16[256,896]{1,0:T(8,128)(2,1)} %slice.222), channel_id=1, source_target_pairs={{0,3},{1,2},{2,1},{3,0},{4,7},{5,6},{6,5},{7,4},{8,11},{9,10},{10,... | collective-permute-start | bytes 1376264 | tf_op jit(solution)/shard_map/ppermute | solution.py:610
  355.1 33.0 %collective-permute-start.47 = (bf16[112,608]{1,0:T(8,128)(2,1)S(1)}, bf16[112,608]{1,0:T(8,128)(2,1)S(1)}, u32[]{:S(2)}, u32[]{:S(2)}) collective-permute-start(bf16[112,608]{1,0:T(8,128)(2,1)S(1)} %get-tuple-element.240), channel_id=1, source_target_pairs={{0,0},{1,8},{2,16},{3,24},{4,4},{5,12},{6,20},{7,28},{8,1},{9,9},{... | collective-permute-start | bytes 408584 | tf_op jit(solution)/shard_map/ppermute | solution.py:667
  358.8 29.3 %collective-permute-start.48 = (bf16[112,608]{1,0:T(8,128)(2,1)S(1)}, bf16[112,608]{1,0:T(8,128)(2,1)S(1)}, u32[]{:S(2)}, u32[]{:S(2)}) collective-permute-start(bf16[112,608]{1,0:T(8,128)(2,1)S(1)} %get-tuple-element.239), channel_id=1, source_target_pairs={{0,4},{1,12},{2,20},{3,28},{4,0},{5,8},{6,16},{7,24},{8,5},{9,13},... | collective-permute-start | bytes 408584 | tf_op jit(solution)/shard_map/ppermute | solution.py:667
  369.7 18.5 %collective-permute-start.44 = (bf16[112,512]{1,0:T(8,128)(2,1)S(1)}, bf16[112,512]{1,0:T(8,128)(2,1)S(1)}, u32[]{:S(2)}, u32[]{:S(2)}) collective-permute-start(bf16[112,512]{1,0:T(8,128)(2,1)S(1)} %get-tuple-element.243), channel_id=1, source_target_pairs={{0,1},{1,0},{2,3},{3,2},{4,5},{5,4},{6,7},{7,6},{8,9},{9,8},{10,11... | collective-permute-start | bytes 344072 | tf_op jit(solution)/shard_map/ppermute | solution.py:610
  372.3 18.1 %collective-permute-start.45 = (bf16[112,512]{1,0:T(8,128)(2,1)S(1)}, bf16[112,512]{1,0:T(8,128)(2,1)S(1)}, u32[]{:S(2)}, u32[]{:S(2)}) collective-permute-start(bf16[112,512]{1,0:T(8,128)(2,1)S(1)} %get-tuple-element.242), channel_id=1, source_target_pairs={{0,2},{1,3},{2,0},{3,1},{4,6},{5,7},{6,4},{7,5},{8,10},{9,11},{10,... | collective-permute-start | bytes 344072 | tf_op jit(solution)/shard_map/ppermute | solution.py:610
  386.9 5.7 %collective-permute-start.46 = (bf16[112,512]{1,0:T(8,128)(2,1)S(1)}, bf16[112,512]{1,0:T(8,128)(2,1)S(1)}, u32[]{:S(2)}, u32[]{:S(2)}) collective-permute-start(bf16[112,512]{1,0:T(8,128)(2,1)S(1)} %get-tuple-element.241), channel_id=1, source_target_pairs={{0,3},{1,2},{2,1},{3,0},{4,7},{5,6},{6,5},{7,4},{8,11},{9,10},{10,... | collective-permute-start | bytes 344072 | tf_op jit(solution)/shard_map/ppermute | solution.py:610
  (37 other events, 178.3 us)
Sparse Core Ops, SparseCore 0:
  10.2 54.2 all-gather.4
  101.4 30.0 all-gather.6
  244.9 73.0 reduce-scatter.2
  322.6 46.0 reduce-scatter.4
